TPU v7x, 32 devices: a whole 2x2x4 slice. The times are simulated.
32 devices in a mesh: replica: 8 (over z, core), expert: 4 (over y, x).
Axes of the slice: x: 2, y: 2, z: 4, core: 2. Of those that a mesh axis runs over, the one named last changes fastest.
Arguments:
- tokens: float32 [6144, 2048], P(('replica', 'expert')), may hold values from -6 to 6
- expert_ids: int32 [6144, 2], P(('replica', 'expert')), may hold values from 0 to 3, all different within a row; in each aligned block of 192 rows (0 to 191, 192 to 383, ...) at most 144 rows name the same one
- combine_weights: float32 [6144, 2], P(('replica', 'expert')), may hold values from 0.3 to 1
- gate_weight: bfloat16 [4, 2048, 768], P('expert', 'replica'), may hold values from -0.125 to 0.125
- up_weight: bfloat16 [4, 2048, 768], P('expert', 'replica'), may hold values from -0.125 to 0.125
- down_weight: bfloat16 [4, 2048, 768], P('expert', 'replica'), may hold values from -0.21875 to 0.21875
- norm_gain: float32 [2048], replicated, may hold values from 0.1 to 1.9
Outputs:
- normed: float32 [6144, 2048], P(('replica', 'expert'))
Inputs may be any that keep to these rules, and one draw needn't show every extreme that they name: `expert_ids`: each row names two different experts. In each aligned block of 192 rows (the rows of one device) no expert is named by more than 144 rows, a bound that some block reaches.
All inputs are finite; a program needn't handle non-finite values.
Results may differ from a plain program's by a relative error of at most 0.0027.
Values may be sent and summed in bfloat16 or wider, within the bound.
No kernel may reach another device: no remote copies, remote signals or barrier semaphores. Data moves between devices by JAX's collectives and lax.ppermute only.
A program may use at most 64 MiB of HBM per device.

v0:
```python
import functools

import jax
import jax.numpy as jnp
from jax import lax
from jax.experimental import pallas as pl
from jax.experimental.pallas import tpu as pltpu
from jax.sharding import PartitionSpec as P


F32, BF16 = jnp.float32, jnp.bfloat16
ANY = pl.BlockSpec(memory_space=pl.ANY)
VMEM = pl.BlockSpec(memory_space=pltpu.VMEM)
CHAIN = 4


def slot_positions(expert_ids, experts, capacity):
    count = expert_ids.shape[0]
    onehot = (expert_ids[:, :, None] == jnp.arange(experts, dtype=jnp.int32)[None, None, :]).astype(
        jnp.int32
    )
    onehot = onehot.reshape(count * 2, experts)
    before = jnp.cumsum(onehot, axis=0) - onehot
    ranks = jnp.sum(before * onehot, axis=1).reshape(count, 2)
    return expert_ids * capacity + ranks


def place_rows(tokens, slot_index, total):
    iota_slots = jnp.arange(total, dtype=jnp.int32)[:, None]
    select = (slot_index[None, :, 0] == iota_slots) | (slot_index[None, :, 1] == iota_slots)
    return jnp.dot(
        select.astype(BF16), tokens.astype(BF16), preferred_element_type=F32
    ).astype(BF16)


def expert_ffn(rows, gate, upward, downward):
    gate_out = jnp.dot(rows, gate, preferred_element_type=F32)
    up_out = jnp.dot(rows, upward, preferred_element_type=F32)
    hidden = (jax.nn.silu(gate_out) * up_out).astype(BF16)
    result = lax.dot_general(hidden, downward, (((1,), (1,)), ((), ())), preferred_element_type=F32)
    return result.astype(BF16)


def combine_rows(tokens, back, slot_index, weights, gain):
    picked = back[slot_index].astype(F32)
    summed = jnp.sum(picked * weights[:, :, None], axis=1)
    mixed = tokens + summed
    scale = lax.rsqrt(jnp.mean(mixed * mixed, axis=-1) + 1e-06)
    return mixed * scale[:, None] * gain[None, :]


def general(tokens, expert_ids, combine_weights, gate_weight, up_weight, down_weight, norm_gain):
    experts = lax.axis_size("expert")
    count, width = tokens.shape
    capacity = 3 * count // experts
    slot_index = slot_positions(expert_ids, experts, capacity)
    placed = place_rows(tokens, slot_index, experts * capacity).reshape(experts, capacity, width)
    gate_all, up_all, down_all = (
        lax.all_gather(w, "replica", axis=1, tiled=True)
        for w in (gate_weight, up_weight, down_weight)
    )
    received = lax.all_to_all(placed, "expert", split_axis=0, concat_axis=0, tiled=True)
    rows = received.reshape(experts * capacity, width)
    outs = expert_ffn(rows, gate_all[0], up_all[0], down_all[0])
    back = lax.all_to_all(
        outs.reshape(experts, capacity, width), "expert", split_axis=0, concat_axis=0, tiled=True
    )
    back = back.reshape(experts * capacity, width)
    return combine_rows(tokens, back, slot_index, combine_weights, norm_gain)


def slice_order():
    replica = lax.axis_index("replica")
    chip, core = replica // 2, replica % 2
    low = chip < CHAIN // 2
    one = jnp.where(chip % 2 == 0, chip + 1, chip - 1)
    chips = (chip, one, jnp.where(low, 2, 1), jnp.where(low, 3, 0))
    return [2 * c + s for c in chips for s in (core, 1 - core)]


def call(kernel, out_shape, args, specs, scratch=(), flops=0, moved=0, limit=16 << 20):
    return pl.pallas_call(
        kernel,
        out_shape=out_shape,
        in_specs=list(specs),
        out_specs=jax.tree.map(lambda _: VMEM, out_shape),
        scratch_shapes=list(scratch),
        cost_estimate=pl.CostEstimate(flops=flops, bytes_accessed=moved, transcendentals=0),
        compiler_params=pltpu.CompilerParams(vmem_limit_bytes=limit),
    )(*args)


def place_kernel(experts, capacity, ids_ref, w_ref, tok_ref, *refs):
    outs, c_ref, tokp = refs[:experts], refs[experts], refs[experts + 1]
    count, width = tok_ref.shape
    part = width // (2 * CHAIN)
    me = lax.axis_index("expert")
    pad = 8
    expert = lax.broadcasted_iota(jnp.int32, (pad, count), 0) ^ me
    first, second = ids_ref[0:1, :] == expert, ids_ref[1:2, :] == expert
    named = first | second
    weight = jnp.where(first, w_ref[0:1, :], jnp.where(second, w_ref[1:2, :], 0.0))
    high = weight.astype(BF16)
    low = (weight - high.astype(F32)).astype(BF16)
    mask = jnp.where(named, 1.0, 0.0).astype(BF16)
    r = lax.broadcasted_iota(jnp.int32, (count, count), 0)
    c = lax.broadcasted_iota(jnp.int32, (count, count), 1)
    upper = jnp.where(r < c, 1.0, 0.0).astype(BF16)
    lower = jnp.where(c < r, 1.0, 0.0).astype(BF16)
    eye = jnp.where(r == c, 1.0, 0.0).astype(BF16)
    nt = (((1,), (1,)), ((), ()))

    def turned(a, b):
        return lax.dot_general(a, b, nt, preferred_element_type=F32)

    rank = jnp.where(named, jnp.dot(mask, upper, preferred_element_type=F32), -1.0)
    for place, s in enumerate(slice_order()):
        tokp[:, place * part : (place + 1) * part] = tok_ref[
            :, pl.ds(pl.multiple_of(s * part, part), part)
        ].astype(BF16)
    slot = lax.broadcasted_iota(jnp.int32, (capacity, count), 0).astype(F32)
    for m in range(experts):
        select = jnp.where(slot == rank[m : m + 1, :], 1.0, 0.0).astype(BF16)
        outs[m][...] = jnp.dot(select, tokp[...], preferred_element_type=F32).astype(BF16)
    column = lax.broadcasted_iota(jnp.int32, (count, experts * capacity), 1).astype(F32)
    rank_c = jnp.where(turned(eye, mask) > 0.5, turned(lower, mask), -float(experts * capacity))
    for half, part_w in enumerate((high, low)):
        w_c = turned(eye, part_w)
        total = jnp.zeros((count, experts * capacity), F32)
        for m in range(experts):
            hit = column == rank_c[:, m : m + 1] + float(m * capacity)
            total = jnp.where(hit, w_c[:, m : m + 1], total)
        c_ref[half * count : (half + 1) * count, :] = total.astype(BF16)


def copies(pairs, sems):
    out = []
    for i, (src, dst) in enumerate(pairs):
        copy = pltpu.make_async_copy(src, dst, sems.at[i])
        copy.start()
        out.append(copy)
    return out


def gate_up_kernel(experts, first, slices, last, *refs):
    blocks, refs = refs[:experts], refs[experts:]
    gates, ups, refs = refs[:slices], refs[slices : 2 * slices], refs[2 * slices :]
    if last:
        acc_g, acc_u, out, rows, wg, wu, ag, au, sems = refs
    else:
        out_g, out_u, rows, wg, wu, sems = refs
    capacity = blocks[0].shape[0]
    part = gates[0].shape[0]
    lo, n = first * part, slices * part
    pairs = [
        (b.at[:, pl.ds(lo, n)], rows.at[pl.ds(m * capacity, capacity), :])
        for m, b in enumerate(blocks)
    ]
    pairs += [(g, wg.at[pl.ds(i * part, part), :]) for i, g in enumerate(gates)]
    n_gate = len(pairs)
    pairs += [(u, wu.at[pl.ds(i * part, part), :]) for i, u in enumerate(ups)]
    if last:
        pairs += [(acc_g, ag), (acc_u, au)]
    started = copies(pairs, sems)
    for copy in started[:n_gate]:
        copy.wait()
    gate = jnp.dot(rows[...], wg[...], preferred_element_type=F32)
    if not last:
        out_g[...] = gate
        for copy in started[n_gate:]:
            copy.wait()
        out_u[...] = jnp.dot(rows[...], wu[...], preferred_element_type=F32)
        return
    for copy in started[n_gate:]:
        copy.wait()
    ag[...] += gate
    up = au[...] + jnp.dot(rows[...], wu[...], preferred_element_type=F32)
    gate = ag[...]
    out[...] = (gate / (1.0 + jnp.exp(-gate)) * up).astype(BF16)


def down_kernel(experts, capacity, hidden, own, other, *outs):
    part = own.shape[0]
    for half, w in enumerate((own, other)):
        result = lax.dot_general(
            hidden[...], w[...], (((1,), (1,)), ((), ())), preferred_element_type=F32
        ).astype(BF16)
        for m in range(experts):
            outs[m][:, half * part : (half + 1) * part] = result[m * capacity : (m + 1) * capacity]


def chunk(stages, blocks, tokens, c_ref, back, tok, sems):
    experts = len(blocks) // len(stages)
    capacity, wide = blocks[0].shape
    part = wide // 2
    order = slice_order()
    pairs = []
    for i, stage in enumerate(stages):
        pairs += [
            (b, back.at[pl.ds(m * capacity, capacity), pl.ds(i * wide, wide)])
            for m, b in enumerate(blocks[i * experts : (i + 1) * experts])
        ]
        pairs += [
            (
                tokens.at[:, pl.ds(pl.multiple_of(order[2 * stage + h] * part, part), part)],
                tok.at[:, pl.ds(i * wide + h * part, part)],
            )
            for h in range(2)
        ]
    for copy in copies(pairs, sems):
        copy.wait()
    both = jnp.dot(c_ref[...], back[...], preferred_element_type=F32)
    count = tok.shape[0]
    here = tok[...] + (both[:count] + both[count:])
    return here, jnp.sum(here * here, axis=1, keepdims=True)


def combine_kernel(stages, n_blocks, *refs):
    blocks, (tokens, c_ref, out, square, back, tok, sems) = refs[:n_blocks], refs[n_blocks:]
    here, total = chunk(stages, blocks, tokens, c_ref, back, tok, sems)
    out[...] = here
    square[...] = jnp.broadcast_to(total, square.shape)


def finish_kernel(stages, n_blocks, *refs):
    blocks, refs = refs[:n_blocks], refs[n_blocks:]
    tokens, c_ref, gain, mixed, square, out, back, tok, sems = refs
    here, total = chunk(stages, blocks, tokens, c_ref, back, tok, sems)
    width = out.shape[1]
    wide = here.shape[1]
    part = wide // 2
    scale = lax.rsqrt((total + square[:, 0:1]) * (1.0 / width) + 1e-06)
    for place, s in enumerate(slice_order()):
        lo = place * part
        value = mixed[:, lo : lo + part] if lo < width - wide else here[:, lo - width + wide :][:, :part]
        at = pl.ds(pl.multiple_of(s * part, part), part)
        out[:, at] = value * scale * gain[:, at]


def staged(tokens, expert_ids, combine_weights, gate_weight, up_weight, down_weight, norm_gain):
    return layer(
        tokens, expert_ids, combine_weights, gate_weight[0], up_weight[0], down_weight[0], norm_gain
    )


MIDDLE = [(1, 2), (2, 1)]
PAIR = [(0, 1), (1, 0), (2, 3), (3, 2)]
INWARD = [(0, 1), (3, 2)]
OUTWARD = [(1, 0), (2, 3)]


def layer(tokens, expert_ids, combine_weights, gate, up, down, norm_gain):
    experts = lax.axis_size("expert")
    count, width = tokens.shape
    capacity = 3 * count // experts
    slots = experts * capacity
    part, ff = gate.shape
    chip = lax.axis_index("replica") // 2
    end = (chip == 0) | (chip == CHAIN - 1)

    def along(x, pairs):
        devices = [(2 * a + c, 2 * b + c) for a, b in pairs for c in (0, 1)]
        return lax.ppermute(x, "replica", devices)

    def swap(x):
        return lax.ppermute(x, "replica", [(r, r ^ 1) for r in range(2 * CHAIN)])

    def across(x, m):
        return lax.ppermute(x, "expert", [(e, e ^ m) for e in range(experts)])

    def line(w, split):
        if split:
            inner = along(w, INWARD)
            outer = along(w, OUTWARD)
            one = jnp.where(end, outer, inner)
        else:
            inner = one = along(w, PAIR)
        mid = along(w, MIDDLE)
        mid_in = along(inner, MIDDLE)
        two = jnp.where(end, along(mid, OUTWARD), mid)
        three = jnp.where(end, along(mid_in, OUTWARD), mid_in)
        return [x for v in (w, one, two, three) for x in (v, swap(v))]

    g_all, u_all, d_all = line(gate, False), line(up, False), line(down, True)

    *placed, mix = call(
        functools.partial(place_kernel, experts, capacity),
        [jax.ShapeDtypeStruct((capacity, width), BF16)] * experts
        + [jax.ShapeDtypeStruct((2 * count, slots), BF16)],
        (expert_ids.T, combine_weights.T, tokens),
        [VMEM] * 3,
        [pltpu.VMEM((count, width), BF16)],
        flops=2 * slots * count * width,
        moved=count * width * 4 + slots * width * 2,
    )
    rows = [placed[0]] + [across(placed[m], m) for m in range(1, experts)]

    def gate_up(first, slices, acc):
        last = acc is not None
        n = slices * part
        flat = jax.ShapeDtypeStruct((slots, ff), F32)
        scratch = [
            pltpu.VMEM((slots, n), BF16),
            pltpu.VMEM((n, ff), BF16),
            pltpu.VMEM((n, ff), BF16),
        ]
        if last:
            scratch += [pltpu.VMEM((slots, ff), F32)] * 2
        args = (*rows, *g_all[first : first + slices], *u_all[first : first + slices])
        args += tuple(acc) if last else ()
        return call(
            functools.partial(gate_up_kernel, experts, first, slices, last),
            jax.ShapeDtypeStruct((slots, ff), BF16) if last else [flat, flat],
            args,
            [ANY] * len(args),
            scratch + [pltpu.SemaphoreType.DMA((experts + 2 * slices + 2 * last,))],
            flops=4 * slots * n * ff,
            moved=slots * n * 2 + 4 * n * ff + slots * ff * 8,
        )

    acc = gate_up(0, 6, None)
    hidden = gate_up(6, 2, acc)

    backs = []
    for stage in range(CHAIN):
        outs = call(
            functools.partial(down_kernel, experts, capacity),
            [jax.ShapeDtypeStruct((capacity, 2 * part), BF16)] * experts,
            (hidden, d_all[2 * stage], d_all[2 * stage + 1]),
            [VMEM] * 3,
            flops=4 * slots * ff * part,
            moved=slots * ff * 2 + 4 * part * ff + slots * part * 4,
        )
        backs.append([outs[0]] + [across(outs[m], m) for m in range(1, experts)])

    def combine(kernel, stages, more, shape):
        blocks = [b for s in stages for b in backs[s]]
        wide = 2 * part * len(stages)
        return call(
            functools.partial(kernel, stages, len(blocks)),
            shape,
            (*blocks, tokens, mix, *more),
            [ANY] * (len(blocks) + 1) + [VMEM] * (1 + len(more)),
            [
                pltpu.VMEM((slots, wide), BF16),
                pltpu.VMEM((count, wide), F32),
                pltpu.SemaphoreType.DMA((len(blocks) + 2 * len(stages),)),
            ],
            flops=4 * count * slots * wide,
            moved=slots * wide * 2 + count * wide * 8,
        )

    early = tuple(range(CHAIN - 1))
    mixed = combine(
        combine_kernel,
        early,
        (),
        [
            jax.ShapeDtypeStruct((count, 2 * part * len(early)), F32),
            jax.ShapeDtypeStruct((count, 128), F32),
        ],
    )
    return combine(
        finish_kernel,
        (CHAIN - 1,),
        (norm_gain.reshape(1, width), *mixed),
        jax.ShapeDtypeStruct((count, width), F32),
    )


def solution(mesh):
    replicas, experts = mesh.shape["replica"], mesh.shape["expert"]
    fits = replicas == 2 * CHAIN and experts & (experts - 1) == 0 and experts <= 8
    placed = (
        P(("replica", "expert"), None),
        P(("replica", "expert"), None),
        P(("replica", "expert"), None),
        P("expert", "replica", None),
        P("expert", "replica", None),
        P("expert", "replica", None),
        P(),
    )
    return jax.shard_map(
        staged if fits else general,
        mesh=mesh,
        in_specs=placed,
        out_specs=P(("replica", "expert"), None),
        check_vma=False,
    )
```

profile of v0, /device:TPU:0, one launch (start us, length us, event | category | flops | bytes accessed | tf_op | source)
XLA Modules:
  0.0 136.9 jit_solution(15330070881580199593)
XLA Ops:
  0.0 1.4 %collective-permute-start.13 = (bf16[256,768]{1,0:T(8,128)(2,1)}, bf16[256,768]{1,0:T(8,128)(2,1)}, u32[]{:S(2)}, u32[]{:S(2)}) collective-permute-start(bf16[256,768]{1,0:T(8,128)(2,1)} %bitcast.7), channel_id=1, source_target_pairs={{8,16},{12,20},{16,8},{20,12},{9,17},{13,21},{17,9},{21,13},{10,18... | collective-permute-start | bytes 1179656 | tf_op jit(solution)/shard_map/ppermute | solution.py:263
  2.1 6.9 %collective-permute-start.3 = (bf16[256,768]{1,0:T(8,128)(2,1)}, bf16[256,768]{1,0:T(8,128)(2,1)S(1)}, u32[]{:S(2)}, u32[]{:S(2)}) collective-permute-start(bf16[256,768]{1,0:T(8,128)(2,1)} %bitcast.8), channel_id=1, source_target_pairs={{0,8},{4,12},{8,0},{12,4},{16,24},{20,28},{24,16},{28,20},{1,9},{5... | collective-permute-start | bytes 1179656 | tf_op jit(solution)/shard_map/ppermute | solution.py:263
  10.3 8.9 %collective-permute-done.3.refs_6_ = bf16[256,768]{1,0:T(8,128)(2,1)S(1)} collective-permute-done((bf16[256,768]{1,0:T(8,128)(2,1)}, bf16[256,768]{1,0:T(8,128)(2,1)S(1)}, u32[]{:S(2)}, u32[]{:S(2)}) %collective-permute-start.3) | collective-permute-done | bytes 393248 | tf_op jit(solution)/shard_map/ppermute | solution.py:263
  19.1 11.4 %collective-permute-start.21 = (bf16[256,768]{1,0:T(8,128)(2,1)}, bf16[256,768]{1,0:T(8,128)(2,1)}, u32[]{:S(2)}, u32[]{:S(2)}) collective-permute-start(bf16[256,768]{1,0:T(8,128)(2,1)} %bitcast.16), channel_id=1, source_target_pairs={{0,8},{4,12},{24,16},{28,20},{1,9},{5,13},{25,17},{29,21},{2,10},{... | collective-permute-start | bytes 1179656 | tf_op jit(solution)/shard_map/ppermute | solution.py:263
  30.6 1.3 collective-permute-start.32
  31.9 1.4 %copy-done = f32[192,2048]{1,0:T(8,128)S(1)} copy-done((f32[192,2048]{1,0:T(8,128)S(1)}, f32[192,2048]{1,0:T(8,128)}, u32[]{:S(2)}) %copy-start) | copy-done | bytes 1572888
  34.7 1.4 %shard_map.73 = (bf16[144,2048]{1,0:T(8,128)(2,1)S(1)}, bf16[144,2048]{1,0:T(8,128)(2,1)}, bf16[144,2048]{1,0:T(8,128)(2,1)S(1)}, bf16[144,2048]{1,0:T(8,128)(2,1)S(1)}, bf16[384,576]{1,0:T(8,128)(2,1)S(1)}) custom-call(s32[2,192]{1,0:T(2,128)S(1)} %bitcast.20, f32[2,192]{1,0:T(2,128)S(1)} %bitcast.21, f32[192,2048]{1,0:T(8,128)S(1)} %copy-done), custom_call_target="tpu_custom_call" | custom-call | flops 452984832 | bytes 3932160 | tf_op jit(solution)/shard_map/pallas_call | solution.py:82
  36.1 0.7 copy-done.10
  36.9 1.5 %collective-permute-start = (bf16[144,2048]{1,0:T(8,128)(2,1)}, bf16[144,2048]{1,0:T(8,128)(2,1)S(1)}, u32[]{:S(2)}, u32[]{:S(2)}) collective-permute-start(bf16[144,2048]{1,0:T(8,128)(2,1)} %get-tuple-element.31), channel_id=1, source_target_pairs={{0,1},{1,0},{2,3},{3,2},{4,5},{5,4},{6,7},{7,6},{8,9},{9,8},{10,11... | collective-permute-start | bytes 1769480 | tf_op jit(solution)/shard_map/ppermute | solution.py:269
  38.4 0.8 copy-done.12
  39.1 1.3 collective-permute-start.14
  40.4 1.6 %collective-permute-start.1 = (bf16[144,2048]{1,0:T(8,128)(2,1)S(1)}, bf16[144,2048]{1,0:T(8,128)(2,1)S(1)}, u32[]{:S(2)}, u32[]{:S(2)}) collective-permute-start(bf16[144,2048]{1,0:T(8,128)(2,1)S(1)} %get-tuple-element.32), channel_id=1, source_target_pairs={{0,2},{1,3},{2,0},{3,1},{4,6},{5,7},{6,4},{7,5},{8,10},{9,11},{10,... | collective-permute-start | bytes 1769480 | tf_op jit(solution)/shard_map/ppermute | solution.py:269
  42.0 1.4 %collective-permute-start.19 = (bf16[256,768]{1,0:T(8,128)(2,1)}, bf16[256,768]{1,0:T(8,128)(2,1)S(1)}, u32[]{:S(2)}, u32[]{:S(2)}) collective-permute-start(bf16[256,768]{1,0:T(8,128)(2,1)} %copy-done.16), channel_id=1, source_target_pairs={{8,0},{12,4},{16,24},{20,28},{9,1},{13,5},{17,25},{21,29},{10,2},{... | collective-permute-start | bytes 1179656 | tf_op jit(solution)/shard_map/ppermute | solution.py:263
  43.5 0.7 collective-permute-start.8
  44.2 1.1 broadcast_select_fusion.1.own
  45.2 5.5 %collective-permute-done.refs_1_ = bf16[144,2048]{1,0:T(8,128)(2,1)S(1)} collective-permute-done((bf16[144,2048]{1,0:T(8,128)(2,1)}, bf16[144,2048]{1,0:T(8,128)(2,1)S(1)}, u32[]{:S(2)}, u32[]{:S(2)}) %collective-permute-start) | collective-permute-done | bytes 589856 | tf_op jit(solution)/shard_map/ppermute | solution.py:269
  51.4 2.6 %collective-permute-done.14 = bf16[256,768]{1,0:T(8,128)(2,1)} collective-permute-done((bf16[256,768]{1,0:T(8,128)(2,1)}, bf16[256,768]{1,0:T(8,128)(2,1)}, u32[]{:S(2)}, u32[]{:S(2)}) %collective-permute-start.14) | collective-permute-done | bytes 393248 | tf_op jit(solution)/shard_map/ppermute | solution.py:263
  54.0 1.3 collective-permute-start.38
  55.3 1.1 broadcast_select_fusion.4.refs_8_
  56.4 1.6 %collective-permute-start.2 = (bf16[144,2048]{1,0:T(8,128)(2,1)S(1)}, bf16[144,2048]{1,0:T(8,128)(2,1)S(1)}, u32[]{:S(2)}, u32[]{:S(2)}) collective-permute-start(bf16[144,2048]{1,0:T(8,128)(2,1)S(1)} %get-tuple-element.33), channel_id=1, source_target_pairs={{0,3},{1,2},{2,1},{3,0},{4,7},{5,6},{6,5},{7,4},{8,11},{9,10},{10,... | collective-permute-start | bytes 1769480 | tf_op jit(solution)/shard_map/ppermute | solution.py:269
  57.9 4.4 %collective-permute-done.19 = bf16[256,768]{1,0:T(8,128)(2,1)S(1)} collective-permute-done((bf16[256,768]{1,0:T(8,128)(2,1)}, bf16[256,768]{1,0:T(8,128)(2,1)S(1)}, u32[]{:S(2)}, u32[]{:S(2)}) %collective-permute-start.19) | collective-permute-done | bytes 393248 | tf_op jit(solution)/shard_map/ppermute | solution.py:263
  63.0 1.3 collective-permute-start.9
  64.5 6.3 %collective-permute-done.38 = bf16[256,768]{1,0:T(8,128)(2,1)S(1)} collective-permute-done((bf16[256,768]{1,0:T(8,128)(2,1)}, bf16[256,768]{1,0:T(8,128)(2,1)S(1)}, u32[]{:S(2)}, u32[]{:S(2)}) %collective-permute-start.38) | collective-permute-done | bytes 393248 | tf_op jit(solution)/shard_map/ppermute | solution.py:263
  70.8 1.3 collective-permute-start.5
  72.3 6.9 %collective-permute-done.9 = bf16[256,768]{1,0:T(8,128)(2,1)S(1)} collective-permute-done((bf16[256,768]{1,0:T(8,128)(2,1)S(1)}, bf16[256,768]{1,0:T(8,128)(2,1)S(1)}, u32[]{:S(2)}, u32[]{:S(2)}) %collective-permute-start.9) | collective-permute-done | bytes 393248 | tf_op jit(solution)/shard_map/ppermute | solution.py:263
  79.2 1.5 %collective-permute-start.23 = (bf16[256,768]{1,0:T(8,128)(2,1)S(1)}, bf16[256,768]{1,0:T(8,128)(2,1)S(1)}, u32[]{:S(2)}, u32[]{:S(2)}) collective-permute-start(bf16[256,768]{1,0:T(8,128)(2,1)S(1)} %collective-permute-done.22), channel_id=1, source_target_pairs={{8,0},{12,4},{16,24},{20,28},{9,1},{13,5},{17,25},{21,29},{10,2},{... | collective-permute-start | bytes 1179656 | tf_op jit(solution)/shard_map/ppermute | solution.py:263
  81.3 6.3 %collective-permute-done.5 = bf16[256,768]{1,0:T(8,128)(2,1)S(1)} collective-permute-done((bf16[256,768]{1,0:T(8,128)(2,1)S(1)}, bf16[256,768]{1,0:T(8,128)(2,1)S(1)}, u32[]{:S(2)}, u32[]{:S(2)}) %collective-permute-start.5) | collective-permute-done | bytes 393248 | tf_op jit(solution)/shard_map/ppermute | solution.py:263
  88.2 5.0 %collective-permute-done.23 = bf16[256,768]{1,0:T(8,128)(2,1)S(1)} collective-permute-done((bf16[256,768]{1,0:T(8,128)(2,1)S(1)}, bf16[256,768]{1,0:T(8,128)(2,1)S(1)}, u32[]{:S(2)}, u32[]{:S(2)}) %collective-permute-start.23) | collective-permute-done | bytes 393248 | tf_op jit(solution)/shard_map/ppermute | solution.py:263
  94.4 6.5 %shard_map.74 = (f32[576,768]{1,0:T(8,128)S(1)}, f32[576,768]{1,0:T(8,128)S(1)}) custom-call(bf16[144,2048]{1,0:T(8,128)(2,1)S(1)} %get-tuple-element.30.refs_0_, bf16[144,2048]{1,0:T(8,128)(2,1)S(1)} %collective-permute-done.refs_1_, bf16[144,2048]{1,0:T(8,128)(2,1)S(1)} %collective-permute-done.1.refs_2_, ...), custom_call_target="tpu_custom_call" | custom-call | flops 2717908992 | bytes 10027008 | tf_op jit(solution)/shard_map/pallas_call | solution.py:82
  100.9 3.2 %shard_map.75.hidden = bf16[576,768]{1,0:T(8,128)(2,1)S(1)} custom-call(bf16[144,2048]{1,0:T(8,128)(2,1)S(1)} %get-tuple-element.30.refs_0_, bf16[144,2048]{1,0:T(8,128)(2,1)S(1)} %collective-permute-done.refs_1_, bf16[144,2048]{1,0:T(8,128)(2,1)S(1)} %collective-permute-done.1.refs_2_, bf16[144,2048]{1,0:T(8,128)(2,1)S(1)} %collective-permute-done.2.refs_3_, ...), custom_call_target="tpu_custom_call" | custom-call | flops 905969664 | bytes 5701632 | tf_op jit(solution)/shard_map/pallas_call | solution.py:82
  104.9 1.0 collective-permute-start.40
  105.9 1.5 %collective-permute-start.41 = (bf16[144,512]{1,0:T(8,128)(2,1)S(1)}, bf16[144,512]{1,0:T(8,128)(2,1)S(1)}, u32[]{:S(2)}, u32[]{:S(2)}) collective-permute-start(bf16[144,512]{1,0:T(8,128)(2,1)S(1)} %get-tuple-element.51), channel_id=1, source_target_pairs={{0,2},{1,3},{2,0},{3,1},{4,6},{5,7},{6,4},{7,5},{8,10},{9,11},{10,... | collective-permute-start | bytes 442376 | tf_op jit(solution)/shard_map/ppermute | solution.py:269
  107.4 1.0 collective-permute-start.42
  109.1 1.0 collective-permute-start.34
  110.8 1.6 %collective-permute-start.35 = (bf16[144,512]{1,0:T(8,128)(2,1)S(1)}, bf16[144,512]{1,0:T(8,128)(2,1)S(1)}, u32[]{:S(2)}, u32[]{:S(2)}) collective-permute-start(bf16[144,512]{1,0:T(8,128)(2,1)S(1)} %get-tuple-element.47), channel_id=1, source_target_pairs={{0,2},{1,3},{2,0},{3,1},{4,6},{5,7},{6,4},{7,5},{8,10},{9,11},{10,... | collective-permute-start | bytes 442376 | tf_op jit(solution)/shard_map/ppermute | solution.py:269
  112.4 1.2 collective-permute-start.36
  114.1 1.2 collective-permute-start.29
  115.8 2.1 %collective-permute-start.30 = (bf16[144,512]{1,0:T(8,128)(2,1)S(1)}, bf16[144,512]{1,0:T(8,128)(2,1)S(1)}, u32[]{:S(2)}, u32[]{:S(2)}) collective-permute-start(bf16[144,512]{1,0:T(8,128)(2,1)S(1)} %get-tuple-element.43), channel_id=1, source_target_pairs={{0,2},{1,3},{2,0},{3,1},{4,6},{5,7},{6,4},{7,5},{8,10},{9,11},{10,... | collective-permute-start | bytes 442376 | tf_op jit(solution)/shard_map/ppermute | solution.py:269
  118.0 1.9 %collective-permute-start.31 = (bf16[144,512]{1,0:T(8,128)(2,1)S(1)}, bf16[144,512]{1,0:T(8,128)(2,1)S(1)}, u32[]{:S(2)}, u32[]{:S(2)}) collective-permute-start(bf16[144,512]{1,0:T(8,128)(2,1)S(1)} %get-tuple-element.44), channel_id=1, source_target_pairs={{0,3},{1,2},{2,1},{3,0},{4,7},{5,6},{6,5},{7,4},{8,11},{9,10},{10,... | collective-permute-start | bytes 442376 | tf_op jit(solution)/shard_map/ppermute | solution.py:269
  120.7 1.1 collective-permute-start.25
  122.2 2.1 %collective-permute-start.26 = (bf16[144,512]{1,0:T(8,128)(2,1)S(1)}, bf16[144,512]{1,0:T(8,128)(2,1)S(1)}, u32[]{:S(2)}, u32[]{:S(2)}) collective-permute-start(bf16[144,512]{1,0:T(8,128)(2,1)S(1)} %get-tuple-element.38), channel_id=1, source_target_pairs={{0,2},{1,3},{2,0},{3,1},{4,6},{5,7},{6,4},{7,5},{8,10},{9,11},{10,... | collective-permute-start | bytes 442376 | tf_op jit(solution)/shard_map/ppermute | solution.py:269
  124.4 1.9 %collective-permute-start.27 = (bf16[144,512]{1,0:T(8,128)(2,1)S(1)}, bf16[144,512]{1,0:T(8,128)(2,1)S(1)}, u32[]{:S(2)}, u32[]{:S(2)}) collective-permute-start(bf16[144,512]{1,0:T(8,128)(2,1)S(1)} %get-tuple-element.39), channel_id=1, source_target_pairs={{0,3},{1,2},{2,1},{3,0},{4,7},{5,6},{6,5},{7,4},{8,11},{9,10},{10,... | collective-permute-start | bytes 442376 | tf_op jit(solution)/shard_map/ppermute | solution.py:269
  126.3 0.7 collective-permute-done.30.refs_2_
  127.0 1.6 %collective-permute-done.31.refs_3_ = bf16[144,512]{1,0:T(8,128)(2,1)S(1)} collective-permute-done((bf16[144,512]{1,0:T(8,128)(2,1)S(1)}, bf16[144,512]{1,0:T(8,128)(2,1)S(1)}, u32[]{:S(2)}, u32[]{:S(2)}) %collective-permute-start.31) | collective-permute-done | bytes 147488 | tf_op jit(solution)/shard_map/ppermute | solution.py:269
  128.5 1.7 %shard_map.80 = (f32[192,1536]{1,0:T(8,128)S(1)}, f32[192,128]{1,0:T(8,128)S(1)}) custom-call(bf16[144,512]{1,0:T(8,128)(2,1)S(1)} %get-tuple-element.41.refs_0_, bf16[144,512]{1,0:T(8,128)(2,1)S(1)} %collective-permute-done.29.refs_1_, bf16[144,512]{1,0:T(8,128)(2,1)S(1)} %collective-permute-done.30.refs_2_, ...), custom_call_target="tpu_custom_call" | custom-call | flops 679477248 | bytes 4128768 | tf_op jit(solution)/shard_map/pallas_call | solution.py:82
  130.7 1.9 %collective-permute-done.26.refs_2_ = bf16[144,512]{1,0:T(8,128)(2,1)S(1)} collective-permute-done((bf16[144,512]{1,0:T(8,128)(2,1)S(1)}, bf16[144,512]{1,0:T(8,128)(2,1)S(1)}, u32[]{:S(2)}, u32[]{:S(2)}) %collective-permute-start.26) | collective-permute-done | bytes 147488 | tf_op jit(solution)/shard_map/ppermute | solution.py:269
  132.6 1.3 collective-permute-done.27.refs_3_
  134.0 2.8 %shard_map.81 = f32[192,2048]{1,0:T(8,128)} custom-call(bf16[144,512]{1,0:T(8,128)(2,1)S(1)} %get-tuple-element.36.refs_0_, bf16[144,512]{1,0:T(8,128)(2,1)S(1)} %collective-permute-done.25.refs_1_, bf16[144,512]{1,0:T(8,128)(2,1)S(1)} %collective-permute-done.26.refs_2_, bf16[144,512]{1,0:T(8,128)(2,1)S(1)} %collective-permute-done.27.refs_3_, ...), custom_call_target="tpu_custom_call" | custom-call | flops 226492416 | bytes 1376256 | tf_op jit(solution)/shard_map/pallas_call | solution.py:82
  (94 shorter events, 12.3 us)
Async XLA Ops:
  0.0 9.1 %collective-permute-start.13 = (bf16[256,768]{1,0:T(8,128)(2,1)}, bf16[256,768]{1,0:T(8,128)(2,1)}, u32[]{:S(2)}, u32[]{:S(2)}) collective-permute-start(bf16[256,768]{1,0:T(8,128)(2,1)} %bitcast.7), channel_id=1, source_target_pairs={{8,16},{12,20},{16,8},{20,12},{9,17},{13,21},{17,9},{21,13},{10,18... | collective-permute-start | bytes 1179656 | tf_op jit(solution)/shard_map/ppermute | solution.py:263
  1.4 8.2 %collective-permute-start.18 = (bf16[256,768]{1,0:T(8,128)(2,1)}, bf16[256,768]{1,0:T(8,128)(2,1)S(1)}, u32[]{:S(2)}, u32[]{:S(2)}) collective-permute-start(bf16[256,768]{1,0:T(8,128)(2,1)} %bitcast.11), channel_id=1, source_target_pairs={{8,16},{12,20},{16,8},{20,12},{9,17},{13,21},{17,9},{21,13},{10,18... | collective-permute-start | bytes 1179656 | tf_op jit(solution)/shard_map/ppermute | solution.py:263
  2.1 17.0 %collective-permute-start.3 = (bf16[256,768]{1,0:T(8,128)(2,1)}, bf16[256,768]{1,0:T(8,128)(2,1)S(1)}, u32[]{:S(2)}, u32[]{:S(2)}) collective-permute-start(bf16[256,768]{1,0:T(8,128)(2,1)} %bitcast.8), channel_id=1, source_target_pairs={{0,8},{4,12},{8,0},{12,4},{16,24},{20,28},{24,16},{28,20},{1,9},{5... | collective-permute-start | bytes 1179656 | tf_op jit(solution)/shard_map/ppermute | solution.py:263
  9.0 21.6 %collective-permute-start.7 = (bf16[256,768]{1,0:T(8,128)(2,1)}, bf16[256,768]{1,0:T(8,128)(2,1)S(1)}, u32[]{:S(2)}, u32[]{:S(2)}) collective-permute-start(bf16[256,768]{1,0:T(8,128)(2,1)} %bitcast.12), channel_id=1, source_target_pairs={{0,8},{4,12},{8,0},{12,4},{16,24},{20,28},{24,16},{28,20},{1,9},{5... | collective-permute-start | bytes 1179656 | tf_op jit(solution)/shard_map/ppermute | solution.py:263
  9.1 27.1 %collective-permute-start.11 = (bf16[256,768]{1,0:T(8,128)(2,1)}, bf16[256,768]{1,0:T(8,128)(2,1)S(1)}, u32[]{:S(2)}, u32[]{:S(2)}) collective-permute-start(bf16[256,768]{1,0:T(8,128)(2,1)} %bitcast.9), channel_id=1, source_target_pairs={{0,4},{4,0},{8,12},{12,8},{16,20},{20,16},{24,28},{28,24},{1,5},{5... | collective-permute-start | bytes 1179656 | tf_op jit(solution)/shard_map/ppermute | solution.py:266
  9.1 29.3 %collective-permute-start.16 = (bf16[256,768]{1,0:T(8,128)(2,1)}, bf16[256,768]{1,0:T(8,128)(2,1)S(1)}, u32[]{:S(2)}, u32[]{:S(2)}) collective-permute-start(bf16[256,768]{1,0:T(8,128)(2,1)} %bitcast.13), channel_id=1, source_target_pairs={{0,4},{4,0},{8,12},{12,8},{16,20},{20,16},{24,28},{28,24},{1,5},{5... | collective-permute-start | bytes 1179656 | tf_op jit(solution)/shard_map/ppermute | solution.py:266
  9.6 22.3 %copy-start.16 = (bf16[256,768]{1,0:T(8,128)(2,1)}, bf16[256,768]{1,0:T(8,128)(2,1)S(1)}, u32[]{:S(2)}) copy-start(bf16[256,768]{1,0:T(8,128)(2,1)S(1)} %collective-permute-done.18) | copy-start | bytes 1179652
  9.6 30.8 %collective-permute-start.37 = (bf16[256,768]{1,0:T(8,128)(2,1)}, bf16[256,768]{1,0:T(8,128)(2,1)S(1)}, u32[]{:S(2)}, u32[]{:S(2)}) collective-permute-start(bf16[256,768]{1,0:T(8,128)(2,1)} %bitcast.15), channel_id=1, source_target_pairs={{8,16},{12,20},{16,8},{20,12},{9,17},{13,21},{17,9},{21,13},{10,18... | collective-permute-start | bytes 1179656 | tf_op jit(solution)/shard_map/ppermute | solution.py:263
  19.1 22.9 %collective-permute-start.21 = (bf16[256,768]{1,0:T(8,128)(2,1)}, bf16[256,768]{1,0:T(8,128)(2,1)}, u32[]{:S(2)}, u32[]{:S(2)}) collective-permute-start(bf16[256,768]{1,0:T(8,128)(2,1)} %bitcast.16), channel_id=1, source_target_pairs={{0,8},{4,12},{24,16},{28,20},{1,9},{5,13},{25,17},{29,21},{2,10},{... | collective-permute-start | bytes 1179656 | tf_op jit(solution)/shard_map/ppermute | solution.py:263
  30.6 12.9 %collective-permute-start.32 = (bf16[256,768]{1,0:T(8,128)(2,1)}, bf16[256,768]{1,0:T(8,128)(2,1)}, u32[]{:S(2)}, u32[]{:S(2)}) collective-permute-start(bf16[256,768]{1,0:T(8,128)(2,1)} %bitcast.17), channel_id=1, source_target_pairs={{8,0},{12,4},{16,24},{20,28},{9,1},{13,5},{17,25},{21,29},{10,2},{... | collective-permute-start | bytes 1179656 | tf_op jit(solution)/shard_map/ppermute | solution.py:263
  36.9 13.9 %collective-permute-start = (bf16[144,2048]{1,0:T(8,128)(2,1)}, bf16[144,2048]{1,0:T(8,128)(2,1)S(1)}, u32[]{:S(2)}, u32[]{:S(2)}) collective-permute-start(bf16[144,2048]{1,0:T(8,128)(2,1)} %get-tuple-element.31), channel_id=1, source_target_pairs={{0,1},{1,0},{2,3},{3,2},{4,5},{5,4},{6,7},{7,6},{8,9},{9,8},{10,11... | collective-permute-start | bytes 1769480 | tf_op jit(solution)/shard_map/ppermute | solution.py:269
  39.1 14.9 %collective-permute-start.14 = (bf16[256,768]{1,0:T(8,128)(2,1)}, bf16[256,768]{1,0:T(8,128)(2,1)}, u32[]{:S(2)}, u32[]{:S(2)}) collective-permute-start(bf16[256,768]{1,0:T(8,128)(2,1)} %collective-permute-done.13), channel_id=1, source_target_pairs={{8,0},{12,4},{16,24},{20,28},{9,1},{13,5},{17,25},{21,29},{10,2},{... | collective-permute-start | bytes 1179656 | tf_op jit(solution)/shard_map/ppermute | solution.py:263
  40.4 15.9 %collective-permute-start.1 = (bf16[144,2048]{1,0:T(8,128)(2,1)S(1)}, bf16[144,2048]{1,0:T(8,128)(2,1)S(1)}, u32[]{:S(2)}, u32[]{:S(2)}) collective-permute-start(bf16[144,2048]{1,0:T(8,128)(2,1)S(1)} %get-tuple-element.32), channel_id=1, source_target_pairs={{0,2},{1,3},{2,0},{3,1},{4,6},{5,7},{6,4},{7,5},{8,10},{9,11},{10,... | collective-permute-start | bytes 1769480 | tf_op jit(solution)/shard_map/ppermute | solution.py:269
  42.0 22.3 %copy-start.17 = (bf16[256,768]{1,0:T(8,128)(2,1)S(1)}, bf16[256,768]{1,0:T(8,128)(2,1)}, u32[]{:S(2)}) copy-start(bf16[256,768]{1,0:T(8,128)(2,1)} %copy-done.16) | copy-start | bytes 1179652
  42.0 22.4 %copy-start.7 = (bf16[256,768]{1,0:T(8,128)(2,1)S(1)}, bf16[256,768]{1,0:T(8,128)(2,1)}, u32[]{:S(2)}) copy-start(bf16[256,768]{1,0:T(8,128)(2,1)} %copy-done.6) | copy-start | bytes 1179652
  42.0 30.0 %copy-start.19 = (bf16[256,768]{1,0:T(8,128)(2,1)S(1)}, bf16[256,768]{1,0:T(8,128)(2,1)}, u32[]{:S(2)}) copy-start(bf16[256,768]{1,0:T(8,128)(2,1)} %copy-done.18) | copy-start | bytes 1179652
  42.0 20.3 %collective-permute-start.19 = (bf16[256,768]{1,0:T(8,128)(2,1)}, bf16[256,768]{1,0:T(8,128)(2,1)S(1)}, u32[]{:S(2)}, u32[]{:S(2)}) collective-permute-start(bf16[256,768]{1,0:T(8,128)(2,1)} %copy-done.16), channel_id=1, source_target_pairs={{8,0},{12,4},{16,24},{20,28},{9,1},{13,5},{17,25},{21,29},{10,2},{... | collective-permute-start | bytes 1179656 | tf_op jit(solution)/shard_map/ppermute | solution.py:263
  43.5 19.5 %collective-permute-start.8 = (bf16[256,768]{1,0:T(8,128)(2,1)}, bf16[256,768]{1,0:T(8,128)(2,1)S(1)}, u32[]{:S(2)}, u32[]{:S(2)}) collective-permute-start(bf16[256,768]{1,0:T(8,128)(2,1)} %copy-done.8), channel_id=1, source_target_pairs={{8,16},{12,20},{16,8},{20,12},{9,17},{13,21},{17,9},{21,13},{10,18... | collective-permute-start | bytes 1179656 | tf_op jit(solution)/shard_map/ppermute | solution.py:263
  45.2 26.9 %copy-start.9 = (bf16[256,768]{1,0:T(8,128)(2,1)S(1)}, bf16[256,768]{1,0:T(8,128)(2,1)}, u32[]{:S(2)}) copy-start(bf16[256,768]{1,0:T(8,128)(2,1)} %copy-done.8) | copy-start | bytes 1179652
  50.7 13.7 %collective-permute-start.4 = (bf16[256,768]{1,0:T(8,128)(2,1)}, bf16[256,768]{1,0:T(8,128)(2,1)S(1)}, u32[]{:S(2)}, u32[]{:S(2)}) collective-permute-start(bf16[256,768]{1,0:T(8,128)(2,1)} %copy-done.6), channel_id=1, source_target_pairs={{8,16},{12,20},{16,8},{20,12},{9,17},{13,21},{17,9},{21,13},{10,18... | collective-permute-start | bytes 1179656 | tf_op jit(solution)/shard_map/ppermute | solution.py:263
  54.0 16.7 %collective-permute-start.38 = (bf16[256,768]{1,0:T(8,128)(2,1)}, bf16[256,768]{1,0:T(8,128)(2,1)S(1)}, u32[]{:S(2)}, u32[]{:S(2)}) collective-permute-start(bf16[256,768]{1,0:T(8,128)(2,1)} %copy-done.18), channel_id=1, source_target_pairs={{8,0},{12,4},{16,24},{20,28},{9,1},{13,5},{17,25},{21,29},{10,2},{... | collective-permute-start | bytes 1179656 | tf_op jit(solution)/shard_map/ppermute | solution.py:263
  56.4 24.3 %collective-permute-start.2 = (bf16[144,2048]{1,0:T(8,128)(2,1)S(1)}, bf16[144,2048]{1,0:T(8,128)(2,1)S(1)}, u32[]{:S(2)}, u32[]{:S(2)}) collective-permute-start(bf16[144,2048]{1,0:T(8,128)(2,1)S(1)} %get-tuple-element.33), channel_id=1, source_target_pairs={{0,3},{1,2},{2,1},{3,0},{4,7},{5,6},{6,5},{7,4},{8,11},{9,10},{10,... | collective-permute-start | bytes 1769480 | tf_op jit(solution)/shard_map/ppermute | solution.py:269
  62.3 9.8 %collective-permute-start.22 = (bf16[256,768]{1,0:T(8,128)(2,1)}, bf16[256,768]{1,0:T(8,128)(2,1)S(1)}, u32[]{:S(2)}, u32[]{:S(2)}) collective-permute-start(bf16[256,768]{1,0:T(8,128)(2,1)} %collective-permute-done.21), channel_id=1, source_target_pairs={{8,16},{12,20},{16,8},{20,12},{9,17},{13,21},{17,9},{21,13},{10,18... | collective-permute-start | bytes 1179656 | tf_op jit(solution)/shard_map/ppermute | solution.py:263
  63.0 16.2 %collective-permute-start.9 = (bf16[256,768]{1,0:T(8,128)(2,1)S(1)}, bf16[256,768]{1,0:T(8,128)(2,1)S(1)}, u32[]{:S(2)}, u32[]{:S(2)}) collective-permute-start(bf16[256,768]{1,0:T(8,128)(2,1)S(1)} %collective-permute-done.8), channel_id=1, source_target_pairs={{8,0},{12,4},{16,24},{20,28},{9,1},{13,5},{17,25},{21,29},{10,2},{... | collective-permute-start | bytes 1179656 | tf_op jit(solution)/shard_map/ppermute | solution.py:263
  64.4 16.4 %collective-permute-start.12 = (bf16[256,768]{1,0:T(8,128)(2,1)S(1)}, bf16[256,768]{1,0:T(8,128)(2,1)S(1)}, u32[]{:S(2)}, u32[]{:S(2)}) collective-permute-start(bf16[256,768]{1,0:T(8,128)(2,1)S(1)} %copy-done.7), channel_id=1, source_target_pairs={{0,4},{4,0},{8,12},{12,8},{16,20},{20,16},{24,28},{28,24},{1,5},{5... | collective-permute-start | bytes 1179656 | tf_op jit(solution)/shard_map/ppermute | solution.py:266
  70.8 16.9 %collective-permute-start.5 = (bf16[256,768]{1,0:T(8,128)(2,1)S(1)}, bf16[256,768]{1,0:T(8,128)(2,1)S(1)}, u32[]{:S(2)}, u32[]{:S(2)}) collective-permute-start(bf16[256,768]{1,0:T(8,128)(2,1)S(1)} %collective-permute-done.4), channel_id=1, source_target_pairs={{8,0},{12,4},{16,24},{20,28},{9,1},{13,5},{17,25},{21,29},{10,2},{... | collective-permute-start | bytes 1179656 | tf_op jit(solution)/shard_map/ppermute | solution.py:263
  72.2 15.5 %collective-permute-start.17 = (bf16[256,768]{1,0:T(8,128)(2,1)S(1)}, bf16[256,768]{1,0:T(8,128)(2,1)S(1)}, u32[]{:S(2)}, u32[]{:S(2)}) collective-permute-start(bf16[256,768]{1,0:T(8,128)(2,1)S(1)} %copy-done.9), channel_id=1, source_target_pairs={{0,4},{4,0},{8,12},{12,8},{16,20},{20,16},{24,28},{28,24},{1,5},{5... | collective-permute-start | bytes 1179656 | tf_op jit(solution)/shard_map/ppermute | solution.py:266
  79.2 14.0 %collective-permute-start.23 = (bf16[256,768]{1,0:T(8,128)(2,1)S(1)}, bf16[256,768]{1,0:T(8,128)(2,1)S(1)}, u32[]{:S(2)}, u32[]{:S(2)}) collective-permute-start(bf16[256,768]{1,0:T(8,128)(2,1)S(1)} %collective-permute-done.22), channel_id=1, source_target_pairs={{8,0},{12,4},{16,24},{20,28},{9,1},{13,5},{17,25},{21,29},{10,2},{... | collective-permute-start | bytes 1179656 | tf_op jit(solution)/shard_map/ppermute | solution.py:263
  80.7 12.6 %collective-permute-start.15 = (bf16[256,768]{1,0:T(8,128)(2,1)S(1)}, bf16[256,768]{1,0:T(8,128)(2,1)S(1)}, u32[]{:S(2)}, u32[]{:S(2)}) collective-permute-start(bf16[256,768]{1,0:T(8,128)(2,1)S(1)} %broadcast_select_fusion.4.refs_8_), channel_id=1, source_target_pairs={{0,4},{4,0},{8,12},{12,8},{16,20},{20,16},{24,28},{28,24},{1,5},{5... | collective-permute-start | bytes 1179656 | tf_op jit(solution)/shard_map/ppermute | solution.py:266
  80.8 13.1 %collective-permute-start.20 = (bf16[256,768]{1,0:T(8,128)(2,1)S(1)}, bf16[256,768]{1,0:T(8,128)(2,1)S(1)}, u32[]{:S(2)}, u32[]{:S(2)}) collective-permute-start(bf16[256,768]{1,0:T(8,128)(2,1)S(1)} %broadcast_select_fusion.3.refs_14_), channel_id=1, source_target_pairs={{0,4},{4,0},{8,12},{12,8},{16,20},{20,16},{24,28},{28,24},{1,5},{5... | collective-permute-start | bytes 1179656 | tf_op jit(solution)/shard_map/ppermute | solution.py:266
  87.6 6.4 %collective-permute-start.10 = (bf16[256,768]{1,0:T(8,128)(2,1)S(1)}, bf16[256,768]{1,0:T(8,128)(2,1)S(1)}, u32[]{:S(2)}, u32[]{:S(2)}) collective-permute-start(bf16[256,768]{1,0:T(8,128)(2,1)S(1)} %broadcast_select_fusion.5.refs_6_), channel_id=1, source_target_pairs={{0,4},{4,0},{8,12},{12,8},{16,20},{20,16},{24,28},{28,24},{1,5},{5... | collective-permute-start | bytes 1179656 | tf_op jit(solution)/shard_map/ppermute | solution.py:266
  87.7 16.5 %collective-permute-start.39 = (bf16[256,768]{1,0:T(8,128)(2,1)S(1)}, bf16[256,768]{1,0:T(8,128)(2,1)S(1)}, u32[]{:S(2)}, u32[]{:S(2)}) collective-permute-start(bf16[256,768]{1,0:T(8,128)(2,1)S(1)} %broadcast_select_fusion.own), channel_id=1, source_target_pairs={{0,4},{4,0},{8,12},{12,8},{16,20},{20,16},{24,28},{28,24},{1,5},{5... | collective-permute-start | bytes 1179656 | tf_op jit(solution)/shard_map/ppermute | solution.py:266
  93.2 7.7 %collective-permute-start.6 = (bf16[256,768]{1,0:T(8,128)(2,1)S(1)}, bf16[256,768]{1,0:T(8,128)(2,1)S(1)}, u32[]{:S(2)}, u32[]{:S(2)}) collective-permute-start(bf16[256,768]{1,0:T(8,128)(2,1)S(1)} %broadcast_select_fusion.6.refs_4_), channel_id=1, source_target_pairs={{0,4},{4,0},{8,12},{12,8},{16,20},{20,16},{24,28},{28,24},{1,5},{5... | collective-permute-start | bytes 1179656 | tf_op jit(solution)/shard_map/ppermute | solution.py:266
  93.3 15.8 %collective-permute-start.28 = (bf16[256,768]{1,0:T(8,128)(2,1)S(1)}, bf16[256,768]{1,0:T(8,128)(2,1)S(1)}, u32[]{:S(2)}, u32[]{:S(2)}) collective-permute-start(bf16[256,768]{1,0:T(8,128)(2,1)S(1)} %bitcast.18), channel_id=1, source_target_pairs={{0,4},{4,0},{8,12},{12,8},{16,20},{20,16},{24,28},{28,24},{1,5},{5... | collective-permute-start | bytes 1179656 | tf_op jit(solution)/shard_map/ppermute | solution.py:266
  93.9 13.5 %collective-permute-start.33 = (bf16[256,768]{1,0:T(8,128)(2,1)S(1)}, bf16[256,768]{1,0:T(8,128)(2,1)S(1)}, u32[]{:S(2)}, u32[]{:S(2)}) collective-permute-start(bf16[256,768]{1,0:T(8,128)(2,1)S(1)} %broadcast_select_fusion.1.own), channel_id=1, source_target_pairs={{0,4},{4,0},{8,12},{12,8},{16,20},{20,16},{24,28},{28,24},{1,5},{5... | collective-permute-start | bytes 1179656 | tf_op jit(solution)/shard_map/ppermute | solution.py:266
  94.0 16.8 %collective-permute-start.24 = (bf16[256,768]{1,0:T(8,128)(2,1)S(1)}, bf16[256,768]{1,0:T(8,128)(2,1)S(1)}, u32[]{:S(2)}, u32[]{:S(2)}) collective-permute-start(bf16[256,768]{1,0:T(8,128)(2,1)S(1)} %broadcast_select_fusion.2.own), channel_id=1, source_target_pairs={{0,4},{4,0},{8,12},{12,8},{16,20},{20,16},{24,28},{28,24},{1,5},{5... | collective-permute-start | bytes 1179656 | tf_op jit(solution)/shard_map/ppermute | solution.py:266
  104.9 7.5 %collective-permute-start.40 = (bf16[144,512]{1,0:T(8,128)(2,1)S(1)}, bf16[144,512]{1,0:T(8,128)(2,1)S(1)}, u32[]{:S(2)}, u32[]{:S(2)}) collective-permute-start(bf16[144,512]{1,0:T(8,128)(2,1)S(1)} %get-tuple-element.50), channel_id=1, source_target_pairs={{0,1},{1,0},{2,3},{3,2},{4,5},{5,4},{6,7},{7,6},{8,9},{9,8},{10,11... | collective-permute-start | bytes 442376 | tf_op jit(solution)/shard_map/ppermute | solution.py:269
  105.9 8.2 %collective-permute-start.41 = (bf16[144,512]{1,0:T(8,128)(2,1)S(1)}, bf16[144,512]{1,0:T(8,128)(2,1)S(1)}, u32[]{:S(2)}, u32[]{:S(2)}) collective-permute-start(bf16[144,512]{1,0:T(8,128)(2,1)S(1)} %get-tuple-element.51), channel_id=1, source_target_pairs={{0,2},{1,3},{2,0},{3,1},{4,6},{5,7},{6,4},{7,5},{8,10},{9,11},{10,... | collective-permute-start | bytes 442376 | tf_op jit(solution)/shard_map/ppermute | solution.py:269
  107.4 8.4 %collective-permute-start.42 = (bf16[144,512]{1,0:T(8,128)(2,1)S(1)}, bf16[144,512]{1,0:T(8,128)(2,1)S(1)}, u32[]{:S(2)}, u32[]{:S(2)}) collective-permute-start(bf16[144,512]{1,0:T(8,128)(2,1)S(1)} %get-tuple-element.52), channel_id=1, source_target_pairs={{0,3},{1,2},{2,1},{3,0},{4,7},{5,6},{6,5},{7,4},{8,11},{9,10},{10,... | collective-permute-start | bytes 442376 | tf_op jit(solution)/shard_map/ppermute | solution.py:269
  109.1 8.9 %collective-permute-start.34 = (bf16[144,512]{1,0:T(8,128)(2,1)S(1)}, bf16[144,512]{1,0:T(8,128)(2,1)S(1)}, u32[]{:S(2)}, u32[]{:S(2)}) collective-permute-start(bf16[144,512]{1,0:T(8,128)(2,1)S(1)} %get-tuple-element.46), channel_id=1, source_target_pairs={{0,1},{1,0},{2,3},{3,2},{4,5},{5,4},{6,7},{7,6},{8,9},{9,8},{10,11... | collective-permute-start | bytes 442376 | tf_op jit(solution)/shard_map/ppermute | solution.py:269
  110.8 9.9 %collective-permute-start.35 = (bf16[144,512]{1,0:T(8,128)(2,1)S(1)}, bf16[144,512]{1,0:T(8,128)(2,1)S(1)}, u32[]{:S(2)}, u32[]{:S(2)}) collective-permute-start(bf16[144,512]{1,0:T(8,128)(2,1)S(1)} %get-tuple-element.47), channel_id=1, source_target_pairs={{0,2},{1,3},{2,0},{3,1},{4,6},{5,7},{6,4},{7,5},{8,10},{9,11},{10,... | collective-permute-start | bytes 442376 | tf_op jit(solution)/shard_map/ppermute | solution.py:269
  112.4 9.8 %collective-permute-start.36 = (bf16[144,512]{1,0:T(8,128)(2,1)S(1)}, bf16[144,512]{1,0:T(8,128)(2,1)S(1)}, u32[]{:S(2)}, u32[]{:S(2)}) collective-permute-start(bf16[144,512]{1,0:T(8,128)(2,1)S(1)} %get-tuple-element.48), channel_id=1, source_target_pairs={{0,3},{1,2},{2,1},{3,0},{4,7},{5,6},{6,5},{7,4},{8,11},{9,10},{10,... | collective-permute-start | bytes 442376 | tf_op jit(solution)/shard_map/ppermute | solution.py:269
  114.1 10.3 %collective-permute-start.29 = (bf16[144,512]{1,0:T(8,128)(2,1)S(1)}, bf16[144,512]{1,0:T(8,128)(2,1)S(1)}, u32[]{:S(2)}, u32[]{:S(2)}) collective-permute-start(bf16[144,512]{1,0:T(8,128)(2,1)S(1)} %get-tuple-element.42), channel_id=1, source_target_pairs={{0,1},{1,0},{2,3},{3,2},{4,5},{5,4},{6,7},{7,6},{8,9},{9,8},{10,11... | collective-permute-start | bytes 442376 | tf_op jit(solution)/shard_map/ppermute | solution.py:269
  115.8 11.2 %collective-permute-start.30 = (bf16[144,512]{1,0:T(8,128)(2,1)S(1)}, bf16[144,512]{1,0:T(8,128)(2,1)S(1)}, u32[]{:S(2)}, u32[]{:S(2)}) collective-permute-start(bf16[144,512]{1,0:T(8,128)(2,1)S(1)} %get-tuple-element.43), channel_id=1, source_target_pairs={{0,2},{1,3},{2,0},{3,1},{4,6},{5,7},{6,4},{7,5},{8,10},{9,11},{10,... | collective-permute-start | bytes 442376 | tf_op jit(solution)/shard_map/ppermute | solution.py:269
  118.0 10.5 %collective-permute-start.31 = (bf16[144,512]{1,0:T(8,128)(2,1)S(1)}, bf16[144,512]{1,0:T(8,128)(2,1)S(1)}, u32[]{:S(2)}, u32[]{:S(2)}) collective-permute-start(bf16[144,512]{1,0:T(8,128)(2,1)S(1)} %get-tuple-element.44), channel_id=1, source_target_pairs={{0,3},{1,2},{2,1},{3,0},{4,7},{5,6},{6,5},{7,4},{8,11},{9,10},{10,... | collective-permute-start | bytes 442376 | tf_op jit(solution)/shard_map/ppermute | solution.py:269
  120.7 10.1 %collective-permute-start.25 = (bf16[144,512]{1,0:T(8,128)(2,1)S(1)}, bf16[144,512]{1,0:T(8,128)(2,1)S(1)}, u32[]{:S(2)}, u32[]{:S(2)}) collective-permute-start(bf16[144,512]{1,0:T(8,128)(2,1)S(1)} %get-tuple-element.37), channel_id=1, source_target_pairs={{0,1},{1,0},{2,3},{3,2},{4,5},{5,4},{6,7},{7,6},{8,9},{9,8},{10,11... | collective-permute-start | bytes 442376 | tf_op jit(solution)/shard_map/ppermute | solution.py:269
  122.2 10.5 %collective-permute-start.26 = (bf16[144,512]{1,0:T(8,128)(2,1)S(1)}, bf16[144,512]{1,0:T(8,128)(2,1)S(1)}, u32[]{:S(2)}, u32[]{:S(2)}) collective-permute-start(bf16[144,512]{1,0:T(8,128)(2,1)S(1)} %get-tuple-element.38), channel_id=1, source_target_pairs={{0,2},{1,3},{2,0},{3,1},{4,6},{5,7},{6,4},{7,5},{8,10},{9,11},{10,... | collective-permute-start | bytes 442376 | tf_op jit(solution)/shard_map/ppermute | solution.py:269
  124.4 9.6 %collective-permute-start.27 = (bf16[144,512]{1,0:T(8,128)(2,1)S(1)}, bf16[144,512]{1,0:T(8,128)(2,1)S(1)}, u32[]{:S(2)}, u32[]{:S(2)}) collective-permute-start(bf16[144,512]{1,0:T(8,128)(2,1)S(1)} %get-tuple-element.39), channel_id=1, source_target_pairs={{0,3},{1,2},{2,1},{3,0},{4,7},{5,6},{6,5},{7,4},{8,11},{9,10},{10,... | collective-permute-start | bytes 442376 | tf_op jit(solution)/shard_map/ppermute | solution.py:269
  (15 other events, 155.0 us)
where the time goes:
time: 137 us
  starting transfers between devices  57.6 us (42%)
  waiting for transfers between devices  53.7 us (39%)
  Pallas kernels  18.3 us (13%)
  local copies, waits for them, and re-layouts  4.34 us (3%)
  other arithmetic  2.32 us (2%)
    ppermute x16, waiting for transfers between devices, along(): return lax.ppermute(x, 'replica', devices)  40.4 us
    ppermute x16, starting transfers between devices, along(): return lax.ppermute(x, 'replica', devices)  32.5 us
    ppermute x15, starting transfers between devices, across(): return lax.ppermute(x, 'expert', [(e, e ^ m) for e in range(experts)])  22.3 us
    pallas_call x9, Pallas kernels, call(): pl.pallas_call(kernel, out_shape=out_shape, in_specs=list(specs), out_spe...  18.3 us
    ppermute x15, waiting for transfers between devices, across(): return lax.ppermute(x, 'expert', [(e, e ^ m) for e in range(experts)])  13.2 us
    unnamed x40, local copies, waits for them, and re-layouts  4.34 us
    ppermute x12, starting transfers between devices, swap(): return lax.ppermute(x, 'replica', [(r, r ^ 1) for r in range(2 * CHAIN)])  2.87 us
  transfers between devices with their start and end apart: 43, of which 19 were waited for; matrix products, arithmetic and copies ran while one was open for 2% of the time, Pallas kernels for 11%

commit v1 on v0

--- a/solution.py
+++ b/solution.py
@@ -11,6 +11,7 @@
 F32, BF16 = jnp.float32, jnp.bfloat16
 ANY = pl.BlockSpec(memory_space=pl.ANY)
 VMEM = pl.BlockSpec(memory_space=pltpu.VMEM)
+HBM = pl.BlockSpec(memory_space=pltpu.HBM)
 CHAIN = 4
 
 
@@ -78,21 +79,30 @@
     return [2 * c + s for c in chips for s in (core, 1 - core)]
 
 
-def call(kernel, out_shape, args, specs, scratch=(), flops=0, moved=0, limit=16 << 20):
+def call(kernel, out_shape, args, specs, scratch=(), flops=0, moved=0, outs=None, grant=8):
     return pl.pallas_call(
         kernel,
         out_shape=out_shape,
         in_specs=list(specs),
-        out_specs=jax.tree.map(lambda _: VMEM, out_shape),
+        out_specs=jax.tree.map(lambda _: VMEM, out_shape) if outs is None else outs,
         scratch_shapes=list(scratch),
         cost_estimate=pl.CostEstimate(flops=flops, bytes_accessed=moved, transcendentals=0),
-        compiler_params=pltpu.CompilerParams(vmem_limit_bytes=limit),
+        compiler_params=pltpu.CompilerParams(vmem_limit_bytes=grant << 20),
     )(*args)
 
 
-def place_kernel(experts, capacity, ids_ref, w_ref, tok_ref, *refs):
-    outs, c_ref, tokp = refs[:experts], refs[experts], refs[experts + 1]
+def stay(x):
+    return pltpu.with_memory_space_constraint(x, pltpu.HBM)
+
+
+def place_kernel(experts, capacity, ids_hbm, w_hbm, tok_hbm, *refs):
+    outs, (c_ref, tokp, ids_ref, w_ref, tok_ref, local, sems) = refs[:experts], refs[experts:]
     count, width = tok_ref.shape
+    ids_copy, w_copy, tok_copy = copies(
+        [(ids_hbm, ids_ref), (w_hbm, w_ref), (tok_hbm, tok_ref)], sems
+    )
+    ids_copy.wait()
+    w_copy.wait()
     part = width // (2 * CHAIN)
     me = lax.axis_index("expert")
     pad = 8
@@ -114,6 +124,7 @@
         return lax.dot_general(a, b, nt, preferred_element_type=F32)
 
     rank = jnp.where(named, jnp.dot(mask, upper, preferred_element_type=F32), -1.0)
+    tok_copy.wait()
     for place, s in enumerate(slice_order()):
         tokp[:, place * part : (place + 1) * part] = tok_ref[
             :, pl.ds(pl.multiple_of(s * part, part), part)
@@ -121,7 +132,13 @@
     slot = lax.broadcasted_iota(jnp.int32, (capacity, count), 0).astype(F32)
     for m in range(experts):
         select = jnp.where(slot == rank[m : m + 1, :], 1.0, 0.0).astype(BF16)
-        outs[m][...] = jnp.dot(select, tokp[...], preferred_element_type=F32).astype(BF16)
+        block = jnp.dot(select, tokp[...], preferred_element_type=F32).astype(BF16)
+        if m == 0:
+            local[...] = block
+            local_copy = pltpu.make_async_copy(local, outs[0], sems.at[3])
+            local_copy.start()
+        else:
+            outs[m][...] = block
     column = lax.broadcasted_iota(jnp.int32, (count, experts * capacity), 1).astype(F32)
     rank_c = jnp.where(turned(eye, mask) > 0.5, turned(lower, mask), -float(experts * capacity))
     for half, part_w in enumerate((high, low)):
@@ -131,6 +148,7 @@
             hit = column == rank_c[:, m : m + 1] + float(m * capacity)
             total = jnp.where(hit, w_c[:, m : m + 1], total)
         c_ref[half * count : (half + 1) * count, :] = total.astype(BF16)
+    local_copy.wait()
 
 
 def copies(pairs, sems):
@@ -142,41 +160,49 @@
     return out
 
 
-def gate_up_kernel(experts, first, slices, last, *refs):
+def open_kernel(experts, slices, *refs):
     blocks, refs = refs[:experts], refs[experts:]
     gates, ups, refs = refs[:slices], refs[slices : 2 * slices], refs[2 * slices :]
-    if last:
-        acc_g, acc_u, out, rows, wg, wu, ag, au, sems = refs
-    else:
-        out_g, out_u, rows, wg, wu, sems = refs
+    out_g, out_u, tail, rows, wg, wu, sems = refs
     capacity = blocks[0].shape[0]
     part = gates[0].shape[0]
-    lo, n = first * part, slices * part
+    n = slices * part
     pairs = [
-        (b.at[:, pl.ds(lo, n)], rows.at[pl.ds(m * capacity, capacity), :])
+        (b.at[:, pl.ds(0, n)], rows.at[pl.ds(m * capacity, capacity), :])
         for m, b in enumerate(blocks)
     ]
     pairs += [(g, wg.at[pl.ds(i * part, part), :]) for i, g in enumerate(gates)]
     n_gate = len(pairs)
     pairs += [(u, wu.at[pl.ds(i * part, part), :]) for i, u in enumerate(ups)]
-    if last:
-        pairs += [(acc_g, ag), (acc_u, au)]
+    pairs += [
+        (b.at[:, pl.ds(n, tail.shape[1])], tail.at[pl.ds(m * capacity, capacity), :])
+        for m, b in enumerate(blocks)
+    ]
     started = copies(pairs, sems)
     for copy in started[:n_gate]:
         copy.wait()
-    gate = jnp.dot(rows[...], wg[...], preferred_element_type=F32)
-    if not last:
-        out_g[...] = gate
-        for copy in started[n_gate:]:
-            copy.wait()
-        out_u[...] = jnp.dot(rows[...], wu[...], preferred_element_type=F32)
-        return
+    out_g[...] = jnp.dot(rows[...], wg[...], preferred_element_type=F32)
     for copy in started[n_gate:]:
         copy.wait()
-    ag[...] += gate
-    up = au[...] + jnp.dot(rows[...], wu[...], preferred_element_type=F32)
-    gate = ag[...]
-    out[...] = (gate / (1.0 + jnp.exp(-gate)) * up).astype(BF16)
+    out_u[...] = jnp.dot(rows[...], wu[...], preferred_element_type=F32)
+
+
+def gate_kernel(rows, own, other, acc, out):
+    part = own.shape[0]
+    gate = acc[...] + jnp.dot(rows[:, :part], own[...], preferred_element_type=F32)
+    gate = gate + jnp.dot(rows[:, part:], other[...], preferred_element_type=F32)
+    out[...] = gate / (1.0 + jnp.exp(-gate))
+
+
+def up_kernel(rows, own, acc, out):
+    part = own.shape[0]
+    out[...] = acc[...] + jnp.dot(rows[:, :part], own[...], preferred_element_type=F32)
+
+
+def hidden_kernel(rows, other, acc, act, out):
+    part = other.shape[0]
+    up = acc[...] + jnp.dot(rows[:, part:], other[...], preferred_element_type=F32)
+    out[...] = (act[...] * up).astype(BF16)
 
 
 def down_kernel(experts, capacity, hidden, own, other, *outs):
@@ -216,25 +242,54 @@
 
 
 def combine_kernel(stages, n_blocks, *refs):
-    blocks, (tokens, c_ref, out, square, back, tok, sems) = refs[:n_blocks], refs[n_blocks:]
+    blocks, refs = refs[:n_blocks], refs[n_blocks:]
+    tokens, c_ref, out, square, rest, back, tok, sems, rest_sems = refs
+    wide = rest.shape[1]
+    part = wide // 2
+    order = slice_order()[2 * len(stages) :]
+    pairs = [
+        (
+            tokens.at[:, pl.ds(pl.multiple_of(s * part, part), part)],
+            rest.at[:, pl.ds(h * part, part)],
+        )
+        for h, s in enumerate(order)
+    ]
+    started = copies(pairs, rest_sems)
     here, total = chunk(stages, blocks, tokens, c_ref, back, tok, sems)
     out[...] = here
     square[...] = jnp.broadcast_to(total, square.shape)
-
-
-def finish_kernel(stages, n_blocks, *refs):
-    blocks, refs = refs[:n_blocks], refs[n_blocks:]
-    tokens, c_ref, gain, mixed, square, out, back, tok, sems = refs
-    here, total = chunk(stages, blocks, tokens, c_ref, back, tok, sems)
+    for copy in started:
+        copy.wait()
+
+
+def finish_kernel(*refs):
+    *blocks, tok, c_ref, gain, mixed, square, out_hbm, back, out, sems = refs
+    capacity = blocks[0].shape[0]
+    count, wide = tok.shape
+    part = wide // 2
+    for m, b in enumerate(blocks):
+        back[m * capacity : (m + 1) * capacity, :] = b[...]
+    both = jnp.dot(c_ref[...], back[...], preferred_element_type=F32)
+    here = tok[...] + (both[:count] + both[count:])
+    total = jnp.sum(here * here, axis=1, keepdims=True) + square[:, 0:1]
     width = out.shape[1]
-    wide = here.shape[1]
-    part = wide // 2
-    scale = lax.rsqrt((total + square[:, 0:1]) * (1.0 / width) + 1e-06)
+    scale = lax.rsqrt(total * (1.0 / width) + 1e-06)
+    started = []
     for place, s in enumerate(slice_order()):
         lo = place * part
-        value = mixed[:, lo : lo + part] if lo < width - wide else here[:, lo - width + wide :][:, :part]
+        if lo < width - wide:
+            value = mixed[:, lo : lo + part]
+        else:
+            value = here[:, lo - (width - wide) :][:, :part]
         at = pl.ds(pl.multiple_of(s * part, part), part)
-        out[:, at] = value * scale * gain[:, at]
+        out[:, lo : lo + part] = value * scale * gain[:, at]
+        copy = pltpu.make_async_copy(
+            out.at[:, pl.ds(lo, part)], out_hbm.at[:, at], sems.at[place]
+        )
+        copy.start()
+        started.append(copy)
+    for copy in started:
+        copy.wait()
 
 
 def staged(tokens, expert_ids, combine_weights, gate_weight, up_weight, down_weight, norm_gain):
@@ -287,39 +342,59 @@
         functools.partial(place_kernel, experts, capacity),
         [jax.ShapeDtypeStruct((capacity, width), BF16)] * experts
         + [jax.ShapeDtypeStruct((2 * count, slots), BF16)],
-        (expert_ids.T, combine_weights.T, tokens),
-        [VMEM] * 3,
-        [pltpu.VMEM((count, width), BF16)],
+        tuple(stay(x) for x in (expert_ids.T, combine_weights.T, tokens)),
+        [HBM] * 3,
+        [
+            pltpu.VMEM((count, width), BF16),
+            pltpu.VMEM((2, count), jnp.int32),
+            pltpu.VMEM((2, count), F32),
+            pltpu.VMEM((count, width), F32),
+            pltpu.VMEM((capacity, width), BF16),
+            pltpu.SemaphoreType.DMA((4,)),
+        ],
         flops=2 * slots * count * width,
         moved=count * width * 4 + slots * width * 2,
+        outs=[HBM] + [VMEM] * experts,
     )
     rows = [placed[0]] + [across(placed[m], m) for m in range(1, experts)]
 
-    def gate_up(first, slices, acc):
-        last = acc is not None
-        n = slices * part
-        flat = jax.ShapeDtypeStruct((slots, ff), F32)
-        scratch = [
+    slices = 2 * (CHAIN - 1)
+    n = slices * part
+    flat = jax.ShapeDtypeStruct((slots, ff), F32)
+    acc_g, acc_u, tail = call(
+        functools.partial(open_kernel, experts, slices),
+        [flat, flat, jax.ShapeDtypeStruct((slots, 2 * part), BF16)],
+        (*rows, *g_all[:slices], *u_all[:slices]),
+        [ANY] * (experts + 2 * slices),
+        [
             pltpu.VMEM((slots, n), BF16),
             pltpu.VMEM((n, ff), BF16),
             pltpu.VMEM((n, ff), BF16),
-        ]
-        if last:
-            scratch += [pltpu.VMEM((slots, ff), F32)] * 2
-        args = (*rows, *g_all[first : first + slices], *u_all[first : first + slices])
-        args += tuple(acc) if last else ()
+            pltpu.SemaphoreType.DMA((2 * experts + 2 * slices,)),
+        ],
+        flops=4 * slots * n * ff,
+        moved=slots * n * 2 + 4 * n * ff + slots * ff * 8,
+        grant=12,
+    )
+
+    def extend(kernel, shape, args, steps):
         return call(
-            functools.partial(gate_up_kernel, experts, first, slices, last),
-            jax.ShapeDtypeStruct((slots, ff), BF16) if last else [flat, flat],
+            kernel,
+            shape,
             args,
-            [ANY] * len(args),
-            scratch + [pltpu.SemaphoreType.DMA((experts + 2 * slices + 2 * last,))],
-            flops=4 * slots * n * ff,
-            moved=slots * n * 2 + 4 * n * ff + slots * ff * 8,
+            [VMEM] * len(args),
+            flops=2 * slots * steps * part * ff,
+            moved=slots * ff * 8,
         )
 
-    acc = gate_up(0, 6, None)
-    hidden = gate_up(6, 2, acc)
+    act = extend(gate_kernel, flat, (tail, *g_all[slices:], acc_g), 2)
+    acc_u = extend(up_kernel, flat, (tail, u_all[slices], acc_u), 1)
+    hidden = extend(
+        hidden_kernel,
+        jax.ShapeDtypeStruct((slots, ff), BF16),
+        (tail, u_all[slices + 1], acc_u, act),
+        1,
+    )
 
     backs = []
     for stage in range(CHAIN):
@@ -333,38 +408,40 @@
         )
         backs.append([outs[0]] + [across(outs[m], m) for m in range(1, experts)])
 
-    def combine(kernel, stages, more, shape):
-        blocks = [b for s in stages for b in backs[s]]
-        wide = 2 * part * len(stages)
-        return call(
-            functools.partial(kernel, stages, len(blocks)),
-            shape,
-            (*blocks, tokens, mix, *more),
-            [ANY] * (len(blocks) + 1) + [VMEM] * (1 + len(more)),
-            [
-                pltpu.VMEM((slots, wide), BF16),
-                pltpu.VMEM((count, wide), F32),
-                pltpu.SemaphoreType.DMA((len(blocks) + 2 * len(stages),)),
-            ],
-            flops=4 * count * slots * wide,
-            moved=slots * wide * 2 + count * wide * 8,
-        )
-
     early = tuple(range(CHAIN - 1))
-    mixed = combine(
-        combine_kernel,
-        early,
-        (),
+    blocks = [b for s in early for b in backs[s]]
+    wide = 2 * part * len(early)
+    mixed, square, rest = call(
+        functools.partial(combine_kernel, early, len(blocks)),
         [
-            jax.ShapeDtypeStruct((count, 2 * part * len(early)), F32),
+            jax.ShapeDtypeStruct((count, wide), F32),
             jax.ShapeDtypeStruct((count, 128), F32),
+            jax.ShapeDtypeStruct((count, 2 * part), F32),
         ],
-    )
-    return combine(
+        (*blocks, stay(tokens), mix),
+        [ANY] * len(blocks) + [HBM, VMEM],
+        [
+            pltpu.VMEM((slots, wide), BF16),
+            pltpu.VMEM((count, wide), F32),
+            pltpu.SemaphoreType.DMA((len(blocks) + 2 * len(early),)),
+            pltpu.SemaphoreType.DMA((2,)),
+        ],
+        flops=4 * count * slots * wide,
+        moved=slots * wide * 2 + count * wide * 8,
+    )
+    return call(
         finish_kernel,
-        (CHAIN - 1,),
-        (norm_gain.reshape(1, width), *mixed),
         jax.ShapeDtypeStruct((count, width), F32),
+        (*backs[-1], rest, mix, norm_gain.reshape(1, width), mixed, square),
+        [VMEM] * (experts + 5),
+        [
+            pltpu.VMEM((slots, 2 * part), BF16),
+            pltpu.VMEM((count, width), F32),
+            pltpu.SemaphoreType.DMA((2 * CHAIN,)),
+        ],
+        flops=8 * count * slots * part,
+        moved=count * width * 8,
+        outs=HBM,
     )
 
 

time: 137 us -> 135 us (0.985)
  local copies, waits for them, and re-layouts: 4.34 us -> 2.39 us
    unnamed x40 -> x36, local copies, waits for them, and re-layouts: 4.34 us -> 2.39 us
    pallas_call x9 -> x11, Pallas kernels: 18.3 us -> 18.8 us  [call(): pl.pallas_call(kernel, out_shape=out_shape, in_specs=list(specs), out_spe...]
  transfers between devices with their start and end apart: 43 -> 43, of which waited for: 19 -> 18; matrix products, arithmetic and copies ran while one was open for 2% -> 2% of each run, Pallas kernels for 11% -> 13%
where the time goes in v1:
time: 135 us; the launch traced here: 134 us
  starting transfers between devices  56.5 us (42%)
  waiting for transfers between devices  53.7 us (40%)
  Pallas kernels  18.8 us (14%)
  local copies, waits for them, and re-layouts  2.39 us (2%)
  other arithmetic  2.32 us (2%)
    ppermute x16, waiting for transfers between devices, along(): return lax.ppermute(x, 'replica', devices)  40.6 us
    ppermute x16, starting transfers between devices, along(): return lax.ppermute(x, 'replica', devices)  32.5 us
    ppermute x15, starting transfers between devices, across(): return lax.ppermute(x, 'expert', [(e, e ^ m) for e in range(experts)])  21.1 us
    pallas_call x11, Pallas kernels, call(): pl.pallas_call(kernel, out_shape=out_shape, in_specs=list(specs), out_spe...  18.8 us
    ppermute x15, waiting for transfers between devices, across(): return lax.ppermute(x, 'expert', [(e, e ^ m) for e in range(experts)])  13 us
    ppermute x12, starting transfers between devices, swap(): return lax.ppermute(x, 'replica', [(r, r ^ 1) for r in range(2 * CHAIN)])  2.87 us
  transfers between devices with their start and end apart: 43, of which 18 were waited for; matrix products, arithmetic and copies ran while one was open for 2% of the time, Pallas kernels for 13%

profile of v1, /device:TPU:0, one launch (start us, length us, event | category | flops | bytes accessed | tf_op | source)
XLA Modules:
  0.0 134.3 jit_solution(17253753008051506168)
XLA Ops:
  0.0 1.4 %collective-permute-start.12 = (bf16[256,768]{1,0:T(8,128)(2,1)}, bf16[256,768]{1,0:T(8,128)(2,1)}, u32[]{:S(2)}, u32[]{:S(2)}) collective-permute-start(bf16[256,768]{1,0:T(8,128)(2,1)} %bitcast.11), channel_id=1, source_target_pairs={{8,16},{12,20},{16,8},{20,12},{9,17},{13,21},{17,9},{21,13},{10,18... | collective-permute-start | bytes 1179656 | tf_op jit(solution)/shard_map/ppermute | solution.py:318
  2.1 6.9 %collective-permute-start.10 = (bf16[256,768]{1,0:T(8,128)(2,1)}, bf16[256,768]{1,0:T(8,128)(2,1)S(1)}, u32[]{:S(2)}, u32[]{:S(2)}) collective-permute-start(bf16[256,768]{1,0:T(8,128)(2,1)} %bitcast.12), channel_id=1, source_target_pairs={{0,8},{4,12},{8,0},{12,4},{16,24},{20,28},{24,16},{28,20},{1,9},{5... | collective-permute-start | bytes 1179656 | tf_op jit(solution)/shard_map/ppermute | solution.py:318
  10.3 8.9 %collective-permute-done.10.refs_12_ = bf16[256,768]{1,0:T(8,128)(2,1)S(1)} collective-permute-done((bf16[256,768]{1,0:T(8,128)(2,1)}, bf16[256,768]{1,0:T(8,128)(2,1)S(1)}, u32[]{:S(2)}, u32[]{:S(2)}) %collective-permute-start.10) | collective-permute-done | bytes 393248 | tf_op jit(solution)/shard_map/ppermute | solution.py:318
  19.1 11.4 %collective-permute-start.21 = (bf16[256,768]{1,0:T(8,128)(2,1)}, bf16[256,768]{1,0:T(8,128)(2,1)}, u32[]{:S(2)}, u32[]{:S(2)}) collective-permute-start(bf16[256,768]{1,0:T(8,128)(2,1)} %bitcast.16), channel_id=1, source_target_pairs={{0,8},{4,12},{24,16},{28,20},{1,9},{5,13},{25,17},{29,21},{2,10},{... | collective-permute-start | bytes 1179656 | tf_op jit(solution)/shard_map/ppermute | solution.py:318
  30.6 1.3 collective-permute-start.32
  31.9 3.1 %shard_map.73 = (bf16[144,2048]{1,0:T(8,128)(2,1)S(1)}, bf16[144,2048]{1,0:T(8,128)(2,1)S(1)}, bf16[144,2048]{1,0:T(8,128)(2,1)S(1)}, bf16[144,2048]{1,0:T(8,128)(2,1)S(1)}, bf16[384,576]{1,0:T(8,128)(2,1)S(1)}) custom-call(s32[2,192]{1,0:T(2,128)} %bitcast.20, f32[2,192]{1,0:T(2,128)} %bitcast.21, f32[192,2048]{1,0:T(8,128)} %refs_12_.1), custom_call_target="tpu_custom_call" | custom-call | flops 452984832 | bytes 3932160 | tf_op jit(solution)/shard_map/pallas_call | solution.py:83
  35.0 0.8 copy-done.12
  35.9 0.8 copy-done.8
  36.6 1.5 %collective-permute-start = (bf16[144,2048]{1,0:T(8,128)(2,1)S(1)}, bf16[144,2048]{1,0:T(8,128)(2,1)S(1)}, u32[]{:S(2)}, u32[]{:S(2)}) collective-permute-start(bf16[144,2048]{1,0:T(8,128)(2,1)S(1)} %get-tuple-element.33), channel_id=1, source_target_pairs={{0,1},{1,0},{2,3},{3,2},{4,5},{5,4},{6,7},{7,6},{8,9},{9,8},{10,11... | collective-permute-start | bytes 1769480 | tf_op jit(solution)/shard_map/ppermute | solution.py:324
  38.1 0.8 copy-done.10
  38.9 1.3 collective-permute-start.13
  40.2 1.6 %collective-permute-start.1 = (bf16[144,2048]{1,0:T(8,128)(2,1)S(1)}, bf16[144,2048]{1,0:T(8,128)(2,1)S(1)}, u32[]{:S(2)}, u32[]{:S(2)}) collective-permute-start(bf16[144,2048]{1,0:T(8,128)(2,1)S(1)} %get-tuple-element.34), channel_id=1, source_target_pairs={{0,2},{1,3},{2,0},{3,1},{4,6},{5,7},{6,4},{7,5},{8,10},{9,11},{10,... | collective-permute-start | bytes 1769480 | tf_op jit(solution)/shard_map/ppermute | solution.py:324
  41.8 1.4 %collective-permute-start.7 = (bf16[256,768]{1,0:T(8,128)(2,1)}, bf16[256,768]{1,0:T(8,128)(2,1)S(1)}, u32[]{:S(2)}, u32[]{:S(2)}) collective-permute-start(bf16[256,768]{1,0:T(8,128)(2,1)} %copy-done.14), channel_id=1, source_target_pairs={{8,0},{12,4},{16,24},{20,28},{9,1},{13,5},{17,25},{21,29},{10,2},{... | collective-permute-start | bytes 1179656 | tf_op jit(solution)/shard_map/ppermute | solution.py:318
  43.2 0.7 collective-permute-start.18
  43.9 1.1 broadcast_select_fusion.1.own
  45.0 5.3 %collective-permute-done.refs_1_ = bf16[144,2048]{1,0:T(8,128)(2,1)S(1)} collective-permute-done((bf16[144,2048]{1,0:T(8,128)(2,1)S(1)}, bf16[144,2048]{1,0:T(8,128)(2,1)S(1)}, u32[]{:S(2)}, u32[]{:S(2)}) %collective-permute-start) | collective-permute-done | bytes 589856 | tf_op jit(solution)/shard_map/ppermute | solution.py:324
  50.9 2.8 %collective-permute-done.13 = bf16[256,768]{1,0:T(8,128)(2,1)} collective-permute-done((bf16[256,768]{1,0:T(8,128)(2,1)}, bf16[256,768]{1,0:T(8,128)(2,1)}, u32[]{:S(2)}, u32[]{:S(2)}) %collective-permute-start.13) | collective-permute-done | bytes 393248 | tf_op jit(solution)/shard_map/ppermute | solution.py:318
  53.8 1.3 collective-permute-start.38
  55.1 1.1 broadcast_select_fusion.5.refs_14_
  56.1 1.6 %collective-permute-start.2 = (bf16[144,2048]{1,0:T(8,128)(2,1)S(1)}, bf16[144,2048]{1,0:T(8,128)(2,1)S(1)}, u32[]{:S(2)}, u32[]{:S(2)}) collective-permute-start(bf16[144,2048]{1,0:T(8,128)(2,1)S(1)} %get-tuple-element.35), channel_id=1, source_target_pairs={{0,3},{1,2},{2,1},{3,0},{4,7},{5,6},{6,5},{7,4},{8,11},{9,10},{10,... | collective-permute-start | bytes 1769480 | tf_op jit(solution)/shard_map/ppermute | solution.py:324
  57.7 4.4 %collective-permute-done.7 = bf16[256,768]{1,0:T(8,128)(2,1)S(1)} collective-permute-done((bf16[256,768]{1,0:T(8,128)(2,1)}, bf16[256,768]{1,0:T(8,128)(2,1)S(1)}, u32[]{:S(2)}, u32[]{:S(2)}) %collective-permute-start.7) | collective-permute-done | bytes 393248 | tf_op jit(solution)/shard_map/ppermute | solution.py:318
  62.8 1.3 collective-permute-start.19
  64.3 6.3 %collective-permute-done.38 = bf16[256,768]{1,0:T(8,128)(2,1)S(1)} collective-permute-done((bf16[256,768]{1,0:T(8,128)(2,1)}, bf16[256,768]{1,0:T(8,128)(2,1)S(1)}, u32[]{:S(2)}, u32[]{:S(2)}) %collective-permute-start.38) | collective-permute-done | bytes 393248 | tf_op jit(solution)/shard_map/ppermute | solution.py:318
  70.5 1.3 collective-permute-start.16
  72.0 6.9 %collective-permute-done.19 = bf16[256,768]{1,0:T(8,128)(2,1)S(1)} collective-permute-done((bf16[256,768]{1,0:T(8,128)(2,1)S(1)}, bf16[256,768]{1,0:T(8,128)(2,1)S(1)}, u32[]{:S(2)}, u32[]{:S(2)}) %collective-permute-start.19) | collective-permute-done | bytes 393248 | tf_op jit(solution)/shard_map/ppermute | solution.py:318
  79.0 1.5 %collective-permute-start.23 = (bf16[256,768]{1,0:T(8,128)(2,1)S(1)}, bf16[256,768]{1,0:T(8,128)(2,1)S(1)}, u32[]{:S(2)}, u32[]{:S(2)}) collective-permute-start(bf16[256,768]{1,0:T(8,128)(2,1)S(1)} %collective-permute-done.22), channel_id=1, source_target_pairs={{8,0},{12,4},{16,24},{20,28},{9,1},{13,5},{17,25},{21,29},{10,2},{... | collective-permute-start | bytes 1179656 | tf_op jit(solution)/shard_map/ppermute | solution.py:318
  81.1 6.3 %collective-permute-done.16 = bf16[256,768]{1,0:T(8,128)(2,1)S(1)} collective-permute-done((bf16[256,768]{1,0:T(8,128)(2,1)S(1)}, bf16[256,768]{1,0:T(8,128)(2,1)S(1)}, u32[]{:S(2)}, u32[]{:S(2)}) %collective-permute-start.16) | collective-permute-done | bytes 393248 | tf_op jit(solution)/shard_map/ppermute | solution.py:318
  88.0 5.0 %collective-permute-done.23 = bf16[256,768]{1,0:T(8,128)(2,1)S(1)} collective-permute-done((bf16[256,768]{1,0:T(8,128)(2,1)S(1)}, bf16[256,768]{1,0:T(8,128)(2,1)S(1)}, u32[]{:S(2)}, u32[]{:S(2)}) %collective-permute-start.23) | collective-permute-done | bytes 393248 | tf_op jit(solution)/shard_map/ppermute | solution.py:318
  94.2 6.7 %shard_map.74 = (f32[576,768]{1,0:T(8,128)S(1)}, f32[576,768]{1,0:T(8,128)S(1)}, bf16[576,512]{1,0:T(8,128)(2,1)S(1)}) custom-call(bf16[144,2048]{1,0:T(8,128)(2,1)S(1)} %copy-done.13, bf16[144,2048]{1,0:T(8,128)(2,1)S(1)} %collective-permute-done.refs_1_, bf16[144,2048]{1,0:T(8,128)(2,1)S(1)} %collective-permute-done.1.refs_2_, ...), custom_call_target="tpu_custom_call" | custom-call | flops 2717908992 | bytes 10027008 | tf_op jit(solution)/shard_map/pallas_call | solution.py:83
  101.2 0.8 shard_map.76.act
  103.2 1.3 collective-permute-start.40
  104.4 1.5 %collective-permute-start.41 = (bf16[144,512]{1,0:T(8,128)(2,1)S(1)}, bf16[144,512]{1,0:T(8,128)(2,1)S(1)}, u32[]{:S(2)}, u32[]{:S(2)}) collective-permute-start(bf16[144,512]{1,0:T(8,128)(2,1)S(1)} %get-tuple-element.53), channel_id=1, source_target_pairs={{0,2},{1,3},{2,0},{3,1},{4,6},{5,7},{6,4},{7,5},{8,10},{9,11},{10,... | collective-permute-start | bytes 442376 | tf_op jit(solution)/shard_map/ppermute | solution.py:324
  106.0 0.8 collective-permute-start.42
  107.4 1.3 collective-permute-start.34
  109.3 1.6 %collective-permute-start.35 = (bf16[144,512]{1,0:T(8,128)(2,1)S(1)}, bf16[144,512]{1,0:T(8,128)(2,1)S(1)}, u32[]{:S(2)}, u32[]{:S(2)}) collective-permute-start(bf16[144,512]{1,0:T(8,128)(2,1)S(1)} %get-tuple-element.49), channel_id=1, source_target_pairs={{0,2},{1,3},{2,0},{3,1},{4,6},{5,7},{6,4},{7,5},{8,10},{9,11},{10,... | collective-permute-start | bytes 442376 | tf_op jit(solution)/shard_map/ppermute | solution.py:324
  110.9 1.2 collective-permute-start.36
  112.1 1.0 collective-permute-done.41.refs_10_
  113.1 0.9 collective-permute-done.42.refs_11_
  114.1 1.9 %collective-permute-start.30 = (bf16[144,512]{1,0:T(8,128)(2,1)S(1)}, bf16[144,512]{1,0:T(8,128)(2,1)S(1)}, u32[]{:S(2)}, u32[]{:S(2)}) collective-permute-start(bf16[144,512]{1,0:T(8,128)(2,1)S(1)} %get-tuple-element.45), channel_id=1, source_target_pairs={{0,2},{1,3},{2,0},{3,1},{4,6},{5,7},{6,4},{7,5},{8,10},{9,11},{10,... | collective-permute-start | bytes 442376 | tf_op jit(solution)/shard_map/ppermute | solution.py:324
  116.3 2.2 %collective-permute-start.31 = (bf16[144,512]{1,0:T(8,128)(2,1)S(1)}, bf16[144,512]{1,0:T(8,128)(2,1)S(1)}, u32[]{:S(2)}, u32[]{:S(2)}) collective-permute-start(bf16[144,512]{1,0:T(8,128)(2,1)S(1)} %get-tuple-element.46), channel_id=1, source_target_pairs={{0,3},{1,2},{2,1},{3,0},{4,7},{5,6},{6,5},{7,4},{8,11},{9,10},{10,... | collective-permute-start | bytes 442376 | tf_op jit(solution)/shard_map/ppermute | solution.py:324
  120.4 1.9 %collective-permute-start.26 = (bf16[144,512]{1,0:T(8,128)(2,1)S(1)}, bf16[144,512]{1,0:T(8,128)(2,1)S(1)}, u32[]{:S(2)}, u32[]{:S(2)}) collective-permute-start(bf16[144,512]{1,0:T(8,128)(2,1)S(1)} %get-tuple-element.41), channel_id=1, source_target_pairs={{0,2},{1,3},{2,0},{3,1},{4,6},{5,7},{6,4},{7,5},{8,10},{9,11},{10,... | collective-permute-start | bytes 442376 | tf_op jit(solution)/shard_map/ppermute | solution.py:324
  122.7 2.2 %collective-permute-start.27 = (bf16[144,512]{1,0:T(8,128)(2,1)S(1)}, bf16[144,512]{1,0:T(8,128)(2,1)S(1)}, u32[]{:S(2)}, u32[]{:S(2)}) collective-permute-start(bf16[144,512]{1,0:T(8,128)(2,1)S(1)} %get-tuple-element.42), channel_id=1, source_target_pairs={{0,3},{1,2},{2,1},{3,0},{4,7},{5,6},{6,5},{7,4},{8,11},{9,10},{10,... | collective-permute-start | bytes 442376 | tf_op jit(solution)/shard_map/ppermute | solution.py:324
  124.8 0.9 collective-permute-done.30.refs_2_
  125.7 1.1 collective-permute-done.31.refs_3_
  126.8 2.9 %shard_map.82 = (f32[192,1536]{1,0:T(8,128)S(1)}, f32[192,128]{1,0:T(8,128)S(1)}, f32[192,512]{1,0:T(8,128)S(1)}) custom-call(bf16[144,512]{1,0:T(8,128)(2,1)S(1)} %get-tuple-element.43.refs_0_, bf16[144,512]{1,0:T(8,128)(2,1)S(1)} %collective-permute-done.29.refs_1_, bf16[144,512]{1,0:T(8,128)(2,1)S(1)} %collective-permute-done.30.refs_2_, ...), custom_call_target="tpu_custom_call" | custom-call | flops 679477248 | bytes 4128768 | tf_op jit(solution)/shard_map/pallas_call | solution.py:83
  129.7 1.5 %collective-permute-done.26.refs_2_ = bf16[144,512]{1,0:T(8,128)(2,1)S(1)} collective-permute-done((bf16[144,512]{1,0:T(8,128)(2,1)S(1)}, bf16[144,512]{1,0:T(8,128)(2,1)S(1)}, u32[]{:S(2)}, u32[]{:S(2)}) %collective-permute-start.26) | collective-permute-done | bytes 147488 | tf_op jit(solution)/shard_map/ppermute | solution.py:324
  131.2 1.1 collective-permute-done.27.refs_3_
  132.2 1.9 %shard_map.83 = f32[192,2048]{1,0:T(8,128)} custom-call(bf16[144,512]{1,0:T(8,128)(2,1)S(1)} %get-tuple-element.39.refs_0_, bf16[144,512]{1,0:T(8,128)(2,1)S(1)} %collective-permute-done.25.refs_1_, bf16[144,512]{1,0:T(8,128)(2,1)S(1)} %collective-permute-done.26.refs_2_, bf16[144,512]{1,0:T(8,128)(2,1)S(1)} %collective-permute-done.27.refs_3_, ...), custom_call_target="tpu_custom_call" | custom-call | flops 226492416 | bytes 3145728 | tf_op jit(solution)/shard_map/pallas_call | solution.py:83
  (92 shorter events, 11.5 us)
Async XLA Ops:
  0.0 9.1 %collective-permute-start.12 = (bf16[256,768]{1,0:T(8,128)(2,1)}, bf16[256,768]{1,0:T(8,128)(2,1)}, u32[]{:S(2)}, u32[]{:S(2)}) collective-permute-start(bf16[256,768]{1,0:T(8,128)(2,1)} %bitcast.11), channel_id=1, source_target_pairs={{8,16},{12,20},{16,8},{20,12},{9,17},{13,21},{17,9},{21,13},{10,18... | collective-permute-start | bytes 1179656 | tf_op jit(solution)/shard_map/ppermute | solution.py:318
  1.4 8.1 %collective-permute-start.6 = (bf16[256,768]{1,0:T(8,128)(2,1)}, bf16[256,768]{1,0:T(8,128)(2,1)S(1)}, u32[]{:S(2)}, u32[]{:S(2)}) collective-permute-start(bf16[256,768]{1,0:T(8,128)(2,1)} %bitcast.7), channel_id=1, source_target_pairs={{8,16},{12,20},{16,8},{20,12},{9,17},{13,21},{17,9},{21,13},{10,18... | collective-permute-start | bytes 1179656 | tf_op jit(solution)/shard_map/ppermute | solution.py:318
  2.1 17.0 %collective-permute-start.10 = (bf16[256,768]{1,0:T(8,128)(2,1)}, bf16[256,768]{1,0:T(8,128)(2,1)S(1)}, u32[]{:S(2)}, u32[]{:S(2)}) collective-permute-start(bf16[256,768]{1,0:T(8,128)(2,1)} %bitcast.12), channel_id=1, source_target_pairs={{0,8},{4,12},{8,0},{12,4},{16,24},{20,28},{24,16},{28,20},{1,9},{5... | collective-permute-start | bytes 1179656 | tf_op jit(solution)/shard_map/ppermute | solution.py:318
  9.0 21.6 %collective-permute-start.4 = (bf16[256,768]{1,0:T(8,128)(2,1)}, bf16[256,768]{1,0:T(8,128)(2,1)S(1)}, u32[]{:S(2)}, u32[]{:S(2)}) collective-permute-start(bf16[256,768]{1,0:T(8,128)(2,1)} %bitcast.8), channel_id=1, source_target_pairs={{0,8},{4,12},{8,0},{12,4},{16,24},{20,28},{24,16},{28,20},{1,9},{5... | collective-permute-start | bytes 1179656 | tf_op jit(solution)/shard_map/ppermute | solution.py:318
  9.1 26.8 %collective-permute-start.3 = (bf16[256,768]{1,0:T(8,128)(2,1)}, bf16[256,768]{1,0:T(8,128)(2,1)S(1)}, u32[]{:S(2)}, u32[]{:S(2)}) collective-permute-start(bf16[256,768]{1,0:T(8,128)(2,1)} %bitcast.9), channel_id=1, source_target_pairs={{0,4},{4,0},{8,12},{12,8},{16,20},{20,16},{24,28},{28,24},{1,5},{5... | collective-permute-start | bytes 1179656 | tf_op jit(solution)/shard_map/ppermute | solution.py:321
  9.1 29.0 %collective-permute-start.9 = (bf16[256,768]{1,0:T(8,128)(2,1)}, bf16[256,768]{1,0:T(8,128)(2,1)S(1)}, u32[]{:S(2)}, u32[]{:S(2)}) collective-permute-start(bf16[256,768]{1,0:T(8,128)(2,1)} %bitcast.13), channel_id=1, source_target_pairs={{0,4},{4,0},{8,12},{12,8},{16,20},{20,16},{24,28},{28,24},{1,5},{5... | collective-permute-start | bytes 1179656 | tf_op jit(solution)/shard_map/ppermute | solution.py:321
  9.6 22.3 %copy-start.14 = (bf16[256,768]{1,0:T(8,128)(2,1)}, bf16[256,768]{1,0:T(8,128)(2,1)S(1)}, u32[]{:S(2)}) copy-start(bf16[256,768]{1,0:T(8,128)(2,1)S(1)} %collective-permute-done.6) | copy-start | bytes 1179652
  9.6 30.6 %collective-permute-start.37 = (bf16[256,768]{1,0:T(8,128)(2,1)}, bf16[256,768]{1,0:T(8,128)(2,1)S(1)}, u32[]{:S(2)}, u32[]{:S(2)}) collective-permute-start(bf16[256,768]{1,0:T(8,128)(2,1)} %bitcast.15), channel_id=1, source_target_pairs={{8,16},{12,20},{16,8},{20,12},{9,17},{13,21},{17,9},{21,13},{10,18... | collective-permute-start | bytes 1179656 | tf_op jit(solution)/shard_map/ppermute | solution.py:318
  19.1 22.6 %collective-permute-start.21 = (bf16[256,768]{1,0:T(8,128)(2,1)}, bf16[256,768]{1,0:T(8,128)(2,1)}, u32[]{:S(2)}, u32[]{:S(2)}) collective-permute-start(bf16[256,768]{1,0:T(8,128)(2,1)} %bitcast.16), channel_id=1, source_target_pairs={{0,8},{4,12},{24,16},{28,20},{1,9},{5,13},{25,17},{29,21},{2,10},{... | collective-permute-start | bytes 1179656 | tf_op jit(solution)/shard_map/ppermute | solution.py:318
  30.6 12.6 %collective-permute-start.32 = (bf16[256,768]{1,0:T(8,128)(2,1)}, bf16[256,768]{1,0:T(8,128)(2,1)}, u32[]{:S(2)}, u32[]{:S(2)}) collective-permute-start(bf16[256,768]{1,0:T(8,128)(2,1)} %bitcast.17), channel_id=1, source_target_pairs={{8,0},{12,4},{16,24},{20,28},{9,1},{13,5},{17,25},{21,29},{10,2},{... | collective-permute-start | bytes 1179656 | tf_op jit(solution)/shard_map/ppermute | solution.py:318
  36.6 13.6 %collective-permute-start = (bf16[144,2048]{1,0:T(8,128)(2,1)S(1)}, bf16[144,2048]{1,0:T(8,128)(2,1)S(1)}, u32[]{:S(2)}, u32[]{:S(2)}) collective-permute-start(bf16[144,2048]{1,0:T(8,128)(2,1)S(1)} %get-tuple-element.33), channel_id=1, source_target_pairs={{0,1},{1,0},{2,3},{3,2},{4,5},{5,4},{6,7},{7,6},{8,9},{9,8},{10,11... | collective-permute-start | bytes 1769480 | tf_op jit(solution)/shard_map/ppermute | solution.py:324
  38.9 14.9 %collective-permute-start.13 = (bf16[256,768]{1,0:T(8,128)(2,1)}, bf16[256,768]{1,0:T(8,128)(2,1)}, u32[]{:S(2)}, u32[]{:S(2)}) collective-permute-start(bf16[256,768]{1,0:T(8,128)(2,1)} %collective-permute-done.12), channel_id=1, source_target_pairs={{8,0},{12,4},{16,24},{20,28},{9,1},{13,5},{17,25},{21,29},{10,2},{... | collective-permute-start | bytes 1179656 | tf_op jit(solution)/shard_map/ppermute | solution.py:318
  40.2 16.0 %collective-permute-start.1 = (bf16[144,2048]{1,0:T(8,128)(2,1)S(1)}, bf16[144,2048]{1,0:T(8,128)(2,1)S(1)}, u32[]{:S(2)}, u32[]{:S(2)}) collective-permute-start(bf16[144,2048]{1,0:T(8,128)(2,1)S(1)} %get-tuple-element.34), channel_id=1, source_target_pairs={{0,2},{1,3},{2,0},{3,1},{4,6},{5,7},{6,4},{7,5},{8,10},{9,11},{10,... | collective-permute-start | bytes 1769480 | tf_op jit(solution)/shard_map/ppermute | solution.py:324
  41.8 22.3 %copy-start.15 = (bf16[256,768]{1,0:T(8,128)(2,1)S(1)}, bf16[256,768]{1,0:T(8,128)(2,1)}, u32[]{:S(2)}) copy-start(bf16[256,768]{1,0:T(8,128)(2,1)} %copy-done.14) | copy-start | bytes 1179652
  41.8 22.4 %copy-start.5 = (bf16[256,768]{1,0:T(8,128)(2,1)S(1)}, bf16[256,768]{1,0:T(8,128)(2,1)}, u32[]{:S(2)}) copy-start(bf16[256,768]{1,0:T(8,128)(2,1)} %copy-done.4) | copy-start | bytes 1179652
  41.8 30.1 %copy-start.17 = (bf16[256,768]{1,0:T(8,128)(2,1)S(1)}, bf16[256,768]{1,0:T(8,128)(2,1)}, u32[]{:S(2)}) copy-start(bf16[256,768]{1,0:T(8,128)(2,1)} %copy-done.16) | copy-start | bytes 1179652
  41.8 20.3 %collective-permute-start.7 = (bf16[256,768]{1,0:T(8,128)(2,1)}, bf16[256,768]{1,0:T(8,128)(2,1)S(1)}, u32[]{:S(2)}, u32[]{:S(2)}) collective-permute-start(bf16[256,768]{1,0:T(8,128)(2,1)} %copy-done.14), channel_id=1, source_target_pairs={{8,0},{12,4},{16,24},{20,28},{9,1},{13,5},{17,25},{21,29},{10,2},{... | collective-permute-start | bytes 1179656 | tf_op jit(solution)/shard_map/ppermute | solution.py:318
  43.2 19.6 %collective-permute-start.18 = (bf16[256,768]{1,0:T(8,128)(2,1)}, bf16[256,768]{1,0:T(8,128)(2,1)S(1)}, u32[]{:S(2)}, u32[]{:S(2)}) collective-permute-start(bf16[256,768]{1,0:T(8,128)(2,1)} %copy-done.6), channel_id=1, source_target_pairs={{8,16},{12,20},{16,8},{20,12},{9,17},{13,21},{17,9},{21,13},{10,18... | collective-permute-start | bytes 1179656 | tf_op jit(solution)/shard_map/ppermute | solution.py:318
  45.0 27.0 %copy-start.7 = (bf16[256,768]{1,0:T(8,128)(2,1)S(1)}, bf16[256,768]{1,0:T(8,128)(2,1)}, u32[]{:S(2)}) copy-start(bf16[256,768]{1,0:T(8,128)(2,1)} %copy-done.6) | copy-start | bytes 1179652
  50.3 13.9 %collective-permute-start.15 = (bf16[256,768]{1,0:T(8,128)(2,1)}, bf16[256,768]{1,0:T(8,128)(2,1)S(1)}, u32[]{:S(2)}, u32[]{:S(2)}) collective-permute-start(bf16[256,768]{1,0:T(8,128)(2,1)} %copy-done.4), channel_id=1, source_target_pairs={{8,16},{12,20},{16,8},{20,12},{9,17},{13,21},{17,9},{21,13},{10,18... | collective-permute-start | bytes 1179656 | tf_op jit(solution)/shard_map/ppermute | solution.py:318
  53.8 16.7 %collective-permute-start.38 = (bf16[256,768]{1,0:T(8,128)(2,1)}, bf16[256,768]{1,0:T(8,128)(2,1)S(1)}, u32[]{:S(2)}, u32[]{:S(2)}) collective-permute-start(bf16[256,768]{1,0:T(8,128)(2,1)} %copy-done.16), channel_id=1, source_target_pairs={{8,0},{12,4},{16,24},{20,28},{9,1},{13,5},{17,25},{21,29},{10,2},{... | collective-permute-start | bytes 1179656 | tf_op jit(solution)/shard_map/ppermute | solution.py:318
  56.1 24.3 %collective-permute-start.2 = (bf16[144,2048]{1,0:T(8,128)(2,1)S(1)}, bf16[144,2048]{1,0:T(8,128)(2,1)S(1)}, u32[]{:S(2)}, u32[]{:S(2)}) collective-permute-start(bf16[144,2048]{1,0:T(8,128)(2,1)S(1)} %get-tuple-element.35), channel_id=1, source_target_pairs={{0,3},{1,2},{2,1},{3,0},{4,7},{5,6},{6,5},{7,4},{8,11},{9,10},{10,... | collective-permute-start | bytes 1769480 | tf_op jit(solution)/shard_map/ppermute | solution.py:324
  62.1 9.8 %collective-permute-start.22 = (bf16[256,768]{1,0:T(8,128)(2,1)}, bf16[256,768]{1,0:T(8,128)(2,1)S(1)}, u32[]{:S(2)}, u32[]{:S(2)}) collective-permute-start(bf16[256,768]{1,0:T(8,128)(2,1)} %collective-permute-done.21), channel_id=1, source_target_pairs={{8,16},{12,20},{16,8},{20,12},{9,17},{13,21},{17,9},{21,13},{10,18... | collective-permute-start | bytes 1179656 | tf_op jit(solution)/shard_map/ppermute | solution.py:318
  62.8 16.2 %collective-permute-start.19 = (bf16[256,768]{1,0:T(8,128)(2,1)S(1)}, bf16[256,768]{1,0:T(8,128)(2,1)S(1)}, u32[]{:S(2)}, u32[]{:S(2)}) collective-permute-start(bf16[256,768]{1,0:T(8,128)(2,1)S(1)} %collective-permute-done.18), channel_id=1, source_target_pairs={{8,0},{12,4},{16,24},{20,28},{9,1},{13,5},{17,25},{21,29},{10,2},{... | collective-permute-start | bytes 1179656 | tf_op jit(solution)/shard_map/ppermute | solution.py:318
  64.2 16.4 %collective-permute-start.11 = (bf16[256,768]{1,0:T(8,128)(2,1)S(1)}, bf16[256,768]{1,0:T(8,128)(2,1)S(1)}, u32[]{:S(2)}, u32[]{:S(2)}) collective-permute-start(bf16[256,768]{1,0:T(8,128)(2,1)S(1)} %copy-done.5), channel_id=1, source_target_pairs={{0,4},{4,0},{8,12},{12,8},{16,20},{20,16},{24,28},{28,24},{1,5},{5... | collective-permute-start | bytes 1179656 | tf_op jit(solution)/shard_map/ppermute | solution.py:321
  70.5 16.9 %collective-permute-start.16 = (bf16[256,768]{1,0:T(8,128)(2,1)S(1)}, bf16[256,768]{1,0:T(8,128)(2,1)S(1)}, u32[]{:S(2)}, u32[]{:S(2)}) collective-permute-start(bf16[256,768]{1,0:T(8,128)(2,1)S(1)} %collective-permute-done.15), channel_id=1, source_target_pairs={{8,0},{12,4},{16,24},{20,28},{9,1},{13,5},{17,25},{21,29},{10,2},{... | collective-permute-start | bytes 1179656 | tf_op jit(solution)/shard_map/ppermute | solution.py:318
  72.0 15.5 %collective-permute-start.5 = (bf16[256,768]{1,0:T(8,128)(2,1)S(1)}, bf16[256,768]{1,0:T(8,128)(2,1)S(1)}, u32[]{:S(2)}, u32[]{:S(2)}) collective-permute-start(bf16[256,768]{1,0:T(8,128)(2,1)S(1)} %copy-done.7), channel_id=1, source_target_pairs={{0,4},{4,0},{8,12},{12,8},{16,20},{20,16},{24,28},{28,24},{1,5},{5... | collective-permute-start | bytes 1179656 | tf_op jit(solution)/shard_map/ppermute | solution.py:321
  79.0 14.0 %collective-permute-start.23 = (bf16[256,768]{1,0:T(8,128)(2,1)S(1)}, bf16[256,768]{1,0:T(8,128)(2,1)S(1)}, u32[]{:S(2)}, u32[]{:S(2)}) collective-permute-start(bf16[256,768]{1,0:T(8,128)(2,1)S(1)} %collective-permute-done.22), channel_id=1, source_target_pairs={{8,0},{12,4},{16,24},{20,28},{9,1},{13,5},{17,25},{21,29},{10,2},{... | collective-permute-start | bytes 1179656 | tf_op jit(solution)/shard_map/ppermute | solution.py:318
  80.5 12.5 %collective-permute-start.14 = (bf16[256,768]{1,0:T(8,128)(2,1)S(1)}, bf16[256,768]{1,0:T(8,128)(2,1)S(1)}, u32[]{:S(2)}, u32[]{:S(2)}) collective-permute-start(bf16[256,768]{1,0:T(8,128)(2,1)S(1)} %broadcast_select_fusion.5.refs_14_), channel_id=1, source_target_pairs={{0,4},{4,0},{8,12},{12,8},{16,20},{20,16},{24,28},{28,24},{1,5},{5... | collective-permute-start | bytes 1179656 | tf_op jit(solution)/shard_map/ppermute | solution.py:321
  80.6 13.0 %collective-permute-start.8 = (bf16[256,768]{1,0:T(8,128)(2,1)S(1)}, bf16[256,768]{1,0:T(8,128)(2,1)S(1)}, u32[]{:S(2)}, u32[]{:S(2)}) collective-permute-start(bf16[256,768]{1,0:T(8,128)(2,1)S(1)} %broadcast_select_fusion.6.refs_8_), channel_id=1, source_target_pairs={{0,4},{4,0},{8,12},{12,8},{16,20},{20,16},{24,28},{28,24},{1,5},{5... | collective-permute-start | bytes 1179656 | tf_op jit(solution)/shard_map/ppermute | solution.py:321
  87.4 6.3 %collective-permute-start.20 = (bf16[256,768]{1,0:T(8,128)(2,1)S(1)}, bf16[256,768]{1,0:T(8,128)(2,1)S(1)}, u32[]{:S(2)}, u32[]{:S(2)}) collective-permute-start(bf16[256,768]{1,0:T(8,128)(2,1)S(1)} %broadcast_select_fusion.3.own), channel_id=1, source_target_pairs={{0,4},{4,0},{8,12},{12,8},{16,20},{20,16},{24,28},{28,24},{1,5},{5... | collective-permute-start | bytes 1179656 | tf_op jit(solution)/shard_map/ppermute | solution.py:321
  87.4 15.0 %collective-permute-start.39 = (bf16[256,768]{1,0:T(8,128)(2,1)S(1)}, bf16[256,768]{1,0:T(8,128)(2,1)S(1)}, u32[]{:S(2)}, u32[]{:S(2)}) collective-permute-start(bf16[256,768]{1,0:T(8,128)(2,1)S(1)} %broadcast_select_fusion.own), channel_id=1, source_target_pairs={{0,4},{4,0},{8,12},{12,8},{16,20},{20,16},{24,28},{28,24},{1,5},{5... | collective-permute-start | bytes 1179656 | tf_op jit(solution)/shard_map/ppermute | solution.py:321
  93.0 9.1 %collective-permute-start.17 = (bf16[256,768]{1,0:T(8,128)(2,1)S(1)}, bf16[256,768]{1,0:T(8,128)(2,1)S(1)}, u32[]{:S(2)}, u32[]{:S(2)}) collective-permute-start(bf16[256,768]{1,0:T(8,128)(2,1)S(1)} %broadcast_select_fusion.4.own), channel_id=1, source_target_pairs={{0,4},{4,0},{8,12},{12,8},{16,20},{20,16},{24,28},{28,24},{1,5},{5... | collective-permute-start | bytes 1179656 | tf_op jit(solution)/shard_map/ppermute | solution.py:321
  93.0 14.3 %collective-permute-start.28 = (bf16[256,768]{1,0:T(8,128)(2,1)S(1)}, bf16[256,768]{1,0:T(8,128)(2,1)S(1)}, u32[]{:S(2)}, u32[]{:S(2)}) collective-permute-start(bf16[256,768]{1,0:T(8,128)(2,1)S(1)} %bitcast.18), channel_id=1, source_target_pairs={{0,4},{4,0},{8,12},{12,8},{16,20},{20,16},{24,28},{28,24},{1,5},{5... | collective-permute-start | bytes 1179656 | tf_op jit(solution)/shard_map/ppermute | solution.py:321
  93.6 12.3 %collective-permute-start.33 = (bf16[256,768]{1,0:T(8,128)(2,1)S(1)}, bf16[256,768]{1,0:T(8,128)(2,1)S(1)}, u32[]{:S(2)}, u32[]{:S(2)}) collective-permute-start(bf16[256,768]{1,0:T(8,128)(2,1)S(1)} %broadcast_select_fusion.1.own), channel_id=1, source_target_pairs={{0,4},{4,0},{8,12},{12,8},{16,20},{20,16},{24,28},{28,24},{1,5},{5... | collective-permute-start | bytes 1179656 | tf_op jit(solution)/shard_map/ppermute | solution.py:321
  93.7 15.6 %collective-permute-start.24 = (bf16[256,768]{1,0:T(8,128)(2,1)S(1)}, bf16[256,768]{1,0:T(8,128)(2,1)S(1)}, u32[]{:S(2)}, u32[]{:S(2)}) collective-permute-start(bf16[256,768]{1,0:T(8,128)(2,1)S(1)} %broadcast_select_fusion.2.own), channel_id=1, source_target_pairs={{0,4},{4,0},{8,12},{12,8},{16,20},{20,16},{24,28},{28,24},{1,5},{5... | collective-permute-start | bytes 1179656 | tf_op jit(solution)/shard_map/ppermute | solution.py:321
  103.2 7.8 %collective-permute-start.40 = (bf16[144,512]{1,0:T(8,128)(2,1)S(1)}, bf16[144,512]{1,0:T(8,128)(2,1)S(1)}, u32[]{:S(2)}, u32[]{:S(2)}) collective-permute-start(bf16[144,512]{1,0:T(8,128)(2,1)S(1)} %get-tuple-element.52), channel_id=1, source_target_pairs={{0,1},{1,0},{2,3},{3,2},{4,5},{5,4},{6,7},{7,6},{8,9},{9,8},{10,11... | collective-permute-start | bytes 442376 | tf_op jit(solution)/shard_map/ppermute | solution.py:324
  104.4 8.7 %collective-permute-start.41 = (bf16[144,512]{1,0:T(8,128)(2,1)S(1)}, bf16[144,512]{1,0:T(8,128)(2,1)S(1)}, u32[]{:S(2)}, u32[]{:S(2)}) collective-permute-start(bf16[144,512]{1,0:T(8,128)(2,1)S(1)} %get-tuple-element.53), channel_id=1, source_target_pairs={{0,2},{1,3},{2,0},{3,1},{4,6},{5,7},{6,4},{7,5},{8,10},{9,11},{10,... | collective-permute-start | bytes 442376 | tf_op jit(solution)/shard_map/ppermute | solution.py:324
  106.0 8.1 %collective-permute-start.42 = (bf16[144,512]{1,0:T(8,128)(2,1)S(1)}, bf16[144,512]{1,0:T(8,128)(2,1)S(1)}, u32[]{:S(2)}, u32[]{:S(2)}) collective-permute-start(bf16[144,512]{1,0:T(8,128)(2,1)S(1)} %get-tuple-element.54), channel_id=1, source_target_pairs={{0,3},{1,2},{2,1},{3,0},{4,7},{5,6},{6,5},{7,4},{8,11},{9,10},{10,... | collective-permute-start | bytes 442376 | tf_op jit(solution)/shard_map/ppermute | solution.py:324
  107.4 8.9 %collective-permute-start.34 = (bf16[144,512]{1,0:T(8,128)(2,1)S(1)}, bf16[144,512]{1,0:T(8,128)(2,1)S(1)}, u32[]{:S(2)}, u32[]{:S(2)}) collective-permute-start(bf16[144,512]{1,0:T(8,128)(2,1)S(1)} %get-tuple-element.48), channel_id=1, source_target_pairs={{0,1},{1,0},{2,3},{3,2},{4,5},{5,4},{6,7},{7,6},{8,9},{9,8},{10,11... | collective-permute-start | bytes 442376 | tf_op jit(solution)/shard_map/ppermute | solution.py:324
  109.3 10.1 %collective-permute-start.35 = (bf16[144,512]{1,0:T(8,128)(2,1)S(1)}, bf16[144,512]{1,0:T(8,128)(2,1)S(1)}, u32[]{:S(2)}, u32[]{:S(2)}) collective-permute-start(bf16[144,512]{1,0:T(8,128)(2,1)S(1)} %get-tuple-element.49), channel_id=1, source_target_pairs={{0,2},{1,3},{2,0},{3,1},{4,6},{5,7},{6,4},{7,5},{8,10},{9,11},{10,... | collective-permute-start | bytes 442376 | tf_op jit(solution)/shard_map/ppermute | solution.py:324
  110.9 9.5 %collective-permute-start.36 = (bf16[144,512]{1,0:T(8,128)(2,1)S(1)}, bf16[144,512]{1,0:T(8,128)(2,1)S(1)}, u32[]{:S(2)}, u32[]{:S(2)}) collective-permute-start(bf16[144,512]{1,0:T(8,128)(2,1)S(1)} %get-tuple-element.50), channel_id=1, source_target_pairs={{0,3},{1,2},{2,1},{3,0},{4,7},{5,6},{6,5},{7,4},{8,11},{9,10},{10,... | collective-permute-start | bytes 442376 | tf_op jit(solution)/shard_map/ppermute | solution.py:324
  113.1 9.6 %collective-permute-start.29 = (bf16[144,512]{1,0:T(8,128)(2,1)S(1)}, bf16[144,512]{1,0:T(8,128)(2,1)S(1)}, u32[]{:S(2)}, u32[]{:S(2)}) collective-permute-start(bf16[144,512]{1,0:T(8,128)(2,1)S(1)} %get-tuple-element.44), channel_id=1, source_target_pairs={{0,1},{1,0},{2,3},{3,2},{4,5},{5,4},{6,7},{7,6},{8,9},{9,8},{10,11... | collective-permute-start | bytes 442376 | tf_op jit(solution)/shard_map/ppermute | solution.py:324
  114.1 11.7 %collective-permute-start.30 = (bf16[144,512]{1,0:T(8,128)(2,1)S(1)}, bf16[144,512]{1,0:T(8,128)(2,1)S(1)}, u32[]{:S(2)}, u32[]{:S(2)}) collective-permute-start(bf16[144,512]{1,0:T(8,128)(2,1)S(1)} %get-tuple-element.45), channel_id=1, source_target_pairs={{0,2},{1,3},{2,0},{3,1},{4,6},{5,7},{6,4},{7,5},{8,10},{9,11},{10,... | collective-permute-start | bytes 442376 | tf_op jit(solution)/shard_map/ppermute | solution.py:324
  116.3 10.5 %collective-permute-start.31 = (bf16[144,512]{1,0:T(8,128)(2,1)S(1)}, bf16[144,512]{1,0:T(8,128)(2,1)S(1)}, u32[]{:S(2)}, u32[]{:S(2)}) collective-permute-start(bf16[144,512]{1,0:T(8,128)(2,1)S(1)} %get-tuple-element.46), channel_id=1, source_target_pairs={{0,3},{1,2},{2,1},{3,0},{4,7},{5,6},{6,5},{7,4},{8,11},{9,10},{10,... | collective-permute-start | bytes 442376 | tf_op jit(solution)/shard_map/ppermute | solution.py:324
  119.4 10.2 %collective-permute-start.25 = (bf16[144,512]{1,0:T(8,128)(2,1)S(1)}, bf16[144,512]{1,0:T(8,128)(2,1)S(1)}, u32[]{:S(2)}, u32[]{:S(2)}) collective-permute-start(bf16[144,512]{1,0:T(8,128)(2,1)S(1)} %get-tuple-element.40), channel_id=1, source_target_pairs={{0,1},{1,0},{2,3},{3,2},{4,5},{5,4},{6,7},{7,6},{8,9},{9,8},{10,11... | collective-permute-start | bytes 442376 | tf_op jit(solution)/shard_map/ppermute | solution.py:324
  120.4 10.7 %collective-permute-start.26 = (bf16[144,512]{1,0:T(8,128)(2,1)S(1)}, bf16[144,512]{1,0:T(8,128)(2,1)S(1)}, u32[]{:S(2)}, u32[]{:S(2)}) collective-permute-start(bf16[144,512]{1,0:T(8,128)(2,1)S(1)} %get-tuple-element.41), channel_id=1, source_target_pairs={{0,2},{1,3},{2,0},{3,1},{4,6},{5,7},{6,4},{7,5},{8,10},{9,11},{10,... | collective-permute-start | bytes 442376 | tf_op jit(solution)/shard_map/ppermute | solution.py:324
  122.7 9.6 %collective-permute-start.27 = (bf16[144,512]{1,0:T(8,128)(2,1)S(1)}, bf16[144,512]{1,0:T(8,128)(2,1)S(1)}, u32[]{:S(2)}, u32[]{:S(2)}) collective-permute-start(bf16[144,512]{1,0:T(8,128)(2,1)S(1)} %get-tuple-element.42), channel_id=1, source_target_pairs={{0,3},{1,2},{2,1},{3,0},{4,7},{5,6},{6,5},{7,4},{8,11},{9,10},{10,... | collective-permute-start | bytes 442376 | tf_op jit(solution)/shard_map/ppermute | solution.py:324
  (13 other events, 155.8 us)

commit v2 on v1

--- a/solution.py
+++ b/solution.py
@@ -123,13 +123,22 @@
     def turned(a, b):
         return lax.dot_general(a, b, nt, preferred_element_type=F32)
 
+    column = lax.broadcasted_iota(jnp.int32, (count, experts * capacity), 1).astype(F32)
+    rank_c = jnp.where(turned(eye, mask) > 0.5, turned(lower, mask), -float(experts * capacity))
+    for half, part_w in enumerate((high, low)):
+        w_c = turned(eye, part_w)
+        total = jnp.zeros((count, experts * capacity), F32)
+        for m in range(experts):
+            hit = column == rank_c[:, m : m + 1] + float(m * capacity)
+            total = jnp.where(hit, w_c[:, m : m + 1], total)
+        c_ref[half * count : (half + 1) * count, :] = total.astype(BF16)
     rank = jnp.where(named, jnp.dot(mask, upper, preferred_element_type=F32), -1.0)
+    slot = lax.broadcasted_iota(jnp.int32, (capacity, count), 0).astype(F32)
     tok_copy.wait()
     for place, s in enumerate(slice_order()):
         tokp[:, place * part : (place + 1) * part] = tok_ref[
             :, pl.ds(pl.multiple_of(s * part, part), part)
         ].astype(BF16)
-    slot = lax.broadcasted_iota(jnp.int32, (capacity, count), 0).astype(F32)
     for m in range(experts):
         select = jnp.where(slot == rank[m : m + 1, :], 1.0, 0.0).astype(BF16)
         block = jnp.dot(select, tokp[...], preferred_element_type=F32).astype(BF16)
@@ -139,15 +148,6 @@
             local_copy.start()
         else:
             outs[m][...] = block
-    column = lax.broadcasted_iota(jnp.int32, (count, experts * capacity), 1).astype(F32)
-    rank_c = jnp.where(turned(eye, mask) > 0.5, turned(lower, mask), -float(experts * capacity))
-    for half, part_w in enumerate((high, low)):
-        w_c = turned(eye, part_w)
-        total = jnp.zeros((count, experts * capacity), F32)
-        for m in range(experts):
-            hit = column == rank_c[:, m : m + 1] + float(m * capacity)
-            total = jnp.where(hit, w_c[:, m : m + 1], total)
-        c_ref[half * count : (half + 1) * count, :] = total.astype(BF16)
     local_copy.wait()
 
 
@@ -206,13 +206,12 @@
 
 
 def down_kernel(experts, capacity, hidden, own, other, *outs):
-    part = own.shape[0]
-    for half, w in enumerate((own, other)):
-        result = lax.dot_general(
-            hidden[...], w[...], (((1,), (1,)), ((), ())), preferred_element_type=F32
-        ).astype(BF16)
-        for m in range(experts):
-            outs[m][:, half * part : (half + 1) * part] = result[m * capacity : (m + 1) * capacity]
+    both = jnp.concatenate([own[...], other[...]], axis=0)
+    result = lax.dot_general(
+        hidden[...], both, (((1,), (1,)), ((), ())), preferred_element_type=F32
+    ).astype(BF16)
+    for m in range(experts):
+        outs[m][...] = result[m * capacity : (m + 1) * capacity]
 
 
 def chunk(stages, blocks, tokens, c_ref, back, tok, sems):
@@ -262,13 +261,17 @@
         copy.wait()
 
 
-def finish_kernel(*refs):
+def finish_kernel(halves, *refs):
     *blocks, tok, c_ref, gain, mixed, square, out_hbm, back, out, sems = refs
-    capacity = blocks[0].shape[0]
+    experts = len(blocks) // halves
+    capacity, piece = blocks[0].shape
     count, wide = tok.shape
-    part = wide // 2
-    for m, b in enumerate(blocks):
-        back[m * capacity : (m + 1) * capacity, :] = b[...]
+    part, step = wide // 2, piece // 2
+    for i, b in enumerate(blocks):
+        rows = slice(i % experts * capacity, (i % experts + 1) * capacity)
+        for h in range(2):
+            lo = h * part + i // experts * step
+            back[rows, lo : lo + step] = b[:, h * step : (h + 1) * step]
     both = jnp.dot(c_ref[...], back[...], preferred_element_type=F32)
     here = tok[...] + (both[:count] + both[count:])
     total = jnp.sum(here * here, axis=1, keepdims=True) + square[:, 0:1]
@@ -302,6 +305,7 @@
 PAIR = [(0, 1), (1, 0), (2, 3), (3, 2)]
 INWARD = [(0, 1), (3, 2)]
 OUTWARD = [(1, 0), (2, 3)]
+HALVES = 2
 
 
 def layer(tokens, expert_ids, combine_weights, gate, up, down, norm_gain):
@@ -323,8 +327,8 @@
     def across(x, m):
         return lax.ppermute(x, "expert", [(e, e ^ m) for e in range(experts)])
 
-    def line(w, split):
-        if split:
+    def line(w, down):
+        if down:
             inner = along(w, INWARD)
             outer = along(w, OUTWARD)
             one = jnp.where(end, outer, inner)
@@ -333,14 +337,20 @@
         mid = along(w, MIDDLE)
         mid_in = along(inner, MIDDLE)
         two = jnp.where(end, along(mid, OUTWARD), mid)
-        three = jnp.where(end, along(mid_in, OUTWARD), mid_in)
-        return [x for v in (w, one, two, three) for x in (v, swap(v))]
+        parts = [mid_in]
+        if down:
+            step = mid_in.shape[0] // HALVES
+            parts = [mid_in[i * step : (i + 1) * step] for i in range(HALVES)]
+            parts = lax.optimization_barrier(parts)
+        three = [jnp.where(end, along(x, OUTWARD), x) for x in parts]
+        return [x for v in (w, one, two, *three) for x in (v, swap(v))]
 
     g_all, u_all, d_all = line(gate, False), line(up, False), line(down, True)
 
     *placed, mix = call(
         functools.partial(place_kernel, experts, capacity),
-        [jax.ShapeDtypeStruct((capacity, width), BF16)] * experts
+        [pltpu.HBM((capacity, width), BF16)]
+        + [jax.ShapeDtypeStruct((capacity, width), BF16)] * (experts - 1)
         + [jax.ShapeDtypeStruct((2 * count, slots), BF16)],
         tuple(stay(x) for x in (expert_ids.T, combine_weights.T, tokens)),
         [HBM] * 3,
@@ -397,14 +407,16 @@
     )
 
     backs = []
-    for stage in range(CHAIN):
+    for stage in range(CHAIN - 1 + HALVES):
+        own, other = d_all[2 * stage : 2 * stage + 2]
+        wide = 2 * own.shape[0]
         outs = call(
             functools.partial(down_kernel, experts, capacity),
-            [jax.ShapeDtypeStruct((capacity, 2 * part), BF16)] * experts,
-            (hidden, d_all[2 * stage], d_all[2 * stage + 1]),
+            [jax.ShapeDtypeStruct((capacity, wide), BF16)] * experts,
+            (hidden, own, other),
             [VMEM] * 3,
-            flops=4 * slots * ff * part,
-            moved=slots * ff * 2 + 4 * part * ff + slots * part * 4,
+            flops=2 * slots * ff * wide,
+            moved=slots * ff * 2 + 2 * wide * ff + slots * wide * 2,
         )
         backs.append([outs[0]] + [across(outs[m], m) for m in range(1, experts)])
 
@@ -430,10 +442,13 @@
         moved=slots * wide * 2 + count * wide * 8,
     )
     return call(
-        finish_kernel,
+        functools.partial(finish_kernel, HALVES),
         jax.ShapeDtypeStruct((count, width), F32),
-        (*backs[-1], rest, mix, norm_gain.reshape(1, width), mixed, square),
-        [VMEM] * (experts + 5),
+        (
+            *(b for x in backs[CHAIN - 1 :] for b in x),
+            *(rest, mix, norm_gain.reshape(1, width), mixed, square),
+        ),
+        [VMEM] * (experts * HALVES + 5),
         [
             pltpu.VMEM((slots, 2 * part), BF16),
             pltpu.VMEM((count, width), F32),

time: 135 us -> 139 us (1.030)
  waiting for transfers between devices: 53.7 us -> 63.4 us
  local copies, waits for them, and re-layouts: 2.39 us -> 0.05 us
  other arithmetic: 2.32 us -> 0.32 us
    ppermute x15 -> x18, waiting for transfers between devices: 13 us -> 18.6 us  [across(): return lax.ppermute(x, 'expert', [(e, e ^ m) for e in range(experts)])]
    ppermute x16 -> x17, waiting for transfers between devices: 40.6 us -> 44.7 us  [along(): return lax.ppermute(x, 'replica', devices)]
    ppermute x15 -> x18, starting transfers between devices: 21.1 us -> 24.6 us  [across(): return lax.ppermute(x, 'expert', [(e, e ^ m) for e in range(experts)])]
    ppermute x16 -> x17, starting transfers between devices: 32.5 us -> 29.1 us  [along(): return lax.ppermute(x, 'replica', devices)]
    unnamed x36 -> x10, local copies, waits for them, and re-layouts: 2.39 us -> 0.03 us
    ppermute x12 -> x13, starting transfers between devices: 2.87 us -> 2.45 us  [swap(): return lax.ppermute(x, 'replica', [(r, r ^ 1) for r in range(2 * CHAIN)])]
    pallas_call x11 -> x12, Pallas kernels: 18.8 us -> 18.4 us  [call(): pl.pallas_call(kernel, out_shape=out_shape, in_specs=list(specs), out_spe...]
  transfers between devices with their start and end apart: 43 -> 48, of which waited for: 18 -> 14; matrix products, arithmetic and copies ran while one was open for 2% -> 0% of each run, Pallas kernels for 13% -> 12%
where the time goes in v2:
time: 139 us
  waiting for transfers between devices  63.4 us (46%)
  starting transfers between devices  56.1 us (40%)
  Pallas kernels  18.4 us (13%)
    ppermute x17, waiting for transfers between devices, along(): return lax.ppermute(x, 'replica', devices)  44.7 us
    ppermute x17, starting transfers between devices, along(): return lax.ppermute(x, 'replica', devices)  29.1 us
    ppermute x18, starting transfers between devices, across(): return lax.ppermute(x, 'expert', [(e, e ^ m) for e in range(experts)])  24.6 us
    ppermute x18, waiting for transfers between devices, across(): return lax.ppermute(x, 'expert', [(e, e ^ m) for e in range(experts)])  18.6 us
    pallas_call x12, Pallas kernels, call(): pl.pallas_call(kernel, out_shape=out_shape, in_specs=list(specs), out_spe...  18.4 us
  transfers between devices with their start and end apart: 48, of which 14 were waited for; matrix products, arithmetic and copies ran while one was open for 0% of the time, Pallas kernels for 12%

profile of v2, /device:TPU:0, one launch (start us, length us, event | category | flops | bytes accessed | tf_op | source)
XLA Modules:
  0.0 139.0 jit_solution(1635381428032292215)
XLA Ops:
  0.0 0.8 collective-permute-start.12
  0.8 0.7 collective-permute-start.6
  1.5 7.6 %collective-permute-start.10 = (bf16[256,768]{1,0:T(8,128)(2,1)}, bf16[256,768]{1,0:T(8,128)(2,1)S(1)}, u32[]{:S(2)}, u32[]{:S(2)}) collective-permute-start(bf16[256,768]{1,0:T(8,128)(2,1)} %bitcast.12), channel_id=1, source_target_pairs={{0,8},{4,12},{8,0},{12,4},{16,24},{20,28},{24,16},{28,20},{1,9},{5... | collective-permute-start | bytes 1179656 | tf_op jit(solution)/shard_map/ppermute | solution.py:322
  9.1 1.9 %collective-permute-start.21 = (bf16[256,768]{1,0:T(8,128)(2,1)}, bf16[256,768]{1,0:T(8,128)(2,1)S(1)}, u32[]{:S(2)}, u32[]{:S(2)}) collective-permute-start(bf16[256,768]{1,0:T(8,128)(2,1)} %bitcast.15), channel_id=1, source_target_pairs={{0,8},{4,12},{24,16},{28,20},{1,9},{5,13},{25,17},{29,21},{2,10},{... | collective-permute-start | bytes 1179656 | tf_op jit(solution)/shard_map/ppermute | solution.py:322
  11.1 1.3 collective-permute-start.37
  12.4 4.9 %collective-permute-start.4 = (bf16[256,768]{1,0:T(8,128)(2,1)}, bf16[256,768]{1,0:T(8,128)(2,1)S(1)}, u32[]{:S(2)}, u32[]{:S(2)}) collective-permute-start(bf16[256,768]{1,0:T(8,128)(2,1)} %bitcast.8), channel_id=1, source_target_pairs={{0,8},{4,12},{8,0},{12,4},{16,24},{20,28},{24,16},{28,20},{1,9},{5... | collective-permute-start | bytes 1179656 | tf_op jit(solution)/shard_map/ppermute | solution.py:322
  17.3 2.0 %collective-permute-done.10.refs_12_ = bf16[256,768]{1,0:T(8,128)(2,1)S(1)} collective-permute-done((bf16[256,768]{1,0:T(8,128)(2,1)}, bf16[256,768]{1,0:T(8,128)(2,1)S(1)}, u32[]{:S(2)}, u32[]{:S(2)}) %collective-permute-start.10) | collective-permute-done | bytes 393248 | tf_op jit(solution)/shard_map/ppermute | solution.py:322
  19.3 1.3 collective-permute-start.13
  20.6 2.6 %shard_map.73 = (bf16[144,2048]{1,0:T(8,128)(2,1)}, bf16[144,2048]{1,0:T(8,128)(2,1)S(1)}, bf16[144,2048]{1,0:T(8,128)(2,1)S(1)}, bf16[144,2048]{1,0:T(8,128)(2,1)S(1)}, bf16[384,576]{1,0:T(8,128)(2,1)S(1)}) custom-call(s32[2,192]{1,0:T(2,128)} %bitcast.20, f32[2,192]{1,0:T(2,128)} %bitcast.21, f32[192,2048]{1,0:T(8,128)} %refs_12_.1), custom_call_target="tpu_custom_call" | custom-call | flops 452984832 | bytes 3932160 | tf_op jit(solution)/shard_map/pallas_call | solution.py:83
  23.2 4.1 %collective-permute-done.21 = bf16[256,768]{1,0:T(8,128)(2,1)S(1)} collective-permute-done((bf16[256,768]{1,0:T(8,128)(2,1)}, bf16[256,768]{1,0:T(8,128)(2,1)S(1)}, u32[]{:S(2)}, u32[]{:S(2)}) %collective-permute-start.21) | collective-permute-done | bytes 393248 | tf_op jit(solution)/shard_map/ppermute | solution.py:322
  28.0 1.3 collective-permute-start.7
  29.4 6.7 %collective-permute-done.4.refs_6_ = bf16[256,768]{1,0:T(8,128)(2,1)S(1)} collective-permute-done((bf16[256,768]{1,0:T(8,128)(2,1)}, bf16[256,768]{1,0:T(8,128)(2,1)S(1)}, u32[]{:S(2)}, u32[]{:S(2)}) %collective-permute-start.4) | collective-permute-done | bytes 393248 | tf_op jit(solution)/shard_map/ppermute | solution.py:322
  36.1 1.6 %collective-permute-start = (bf16[144,2048]{1,0:T(8,128)(2,1)S(1)}, bf16[144,2048]{1,0:T(8,128)(2,1)S(1)}, u32[]{:S(2)}, u32[]{:S(2)}) collective-permute-start(bf16[144,2048]{1,0:T(8,128)(2,1)S(1)} %get-tuple-element.39), channel_id=1, source_target_pairs={{0,1},{1,0},{2,3},{3,2},{4,5},{5,4},{6,7},{7,6},{8,9},{9,8},{10,11... | collective-permute-start | bytes 1769480 | tf_op jit(solution)/shard_map/ppermute | solution.py:328
  37.7 6.9 %collective-permute-done.13 = bf16[256,768]{1,0:T(8,128)(2,1)S(1)} collective-permute-done((bf16[256,768]{1,0:T(8,128)(2,1)S(1)}, bf16[256,768]{1,0:T(8,128)(2,1)S(1)}, u32[]{:S(2)}, u32[]{:S(2)}) %collective-permute-start.13) | collective-permute-done | bytes 393248 | tf_op jit(solution)/shard_map/ppermute | solution.py:322
  44.6 0.7 collective-permute-start.22
  45.3 0.7 collective-permute-start.18
  46.0 5.6 %collective-permute-done.7 = bf16[256,768]{1,0:T(8,128)(2,1)S(1)} collective-permute-done((bf16[256,768]{1,0:T(8,128)(2,1)S(1)}, bf16[256,768]{1,0:T(8,128)(2,1)S(1)}, u32[]{:S(2)}, u32[]{:S(2)}) %collective-permute-start.7) | collective-permute-done | bytes 393248 | tf_op jit(solution)/shard_map/ppermute | solution.py:322
  51.6 1.3 collective-permute-start.43
  52.9 1.6 %collective-permute-start.1 = (bf16[144,2048]{1,0:T(8,128)(2,1)S(1)}, bf16[144,2048]{1,0:T(8,128)(2,1)S(1)}, u32[]{:S(2)}, u32[]{:S(2)}) collective-permute-start(bf16[144,2048]{1,0:T(8,128)(2,1)S(1)} %get-tuple-element.40), channel_id=1, source_target_pairs={{0,2},{1,3},{2,0},{3,1},{4,6},{5,7},{6,4},{7,5},{8,10},{9,11},{10,... | collective-permute-start | bytes 1769480 | tf_op jit(solution)/shard_map/ppermute | solution.py:328
  54.5 0.7 collective-permute-start.15
  55.2 1.5 %collective-permute-start.2 = (bf16[144,2048]{1,0:T(8,128)(2,1)S(1)}, bf16[144,2048]{1,0:T(8,128)(2,1)S(1)}, u32[]{:S(2)}, u32[]{:S(2)}) collective-permute-start(bf16[144,2048]{1,0:T(8,128)(2,1)S(1)} %get-tuple-element.41), channel_id=1, source_target_pairs={{0,3},{1,2},{2,1},{3,0},{4,7},{5,6},{6,5},{7,4},{8,11},{9,10},{10,... | collective-permute-start | bytes 1769480 | tf_op jit(solution)/shard_map/ppermute | solution.py:328
  56.7 1.3 collective-permute-start.28
  58.0 6.4 %collective-permute-done.43 = bf16[256,768]{1,0:T(8,128)(2,1)S(1)} collective-permute-done((bf16[256,768]{1,0:T(8,128)(2,1)S(1)}, bf16[256,768]{1,0:T(8,128)(2,1)S(1)}, u32[]{:S(2)}, u32[]{:S(2)}) %collective-permute-start.43) | collective-permute-done | bytes 393248 | tf_op jit(solution)/shard_map/ppermute | solution.py:322
  64.4 1.3 collective-permute-start.19
  65.9 5.9 %collective-permute-done.28 = bf16[128,768]{1,0:T(8,128)(2,1)S(1)} collective-permute-done((bf16[128,768]{1,0:T(8,128)(2,1)S(1)}, bf16[128,768]{1,0:T(8,128)(2,1)S(1)}, u32[]{:S(2)}, u32[]{:S(2)}) %collective-permute-start.28) | collective-permute-done | bytes 196640 | tf_op jit(solution)/shard_map/ppermute | solution.py:322
  71.8 1.3 collective-permute-start.16
  73.1 6.4 %collective-permute-done.1.refs_2_ = bf16[144,2048]{1,0:T(8,128)(2,1)S(1)} collective-permute-done((bf16[144,2048]{1,0:T(8,128)(2,1)S(1)}, bf16[144,2048]{1,0:T(8,128)(2,1)S(1)}, u32[]{:S(2)}, u32[]{:S(2)}) %collective-permute-start.1) | collective-permute-done | bytes 589856 | tf_op jit(solution)/shard_map/ppermute | solution.py:328
  80.2 1.5 %collective-permute-start.23 = (bf16[128,768]{1,0:T(8,128)(2,1)S(1)}, bf16[128,768]{1,0:T(8,128)(2,1)S(1)}, u32[]{:S(2)}, u32[]{:S(2)}) collective-permute-start(bf16[128,768]{1,0:T(8,128)(2,1)S(1)} %get-tuple-element.45), channel_id=1, source_target_pairs={{8,0},{12,4},{16,24},{20,28},{9,1},{13,5},{17,25},{21,29},{10,2},{... | collective-permute-start | bytes 589832 | tf_op jit(solution)/shard_map/ppermute | solution.py:322
  81.7 2.8 %collective-permute-done.16 = bf16[256,768]{1,0:T(8,128)(2,1)S(1)} collective-permute-done((bf16[256,768]{1,0:T(8,128)(2,1)S(1)}, bf16[256,768]{1,0:T(8,128)(2,1)S(1)}, u32[]{:S(2)}, u32[]{:S(2)}) %collective-permute-start.16) | collective-permute-done | bytes 393248 | tf_op jit(solution)/shard_map/ppermute | solution.py:322
  85.1 4.3 %collective-permute-done.23 = bf16[128,768]{1,0:T(8,128)(2,1)S(1)} collective-permute-done((bf16[128,768]{1,0:T(8,128)(2,1)S(1)}, bf16[128,768]{1,0:T(8,128)(2,1)S(1)}, u32[]{:S(2)}, u32[]{:S(2)}) %collective-permute-start.23) | collective-permute-done | bytes 196640 | tf_op jit(solution)/shard_map/ppermute | solution.py:322
  90.6 6.6 %shard_map.74 = (f32[576,768]{1,0:T(8,128)S(1)}, f32[576,768]{1,0:T(8,128)S(1)}, bf16[576,512]{1,0:T(8,128)(2,1)S(1)}) custom-call(bf16[144,2048]{1,0:T(8,128)(2,1)S(1)} %copy-done.4, bf16[144,2048]{1,0:T(8,128)(2,1)S(1)} %collective-permute-done.refs_1_, bf16[144,2048]{1,0:T(8,128)(2,1)S(1)} %collective-permute-done.1.refs_2_, ...), custom_call_target="tpu_custom_call" | custom-call | flops 2717908992 | bytes 10027008 | tf_op jit(solution)/shard_map/pallas_call | solution.py:83
  97.8 0.8 shard_map.76.act
  99.7 1.6 %collective-permute-start.45 = (bf16[144,512]{1,0:T(8,128)(2,1)S(1)}, bf16[144,512]{1,0:T(8,128)(2,1)S(1)}, u32[]{:S(2)}, u32[]{:S(2)}) collective-permute-start(bf16[144,512]{1,0:T(8,128)(2,1)S(1)} %get-tuple-element.64), channel_id=1, source_target_pairs={{0,1},{1,0},{2,3},{3,2},{4,5},{5,4},{6,7},{7,6},{8,9},{9,8},{10,11... | collective-permute-start | bytes 442376 | tf_op jit(solution)/shard_map/ppermute | solution.py:328
  101.2 1.5 %collective-permute-start.46 = (bf16[144,512]{1,0:T(8,128)(2,1)S(1)}, bf16[144,512]{1,0:T(8,128)(2,1)S(1)}, u32[]{:S(2)}, u32[]{:S(2)}) collective-permute-start(bf16[144,512]{1,0:T(8,128)(2,1)S(1)} %get-tuple-element.65), channel_id=1, source_target_pairs={{0,2},{1,3},{2,0},{3,1},{4,6},{5,7},{6,4},{7,5},{8,10},{9,11},{10,... | collective-permute-start | bytes 442376 | tf_op jit(solution)/shard_map/ppermute | solution.py:328
  104.0 1.5 %collective-permute-start.39 = (bf16[144,512]{1,0:T(8,128)(2,1)S(1)}, bf16[144,512]{1,0:T(8,128)(2,1)S(1)}, u32[]{:S(2)}, u32[]{:S(2)}) collective-permute-start(bf16[144,512]{1,0:T(8,128)(2,1)S(1)} %get-tuple-element.60), channel_id=1, source_target_pairs={{0,1},{1,0},{2,3},{3,2},{4,5},{5,4},{6,7},{7,6},{8,9},{9,8},{10,11... | collective-permute-start | bytes 442376 | tf_op jit(solution)/shard_map/ppermute | solution.py:328
  107.1 6.7 %collective-permute-done.30.refs_5_ = bf16[144,256]{1,0:T(8,128)(2,1)S(1)} collective-permute-done((bf16[144,256]{1,0:T(8,128)(2,1)S(1)}, bf16[144,256]{1,0:T(8,128)(2,1)S(1)}, u32[]{:S(2)}, u32[]{:S(2)}) %collective-permute-start.30) | collective-permute-done | bytes 73760 | tf_op jit(solution)/shard_map/ppermute | solution.py:328
  113.8 1.5 %collective-permute-start.40 = (bf16[144,512]{1,0:T(8,128)(2,1)S(1)}, bf16[144,512]{1,0:T(8,128)(2,1)S(1)}, u32[]{:S(2)}, u32[]{:S(2)}) collective-permute-start(bf16[144,512]{1,0:T(8,128)(2,1)S(1)} %get-tuple-element.61), channel_id=1, source_target_pairs={{0,2},{1,3},{2,0},{3,1},{4,6},{5,7},{6,4},{7,5},{8,10},{9,11},{10,... | collective-permute-start | bytes 442376 | tf_op jit(solution)/shard_map/ppermute | solution.py:328
  115.4 1.4 %collective-permute-start.41 = (bf16[144,512]{1,0:T(8,128)(2,1)S(1)}, bf16[144,512]{1,0:T(8,128)(2,1)S(1)}, u32[]{:S(2)}, u32[]{:S(2)}) collective-permute-start(bf16[144,512]{1,0:T(8,128)(2,1)S(1)} %get-tuple-element.62), channel_id=1, source_target_pairs={{0,3},{1,2},{2,1},{3,0},{4,7},{5,6},{6,5},{7,4},{8,11},{9,10},{10,... | collective-permute-start | bytes 442376 | tf_op jit(solution)/shard_map/ppermute | solution.py:328
  117.3 1.5 %collective-permute-start.35 = (bf16[144,512]{1,0:T(8,128)(2,1)S(1)}, bf16[144,512]{1,0:T(8,128)(2,1)S(1)}, u32[]{:S(2)}, u32[]{:S(2)}) collective-permute-start(bf16[144,512]{1,0:T(8,128)(2,1)S(1)} %get-tuple-element.57), channel_id=1, source_target_pairs={{0,2},{1,3},{2,0},{3,1},{4,6},{5,7},{6,4},{7,5},{8,10},{9,11},{10,... | collective-permute-start | bytes 442376 | tf_op jit(solution)/shard_map/ppermute | solution.py:328
  118.9 1.4 %collective-permute-start.36 = (bf16[144,512]{1,0:T(8,128)(2,1)S(1)}, bf16[144,512]{1,0:T(8,128)(2,1)S(1)}, u32[]{:S(2)}, u32[]{:S(2)}) collective-permute-start(bf16[144,512]{1,0:T(8,128)(2,1)S(1)} %get-tuple-element.58), channel_id=1, source_target_pairs={{0,3},{1,2},{2,1},{3,0},{4,7},{5,6},{6,5},{7,4},{8,11},{9,10},{10,... | collective-permute-start | bytes 442376 | tf_op jit(solution)/shard_map/ppermute | solution.py:328
  120.7 4.0 %collective-permute-done.40.refs_6_ = bf16[144,512]{1,0:T(8,128)(2,1)S(1)} collective-permute-done((bf16[144,512]{1,0:T(8,128)(2,1)S(1)}, bf16[144,512]{1,0:T(8,128)(2,1)S(1)}, u32[]{:S(2)}, u32[]{:S(2)}) %collective-permute-start.40) | collective-permute-done | bytes 147488 | tf_op jit(solution)/shard_map/ppermute | solution.py:328
  124.7 3.0 %collective-permute-start.31 = (bf16[144,256]{1,0:T(8,128)(2,1)S(1)}, bf16[144,256]{1,0:T(8,128)(2,1)S(1)}, u32[]{:S(2)}, u32[]{:S(2)}) collective-permute-start(bf16[144,256]{1,0:T(8,128)(2,1)S(1)} %get-tuple-element.53), channel_id=1, source_target_pairs={{0,2},{1,3},{2,0},{3,1},{4,6},{5,7},{6,4},{7,5},{8,10},{9,11},{10,... | collective-permute-start | bytes 221192 | tf_op jit(solution)/shard_map/ppermute | solution.py:328
  127.8 1.4 %collective-permute-start.32 = (bf16[144,256]{1,0:T(8,128)(2,1)S(1)}, bf16[144,256]{1,0:T(8,128)(2,1)S(1)}, u32[]{:S(2)}, u32[]{:S(2)}) collective-permute-start(bf16[144,256]{1,0:T(8,128)(2,1)S(1)} %get-tuple-element.54), channel_id=1, source_target_pairs={{0,3},{1,2},{2,1},{3,0},{4,7},{5,6},{6,5},{7,4},{8,11},{9,10},{10,... | collective-permute-start | bytes 221192 | tf_op jit(solution)/shard_map/ppermute | solution.py:328
  130.5 1.2 collective-permute-start.26
  131.6 1.6 %collective-permute-start.27 = (bf16[144,256]{1,0:T(8,128)(2,1)S(1)}, bf16[144,256]{1,0:T(8,128)(2,1)S(1)}, u32[]{:S(2)}, u32[]{:S(2)}) collective-permute-start(bf16[144,256]{1,0:T(8,128)(2,1)S(1)} %get-tuple-element.49), channel_id=1, source_target_pairs={{0,3},{1,2},{2,1},{3,0},{4,7},{5,6},{6,5},{7,4},{8,11},{9,10},{10,... | collective-permute-start | bytes 221192 | tf_op jit(solution)/shard_map/ppermute | solution.py:328
  133.2 2.9 %shard_map.83 = (f32[192,1536]{1,0:T(8,128)S(1)}, f32[192,128]{1,0:T(8,128)S(1)}, f32[192,512]{1,0:T(8,128)S(1)}) custom-call(bf16[144,512]{1,0:T(8,128)(2,1)S(1)} %get-tuple-element.55.refs_0_, bf16[144,512]{1,0:T(8,128)(2,1)S(1)} %collective-permute-done.34.refs_1_, bf16[144,512]{1,0:T(8,128)(2,1)S(1)} %collective-permute-done.35.refs_2_, ...), custom_call_target="tpu_custom_call" | custom-call | flops 679477248 | bytes 4128768 | tf_op jit(solution)/shard_map/pallas_call | solution.py:83
  136.1 0.8 collective-permute-done.27.refs_3_
  136.9 1.9 %shard_map.84 = f32[192,2048]{1,0:T(8,128)} custom-call(bf16[144,256]{1,0:T(8,128)(2,1)S(1)} %get-tuple-element.46.refs_0_, bf16[144,256]{1,0:T(8,128)(2,1)S(1)} %collective-permute-done.25.refs_1_, bf16[144,256]{1,0:T(8,128)(2,1)S(1)} %collective-permute-done.26.refs_2_, bf16[144,256]{1,0:T(8,128)(2,1)S(1)} %collective-permute-done.27.refs_3_, ...), custom_call_target="tpu_custom_call" | custom-call | flops 226492416 | bytes 3145728 | tf_op jit(solution)/shard_map/pallas_call | solution.py:83
  (79 shorter events, 10.2 us)
Async XLA Ops:
  0.0 12.4 %collective-permute-start.12 = (bf16[256,768]{1,0:T(8,128)(2,1)}, bf16[256,768]{1,0:T(8,128)(2,1)S(1)}, u32[]{:S(2)}, u32[]{:S(2)}) collective-permute-start(bf16[256,768]{1,0:T(8,128)(2,1)} %bitcast.11), channel_id=1, source_target_pairs={{8,16},{12,20},{16,8},{20,12},{9,17},{13,21},{17,9},{21,13},{10,18... | collective-permute-start | bytes 1179656 | tf_op jit(solution)/shard_map/ppermute | solution.py:322
  0.8 16.5 %collective-permute-start.6 = (bf16[256,768]{1,0:T(8,128)(2,1)}, bf16[256,768]{1,0:T(8,128)(2,1)S(1)}, u32[]{:S(2)}, u32[]{:S(2)}) collective-permute-start(bf16[256,768]{1,0:T(8,128)(2,1)} %bitcast.7), channel_id=1, source_target_pairs={{8,16},{12,20},{16,8},{20,12},{9,17},{13,21},{17,9},{21,13},{10,18... | collective-permute-start | bytes 1179656 | tf_op jit(solution)/shard_map/ppermute | solution.py:322
  1.5 17.8 %collective-permute-start.10 = (bf16[256,768]{1,0:T(8,128)(2,1)}, bf16[256,768]{1,0:T(8,128)(2,1)S(1)}, u32[]{:S(2)}, u32[]{:S(2)}) collective-permute-start(bf16[256,768]{1,0:T(8,128)(2,1)} %bitcast.12), channel_id=1, source_target_pairs={{0,8},{4,12},{8,0},{12,4},{16,24},{20,28},{24,16},{28,20},{1,9},{5... | collective-permute-start | bytes 1179656 | tf_op jit(solution)/shard_map/ppermute | solution.py:322
  9.1 18.3 %collective-permute-start.21 = (bf16[256,768]{1,0:T(8,128)(2,1)}, bf16[256,768]{1,0:T(8,128)(2,1)S(1)}, u32[]{:S(2)}, u32[]{:S(2)}) collective-permute-start(bf16[256,768]{1,0:T(8,128)(2,1)} %bitcast.15), channel_id=1, source_target_pairs={{0,8},{4,12},{24,16},{28,20},{1,9},{5,13},{25,17},{29,21},{2,10},{... | collective-permute-start | bytes 1179656 | tf_op jit(solution)/shard_map/ppermute | solution.py:322
  11.1 17.0 %collective-permute-start.37 = (bf16[256,768]{1,0:T(8,128)(2,1)}, bf16[256,768]{1,0:T(8,128)(2,1)S(1)}, u32[]{:S(2)}, u32[]{:S(2)}) collective-permute-start(bf16[256,768]{1,0:T(8,128)(2,1)} %bitcast.16), channel_id=1, source_target_pairs={{8,0},{12,4},{16,24},{20,28},{9,1},{13,5},{17,25},{21,29},{10,2},{... | collective-permute-start | bytes 1179656 | tf_op jit(solution)/shard_map/ppermute | solution.py:322
  12.4 23.8 %collective-permute-start.4 = (bf16[256,768]{1,0:T(8,128)(2,1)}, bf16[256,768]{1,0:T(8,128)(2,1)S(1)}, u32[]{:S(2)}, u32[]{:S(2)}) collective-permute-start(bf16[256,768]{1,0:T(8,128)(2,1)} %bitcast.8), channel_id=1, source_target_pairs={{0,8},{4,12},{8,0},{12,4},{16,24},{20,28},{24,16},{28,20},{1,9},{5... | collective-permute-start | bytes 1179656 | tf_op jit(solution)/shard_map/ppermute | solution.py:322
  17.3 18.9 %collective-permute-start.3 = (bf16[256,768]{1,0:T(8,128)(2,1)}, bf16[256,768]{1,0:T(8,128)(2,1)S(1)}, u32[]{:S(2)}, u32[]{:S(2)}) collective-permute-start(bf16[256,768]{1,0:T(8,128)(2,1)} %bitcast.9), channel_id=1, source_target_pairs={{0,4},{4,0},{8,12},{12,8},{16,20},{20,16},{24,28},{28,24},{1,5},{5... | collective-permute-start | bytes 1179656 | tf_op jit(solution)/shard_map/ppermute | solution.py:325
  19.3 25.3 %collective-permute-start.13 = (bf16[256,768]{1,0:T(8,128)(2,1)S(1)}, bf16[256,768]{1,0:T(8,128)(2,1)S(1)}, u32[]{:S(2)}, u32[]{:S(2)}) collective-permute-start(bf16[256,768]{1,0:T(8,128)(2,1)S(1)} %collective-permute-done.12), channel_id=1, source_target_pairs={{8,0},{12,4},{16,24},{20,28},{9,1},{13,5},{17,25},{21,29},{10,2},{... | collective-permute-start | bytes 1179656 | tf_op jit(solution)/shard_map/ppermute | solution.py:322
  27.4 17.9 %collective-permute-start.42 = (bf16[256,768]{1,0:T(8,128)(2,1)}, bf16[256,768]{1,0:T(8,128)(2,1)S(1)}, u32[]{:S(2)}, u32[]{:S(2)}) collective-permute-start(bf16[256,768]{1,0:T(8,128)(2,1)} %bitcast.17), channel_id=1, source_target_pairs={{8,16},{12,20},{16,8},{20,12},{9,17},{13,21},{17,9},{21,13},{10,18... | collective-permute-start | bytes 1179656 | tf_op jit(solution)/shard_map/ppermute | solution.py:322
  28.0 23.5 %collective-permute-start.7 = (bf16[256,768]{1,0:T(8,128)(2,1)S(1)}, bf16[256,768]{1,0:T(8,128)(2,1)S(1)}, u32[]{:S(2)}, u32[]{:S(2)}) collective-permute-start(bf16[256,768]{1,0:T(8,128)(2,1)S(1)} %collective-permute-done.6), channel_id=1, source_target_pairs={{8,0},{12,4},{16,24},{20,28},{9,1},{13,5},{17,25},{21,29},{10,2},{... | collective-permute-start | bytes 1179656 | tf_op jit(solution)/shard_map/ppermute | solution.py:322
  36.1 16.8 %collective-permute-start.9 = (bf16[256,768]{1,0:T(8,128)(2,1)S(1)}, bf16[256,768]{1,0:T(8,128)(2,1)S(1)}, u32[]{:S(2)}, u32[]{:S(2)}) collective-permute-start(bf16[256,768]{1,0:T(8,128)(2,1)S(1)} %bitcast.13), channel_id=1, source_target_pairs={{0,4},{4,0},{8,12},{12,8},{16,20},{20,16},{24,28},{28,24},{1,5},{5... | collective-permute-start | bytes 1179656 | tf_op jit(solution)/shard_map/ppermute | solution.py:325
  36.1 19.1 %collective-permute-start = (bf16[144,2048]{1,0:T(8,128)(2,1)S(1)}, bf16[144,2048]{1,0:T(8,128)(2,1)S(1)}, u32[]{:S(2)}, u32[]{:S(2)}) collective-permute-start(bf16[144,2048]{1,0:T(8,128)(2,1)S(1)} %get-tuple-element.39), channel_id=1, source_target_pairs={{0,1},{1,0},{2,3},{3,2},{4,5},{5,4},{6,7},{7,6},{8,9},{9,8},{10,11... | collective-permute-start | bytes 1769480 | tf_op jit(solution)/shard_map/ppermute | solution.py:328
  44.6 10.0 %collective-permute-start.22 = (bf16[256,768]{1,0:T(8,128)(2,1)S(1)}, bf16[256,768]{1,0:T(8,128)(2,1)S(1)}, u32[]{:S(2)}, u32[]{:S(2)}) collective-permute-start(bf16[256,768]{1,0:T(8,128)(2,1)S(1)} %collective-permute-done.21), channel_id=1, source_target_pairs={{8,16},{12,20},{16,8},{20,12},{9,17},{13,21},{17,9},{21,13},{10,18... | collective-permute-start | bytes 1179656 | tf_op jit(solution)/shard_map/ppermute | solution.py:322
  45.3 11.4 %collective-permute-start.18 = (bf16[256,768]{1,0:T(8,128)(2,1)S(1)}, bf16[256,768]{1,0:T(8,128)(2,1)S(1)}, u32[]{:S(2)}, u32[]{:S(2)}) collective-permute-start(bf16[256,768]{1,0:T(8,128)(2,1)S(1)} %collective-permute-done.4.refs_6_), channel_id=1, source_target_pairs={{8,16},{12,20},{16,8},{20,12},{9,17},{13,21},{17,9},{21,13},{10,18... | collective-permute-start | bytes 1179656 | tf_op jit(solution)/shard_map/ppermute | solution.py:322
  51.6 12.9 %collective-permute-start.43 = (bf16[256,768]{1,0:T(8,128)(2,1)S(1)}, bf16[256,768]{1,0:T(8,128)(2,1)S(1)}, u32[]{:S(2)}, u32[]{:S(2)}) collective-permute-start(bf16[256,768]{1,0:T(8,128)(2,1)S(1)} %collective-permute-done.42), channel_id=1, source_target_pairs={{8,0},{12,4},{16,24},{20,28},{9,1},{13,5},{17,25},{21,29},{10,2},{... | collective-permute-start | bytes 1179656 | tf_op jit(solution)/shard_map/ppermute | solution.py:322
  52.9 26.6 %collective-permute-start.1 = (bf16[144,2048]{1,0:T(8,128)(2,1)S(1)}, bf16[144,2048]{1,0:T(8,128)(2,1)S(1)}, u32[]{:S(2)}, u32[]{:S(2)}) collective-permute-start(bf16[144,2048]{1,0:T(8,128)(2,1)S(1)} %get-tuple-element.40), channel_id=1, source_target_pairs={{0,2},{1,3},{2,0},{3,1},{4,6},{5,7},{6,4},{7,5},{8,10},{9,11},{10,... | collective-permute-start | bytes 1769480 | tf_op jit(solution)/shard_map/ppermute | solution.py:328
  54.5 11.3 %collective-permute-start.15 = (bf16[256,768]{1,0:T(8,128)(2,1)S(1)}, bf16[256,768]{1,0:T(8,128)(2,1)S(1)}, u32[]{:S(2)}, u32[]{:S(2)}) collective-permute-start(bf16[256,768]{1,0:T(8,128)(2,1)S(1)} %collective-permute-done.10.refs_12_), channel_id=1, source_target_pairs={{8,16},{12,20},{16,8},{20,12},{9,17},{13,21},{17,9},{21,13},{10,18... | collective-permute-start | bytes 1179656 | tf_op jit(solution)/shard_map/ppermute | solution.py:322
  55.2 24.9 %collective-permute-start.2 = (bf16[144,2048]{1,0:T(8,128)(2,1)S(1)}, bf16[144,2048]{1,0:T(8,128)(2,1)S(1)}, u32[]{:S(2)}, u32[]{:S(2)}) collective-permute-start(bf16[144,2048]{1,0:T(8,128)(2,1)S(1)} %get-tuple-element.41), channel_id=1, source_target_pairs={{0,3},{1,2},{2,1},{3,0},{4,7},{5,6},{6,5},{7,4},{8,11},{9,10},{10,... | collective-permute-start | bytes 1769480 | tf_op jit(solution)/shard_map/ppermute | solution.py:328
  56.7 15.1 %collective-permute-start.28 = (bf16[128,768]{1,0:T(8,128)(2,1)S(1)}, bf16[128,768]{1,0:T(8,128)(2,1)S(1)}, u32[]{:S(2)}, u32[]{:S(2)}) collective-permute-start(bf16[128,768]{1,0:T(8,128)(2,1)S(1)} %get-tuple-element.50), channel_id=1, source_target_pairs={{8,0},{12,4},{16,24},{20,28},{9,1},{13,5},{17,25},{21,29},{10,2},{... | collective-permute-start | bytes 589832 | tf_op jit(solution)/shard_map/ppermute | solution.py:322
  64.4 15.1 %collective-permute-start.19 = (bf16[256,768]{1,0:T(8,128)(2,1)S(1)}, bf16[256,768]{1,0:T(8,128)(2,1)S(1)}, u32[]{:S(2)}, u32[]{:S(2)}) collective-permute-start(bf16[256,768]{1,0:T(8,128)(2,1)S(1)} %collective-permute-done.18), channel_id=1, source_target_pairs={{8,0},{12,4},{16,24},{20,28},{9,1},{13,5},{17,25},{21,29},{10,2},{... | collective-permute-start | bytes 1179656 | tf_op jit(solution)/shard_map/ppermute | solution.py:322
  65.8 14.4 %collective-permute-start.11 = (bf16[256,768]{1,0:T(8,128)(2,1)S(1)}, bf16[256,768]{1,0:T(8,128)(2,1)S(1)}, u32[]{:S(2)}, u32[]{:S(2)}) collective-permute-start(bf16[256,768]{1,0:T(8,128)(2,1)S(1)} %collective-permute-done.10.refs_12_), channel_id=1, source_target_pairs={{0,4},{4,0},{8,12},{12,8},{16,20},{20,16},{24,28},{28,24},{1,5},{5... | collective-permute-start | bytes 1179656 | tf_op jit(solution)/shard_map/ppermute | solution.py:325
  71.8 12.6 %collective-permute-start.16 = (bf16[256,768]{1,0:T(8,128)(2,1)S(1)}, bf16[256,768]{1,0:T(8,128)(2,1)S(1)}, u32[]{:S(2)}, u32[]{:S(2)}) collective-permute-start(bf16[256,768]{1,0:T(8,128)(2,1)S(1)} %collective-permute-done.15), channel_id=1, source_target_pairs={{8,0},{12,4},{16,24},{20,28},{9,1},{13,5},{17,25},{21,29},{10,2},{... | collective-permute-start | bytes 1179656 | tf_op jit(solution)/shard_map/ppermute | solution.py:322
  79.6 4.9 %collective-permute-start.5 = (bf16[256,768]{1,0:T(8,128)(2,1)S(1)}, bf16[256,768]{1,0:T(8,128)(2,1)S(1)}, u32[]{:S(2)}, u32[]{:S(2)}) collective-permute-start(bf16[256,768]{1,0:T(8,128)(2,1)S(1)} %collective-permute-done.4.refs_6_), channel_id=1, source_target_pairs={{0,4},{4,0},{8,12},{12,8},{16,20},{20,16},{24,28},{28,24},{1,5},{5... | collective-permute-start | bytes 1179656 | tf_op jit(solution)/shard_map/ppermute | solution.py:325
  79.6 9.9 %collective-permute-start.14 = (bf16[256,768]{1,0:T(8,128)(2,1)S(1)}, bf16[256,768]{1,0:T(8,128)(2,1)S(1)}, u32[]{:S(2)}, u32[]{:S(2)}) collective-permute-start(bf16[256,768]{1,0:T(8,128)(2,1)S(1)} %broadcast_select_fusion.4.refs_14_), channel_id=1, source_target_pairs={{0,4},{4,0},{8,12},{12,8},{16,20},{20,16},{24,28},{28,24},{1,5},{5... | collective-permute-start | bytes 1179656 | tf_op jit(solution)/shard_map/ppermute | solution.py:325
  80.1 9.8 %collective-permute-start.8 = (bf16[256,768]{1,0:T(8,128)(2,1)S(1)}, bf16[256,768]{1,0:T(8,128)(2,1)S(1)}, u32[]{:S(2)}, u32[]{:S(2)}) collective-permute-start(bf16[256,768]{1,0:T(8,128)(2,1)S(1)} %broadcast_select_fusion.5.refs_8_), channel_id=1, source_target_pairs={{0,4},{4,0},{8,12},{12,8},{16,20},{20,16},{24,28},{28,24},{1,5},{5... | collective-permute-start | bytes 1179656 | tf_op jit(solution)/shard_map/ppermute | solution.py:325
  80.2 9.2 %collective-permute-start.23 = (bf16[128,768]{1,0:T(8,128)(2,1)S(1)}, bf16[128,768]{1,0:T(8,128)(2,1)S(1)}, u32[]{:S(2)}, u32[]{:S(2)}) collective-permute-start(bf16[128,768]{1,0:T(8,128)(2,1)S(1)} %get-tuple-element.45), channel_id=1, source_target_pairs={{8,0},{12,4},{16,24},{20,28},{9,1},{13,5},{17,25},{21,29},{10,2},{... | collective-permute-start | bytes 589832 | tf_op jit(solution)/shard_map/ppermute | solution.py:322
  84.5 5.6 %collective-permute-start.20 = (bf16[256,768]{1,0:T(8,128)(2,1)S(1)}, bf16[256,768]{1,0:T(8,128)(2,1)S(1)}, u32[]{:S(2)}, u32[]{:S(2)}) collective-permute-start(bf16[256,768]{1,0:T(8,128)(2,1)S(1)} %broadcast_select_fusion.2.own), channel_id=1, source_target_pairs={{0,4},{4,0},{8,12},{12,8},{16,20},{20,16},{24,28},{28,24},{1,5},{5... | collective-permute-start | bytes 1179656 | tf_op jit(solution)/shard_map/ppermute | solution.py:325
  84.5 16.7 %collective-permute-start.38 = (bf16[256,768]{1,0:T(8,128)(2,1)S(1)}, bf16[256,768]{1,0:T(8,128)(2,1)S(1)}, u32[]{:S(2)}, u32[]{:S(2)}) collective-permute-start(bf16[256,768]{1,0:T(8,128)(2,1)S(1)} %broadcast_select_fusion.1.own), channel_id=1, source_target_pairs={{0,4},{4,0},{8,12},{12,8},{16,20},{20,16},{24,28},{28,24},{1,5},{5... | collective-permute-start | bytes 1179656 | tf_op jit(solution)/shard_map/ppermute | solution.py:325
  89.4 9.6 %collective-permute-start.44 = (bf16[256,768]{1,0:T(8,128)(2,1)S(1)}, bf16[256,768]{1,0:T(8,128)(2,1)S(1)}, u32[]{:S(2)}, u32[]{:S(2)}) collective-permute-start(bf16[256,768]{1,0:T(8,128)(2,1)S(1)} %broadcast_select_fusion.own), channel_id=1, source_target_pairs={{0,4},{4,0},{8,12},{12,8},{16,20},{20,16},{24,28},{28,24},{1,5},{5... | collective-permute-start | bytes 1179656 | tf_op jit(solution)/shard_map/ppermute | solution.py:325
  89.4 8.2 %collective-permute-start.17 = (bf16[256,768]{1,0:T(8,128)(2,1)S(1)}, bf16[256,768]{1,0:T(8,128)(2,1)S(1)}, u32[]{:S(2)}, u32[]{:S(2)}) collective-permute-start(bf16[256,768]{1,0:T(8,128)(2,1)S(1)} %broadcast_select_fusion.3.own), channel_id=1, source_target_pairs={{0,4},{4,0},{8,12},{12,8},{16,20},{20,16},{24,28},{28,24},{1,5},{5... | collective-permute-start | bytes 1179656 | tf_op jit(solution)/shard_map/ppermute | solution.py:325
  90.0 13.4 %collective-permute-start.33 = (bf16[256,768]{1,0:T(8,128)(2,1)S(1)}, bf16[256,768]{1,0:T(8,128)(2,1)S(1)}, u32[]{:S(2)}, u32[]{:S(2)}) collective-permute-start(bf16[256,768]{1,0:T(8,128)(2,1)S(1)} %bitcast.18), channel_id=1, source_target_pairs={{0,4},{4,0},{8,12},{12,8},{16,20},{20,16},{24,28},{28,24},{1,5},{5... | collective-permute-start | bytes 1179656 | tf_op jit(solution)/shard_map/ppermute | solution.py:325
  90.1 13.9 %collective-permute-start.29 = (bf16[128,768]{1,0:T(8,128)(2,1)S(1)}, bf16[128,768]{1,0:T(8,128)(2,1)S(1)}, u32[]{:S(2)}, u32[]{:S(2)}) collective-permute-start(bf16[128,768]{1,0:T(8,128)(2,1)S(1)} %broadcast_select_fusion.6.own), channel_id=1, source_target_pairs={{0,4},{4,0},{8,12},{12,8},{16,20},{20,16},{24,28},{28,24},{1,5},{5... | collective-permute-start | bytes 589832 | tf_op jit(solution)/shard_map/ppermute | solution.py:325
  97.6 8.2 %collective-permute-start.24 = (bf16[128,768]{1,0:T(8,128)(2,1)S(1)}, bf16[128,768]{1,0:T(8,128)(2,1)S(1)}, u32[]{:S(2)}, u32[]{:S(2)}) collective-permute-start(bf16[128,768]{1,0:T(8,128)(2,1)S(1)} %broadcast_select_fusion.7.own), channel_id=1, source_target_pairs={{0,4},{4,0},{8,12},{12,8},{16,20},{20,16},{24,28},{28,24},{1,5},{5... | collective-permute-start | bytes 589832 | tf_op jit(solution)/shard_map/ppermute | solution.py:325
  99.7 15.7 %collective-permute-start.45 = (bf16[144,512]{1,0:T(8,128)(2,1)S(1)}, bf16[144,512]{1,0:T(8,128)(2,1)S(1)}, u32[]{:S(2)}, u32[]{:S(2)}) collective-permute-start(bf16[144,512]{1,0:T(8,128)(2,1)S(1)} %get-tuple-element.64), channel_id=1, source_target_pairs={{0,1},{1,0},{2,3},{3,2},{4,5},{5,4},{6,7},{7,6},{8,9},{9,8},{10,11... | collective-permute-start | bytes 442376 | tf_op jit(solution)/shard_map/ppermute | solution.py:328
  101.2 15.6 %collective-permute-start.46 = (bf16[144,512]{1,0:T(8,128)(2,1)S(1)}, bf16[144,512]{1,0:T(8,128)(2,1)S(1)}, u32[]{:S(2)}, u32[]{:S(2)}) collective-permute-start(bf16[144,512]{1,0:T(8,128)(2,1)S(1)} %get-tuple-element.65), channel_id=1, source_target_pairs={{0,2},{1,3},{2,0},{3,1},{4,6},{5,7},{6,4},{7,5},{8,10},{9,11},{10,... | collective-permute-start | bytes 442376 | tf_op jit(solution)/shard_map/ppermute | solution.py:328
  103.4 13.9 %collective-permute-start.47 = (bf16[144,512]{1,0:T(8,128)(2,1)S(1)}, bf16[144,512]{1,0:T(8,128)(2,1)S(1)}, u32[]{:S(2)}, u32[]{:S(2)}) collective-permute-start(bf16[144,512]{1,0:T(8,128)(2,1)S(1)} %get-tuple-element.66), channel_id=1, source_target_pairs={{0,3},{1,2},{2,1},{3,0},{4,7},{5,6},{6,5},{7,4},{8,11},{9,10},{10,... | collective-permute-start | bytes 442376 | tf_op jit(solution)/shard_map/ppermute | solution.py:328
  104.0 14.9 %collective-permute-start.39 = (bf16[144,512]{1,0:T(8,128)(2,1)S(1)}, bf16[144,512]{1,0:T(8,128)(2,1)S(1)}, u32[]{:S(2)}, u32[]{:S(2)}) collective-permute-start(bf16[144,512]{1,0:T(8,128)(2,1)S(1)} %get-tuple-element.60), channel_id=1, source_target_pairs={{0,1},{1,0},{2,3},{3,2},{4,5},{5,4},{6,7},{7,6},{8,9},{9,8},{10,11... | collective-permute-start | bytes 442376 | tf_op jit(solution)/shard_map/ppermute | solution.py:328
  105.9 8.0 %collective-permute-start.30 = (bf16[144,256]{1,0:T(8,128)(2,1)S(1)}, bf16[144,256]{1,0:T(8,128)(2,1)S(1)}, u32[]{:S(2)}, u32[]{:S(2)}) collective-permute-start(bf16[144,256]{1,0:T(8,128)(2,1)S(1)} %get-tuple-element.52), channel_id=1, source_target_pairs={{0,1},{1,0},{2,3},{3,2},{4,5},{5,4},{6,7},{7,6},{8,9},{9,8},{10,11... | collective-permute-start | bytes 221192 | tf_op jit(solution)/shard_map/ppermute | solution.py:328
  113.8 10.9 %collective-permute-start.40 = (bf16[144,512]{1,0:T(8,128)(2,1)S(1)}, bf16[144,512]{1,0:T(8,128)(2,1)S(1)}, u32[]{:S(2)}, u32[]{:S(2)}) collective-permute-start(bf16[144,512]{1,0:T(8,128)(2,1)S(1)} %get-tuple-element.61), channel_id=1, source_target_pairs={{0,2},{1,3},{2,0},{3,1},{4,6},{5,7},{6,4},{7,5},{8,10},{9,11},{10,... | collective-permute-start | bytes 442376 | tf_op jit(solution)/shard_map/ppermute | solution.py:328
  115.4 12.4 %collective-permute-start.41 = (bf16[144,512]{1,0:T(8,128)(2,1)S(1)}, bf16[144,512]{1,0:T(8,128)(2,1)S(1)}, u32[]{:S(2)}, u32[]{:S(2)}) collective-permute-start(bf16[144,512]{1,0:T(8,128)(2,1)S(1)} %get-tuple-element.62), channel_id=1, source_target_pairs={{0,3},{1,2},{2,1},{3,0},{4,7},{5,6},{6,5},{7,4},{8,11},{9,10},{10,... | collective-permute-start | bytes 442376 | tf_op jit(solution)/shard_map/ppermute | solution.py:328
  116.8 12.4 %collective-permute-start.34 = (bf16[144,512]{1,0:T(8,128)(2,1)S(1)}, bf16[144,512]{1,0:T(8,128)(2,1)S(1)}, u32[]{:S(2)}, u32[]{:S(2)}) collective-permute-start(bf16[144,512]{1,0:T(8,128)(2,1)S(1)} %get-tuple-element.56), channel_id=1, source_target_pairs={{0,1},{1,0},{2,3},{3,2},{4,5},{5,4},{6,7},{7,6},{8,9},{9,8},{10,11... | collective-permute-start | bytes 442376 | tf_op jit(solution)/shard_map/ppermute | solution.py:328
  117.3 13.1 %collective-permute-start.35 = (bf16[144,512]{1,0:T(8,128)(2,1)S(1)}, bf16[144,512]{1,0:T(8,128)(2,1)S(1)}, u32[]{:S(2)}, u32[]{:S(2)}) collective-permute-start(bf16[144,512]{1,0:T(8,128)(2,1)S(1)} %get-tuple-element.57), channel_id=1, source_target_pairs={{0,2},{1,3},{2,0},{3,1},{4,6},{5,7},{6,4},{7,5},{8,10},{9,11},{10,... | collective-permute-start | bytes 442376 | tf_op jit(solution)/shard_map/ppermute | solution.py:328
  118.9 12.8 %collective-permute-start.36 = (bf16[144,512]{1,0:T(8,128)(2,1)S(1)}, bf16[144,512]{1,0:T(8,128)(2,1)S(1)}, u32[]{:S(2)}, u32[]{:S(2)}) collective-permute-start(bf16[144,512]{1,0:T(8,128)(2,1)S(1)} %get-tuple-element.58), channel_id=1, source_target_pairs={{0,3},{1,2},{2,1},{3,0},{4,7},{5,6},{6,5},{7,4},{8,11},{9,10},{10,... | collective-permute-start | bytes 442376 | tf_op jit(solution)/shard_map/ppermute | solution.py:328
  124.7 11.3 %collective-permute-start.31 = (bf16[144,256]{1,0:T(8,128)(2,1)S(1)}, bf16[144,256]{1,0:T(8,128)(2,1)S(1)}, u32[]{:S(2)}, u32[]{:S(2)}) collective-permute-start(bf16[144,256]{1,0:T(8,128)(2,1)S(1)} %get-tuple-element.53), channel_id=1, source_target_pairs={{0,2},{1,3},{2,0},{3,1},{4,6},{5,7},{6,4},{7,5},{8,10},{9,11},{10,... | collective-permute-start | bytes 221192 | tf_op jit(solution)/shard_map/ppermute | solution.py:328
  127.8 8.3 %collective-permute-start.32 = (bf16[144,256]{1,0:T(8,128)(2,1)S(1)}, bf16[144,256]{1,0:T(8,128)(2,1)S(1)}, u32[]{:S(2)}, u32[]{:S(2)}) collective-permute-start(bf16[144,256]{1,0:T(8,128)(2,1)S(1)} %get-tuple-element.54), channel_id=1, source_target_pairs={{0,3},{1,2},{2,1},{3,0},{4,7},{5,6},{6,5},{7,4},{8,11},{9,10},{10,... | collective-permute-start | bytes 221192 | tf_op jit(solution)/shard_map/ppermute | solution.py:328
  129.2 6.9 %collective-permute-start.25 = (bf16[144,256]{1,0:T(8,128)(2,1)S(1)}, bf16[144,256]{1,0:T(8,128)(2,1)S(1)}, u32[]{:S(2)}, u32[]{:S(2)}) collective-permute-start(bf16[144,256]{1,0:T(8,128)(2,1)S(1)} %get-tuple-element.47), channel_id=1, source_target_pairs={{0,1},{1,0},{2,3},{3,2},{4,5},{5,4},{6,7},{7,6},{8,9},{9,8},{10,11... | collective-permute-start | bytes 221192 | tf_op jit(solution)/shard_map/ppermute | solution.py:328
  130.5 5.6 %collective-permute-start.26 = (bf16[144,256]{1,0:T(8,128)(2,1)S(1)}, bf16[144,256]{1,0:T(8,128)(2,1)S(1)}, u32[]{:S(2)}, u32[]{:S(2)}) collective-permute-start(bf16[144,256]{1,0:T(8,128)(2,1)S(1)} %get-tuple-element.48), channel_id=1, source_target_pairs={{0,2},{1,3},{2,0},{3,1},{4,6},{5,7},{6,4},{7,5},{8,10},{9,11},{10,... | collective-permute-start | bytes 221192 | tf_op jit(solution)/shard_map/ppermute | solution.py:328
  131.6 5.3 %collective-permute-start.27 = (bf16[144,256]{1,0:T(8,128)(2,1)S(1)}, bf16[144,256]{1,0:T(8,128)(2,1)S(1)}, u32[]{:S(2)}, u32[]{:S(2)}) collective-permute-start(bf16[144,256]{1,0:T(8,128)(2,1)S(1)} %get-tuple-element.49), channel_id=1, source_target_pairs={{0,3},{1,2},{2,1},{3,0},{4,7},{5,6},{6,5},{7,4},{8,11},{9,10},{10,... | collective-permute-start | bytes 221192 | tf_op jit(solution)/shard_map/ppermute | solution.py:328
  (5 other events, 113.5 us)

commit v3 on v2

--- a/solution.py
+++ b/solution.py
@@ -96,7 +96,7 @@
 
 
 def place_kernel(experts, capacity, ids_hbm, w_hbm, tok_hbm, *refs):
-    outs, (c_ref, tokp, ids_ref, w_ref, tok_ref, local, sems) = refs[:experts], refs[experts:]
+    outs, (c_ref, tokf, tokp, ids_ref, w_ref, tok_ref, local, sems) = refs[:experts], refs[experts:]
     count, width = tok_ref.shape
     ids_copy, w_copy, tok_copy = copies(
         [(ids_hbm, ids_ref), (w_hbm, w_ref), (tok_hbm, tok_ref)], sems
@@ -136,9 +136,9 @@
     slot = lax.broadcasted_iota(jnp.int32, (capacity, count), 0).astype(F32)
     tok_copy.wait()
     for place, s in enumerate(slice_order()):
-        tokp[:, place * part : (place + 1) * part] = tok_ref[
-            :, pl.ds(pl.multiple_of(s * part, part), part)
-        ].astype(BF16)
+        value = tok_ref[:, pl.ds(pl.multiple_of(s * part, part), part)]
+        tokf[:, place * part : (place + 1) * part] = value
+        tokp[:, place * part : (place + 1) * part] = value.astype(BF16)
     for m in range(experts):
         select = jnp.where(slot == rank[m : m + 1, :], 1.0, 0.0).astype(BF16)
         block = jnp.dot(select, tokp[...], preferred_element_type=F32).astype(BF16)
@@ -162,135 +162,110 @@
 
 def open_kernel(experts, slices, *refs):
     blocks, refs = refs[:experts], refs[experts:]
-    gates, ups, refs = refs[:slices], refs[slices : 2 * slices], refs[2 * slices :]
-    out_g, out_u, tail, rows, wg, wu, sems = refs
+    gates, (out, rows, weight, sems) = refs[:slices], refs[slices:]
     capacity = blocks[0].shape[0]
     part = gates[0].shape[0]
-    n = slices * part
-    pairs = [
-        (b.at[:, pl.ds(0, n)], rows.at[pl.ds(m * capacity, capacity), :])
-        for m, b in enumerate(blocks)
-    ]
-    pairs += [(g, wg.at[pl.ds(i * part, part), :]) for i, g in enumerate(gates)]
-    n_gate = len(pairs)
-    pairs += [(u, wu.at[pl.ds(i * part, part), :]) for i, u in enumerate(ups)]
-    pairs += [
-        (b.at[:, pl.ds(n, tail.shape[1])], tail.at[pl.ds(m * capacity, capacity), :])
-        for m, b in enumerate(blocks)
-    ]
-    started = copies(pairs, sems)
-    for copy in started[:n_gate]:
+    pairs = [(g, weight.at[pl.ds(i * part, part), :]) for i, g in enumerate(gates)]
+    pairs += [(b, rows.at[pl.ds(m * capacity, capacity), :]) for m, b in enumerate(blocks)]
+    for copy in copies(pairs, sems):
         copy.wait()
-    out_g[...] = jnp.dot(rows[...], wg[...], preferred_element_type=F32)
-    for copy in started[n_gate:]:
-        copy.wait()
-    out_u[...] = jnp.dot(rows[...], wu[...], preferred_element_type=F32)
-
-
-def gate_kernel(rows, own, other, acc, out):
+    out[...] = jnp.dot(rows[:, : slices * part], weight[...], preferred_element_type=F32)
+
+
+def more_kernel(slices, rows, *refs):
+    ups, (out, weight) = refs[:slices], refs[slices:]
+    part = ups[0].shape[0]
+    for i, u in enumerate(ups):
+        weight[i * part : (i + 1) * part, :] = u[...]
+    out[...] = jnp.dot(rows[:, : slices * part], weight[...], preferred_element_type=F32)
+
+
+def gate_kernel(first, rows, own, other, acc, out):
     part = own.shape[0]
-    gate = acc[...] + jnp.dot(rows[:, :part], own[...], preferred_element_type=F32)
-    gate = gate + jnp.dot(rows[:, part:], other[...], preferred_element_type=F32)
+    lo, mid, hi = first * part, (first + 1) * part, (first + 2) * part
+    gate = acc[...] + jnp.dot(rows[:, lo:mid], own[...], preferred_element_type=F32)
+    gate = gate + jnp.dot(rows[:, mid:hi], other[...], preferred_element_type=F32)
     out[...] = gate / (1.0 + jnp.exp(-gate))
 
 
-def up_kernel(rows, own, acc, out):
-    part = own.shape[0]
-    out[...] = acc[...] + jnp.dot(rows[:, :part], own[...], preferred_element_type=F32)
-
-
-def hidden_kernel(rows, other, acc, act, out):
-    part = other.shape[0]
-    up = acc[...] + jnp.dot(rows[:, part:], other[...], preferred_element_type=F32)
+def up_kernel(first, rows, own, acc, out):
+    lo = first * own.shape[0]
+    hi = lo + own.shape[0]
+    out[...] = acc[...] + jnp.dot(rows[:, lo:hi], own[...], preferred_element_type=F32)
+
+
+def hidden_kernel(first, rows, other, acc, act, out):
+    lo = first * other.shape[0]
+    hi = lo + other.shape[0]
+    up = acc[...] + jnp.dot(rows[:, lo:hi], other[...], preferred_element_type=F32)
     out[...] = (act[...] * up).astype(BF16)
 
 
-def down_kernel(experts, capacity, hidden, own, other, *outs):
-    both = jnp.concatenate([own[...], other[...]], axis=0)
+def down_kernel(experts, capacity, hidden, *refs):
+    weights, outs = refs[:-experts], refs[-experts:]
+    weight = jnp.concatenate([w[...] for w in weights], axis=0)
     result = lax.dot_general(
-        hidden[...], both, (((1,), (1,)), ((), ())), preferred_element_type=F32
+        hidden[...], weight, (((1,), (1,)), ((), ())), preferred_element_type=F32
     ).astype(BF16)
     for m in range(experts):
         outs[m][...] = result[m * capacity : (m + 1) * capacity]
 
 
-def chunk(stages, blocks, tokens, c_ref, back, tok, sems):
-    experts = len(blocks) // len(stages)
-    capacity, wide = blocks[0].shape
-    part = wide // 2
+def mixed_columns(experts, chunks, blocks, tokens, c_ref, back):
+    capacity = blocks[0].shape[0]
+    count = tokens.shape[0]
+    unit = tokens.shape[1] // (2 * CHAIN * HALVES)
+    lo = 0
+    for i, b in enumerate(blocks):
+        m = i % experts
+        back[m * capacity : (m + 1) * capacity, lo : lo + b.shape[1]] = b[...]
+        lo += b.shape[1] if m == experts - 1 else 0
+    both = jnp.dot(c_ref[...], back[...], preferred_element_type=F32)
+    summed = both[:count] + both[count:]
+    out, lo = [], 0
+    total = jnp.zeros((count, 1), F32)
+    for place, first, n in [p for c in chunks for p in c]:
+        at = (place * HALVES + first) * unit
+        value = tokens[:, at : at + n * unit] + summed[:, lo : lo + n * unit]
+        total = total + jnp.sum(value * value, axis=1, keepdims=True)
+        out.append(value)
+        lo += n * unit
+    return out, total
+
+
+def combine_kernel(experts, chunks, *refs):
+    *blocks, tokens, c_ref, out, square, back = refs
+    values, total = mixed_columns(experts, chunks, blocks, tokens, c_ref, back)
+    lo = 0
+    for value in values:
+        out[:, lo : lo + value.shape[1]] = value
+        lo += value.shape[1]
+    square[...] = jnp.broadcast_to(total, square.shape)
+
+
+def finish_kernel(experts, before, chunks, *refs):
+    *blocks, mixed, square, tokens, c_ref, gain, out_hbm, back, out, sems = refs
+    values, total = mixed_columns(experts, chunks, blocks, tokens, c_ref, back)
+    width = out.shape[1]
+    part = width // (2 * CHAIN)
+    unit = part // HALVES
+    total = total + square[:, 0:1]
+    scale = lax.rsqrt(total * (1.0 / width) + 1e-06)
     order = slice_order()
-    pairs = []
-    for i, stage in enumerate(stages):
-        pairs += [
-            (b, back.at[pl.ds(m * capacity, capacity), pl.ds(i * wide, wide)])
-            for m, b in enumerate(blocks[i * experts : (i + 1) * experts])
-        ]
-        pairs += [
-            (
-                tokens.at[:, pl.ds(pl.multiple_of(order[2 * stage + h] * part, part), part)],
-                tok.at[:, pl.ds(i * wide + h * part, part)],
-            )
-            for h in range(2)
-        ]
-    for copy in copies(pairs, sems):
-        copy.wait()
-    both = jnp.dot(c_ref[...], back[...], preferred_element_type=F32)
-    count = tok.shape[0]
-    here = tok[...] + (both[:count] + both[count:])
-    return here, jnp.sum(here * here, axis=1, keepdims=True)
-
-
-def combine_kernel(stages, n_blocks, *refs):
-    blocks, refs = refs[:n_blocks], refs[n_blocks:]
-    tokens, c_ref, out, square, rest, back, tok, sems, rest_sems = refs
-    wide = rest.shape[1]
-    part = wide // 2
-    order = slice_order()[2 * len(stages) :]
-    pairs = [
-        (
-            tokens.at[:, pl.ds(pl.multiple_of(s * part, part), part)],
-            rest.at[:, pl.ds(h * part, part)],
-        )
-        for h, s in enumerate(order)
-    ]
-    started = copies(pairs, rest_sems)
-    here, total = chunk(stages, blocks, tokens, c_ref, back, tok, sems)
-    out[...] = here
-    square[...] = jnp.broadcast_to(total, square.shape)
-    for copy in started:
-        copy.wait()
-
-
-def finish_kernel(halves, *refs):
-    *blocks, tok, c_ref, gain, mixed, square, out_hbm, back, out, sems = refs
-    experts = len(blocks) // halves
-    capacity, piece = blocks[0].shape
-    count, wide = tok.shape
-    part, step = wide // 2, piece // 2
-    for i, b in enumerate(blocks):
-        rows = slice(i % experts * capacity, (i % experts + 1) * capacity)
-        for h in range(2):
-            lo = h * part + i // experts * step
-            back[rows, lo : lo + step] = b[:, h * step : (h + 1) * step]
-    both = jnp.dot(c_ref[...], back[...], preferred_element_type=F32)
-    here = tok[...] + (both[:count] + both[count:])
-    total = jnp.sum(here * here, axis=1, keepdims=True) + square[:, 0:1]
-    width = out.shape[1]
-    scale = lax.rsqrt(total * (1.0 / width) + 1e-06)
     started = []
-    for place, s in enumerate(slice_order()):
-        lo = place * part
-        if lo < width - wide:
-            value = mixed[:, lo : lo + part]
-        else:
-            value = here[:, lo - (width - wide) :][:, :part]
-        at = pl.ds(pl.multiple_of(s * part, part), part)
-        out[:, lo : lo + part] = value * scale * gain[:, at]
+    lo = 0
+    for i, (place, first, n) in enumerate([p for c in before + chunks for p in c]):
+        late = i - 2 * len(before)
+        size = n * unit
+        value = mixed[:, lo : lo + size] if late < 0 else values[late]
+        at = pl.ds(pl.multiple_of(order[place] * part + first * unit, unit), size)
+        out[:, lo : lo + size] = value * scale * gain[:, at]
         copy = pltpu.make_async_copy(
-            out.at[:, pl.ds(lo, part)], out_hbm.at[:, at], sems.at[place]
+            out.at[:, pl.ds(lo, size)], out_hbm.at[:, at], sems.at[i]
         )
         copy.start()
         started.append(copy)
+        lo += size
     for copy in started:
         copy.wait()
 
@@ -305,7 +280,12 @@
 PAIR = [(0, 1), (1, 0), (2, 3), (3, 2)]
 INWARD = [(0, 1), (3, 2)]
 OUTWARD = [(1, 0), (2, 3)]
-HALVES = 2
+HALVES = 1
+
+
+def pieces():
+    whole = [[(2 * s, 0, HALVES), (2 * s + 1, 0, HALVES)] for s in range(CHAIN - 1)]
+    return whole + [[(2 * CHAIN - 2, h, 1), (2 * CHAIN - 1, h, 1)] for h in range(HALVES)]
 
 
 def layer(tokens, expert_ids, combine_weights, gate, up, down, norm_gain):
@@ -338,7 +318,7 @@
         mid_in = along(inner, MIDDLE)
         two = jnp.where(end, along(mid, OUTWARD), mid)
         parts = [mid_in]
-        if down:
+        if down and HALVES > 1:
             step = mid_in.shape[0] // HALVES
             parts = [mid_in[i * step : (i + 1) * step] for i in range(HALVES)]
             parts = lax.optimization_barrier(parts)
@@ -347,11 +327,12 @@
 
     g_all, u_all, d_all = line(gate, False), line(up, False), line(down, True)
 
-    *placed, mix = call(
+    *placed, mix, sorted_tokens = call(
         functools.partial(place_kernel, experts, capacity),
         [pltpu.HBM((capacity, width), BF16)]
         + [jax.ShapeDtypeStruct((capacity, width), BF16)] * (experts - 1)
-        + [jax.ShapeDtypeStruct((2 * count, slots), BF16)],
+        + [jax.ShapeDtypeStruct((2 * count, slots), BF16)]
+        + [jax.ShapeDtypeStruct((count, width), F32)],
         tuple(stay(x) for x in (expert_ids.T, combine_weights.T, tokens)),
         [HBM] * 3,
         [
@@ -364,28 +345,14 @@
         ],
         flops=2 * slots * count * width,
         moved=count * width * 4 + slots * width * 2,
-        outs=[HBM] + [VMEM] * experts,
+        outs=[HBM] + [VMEM] * (experts + 1),
+        grant=10,
     )
     rows = [placed[0]] + [across(placed[m], m) for m in range(1, experts)]
 
     slices = 2 * (CHAIN - 1)
     n = slices * part
     flat = jax.ShapeDtypeStruct((slots, ff), F32)
-    acc_g, acc_u, tail = call(
-        functools.partial(open_kernel, experts, slices),
-        [flat, flat, jax.ShapeDtypeStruct((slots, 2 * part), BF16)],
-        (*rows, *g_all[:slices], *u_all[:slices]),
-        [ANY] * (experts + 2 * slices),
-        [
-            pltpu.VMEM((slots, n), BF16),
-            pltpu.VMEM((n, ff), BF16),
-            pltpu.VMEM((n, ff), BF16),
-            pltpu.SemaphoreType.DMA((2 * experts + 2 * slices,)),
-        ],
-        flops=4 * slots * n * ff,
-        moved=slots * n * 2 + 4 * n * ff + slots * ff * 8,
-        grant=12,
-    )
 
     def extend(kernel, shape, args, steps):
         return call(
@@ -397,18 +364,40 @@
             moved=slots * ff * 8,
         )
 
-    act = extend(gate_kernel, flat, (tail, *g_all[slices:], acc_g), 2)
-    acc_u = extend(up_kernel, flat, (tail, u_all[slices], acc_u), 1)
+    acc_g, whole = call(
+        functools.partial(open_kernel, experts, slices),
+        [flat, jax.ShapeDtypeStruct((slots, width), BF16)],
+        (*rows, *g_all[:slices]),
+        [ANY] * (experts + slices),
+        [pltpu.VMEM((n, ff), BF16), pltpu.SemaphoreType.DMA((experts + slices,))],
+        flops=2 * slots * n * ff,
+        moved=slots * width * 2 + 2 * n * ff + slots * ff * 4,
+        grant=12,
+    )
+    acc_u = call(
+        functools.partial(more_kernel, slices),
+        flat,
+        (whole, *u_all[:slices]),
+        [VMEM] * (1 + slices),
+        [pltpu.VMEM((n, ff), BF16)],
+        flops=2 * slots * n * ff,
+        moved=slots * width * 2 + 2 * n * ff + slots * ff * 4,
+        grant=12,
+    )
+    tail = functools.partial
+    act = extend(tail(gate_kernel, slices), flat, (whole, *g_all[slices:], acc_g), 2)
+    acc_u = extend(tail(up_kernel, slices), flat, (whole, u_all[slices], acc_u), 1)
     hidden = extend(
-        hidden_kernel,
+        tail(hidden_kernel, slices + 1),
         jax.ShapeDtypeStruct((slots, ff), BF16),
-        (tail, u_all[slices + 1], acc_u, act),
+        (whole, u_all[slices + 1], acc_u, act),
         1,
     )
 
+    chunks = pieces()
     backs = []
-    for stage in range(CHAIN - 1 + HALVES):
-        own, other = d_all[2 * stage : 2 * stage + 2]
+    for i in range(len(chunks)):
+        own, other = d_all[2 * i : 2 * i + 2]
         wide = 2 * own.shape[0]
         outs = call(
             functools.partial(down_kernel, experts, capacity),
@@ -420,39 +409,28 @@
         )
         backs.append([outs[0]] + [across(outs[m], m) for m in range(1, experts)])
 
-    early = tuple(range(CHAIN - 1))
-    blocks = [b for s in early for b in backs[s]]
-    wide = 2 * part * len(early)
-    mixed, square, rest = call(
-        functools.partial(combine_kernel, early, len(blocks)),
-        [
-            jax.ShapeDtypeStruct((count, wide), F32),
-            jax.ShapeDtypeStruct((count, 128), F32),
-            jax.ShapeDtypeStruct((count, 2 * part), F32),
-        ],
-        (*blocks, stay(tokens), mix),
-        [ANY] * len(blocks) + [HBM, VMEM],
-        [
-            pltpu.VMEM((slots, wide), BF16),
-            pltpu.VMEM((count, wide), F32),
-            pltpu.SemaphoreType.DMA((len(blocks) + 2 * len(early),)),
-            pltpu.SemaphoreType.DMA((2,)),
-        ],
+    early, late = chunks[: CHAIN - 1], chunks[CHAIN - 1 :]
+    blocks = [b for x in backs[: CHAIN - 1] for b in x]
+    wide = 2 * part * (CHAIN - 1)
+    mixed, square = call(
+        functools.partial(combine_kernel, experts, early),
+        [jax.ShapeDtypeStruct((count, wide), F32), jax.ShapeDtypeStruct((count, 128), F32)],
+        (*blocks, sorted_tokens, mix),
+        [VMEM] * (len(blocks) + 2),
+        [pltpu.VMEM((slots, wide), BF16)],
         flops=4 * count * slots * wide,
         moved=slots * wide * 2 + count * wide * 8,
     )
+    blocks = [b for x in backs[CHAIN - 1 :] for b in x]
     return call(
-        functools.partial(finish_kernel, HALVES),
+        functools.partial(finish_kernel, experts, early, late),
         jax.ShapeDtypeStruct((count, width), F32),
-        (
-            *(b for x in backs[CHAIN - 1 :] for b in x),
-            *(rest, mix, norm_gain.reshape(1, width), mixed, square),
-        ),
-        [VMEM] * (experts * HALVES + 5),
+        (*blocks, mixed, square, sorted_tokens, mix, norm_gain.reshape(1, width)),
+        [VMEM] * (len(blocks) + 5),
         [
             pltpu.VMEM((slots, 2 * part), BF16),
             pltpu.VMEM((count, width), F32),
-            pltpu.SemaphoreType.DMA((2 * CHAIN,)),
+            pltpu.SemaphoreType.DMA((2 * len(chunks),)),
         ],
         flops=8 * count * slots * part,
         moved=count * width * 8,

time: 139 us -> 129 us (0.928)
  waiting for transfers between devices: 63.4 us -> 53.5 us
  starting transfers between devices: 56.1 us -> 53.5 us
  other arithmetic: 0.32 us -> 2.33 us
  Pallas kernels: 18.4 us -> 16.6 us
  local copies, waits for them, and re-layouts: 0.05 us -> 1.62 us
    ppermute x17 -> x16, waiting for transfers between devices: 44.7 us -> 39.5 us  [along(): return lax.ppermute(x, 'replica', devices)]
    ppermute x18 -> x15, waiting for transfers between devices: 18.6 us -> 14 us  [across(): return lax.ppermute(x, 'expert', [(e, e ^ m) for e in range(experts)])]
    pallas_call x12, Pallas kernels: 18.4 us -> 16.6 us  [call(): pl.pallas_call(kernel, out_shape=out_shape, in_specs=list(specs), out_spe...]
    unnamed x10 -> x26, local copies, waits for them, and re-layouts: 0.03 us -> 1.62 us
    ppermute x18 -> x15, starting transfers between devices: 24.6 us -> 23.2 us  [across(): return lax.ppermute(x, 'expert', [(e, e ^ m) for e in range(experts)])]
    ppermute x17 -> x16, starting transfers between devices: 29.1 us -> 27.9 us  [along(): return lax.ppermute(x, 'replica', devices)]
  transfers between devices with their start and end apart: 48 -> 43, of which waited for: 14 -> 19; matrix products, arithmetic and copies ran while one was open for 0% -> 2% of each run, Pallas kernels for 12% -> 11%
where the time goes in v3:
time: 129 us; the launch traced here: 128 us
  starting transfers between devices  53.5 us (41%)
  waiting for transfers between devices  53.5 us (41%)
  Pallas kernels  16.6 us (13%)
  other arithmetic  2.33 us (2%)
  local copies, waits for them, and re-layouts  1.62 us (1%)
    ppermute x16, waiting for transfers between devices, along(): return lax.ppermute(x, 'replica', devices)  39.5 us
    ppermute x16, starting transfers between devices, along(): return lax.ppermute(x, 'replica', devices)  27.9 us
    ppermute x15, starting transfers between devices, across(): return lax.ppermute(x, 'expert', [(e, e ^ m) for e in range(experts)])  23.2 us
    pallas_call x12, Pallas kernels, call(): pl.pallas_call(kernel, out_shape=out_shape, in_specs=list(specs), out_spe...  16.6 us
    ppermute x15, waiting for transfers between devices, across(): return lax.ppermute(x, 'expert', [(e, e ^ m) for e in range(experts)])  14 us
  transfers between devices with their start and end apart: 43, of which 19 were waited for; matrix products, arithmetic and copies ran while one was open for 2% of the time, Pallas kernels for 11%

profile of v3, /device:TPU:0, one launch (start us, length us, event | category | flops | bytes accessed | tf_op | source)
XLA Modules:
  0.0 128.3 jit_solution(7669083257223307510)
XLA Ops:
  0.0 1.4 %collective-permute-start.6 = (bf16[256,768]{1,0:T(8,128)(2,1)}, bf16[256,768]{1,0:T(8,128)(2,1)}, u32[]{:S(2)}, u32[]{:S(2)}) collective-permute-start(bf16[256,768]{1,0:T(8,128)(2,1)} %bitcast.11), channel_id=1, source_target_pairs={{8,16},{12,20},{16,8},{20,12},{9,17},{13,21},{17,9},{21,13},{10,18... | collective-permute-start | bytes 1179656 | tf_op jit(solution)/shard_map/ppermute | solution.py:302
  1.4 5.2 %collective-permute-start.4 = (bf16[256,768]{1,0:T(8,128)(2,1)}, bf16[256,768]{1,0:T(8,128)(2,1)S(1)}, u32[]{:S(2)}, u32[]{:S(2)}) collective-permute-start(bf16[256,768]{1,0:T(8,128)(2,1)} %bitcast.12), channel_id=1, source_target_pairs={{0,8},{4,12},{8,0},{12,4},{16,24},{20,28},{24,16},{28,20},{1,9},{5... | collective-permute-start | bytes 1179656 | tf_op jit(solution)/shard_map/ppermute | solution.py:302
  7.3 2.3 %collective-permute-start.9 = (bf16[256,768]{1,0:T(8,128)(2,1)}, bf16[256,768]{1,0:T(8,128)(2,1)S(1)}, u32[]{:S(2)}, u32[]{:S(2)}) collective-permute-start(bf16[256,768]{1,0:T(8,128)(2,1)} %bitcast.7), channel_id=1, source_target_pairs={{0,8},{4,12},{8,0},{12,4},{16,24},{20,28},{24,16},{28,20},{1,9},{5... | collective-permute-start | bytes 1179656 | tf_op jit(solution)/shard_map/ppermute | solution.py:302
  9.6 7.2 %collective-permute-done.4.refs_6_ = bf16[256,768]{1,0:T(8,128)(2,1)S(1)} collective-permute-done((bf16[256,768]{1,0:T(8,128)(2,1)}, bf16[256,768]{1,0:T(8,128)(2,1)S(1)}, u32[]{:S(2)}, u32[]{:S(2)}) %collective-permute-start.4) | collective-permute-done | bytes 393248 | tf_op jit(solution)/shard_map/ppermute | solution.py:302
  16.8 1.4 %collective-permute-start.37 = (bf16[256,768]{1,0:T(8,128)(2,1)}, bf16[256,768]{1,0:T(8,128)(2,1)}, u32[]{:S(2)}, u32[]{:S(2)}) collective-permute-start(bf16[256,768]{1,0:T(8,128)(2,1)} %bitcast.15), channel_id=1, source_target_pairs={{8,16},{12,20},{16,8},{20,12},{9,17},{13,21},{17,9},{21,13},{10,18... | collective-permute-start | bytes 1179656 | tf_op jit(solution)/shard_map/ppermute | solution.py:302
  18.2 0.8 copy-done.8
  19.0 5.6 %collective-permute-start.21 = (bf16[256,768]{1,0:T(8,128)(2,1)}, bf16[256,768]{1,0:T(8,128)(2,1)}, u32[]{:S(2)}, u32[]{:S(2)}) collective-permute-start(bf16[256,768]{1,0:T(8,128)(2,1)} %bitcast.16), channel_id=1, source_target_pairs={{0,8},{4,12},{24,16},{28,20},{1,9},{5,13},{25,17},{29,21},{2,10},{... | collective-permute-start | bytes 1179656 | tf_op jit(solution)/shard_map/ppermute | solution.py:302
  24.6 1.3 collective-permute-start.32
  25.9 3.7 %shard_map.73 = (bf16[144,2048]{1,0:T(8,128)(2,1)}, bf16[144,2048]{1,0:T(8,128)(2,1)}, bf16[144,2048]{1,0:T(8,128)(2,1)}, bf16[144,2048]{1,0:T(8,128)(2,1)S(1)},...) custom-call(s32[2,192]{1,0:T(2,128)} %bitcast.20, f32[2,192]{1,0:T(2,128)} %bitcast.21, f32[192,2048]{1,0:T(8,128)} %tok_hbm.1), custom_call_target="tpu_custom_call" | custom-call | flops 452984832 | bytes 3932160 | tf_op jit(solution)/shard_map/pallas_call | solution.py:83
  29.6 0.8 copy-done.2
  30.5 1.5 %collective-permute-start = (bf16[144,2048]{1,0:T(8,128)(2,1)}, bf16[144,2048]{1,0:T(8,128)(2,1)S(1)}, u32[]{:S(2)}, u32[]{:S(2)}) collective-permute-start(bf16[144,2048]{1,0:T(8,128)(2,1)} %get-tuple-element.32), channel_id=1, source_target_pairs={{0,1},{1,0},{2,3},{3,2},{4,5},{5,4},{6,7},{7,6},{8,9},{9,8},{10,11... | collective-permute-start | bytes 1769480 | tf_op jit(solution)/shard_map/ppermute | solution.py:308
  32.0 1.3 collective-permute-start.7
  33.3 1.6 %collective-permute-start.1 = (bf16[144,2048]{1,0:T(8,128)(2,1)}, bf16[144,2048]{1,0:T(8,128)(2,1)}, u32[]{:S(2)}, u32[]{:S(2)}) collective-permute-start(bf16[144,2048]{1,0:T(8,128)(2,1)} %get-tuple-element.33), channel_id=1, source_target_pairs={{0,2},{1,3},{2,0},{3,1},{4,6},{5,7},{6,4},{7,5},{8,10},{9,11},{10,... | collective-permute-start | bytes 1769480 | tf_op jit(solution)/shard_map/ppermute | solution.py:308
  34.9 0.8 collective-permute-start.18
  35.7 2.2 %collective-permute-done.32 = bf16[256,768]{1,0:T(8,128)(2,1)} collective-permute-done((bf16[256,768]{1,0:T(8,128)(2,1)}, bf16[256,768]{1,0:T(8,128)(2,1)}, u32[]{:S(2)}, u32[]{:S(2)}) %collective-permute-start.32) | collective-permute-done | bytes 393248 | tf_op jit(solution)/shard_map/ppermute | solution.py:302
  37.9 1.3 collective-permute-start.16
  39.2 1.1 broadcast_select_fusion.1.refs_0_
  40.3 5.2 %collective-permute-done.refs_1_ = bf16[144,2048]{1,0:T(8,128)(2,1)S(1)} collective-permute-done((bf16[144,2048]{1,0:T(8,128)(2,1)}, bf16[144,2048]{1,0:T(8,128)(2,1)S(1)}, u32[]{:S(2)}, u32[]{:S(2)}) %collective-permute-start) | collective-permute-done | bytes 589856 | tf_op jit(solution)/shard_map/ppermute | solution.py:308
  46.1 0.8 collective-permute-done.7
  46.9 1.3 collective-permute-start.38
  48.2 1.1 broadcast_select_fusion.6.refs_8_
  49.2 2.8 %collective-permute-start.2 = (bf16[144,2048]{1,0:T(8,128)(2,1)S(1)}, bf16[144,2048]{1,0:T(8,128)(2,1)S(1)}, u32[]{:S(2)}, u32[]{:S(2)}) collective-permute-start(bf16[144,2048]{1,0:T(8,128)(2,1)S(1)} %copy-done.3), channel_id=1, source_target_pairs={{0,3},{1,2},{2,1},{3,0},{4,7},{5,6},{6,5},{7,4},{8,11},{9,10},{10,... | collective-permute-start | bytes 1769480 | tf_op jit(solution)/shard_map/ppermute | solution.py:308
  52.8 2.4 %collective-permute-done.16 = bf16[256,768]{1,0:T(8,128)(2,1)S(1)} collective-permute-done((bf16[256,768]{1,0:T(8,128)(2,1)}, bf16[256,768]{1,0:T(8,128)(2,1)S(1)}, u32[]{:S(2)}, u32[]{:S(2)}) %collective-permute-start.16) | collective-permute-done | bytes 393248 | tf_op jit(solution)/shard_map/ppermute | solution.py:302
  55.2 1.3 collective-permute-start.19
  56.7 7.0 %collective-permute-done.38 = bf16[256,768]{1,0:T(8,128)(2,1)S(1)} collective-permute-done((bf16[256,768]{1,0:T(8,128)(2,1)}, bf16[256,768]{1,0:T(8,128)(2,1)S(1)}, u32[]{:S(2)}, u32[]{:S(2)}) %collective-permute-start.38) | collective-permute-done | bytes 393248 | tf_op jit(solution)/shard_map/ppermute | solution.py:302
  63.6 1.3 collective-permute-start.11
  65.1 6.9 %collective-permute-done.19 = bf16[256,768]{1,0:T(8,128)(2,1)S(1)} collective-permute-done((bf16[256,768]{1,0:T(8,128)(2,1)S(1)}, bf16[256,768]{1,0:T(8,128)(2,1)S(1)}, u32[]{:S(2)}, u32[]{:S(2)}) %collective-permute-start.19) | collective-permute-done | bytes 393248 | tf_op jit(solution)/shard_map/ppermute | solution.py:302
  72.1 1.5 %collective-permute-start.23 = (bf16[256,768]{1,0:T(8,128)(2,1)S(1)}, bf16[256,768]{1,0:T(8,128)(2,1)S(1)}, u32[]{:S(2)}, u32[]{:S(2)}) collective-permute-start(bf16[256,768]{1,0:T(8,128)(2,1)S(1)} %collective-permute-done.22), channel_id=1, source_target_pairs={{8,0},{12,4},{16,24},{20,28},{9,1},{13,5},{17,25},{21,29},{10,2},{... | collective-permute-start | bytes 1179656 | tf_op jit(solution)/shard_map/ppermute | solution.py:302
  74.2 6.3 %collective-permute-done.11 = bf16[256,768]{1,0:T(8,128)(2,1)S(1)} collective-permute-done((bf16[256,768]{1,0:T(8,128)(2,1)S(1)}, bf16[256,768]{1,0:T(8,128)(2,1)S(1)}, u32[]{:S(2)}, u32[]{:S(2)}) %collective-permute-start.11) | collective-permute-done | bytes 393248 | tf_op jit(solution)/shard_map/ppermute | solution.py:302
  81.1 6.7 %collective-permute-done.23 = bf16[256,768]{1,0:T(8,128)(2,1)S(1)} collective-permute-done((bf16[256,768]{1,0:T(8,128)(2,1)S(1)}, bf16[256,768]{1,0:T(8,128)(2,1)S(1)}, u32[]{:S(2)}, u32[]{:S(2)}) %collective-permute-start.23) | collective-permute-done | bytes 393248 | tf_op jit(solution)/shard_map/ppermute | solution.py:302
  88.5 4.1 %shard_map.74 = (f32[576,768]{1,0:T(8,128)S(1)}, bf16[576,2048]{1,0:T(8,128)(2,1)S(1)}) custom-call(bf16[144,2048]{1,0:T(8,128)(2,1)S(1)} %copy-done.10, bf16[144,2048]{1,0:T(8,128)(2,1)S(1)} %collective-permute-done.refs_1_, bf16[144,2048]{1,0:T(8,128)(2,1)} %collective-permute-done.1.refs_2_, bf16[144,2048]{1,0:T(8,128)(2,1)S(1)} %collective-permute-done.2.refs_3_, ...), custom_call_target="tpu_custom_call" | custom-call | flops 1358954496 | bytes 6488064 | tf_op jit(solution)/shard_map/pallas_call | solution.py:83
  93.1 1.5 %shard_map.75.acc = f32[576,768]{1,0:T(8,128)S(1)} custom-call(bf16[576,2048]{1,0:T(8,128)(2,1)S(1)} %get-tuple-element.35.rows, bf16[256,768]{1,0:T(8,128)(2,1)S(1)} %bitcast.9, bf16[256,768]{1,0:T(8,128)(2,1)S(1)} %collective-permute-done.13.refs_1_, bf16[256,768]{1,0:T(8,128)(2,1)S(1)} %collective-permute-done.9.refs_2_, ...), custom_call_target="tpu_custom_call" | custom-call | flops 1358954496 | bytes 6488064 | tf_op jit(solution)/shard_map/pallas_call | solution.py:83
  95.0 0.8 shard_map.77.act
  97.0 1.5 %collective-permute-start.40 = (bf16[144,512]{1,0:T(8,128)(2,1)S(1)}, bf16[144,512]{1,0:T(8,128)(2,1)S(1)}, u32[]{:S(2)}, u32[]{:S(2)}) collective-permute-start(bf16[144,512]{1,0:T(8,128)(2,1)S(1)} %get-tuple-element.50), channel_id=1, source_target_pairs={{0,1},{1,0},{2,3},{3,2},{4,5},{5,4},{6,7},{7,6},{8,9},{9,8},{10,11... | collective-permute-start | bytes 442376 | tf_op jit(solution)/shard_map/ppermute | solution.py:308
  98.5 1.5 %collective-permute-start.41 = (bf16[144,512]{1,0:T(8,128)(2,1)S(1)}, bf16[144,512]{1,0:T(8,128)(2,1)S(1)}, u32[]{:S(2)}, u32[]{:S(2)}) collective-permute-start(bf16[144,512]{1,0:T(8,128)(2,1)S(1)} %get-tuple-element.51), channel_id=1, source_target_pairs={{0,2},{1,3},{2,0},{3,1},{4,6},{5,7},{6,4},{7,5},{8,10},{9,11},{10,... | collective-permute-start | bytes 442376 | tf_op jit(solution)/shard_map/ppermute | solution.py:308
  101.2 1.5 %collective-permute-start.34 = (bf16[144,512]{1,0:T(8,128)(2,1)S(1)}, bf16[144,512]{1,0:T(8,128)(2,1)S(1)}, u32[]{:S(2)}, u32[]{:S(2)}) collective-permute-start(bf16[144,512]{1,0:T(8,128)(2,1)S(1)} %get-tuple-element.46), channel_id=1, source_target_pairs={{0,1},{1,0},{2,3},{3,2},{4,5},{5,4},{6,7},{7,6},{8,9},{9,8},{10,11... | collective-permute-start | bytes 442376 | tf_op jit(solution)/shard_map/ppermute | solution.py:308
  103.4 1.6 %collective-permute-start.35 = (bf16[144,512]{1,0:T(8,128)(2,1)S(1)}, bf16[144,512]{1,0:T(8,128)(2,1)S(1)}, u32[]{:S(2)}, u32[]{:S(2)}) collective-permute-start(bf16[144,512]{1,0:T(8,128)(2,1)S(1)} %get-tuple-element.47), channel_id=1, source_target_pairs={{0,2},{1,3},{2,0},{3,1},{4,6},{5,7},{6,4},{7,5},{8,10},{9,11},{10,... | collective-permute-start | bytes 442376 | tf_op jit(solution)/shard_map/ppermute | solution.py:308
  105.0 1.2 collective-permute-start.36
  106.2 1.2 collective-permute-done.41.refs_10_
  107.8 2.1 %collective-permute-start.30 = (bf16[144,512]{1,0:T(8,128)(2,1)S(1)}, bf16[144,512]{1,0:T(8,128)(2,1)S(1)}, u32[]{:S(2)}, u32[]{:S(2)}) collective-permute-start(bf16[144,512]{1,0:T(8,128)(2,1)S(1)} %get-tuple-element.43), channel_id=1, source_target_pairs={{0,2},{1,3},{2,0},{3,1},{4,6},{5,7},{6,4},{7,5},{8,10},{9,11},{10,... | collective-permute-start | bytes 442376 | tf_op jit(solution)/shard_map/ppermute | solution.py:308
  110.0 2.6 %collective-permute-start.31 = (bf16[144,512]{1,0:T(8,128)(2,1)S(1)}, bf16[144,512]{1,0:T(8,128)(2,1)S(1)}, u32[]{:S(2)}, u32[]{:S(2)}) collective-permute-start(bf16[144,512]{1,0:T(8,128)(2,1)S(1)} %get-tuple-element.44), channel_id=1, source_target_pairs={{0,3},{1,2},{2,1},{3,0},{4,7},{5,6},{6,5},{7,4},{8,11},{9,10},{10,... | collective-permute-start | bytes 442376 | tf_op jit(solution)/shard_map/ppermute | solution.py:308
  114.2 2.1 %collective-permute-start.26 = (bf16[144,512]{1,0:T(8,128)(2,1)S(1)}, bf16[144,512]{1,0:T(8,128)(2,1)S(1)}, u32[]{:S(2)}, u32[]{:S(2)}) collective-permute-start(bf16[144,512]{1,0:T(8,128)(2,1)S(1)} %get-tuple-element.39), channel_id=1, source_target_pairs={{0,2},{1,3},{2,0},{3,1},{4,6},{5,7},{6,4},{7,5},{8,10},{9,11},{10,... | collective-permute-start | bytes 442376 | tf_op jit(solution)/shard_map/ppermute | solution.py:308
  116.4 2.6 %collective-permute-start.27 = (bf16[144,512]{1,0:T(8,128)(2,1)S(1)}, bf16[144,512]{1,0:T(8,128)(2,1)S(1)}, u32[]{:S(2)}, u32[]{:S(2)}) collective-permute-start(bf16[144,512]{1,0:T(8,128)(2,1)S(1)} %get-tuple-element.40), channel_id=1, source_target_pairs={{0,3},{1,2},{2,1},{3,0},{4,7},{5,6},{6,5},{7,4},{8,11},{9,10},{10,... | collective-permute-start | bytes 442376 | tf_op jit(solution)/shard_map/ppermute | solution.py:308
  119.0 1.1 collective-permute-done.30.refs_2_
  120.5 1.2 shard_map.83
  121.7 1.0 collective-permute-done.25.refs_1_
  122.7 3.5 %collective-permute-done.26.refs_2_ = bf16[144,512]{1,0:T(8,128)(2,1)S(1)} collective-permute-done((bf16[144,512]{1,0:T(8,128)(2,1)S(1)}, bf16[144,512]{1,0:T(8,128)(2,1)S(1)}, u32[]{:S(2)}, u32[]{:S(2)}) %collective-permute-start.26) | collective-permute-done | bytes 147488 | tf_op jit(solution)/shard_map/ppermute | solution.py:308
  126.2 1.9 %shard_map.84 = f32[192,2048]{1,0:T(8,128)} custom-call(bf16[144,512]{1,0:T(8,128)(2,1)S(1)} %get-tuple-element.37.refs_0_, bf16[144,512]{1,0:T(8,128)(2,1)S(1)} %collective-permute-done.25.refs_1_, bf16[144,512]{1,0:T(8,128)(2,1)S(1)} %collective-permute-done.26.refs_2_, bf16[144,512]{1,0:T(8,128)(2,1)S(1)} %collective-permute-done.27.refs_3_, ...), custom_call_target="tpu_custom_call" | custom-call | flops 226492416 | bytes 3145728 | tf_op jit(solution)/shard_map/pallas_call | solution.py:83
  (83 shorter events, 10.6 us)
Async XLA Ops:
  0.0 9.6 %collective-permute-start.6 = (bf16[256,768]{1,0:T(8,128)(2,1)}, bf16[256,768]{1,0:T(8,128)(2,1)}, u32[]{:S(2)}, u32[]{:S(2)}) collective-permute-start(bf16[256,768]{1,0:T(8,128)(2,1)} %bitcast.11), channel_id=1, source_target_pairs={{8,16},{12,20},{16,8},{20,12},{9,17},{13,21},{17,9},{21,13},{10,18... | collective-permute-start | bytes 1179656 | tf_op jit(solution)/shard_map/ppermute | solution.py:302
  1.4 15.4 %collective-permute-start.4 = (bf16[256,768]{1,0:T(8,128)(2,1)}, bf16[256,768]{1,0:T(8,128)(2,1)S(1)}, u32[]{:S(2)}, u32[]{:S(2)}) collective-permute-start(bf16[256,768]{1,0:T(8,128)(2,1)} %bitcast.12), channel_id=1, source_target_pairs={{0,8},{4,12},{8,0},{12,4},{16,24},{20,28},{24,16},{28,20},{1,9},{5... | collective-permute-start | bytes 1179656 | tf_op jit(solution)/shard_map/ppermute | solution.py:302
  6.6 11.6 %collective-permute-start.3 = (bf16[256,768]{1,0:T(8,128)(2,1)}, bf16[256,768]{1,0:T(8,128)(2,1)S(1)}, u32[]{:S(2)}, u32[]{:S(2)}) collective-permute-start(bf16[256,768]{1,0:T(8,128)(2,1)} %bitcast.13), channel_id=1, source_target_pairs={{0,4},{4,0},{8,12},{12,8},{16,20},{20,16},{24,28},{28,24},{1,5},{5... | collective-permute-start | bytes 1179656 | tf_op jit(solution)/shard_map/ppermute | solution.py:305
  6.6 18.0 %collective-permute-start.15 = (bf16[256,768]{1,0:T(8,128)(2,1)}, bf16[256,768]{1,0:T(8,128)(2,1)S(1)}, u32[]{:S(2)}, u32[]{:S(2)}) collective-permute-start(bf16[256,768]{1,0:T(8,128)(2,1)} %bitcast.6), channel_id=1, source_target_pairs={{8,16},{12,20},{16,8},{20,12},{9,17},{13,21},{17,9},{21,13},{10,18... | collective-permute-start | bytes 1179656 | tf_op jit(solution)/shard_map/ppermute | solution.py:302
  7.3 23.2 %collective-permute-start.9 = (bf16[256,768]{1,0:T(8,128)(2,1)}, bf16[256,768]{1,0:T(8,128)(2,1)S(1)}, u32[]{:S(2)}, u32[]{:S(2)}) collective-permute-start(bf16[256,768]{1,0:T(8,128)(2,1)} %bitcast.7), channel_id=1, source_target_pairs={{0,8},{4,12},{8,0},{12,4},{16,24},{20,28},{24,16},{28,20},{1,9},{5... | collective-permute-start | bytes 1179656 | tf_op jit(solution)/shard_map/ppermute | solution.py:302
  9.6 22.4 %collective-permute-start.13 = (bf16[256,768]{1,0:T(8,128)(2,1)}, bf16[256,768]{1,0:T(8,128)(2,1)S(1)}, u32[]{:S(2)}, u32[]{:S(2)}) collective-permute-start(bf16[256,768]{1,0:T(8,128)(2,1)} %bitcast.8), channel_id=1, source_target_pairs={{0,4},{4,0},{8,12},{12,8},{16,20},{20,16},{24,28},{28,24},{1,5},{5... | collective-permute-start | bytes 1179656 | tf_op jit(solution)/shard_map/ppermute | solution.py:305
  16.8 16.5 %collective-permute-start.37 = (bf16[256,768]{1,0:T(8,128)(2,1)}, bf16[256,768]{1,0:T(8,128)(2,1)}, u32[]{:S(2)}, u32[]{:S(2)}) collective-permute-start(bf16[256,768]{1,0:T(8,128)(2,1)} %bitcast.15), channel_id=1, source_target_pairs={{8,16},{12,20},{16,8},{20,12},{9,17},{13,21},{17,9},{21,13},{10,18... | collective-permute-start | bytes 1179656 | tf_op jit(solution)/shard_map/ppermute | solution.py:302
  19.0 15.9 %collective-permute-start.21 = (bf16[256,768]{1,0:T(8,128)(2,1)}, bf16[256,768]{1,0:T(8,128)(2,1)}, u32[]{:S(2)}, u32[]{:S(2)}) collective-permute-start(bf16[256,768]{1,0:T(8,128)(2,1)} %bitcast.16), channel_id=1, source_target_pairs={{0,8},{4,12},{24,16},{28,20},{1,9},{5,13},{25,17},{29,21},{2,10},{... | collective-permute-start | bytes 1179656 | tf_op jit(solution)/shard_map/ppermute | solution.py:302
  24.6 13.3 %collective-permute-start.32 = (bf16[256,768]{1,0:T(8,128)(2,1)}, bf16[256,768]{1,0:T(8,128)(2,1)}, u32[]{:S(2)}, u32[]{:S(2)}) collective-permute-start(bf16[256,768]{1,0:T(8,128)(2,1)} %bitcast.17), channel_id=1, source_target_pairs={{8,0},{12,4},{16,24},{20,28},{9,1},{13,5},{17,25},{21,29},{10,2},{... | collective-permute-start | bytes 1179656 | tf_op jit(solution)/shard_map/ppermute | solution.py:302
  30.5 15.0 %collective-permute-start = (bf16[144,2048]{1,0:T(8,128)(2,1)}, bf16[144,2048]{1,0:T(8,128)(2,1)S(1)}, u32[]{:S(2)}, u32[]{:S(2)}) collective-permute-start(bf16[144,2048]{1,0:T(8,128)(2,1)} %get-tuple-element.32), channel_id=1, source_target_pairs={{0,1},{1,0},{2,3},{3,2},{4,5},{5,4},{6,7},{7,6},{8,9},{9,8},{10,11... | collective-permute-start | bytes 1769480 | tf_op jit(solution)/shard_map/ppermute | solution.py:308
  32.0 14.9 %collective-permute-start.7 = (bf16[256,768]{1,0:T(8,128)(2,1)}, bf16[256,768]{1,0:T(8,128)(2,1)}, u32[]{:S(2)}, u32[]{:S(2)}) collective-permute-start(bf16[256,768]{1,0:T(8,128)(2,1)} %collective-permute-done.6), channel_id=1, source_target_pairs={{8,0},{12,4},{16,24},{20,28},{9,1},{13,5},{17,25},{21,29},{10,2},{... | collective-permute-start | bytes 1179656 | tf_op jit(solution)/shard_map/ppermute | solution.py:302
  33.3 16.0 %collective-permute-start.1 = (bf16[144,2048]{1,0:T(8,128)(2,1)}, bf16[144,2048]{1,0:T(8,128)(2,1)}, u32[]{:S(2)}, u32[]{:S(2)}) collective-permute-start(bf16[144,2048]{1,0:T(8,128)(2,1)} %get-tuple-element.33), channel_id=1, source_target_pairs={{0,2},{1,3},{2,0},{3,1},{4,6},{5,7},{6,4},{7,5},{8,10},{9,11},{10,... | collective-permute-start | bytes 1769480 | tf_op jit(solution)/shard_map/ppermute | solution.py:308
  34.9 21.7 %copy-start.7 = (bf16[256,768]{1,0:T(8,128)(2,1)S(1)}, bf16[256,768]{1,0:T(8,128)(2,1)}, u32[]{:S(2)}) copy-start(bf16[256,768]{1,0:T(8,128)(2,1)} %copy-done.6) | copy-start | bytes 1179652
  34.9 17.2 %collective-permute-start.18 = (bf16[256,768]{1,0:T(8,128)(2,1)}, bf16[256,768]{1,0:T(8,128)(2,1)S(1)}, u32[]{:S(2)}, u32[]{:S(2)}) collective-permute-start(bf16[256,768]{1,0:T(8,128)(2,1)} %copy-done.6), channel_id=1, source_target_pairs={{8,16},{12,20},{16,8},{20,12},{9,17},{13,21},{17,9},{21,13},{10,18... | collective-permute-start | bytes 1179656 | tf_op jit(solution)/shard_map/ppermute | solution.py:302
  37.9 17.3 %collective-permute-start.16 = (bf16[256,768]{1,0:T(8,128)(2,1)}, bf16[256,768]{1,0:T(8,128)(2,1)S(1)}, u32[]{:S(2)}, u32[]{:S(2)}) collective-permute-start(bf16[256,768]{1,0:T(8,128)(2,1)} %copy-done.11), channel_id=1, source_target_pairs={{8,0},{12,4},{16,24},{20,28},{9,1},{13,5},{17,25},{21,29},{10,2},{... | collective-permute-start | bytes 1179656 | tf_op jit(solution)/shard_map/ppermute | solution.py:302
  45.4 11.1 %collective-permute-start.10 = (bf16[256,768]{1,0:T(8,128)(2,1)S(1)}, bf16[256,768]{1,0:T(8,128)(2,1)S(1)}, u32[]{:S(2)}, u32[]{:S(2)}) collective-permute-start(bf16[256,768]{1,0:T(8,128)(2,1)S(1)} %collective-permute-done.9.refs_2_), channel_id=1, source_target_pairs={{8,16},{12,20},{16,8},{20,12},{9,17},{13,21},{17,9},{21,13},{10,18... | collective-permute-start | bytes 1179656 | tf_op jit(solution)/shard_map/ppermute | solution.py:302
  46.9 16.7 %collective-permute-start.38 = (bf16[256,768]{1,0:T(8,128)(2,1)}, bf16[256,768]{1,0:T(8,128)(2,1)S(1)}, u32[]{:S(2)}, u32[]{:S(2)}) collective-permute-start(bf16[256,768]{1,0:T(8,128)(2,1)} %collective-permute-done.37), channel_id=1, source_target_pairs={{8,0},{12,4},{16,24},{20,28},{9,1},{13,5},{17,25},{21,29},{10,2},{... | collective-permute-start | bytes 1179656 | tf_op jit(solution)/shard_map/ppermute | solution.py:302
  49.2 24.3 %collective-permute-start.2 = (bf16[144,2048]{1,0:T(8,128)(2,1)S(1)}, bf16[144,2048]{1,0:T(8,128)(2,1)S(1)}, u32[]{:S(2)}, u32[]{:S(2)}) collective-permute-start(bf16[144,2048]{1,0:T(8,128)(2,1)S(1)} %copy-done.3), channel_id=1, source_target_pairs={{0,3},{1,2},{2,1},{3,0},{4,7},{5,6},{6,5},{7,4},{8,11},{9,10},{10,... | collective-permute-start | bytes 1769480 | tf_op jit(solution)/shard_map/ppermute | solution.py:308
  52.1 13.0 %collective-permute-start.22 = (bf16[256,768]{1,0:T(8,128)(2,1)}, bf16[256,768]{1,0:T(8,128)(2,1)S(1)}, u32[]{:S(2)}, u32[]{:S(2)}) collective-permute-start(bf16[256,768]{1,0:T(8,128)(2,1)} %collective-permute-done.21), channel_id=1, source_target_pairs={{8,16},{12,20},{16,8},{20,12},{9,17},{13,21},{17,9},{21,13},{10,18... | collective-permute-start | bytes 1179656 | tf_op jit(solution)/shard_map/ppermute | solution.py:302
  55.2 16.9 %collective-permute-start.19 = (bf16[256,768]{1,0:T(8,128)(2,1)S(1)}, bf16[256,768]{1,0:T(8,128)(2,1)S(1)}, u32[]{:S(2)}, u32[]{:S(2)}) collective-permute-start(bf16[256,768]{1,0:T(8,128)(2,1)S(1)} %collective-permute-done.18), channel_id=1, source_target_pairs={{8,0},{12,4},{16,24},{20,28},{9,1},{13,5},{17,25},{21,29},{10,2},{... | collective-permute-start | bytes 1179656 | tf_op jit(solution)/shard_map/ppermute | solution.py:302
  56.6 17.1 %collective-permute-start.5 = (bf16[256,768]{1,0:T(8,128)(2,1)S(1)}, bf16[256,768]{1,0:T(8,128)(2,1)S(1)}, u32[]{:S(2)}, u32[]{:S(2)}) collective-permute-start(bf16[256,768]{1,0:T(8,128)(2,1)S(1)} %copy-done.7), channel_id=1, source_target_pairs={{0,4},{4,0},{8,12},{12,8},{16,20},{20,16},{24,28},{28,24},{1,5},{5... | collective-permute-start | bytes 1179656 | tf_op jit(solution)/shard_map/ppermute | solution.py:305
  63.6 16.9 %collective-permute-start.11 = (bf16[256,768]{1,0:T(8,128)(2,1)S(1)}, bf16[256,768]{1,0:T(8,128)(2,1)S(1)}, u32[]{:S(2)}, u32[]{:S(2)}) collective-permute-start(bf16[256,768]{1,0:T(8,128)(2,1)S(1)} %collective-permute-done.10), channel_id=1, source_target_pairs={{8,0},{12,4},{16,24},{20,28},{9,1},{13,5},{17,25},{21,29},{10,2},{... | collective-permute-start | bytes 1179656 | tf_op jit(solution)/shard_map/ppermute | solution.py:302
  65.0 22.9 %copy-start.5 = (bf16[1,256,768]{2,1,0:T(8,128)(2,1)S(1)}, bf16[1,256,768]{2,1,0:T(8,128)(2,1)}, u32[]{:S(2)}) copy-start(bf16[1,256,768]{2,1,0:T(8,128)(2,1)} %param.12) | copy-start | bytes 1179652
  65.0 23.5 %copy-start.4 = (bf16[1,256,768]{2,1,0:T(8,128)(2,1)S(1)}, bf16[1,256,768]{2,1,0:T(8,128)(2,1)}, u32[]{:S(2)}) copy-start(bf16[1,256,768]{2,1,0:T(8,128)(2,1)} %param.10) | copy-start | bytes 1179652
  65.0 23.5 %copy-start.9 = (bf16[256,768]{1,0:T(8,128)(2,1)S(1)}, bf16[256,768]{1,0:T(8,128)(2,1)}, u32[]{:S(2)}) copy-start(bf16[256,768]{1,0:T(8,128)(2,1)} %copy-done.8) | copy-start | bytes 1179652
  65.0 23.5 %copy-start.10 = (bf16[144,2048]{1,0:T(8,128)(2,1)S(1)}, bf16[144,2048]{1,0:T(8,128)(2,1)}, u32[]{:S(2)}) copy-start(bf16[144,2048]{1,0:T(8,128)(2,1)} %get-tuple-element.31.refs_0_) | copy-start | bytes 1769476
  65.0 15.5 %collective-permute-start.14 = (bf16[256,768]{1,0:T(8,128)(2,1)S(1)}, bf16[256,768]{1,0:T(8,128)(2,1)S(1)}, u32[]{:S(2)}, u32[]{:S(2)}) collective-permute-start(bf16[256,768]{1,0:T(8,128)(2,1)S(1)} %collective-permute-done.9.refs_2_), channel_id=1, source_target_pairs={{0,4},{4,0},{8,12},{12,8},{16,20},{20,16},{24,28},{28,24},{1,5},{5... | collective-permute-start | bytes 1179656 | tf_op jit(solution)/shard_map/ppermute | solution.py:305
  72.1 15.7 %collective-permute-start.23 = (bf16[256,768]{1,0:T(8,128)(2,1)S(1)}, bf16[256,768]{1,0:T(8,128)(2,1)S(1)}, u32[]{:S(2)}, u32[]{:S(2)}) collective-permute-start(bf16[256,768]{1,0:T(8,128)(2,1)S(1)} %collective-permute-done.22), channel_id=1, source_target_pairs={{8,0},{12,4},{16,24},{20,28},{9,1},{13,5},{17,25},{21,29},{10,2},{... | collective-permute-start | bytes 1179656 | tf_op jit(solution)/shard_map/ppermute | solution.py:302
  73.6 14.2 %collective-permute-start.8 = (bf16[256,768]{1,0:T(8,128)(2,1)S(1)}, bf16[256,768]{1,0:T(8,128)(2,1)S(1)}, u32[]{:S(2)}, u32[]{:S(2)}) collective-permute-start(bf16[256,768]{1,0:T(8,128)(2,1)S(1)} %broadcast_select_fusion.6.refs_8_), channel_id=1, source_target_pairs={{0,4},{4,0},{8,12},{12,8},{16,20},{20,16},{24,28},{28,24},{1,5},{5... | collective-permute-start | bytes 1179656 | tf_op jit(solution)/shard_map/ppermute | solution.py:305
  73.7 14.7 %collective-permute-start.17 = (bf16[256,768]{1,0:T(8,128)(2,1)S(1)}, bf16[256,768]{1,0:T(8,128)(2,1)S(1)}, u32[]{:S(2)}, u32[]{:S(2)}) collective-permute-start(bf16[256,768]{1,0:T(8,128)(2,1)S(1)} %broadcast_select_fusion.4.refs_4_), channel_id=1, source_target_pairs={{0,4},{4,0},{8,12},{12,8},{16,20},{20,16},{24,28},{28,24},{1,5},{5... | collective-permute-start | bytes 1179656 | tf_op jit(solution)/shard_map/ppermute | solution.py:305
  80.5 12.1 %collective-permute-start.20 = (bf16[256,768]{1,0:T(8,128)(2,1)S(1)}, bf16[256,768]{1,0:T(8,128)(2,1)S(1)}, u32[]{:S(2)}, u32[]{:S(2)}) collective-permute-start(bf16[256,768]{1,0:T(8,128)(2,1)S(1)} %broadcast_select_fusion.3.own), channel_id=1, source_target_pairs={{0,4},{4,0},{8,12},{12,8},{16,20},{20,16},{24,28},{28,24},{1,5},{5... | collective-permute-start | bytes 1179656 | tf_op jit(solution)/shard_map/ppermute | solution.py:305
  80.5 15.8 %collective-permute-start.39 = (bf16[256,768]{1,0:T(8,128)(2,1)S(1)}, bf16[256,768]{1,0:T(8,128)(2,1)S(1)}, u32[]{:S(2)}, u32[]{:S(2)}) collective-permute-start(bf16[256,768]{1,0:T(8,128)(2,1)S(1)} %broadcast_select_fusion.refs_0_), channel_id=1, source_target_pairs={{0,4},{4,0},{8,12},{12,8},{16,20},{20,16},{24,28},{28,24},{1,5},{5... | collective-permute-start | bytes 1179656 | tf_op jit(solution)/shard_map/ppermute | solution.py:305
  87.8 8.1 %collective-permute-start.12 = (bf16[256,768]{1,0:T(8,128)(2,1)S(1)}, bf16[256,768]{1,0:T(8,128)(2,1)S(1)}, u32[]{:S(2)}, u32[]{:S(2)}) collective-permute-start(bf16[256,768]{1,0:T(8,128)(2,1)S(1)} %broadcast_select_fusion.5.own), channel_id=1, source_target_pairs={{0,4},{4,0},{8,12},{12,8},{16,20},{20,16},{24,28},{28,24},{1,5},{5... | collective-permute-start | bytes 1179656 | tf_op jit(solution)/shard_map/ppermute | solution.py:305
  87.9 13.4 %collective-permute-start.28 = (bf16[256,768]{1,0:T(8,128)(2,1)S(1)}, bf16[256,768]{1,0:T(8,128)(2,1)S(1)}, u32[]{:S(2)}, u32[]{:S(2)}) collective-permute-start(bf16[256,768]{1,0:T(8,128)(2,1)S(1)} %bitcast.18), channel_id=1, source_target_pairs={{0,4},{4,0},{8,12},{12,8},{16,20},{20,16},{24,28},{28,24},{1,5},{5... | collective-permute-start | bytes 1179656 | tf_op jit(solution)/shard_map/ppermute | solution.py:305
  88.4 11.6 %collective-permute-start.33 = (bf16[256,768]{1,0:T(8,128)(2,1)S(1)}, bf16[256,768]{1,0:T(8,128)(2,1)S(1)}, u32[]{:S(2)}, u32[]{:S(2)}) collective-permute-start(bf16[256,768]{1,0:T(8,128)(2,1)S(1)} %broadcast_select_fusion.1.refs_0_), channel_id=1, source_target_pairs={{0,4},{4,0},{8,12},{12,8},{16,20},{20,16},{24,28},{28,24},{1,5},{5... | collective-permute-start | bytes 1179656 | tf_op jit(solution)/shard_map/ppermute | solution.py:305
  92.6 10.8 %collective-permute-start.24 = (bf16[256,768]{1,0:T(8,128)(2,1)S(1)}, bf16[256,768]{1,0:T(8,128)(2,1)S(1)}, u32[]{:S(2)}, u32[]{:S(2)}) collective-permute-start(bf16[256,768]{1,0:T(8,128)(2,1)S(1)} %broadcast_select_fusion.2.refs_0_), channel_id=1, source_target_pairs={{0,4},{4,0},{8,12},{12,8},{16,20},{20,16},{24,28},{28,24},{1,5},{5... | collective-permute-start | bytes 1179656 | tf_op jit(solution)/shard_map/ppermute | solution.py:305
  97.0 8.0 %collective-permute-start.40 = (bf16[144,512]{1,0:T(8,128)(2,1)S(1)}, bf16[144,512]{1,0:T(8,128)(2,1)S(1)}, u32[]{:S(2)}, u32[]{:S(2)}) collective-permute-start(bf16[144,512]{1,0:T(8,128)(2,1)S(1)} %get-tuple-element.50), channel_id=1, source_target_pairs={{0,1},{1,0},{2,3},{3,2},{4,5},{5,4},{6,7},{7,6},{8,9},{9,8},{10,11... | collective-permute-start | bytes 442376 | tf_op jit(solution)/shard_map/ppermute | solution.py:308
  98.5 8.9 %collective-permute-start.41 = (bf16[144,512]{1,0:T(8,128)(2,1)S(1)}, bf16[144,512]{1,0:T(8,128)(2,1)S(1)}, u32[]{:S(2)}, u32[]{:S(2)}) collective-permute-start(bf16[144,512]{1,0:T(8,128)(2,1)S(1)} %get-tuple-element.51), channel_id=1, source_target_pairs={{0,2},{1,3},{2,0},{3,1},{4,6},{5,7},{6,4},{7,5},{8,10},{9,11},{10,... | collective-permute-start | bytes 442376 | tf_op jit(solution)/shard_map/ppermute | solution.py:308
  100.1 7.7 %collective-permute-start.42 = (bf16[144,512]{1,0:T(8,128)(2,1)S(1)}, bf16[144,512]{1,0:T(8,128)(2,1)S(1)}, u32[]{:S(2)}, u32[]{:S(2)}) collective-permute-start(bf16[144,512]{1,0:T(8,128)(2,1)S(1)} %get-tuple-element.52), channel_id=1, source_target_pairs={{0,3},{1,2},{2,1},{3,0},{4,7},{5,6},{6,5},{7,4},{8,11},{9,10},{10,... | collective-permute-start | bytes 442376 | tf_op jit(solution)/shard_map/ppermute | solution.py:308
  101.2 8.8 %collective-permute-start.34 = (bf16[144,512]{1,0:T(8,128)(2,1)S(1)}, bf16[144,512]{1,0:T(8,128)(2,1)S(1)}, u32[]{:S(2)}, u32[]{:S(2)}) collective-permute-start(bf16[144,512]{1,0:T(8,128)(2,1)S(1)} %get-tuple-element.46), channel_id=1, source_target_pairs={{0,1},{1,0},{2,3},{3,2},{4,5},{5,4},{6,7},{7,6},{8,9},{9,8},{10,11... | collective-permute-start | bytes 442376 | tf_op jit(solution)/shard_map/ppermute | solution.py:308
  103.4 10.3 %collective-permute-start.35 = (bf16[144,512]{1,0:T(8,128)(2,1)S(1)}, bf16[144,512]{1,0:T(8,128)(2,1)S(1)}, u32[]{:S(2)}, u32[]{:S(2)}) collective-permute-start(bf16[144,512]{1,0:T(8,128)(2,1)S(1)} %get-tuple-element.47), channel_id=1, source_target_pairs={{0,2},{1,3},{2,0},{3,1},{4,6},{5,7},{6,4},{7,5},{8,10},{9,11},{10,... | collective-permute-start | bytes 442376 | tf_op jit(solution)/shard_map/ppermute | solution.py:308
  105.0 9.1 %collective-permute-start.36 = (bf16[144,512]{1,0:T(8,128)(2,1)S(1)}, bf16[144,512]{1,0:T(8,128)(2,1)S(1)}, u32[]{:S(2)}, u32[]{:S(2)}) collective-permute-start(bf16[144,512]{1,0:T(8,128)(2,1)S(1)} %get-tuple-element.48), channel_id=1, source_target_pairs={{0,3},{1,2},{2,1},{3,0},{4,7},{5,6},{6,5},{7,4},{8,11},{9,10},{10,... | collective-permute-start | bytes 442376 | tf_op jit(solution)/shard_map/ppermute | solution.py:308
  107.5 8.9 %collective-permute-start.29 = (bf16[144,512]{1,0:T(8,128)(2,1)S(1)}, bf16[144,512]{1,0:T(8,128)(2,1)S(1)}, u32[]{:S(2)}, u32[]{:S(2)}) collective-permute-start(bf16[144,512]{1,0:T(8,128)(2,1)S(1)} %get-tuple-element.42), channel_id=1, source_target_pairs={{0,1},{1,0},{2,3},{3,2},{4,5},{5,4},{6,7},{7,6},{8,9},{9,8},{10,11... | collective-permute-start | bytes 442376 | tf_op jit(solution)/shard_map/ppermute | solution.py:308
  107.8 12.3 %collective-permute-start.30 = (bf16[144,512]{1,0:T(8,128)(2,1)S(1)}, bf16[144,512]{1,0:T(8,128)(2,1)S(1)}, u32[]{:S(2)}, u32[]{:S(2)}) collective-permute-start(bf16[144,512]{1,0:T(8,128)(2,1)S(1)} %get-tuple-element.43), channel_id=1, source_target_pairs={{0,2},{1,3},{2,0},{3,1},{4,6},{5,7},{6,4},{7,5},{8,10},{9,11},{10,... | collective-permute-start | bytes 442376 | tf_op jit(solution)/shard_map/ppermute | solution.py:308
  110.0 10.5 %collective-permute-start.31 = (bf16[144,512]{1,0:T(8,128)(2,1)S(1)}, bf16[144,512]{1,0:T(8,128)(2,1)S(1)}, u32[]{:S(2)}, u32[]{:S(2)}) collective-permute-start(bf16[144,512]{1,0:T(8,128)(2,1)S(1)} %get-tuple-element.44), channel_id=1, source_target_pairs={{0,3},{1,2},{2,1},{3,0},{4,7},{5,6},{6,5},{7,4},{8,11},{9,10},{10,... | collective-permute-start | bytes 442376 | tf_op jit(solution)/shard_map/ppermute | solution.py:308
  113.8 9.0 %collective-permute-start.25 = (bf16[144,512]{1,0:T(8,128)(2,1)S(1)}, bf16[144,512]{1,0:T(8,128)(2,1)S(1)}, u32[]{:S(2)}, u32[]{:S(2)}) collective-permute-start(bf16[144,512]{1,0:T(8,128)(2,1)S(1)} %get-tuple-element.38), channel_id=1, source_target_pairs={{0,1},{1,0},{2,3},{3,2},{4,5},{5,4},{6,7},{7,6},{8,9},{9,8},{10,11... | collective-permute-start | bytes 442376 | tf_op jit(solution)/shard_map/ppermute | solution.py:308
  114.2 12.1 %collective-permute-start.26 = (bf16[144,512]{1,0:T(8,128)(2,1)S(1)}, bf16[144,512]{1,0:T(8,128)(2,1)S(1)}, u32[]{:S(2)}, u32[]{:S(2)}) collective-permute-start(bf16[144,512]{1,0:T(8,128)(2,1)S(1)} %get-tuple-element.39), channel_id=1, source_target_pairs={{0,2},{1,3},{2,0},{3,1},{4,6},{5,7},{6,4},{7,5},{8,10},{9,11},{10,... | collective-permute-start | bytes 442376 | tf_op jit(solution)/shard_map/ppermute | solution.py:308
  116.4 9.8 %collective-permute-start.27 = (bf16[144,512]{1,0:T(8,128)(2,1)S(1)}, bf16[144,512]{1,0:T(8,128)(2,1)S(1)}, u32[]{:S(2)}, u32[]{:S(2)}) collective-permute-start(bf16[144,512]{1,0:T(8,128)(2,1)S(1)} %get-tuple-element.40), channel_id=1, source_target_pairs={{0,3},{1,2},{2,1},{3,0},{4,7},{5,6},{6,5},{7,4},{8,11},{9,10},{10,... | collective-permute-start | bytes 442376 | tf_op jit(solution)/shard_map/ppermute | solution.py:308
  (8 other events, 58.3 us)

commit v4 on v3

--- a/solution.py
+++ b/solution.py
@@ -211,61 +211,48 @@
         outs[m][...] = result[m * capacity : (m + 1) * capacity]
 
 
-def mixed_columns(experts, chunks, blocks, tokens, c_ref, back):
+def mixed_columns(experts, places, blocks, tokens, c_ref, back):
     capacity = blocks[0].shape[0]
     count = tokens.shape[0]
-    unit = tokens.shape[1] // (2 * CHAIN * HALVES)
     lo = 0
     for i, b in enumerate(blocks):
         m = i % experts
         back[m * capacity : (m + 1) * capacity, lo : lo + b.shape[1]] = b[...]
         lo += b.shape[1] if m == experts - 1 else 0
     both = jnp.dot(c_ref[...], back[...], preferred_element_type=F32)
-    summed = both[:count] + both[count:]
-    out, lo = [], 0
-    total = jnp.zeros((count, 1), F32)
-    for place, first, n in [p for c in chunks for p in c]:
-        at = (place * HALVES + first) * unit
-        value = tokens[:, at : at + n * unit] + summed[:, lo : lo + n * unit]
-        total = total + jnp.sum(value * value, axis=1, keepdims=True)
-        out.append(value)
-        lo += n * unit
-    return out, total
-
-
-def combine_kernel(experts, chunks, *refs):
+    at = places[0] * (lo // len(places))
+    value = tokens[:, at : at + lo] + (both[:count] + both[count:])
+    return value, jnp.sum(value * value, axis=1, keepdims=True)
+
+
+def combine_kernel(experts, places, *refs):
     *blocks, tokens, c_ref, out, square, back = refs
-    values, total = mixed_columns(experts, chunks, blocks, tokens, c_ref, back)
-    lo = 0
-    for value in values:
-        out[:, lo : lo + value.shape[1]] = value
-        lo += value.shape[1]
+    value, total = mixed_columns(experts, places, blocks, tokens, c_ref, back)
+    out[...] = value
     square[...] = jnp.broadcast_to(total, square.shape)
 
 
-def finish_kernel(experts, before, chunks, *refs):
+def finish_kernel(experts, places, *refs):
     *blocks, mixed, square, tokens, c_ref, gain, out_hbm, back, out, sems = refs
-    values, total = mixed_columns(experts, chunks, blocks, tokens, c_ref, back)
+    late, total = mixed_columns(experts, places, blocks, tokens, c_ref, back)
     width = out.shape[1]
     part = width // (2 * CHAIN)
-    unit = part // HALVES
     total = total + square[:, 0:1]
     scale = lax.rsqrt(total * (1.0 / width) + 1e-06)
-    order = slice_order()
     started = []
-    lo = 0
-    for i, (place, first, n) in enumerate([p for c in before + chunks for p in c]):
-        late = i - 2 * len(before)
-        size = n * unit
-        value = mixed[:, lo : lo + size] if late < 0 else values[late]
-        at = pl.ds(pl.multiple_of(order[place] * part + first * unit, unit), size)
-        out[:, lo : lo + size] = value * scale * gain[:, at]
+    for place, s in enumerate(slice_order()):
+        lo = place * part
+        if place < places[0]:
+            value = mixed[:, lo : lo + part]
+        else:
+            value = late[:, lo - places[0] * part :][:, :part]
+        at = pl.ds(pl.multiple_of(s * part, part), part)
+        out[:, lo : lo + part] = value * scale * gain[:, at]
         copy = pltpu.make_async_copy(
-            out.at[:, pl.ds(lo, size)], out_hbm.at[:, at], sems.at[i]
+            out.at[:, pl.ds(lo, part)], out_hbm.at[:, at], sems.at[place]
         )
         copy.start()
         started.append(copy)
-        lo += size
     for copy in started:
         copy.wait()
 
@@ -280,12 +267,8 @@
 PAIR = [(0, 1), (1, 0), (2, 3), (3, 2)]
 INWARD = [(0, 1), (3, 2)]
 OUTWARD = [(1, 0), (2, 3)]
-HALVES = 1
-
-
-def pieces():
-    whole = [[(2 * s, 0, HALVES), (2 * s + 1, 0, HALVES)] for s in range(CHAIN - 1)]
-    return whole + [[(2 * CHAIN - 2, h, 1), (2 * CHAIN - 1, h, 1)] for h in range(HALVES)]
+CHUNKS = [(2 * s, 2 * s + 1) for s in range(CHAIN - 1)] + [(2 * CHAIN - 2,), (2 * CHAIN - 1,)]
+LATE = 1
 
 
 def layer(tokens, expert_ids, combine_weights, gate, up, down, norm_gain):
@@ -316,14 +299,10 @@
             inner = one = along(w, PAIR)
         mid = along(w, MIDDLE)
         mid_in = along(inner, MIDDLE)
+
         two = jnp.where(end, along(mid, OUTWARD), mid)
-        parts = [mid_in]
-        if down and HALVES > 1:
-            step = mid_in.shape[0] // HALVES
-            parts = [mid_in[i * step : (i + 1) * step] for i in range(HALVES)]
-            parts = lax.optimization_barrier(parts)
-        three = [jnp.where(end, along(x, OUTWARD), x) for x in parts]
-        return [x for v in (w, one, two, *three) for x in (v, swap(v))]
+        three = jnp.where(end, along(mid_in, OUTWARD), mid_in)
+        return [x for v in (w, one, two, three) for x in (v, swap(v))]
 
     g_all, u_all, d_all = line(gate, False), line(up, False), line(down, True)
 
@@ -394,24 +373,23 @@
         1,
     )
 
-    chunks = pieces()
     backs = []
-    for i in range(len(chunks)):
-        own, other = d_all[2 * i : 2 * i + 2]
-        wide = 2 * own.shape[0]
+    for chunk in CHUNKS:
+        weights = [d_all[p] for p in chunk]
+        wide = sum(w.shape[0] for w in weights)
         outs = call(
             functools.partial(down_kernel, experts, capacity),
             [jax.ShapeDtypeStruct((capacity, wide), BF16)] * experts,
-            (hidden, own, other),
-            [VMEM] * 3,
+            (hidden, *weights),
+            [VMEM] * (1 + len(weights)),
             flops=2 * slots * ff * wide,
             moved=slots * ff * 2 + 2 * wide * ff + slots * wide * 2,
         )
         backs.append([outs[0]] + [across(outs[m], m) for m in range(1, experts)])
 
-    early, late = chunks[: CHAIN - 1], chunks[CHAIN - 1 :]
-    blocks = [b for x in backs[: CHAIN - 1] for b in x]
-    wide = 2 * part * (CHAIN - 1)
+    early = [p for c in CHUNKS[:-LATE] for p in c]
+    blocks = [b for x in backs[:-LATE] for b in x]
+    wide = part * len(early)
     mixed, square = call(
         functools.partial(combine_kernel, experts, early),
         [jax.ShapeDtypeStruct((count, wide), F32), jax.ShapeDtypeStruct((count, 128), F32)],
@@ -421,18 +399,19 @@
         flops=4 * count * slots * wide,
         moved=slots * wide * 2 + count * wide * 8,
     )
-    blocks = [b for x in backs[CHAIN - 1 :] for b in x]
+    late = [p for c in CHUNKS[-LATE:] for p in c]
+    blocks = [b for x in backs[-LATE:] for b in x]
     return call(
-        functools.partial(finish_kernel, experts, early, late),
+        functools.partial(finish_kernel, experts, late),
         jax.ShapeDtypeStruct((count, width), F32),
         (*blocks, mixed, square, sorted_tokens, mix, norm_gain.reshape(1, width)),
         [VMEM] * (len(blocks) + 5),
         [
-            pltpu.VMEM((slots, 2 * part), BF16),
+            pltpu.VMEM((slots, width - wide), BF16),
             pltpu.VMEM((count, width), F32),
-            pltpu.SemaphoreType.DMA((2 * len(chunks),)),
+            pltpu.SemaphoreType.DMA((2 * CHAIN,)),
         ],
-        flops=8 * count * slots * part,
+        flops=4 * count * slots * (width - wide),
         moved=count * width * 8,
         outs=HBM,
     )

time: 129 us -> 134 us (1.039)
  waiting for transfers between devices: 53.5 us -> 57 us
  starting transfers between devices: 53.5 us -> 54.9 us
    ppermute x15 -> x18, waiting for transfers between devices: 14 us -> 17.5 us  [across(): return lax.ppermute(x, 'expert', [(e, e ^ m) for e in range(experts)])]
    ppermute x15 -> x18, starting transfers between devices: 23.2 us -> 24.6 us  [across(): return lax.ppermute(x, 'expert', [(e, e ^ m) for e in range(experts)])]
    pallas_call x12 -> x13, Pallas kernels: 16.6 us -> 16.9 us  [call(): pl.pallas_call(kernel, out_shape=out_shape, in_specs=list(specs), out_spe...]
  transfers between devices with their start and end apart: 43 -> 46, of which waited for: 19 -> 13; matrix products, arithmetic and copies ran while one was open for 2% -> 2% of each run, Pallas kernels for 11% -> 11%
where the time goes in v4:
time: 134 us; the launch traced here: 133 us
  waiting for transfers between devices  57 us (43%)
  starting transfers between devices  54.9 us (41%)
  Pallas kernels  16.9 us (13%)
  other arithmetic  2.33 us (2%)
  local copies, waits for them, and re-layouts  1.64 us (1%)
    ppermute x16, waiting for transfers between devices, along(): return lax.ppermute(x, 'replica', devices)  39.5 us
    ppermute x16, starting transfers between devices, along(): return lax.ppermute(x, 'replica', devices)  27.9 us
    ppermute x18, starting transfers between devices, across(): return lax.ppermute(x, 'expert', [(e, e ^ m) for e in range(experts)])  24.6 us
    ppermute x18, waiting for transfers between devices, across(): return lax.ppermute(x, 'expert', [(e, e ^ m) for e in range(experts)])  17.5 us
    pallas_call x13, Pallas kernels, call(): pl.pallas_call(kernel, out_shape=out_shape, in_specs=list(specs), out_spe...  16.9 us
  transfers between devices with their start and end apart: 46, of which 13 were waited for; matrix products, arithmetic and copies ran while one was open for 2% of the time, Pallas kernels for 11%

profile of v4, /device:TPU:0, one launch (start us, length us, event | category | flops | bytes accessed | tf_op | source)
XLA Modules:
  0.0 133.4 jit_solution(9855788120554036307)
XLA Ops:
  0.0 1.4 %collective-permute-start.6 = (bf16[256,768]{1,0:T(8,128)(2,1)}, bf16[256,768]{1,0:T(8,128)(2,1)}, u32[]{:S(2)}, u32[]{:S(2)}) collective-permute-start(bf16[256,768]{1,0:T(8,128)(2,1)} %bitcast.11), channel_id=1, source_target_pairs={{8,16},{12,20},{16,8},{20,12},{9,17},{13,21},{17,9},{21,13},{10,18... | collective-permute-start | bytes 1179656 | tf_op jit(solution)/shard_map/ppermute | solution.py:285
  1.4 5.2 %collective-permute-start.4 = (bf16[256,768]{1,0:T(8,128)(2,1)}, bf16[256,768]{1,0:T(8,128)(2,1)S(1)}, u32[]{:S(2)}, u32[]{:S(2)}) collective-permute-start(bf16[256,768]{1,0:T(8,128)(2,1)} %bitcast.12), channel_id=1, source_target_pairs={{0,8},{4,12},{8,0},{12,4},{16,24},{20,28},{24,16},{28,20},{1,9},{5... | collective-permute-start | bytes 1179656 | tf_op jit(solution)/shard_map/ppermute | solution.py:285
  7.3 2.3 %collective-permute-start.9 = (bf16[256,768]{1,0:T(8,128)(2,1)}, bf16[256,768]{1,0:T(8,128)(2,1)S(1)}, u32[]{:S(2)}, u32[]{:S(2)}) collective-permute-start(bf16[256,768]{1,0:T(8,128)(2,1)} %bitcast.7), channel_id=1, source_target_pairs={{0,8},{4,12},{8,0},{12,4},{16,24},{20,28},{24,16},{28,20},{1,9},{5... | collective-permute-start | bytes 1179656 | tf_op jit(solution)/shard_map/ppermute | solution.py:285
  9.6 7.2 %collective-permute-done.4.refs_6_ = bf16[256,768]{1,0:T(8,128)(2,1)S(1)} collective-permute-done((bf16[256,768]{1,0:T(8,128)(2,1)}, bf16[256,768]{1,0:T(8,128)(2,1)S(1)}, u32[]{:S(2)}, u32[]{:S(2)}) %collective-permute-start.4) | collective-permute-done | bytes 393248 | tf_op jit(solution)/shard_map/ppermute | solution.py:285
  16.8 1.4 %collective-permute-start.37 = (bf16[256,768]{1,0:T(8,128)(2,1)}, bf16[256,768]{1,0:T(8,128)(2,1)}, u32[]{:S(2)}, u32[]{:S(2)}) collective-permute-start(bf16[256,768]{1,0:T(8,128)(2,1)} %bitcast.15), channel_id=1, source_target_pairs={{8,16},{12,20},{16,8},{20,12},{9,17},{13,21},{17,9},{21,13},{10,18... | collective-permute-start | bytes 1179656 | tf_op jit(solution)/shard_map/ppermute | solution.py:285
  19.0 5.6 %collective-permute-start.21 = (bf16[256,768]{1,0:T(8,128)(2,1)}, bf16[256,768]{1,0:T(8,128)(2,1)}, u32[]{:S(2)}, u32[]{:S(2)}) collective-permute-start(bf16[256,768]{1,0:T(8,128)(2,1)} %bitcast.16), channel_id=1, source_target_pairs={{0,8},{4,12},{24,16},{28,20},{1,9},{5,13},{25,17},{29,21},{2,10},{... | collective-permute-start | bytes 1179656 | tf_op jit(solution)/shard_map/ppermute | solution.py:285
  24.6 1.3 collective-permute-start.32
  25.9 3.8 %shard_map.73 = (bf16[144,2048]{1,0:T(8,128)(2,1)}, bf16[144,2048]{1,0:T(8,128)(2,1)}, bf16[144,2048]{1,0:T(8,128)(2,1)}, bf16[144,2048]{1,0:T(8,128)(2,1)S(1)},...) custom-call(s32[2,192]{1,0:T(2,128)} %bitcast.20, f32[2,192]{1,0:T(2,128)} %bitcast.21, f32[192,2048]{1,0:T(8,128)} %tok_hbm.1), custom_call_target="tpu_custom_call" | custom-call | flops 452984832 | bytes 3932160 | tf_op jit(solution)/shard_map/pallas_call | solution.py:83
  29.7 0.8 copy-done.2
  30.5 1.5 %collective-permute-start = (bf16[144,2048]{1,0:T(8,128)(2,1)}, bf16[144,2048]{1,0:T(8,128)(2,1)S(1)}, u32[]{:S(2)}, u32[]{:S(2)}) collective-permute-start(bf16[144,2048]{1,0:T(8,128)(2,1)} %get-tuple-element.36), channel_id=1, source_target_pairs={{0,1},{1,0},{2,3},{3,2},{4,5},{5,4},{6,7},{7,6},{8,9},{9,8},{10,11... | collective-permute-start | bytes 1769480 | tf_op jit(solution)/shard_map/ppermute | solution.py:291
  32.0 1.3 collective-permute-start.7
  33.3 1.6 %collective-permute-start.1 = (bf16[144,2048]{1,0:T(8,128)(2,1)}, bf16[144,2048]{1,0:T(8,128)(2,1)}, u32[]{:S(2)}, u32[]{:S(2)}) collective-permute-start(bf16[144,2048]{1,0:T(8,128)(2,1)} %get-tuple-element.37), channel_id=1, source_target_pairs={{0,2},{1,3},{2,0},{3,1},{4,6},{5,7},{6,4},{7,5},{8,10},{9,11},{10,... | collective-permute-start | bytes 1769480 | tf_op jit(solution)/shard_map/ppermute | solution.py:291
  34.9 0.8 collective-permute-start.18
  35.7 2.2 %collective-permute-done.32 = bf16[256,768]{1,0:T(8,128)(2,1)} collective-permute-done((bf16[256,768]{1,0:T(8,128)(2,1)}, bf16[256,768]{1,0:T(8,128)(2,1)}, u32[]{:S(2)}, u32[]{:S(2)}) %collective-permute-start.32) | collective-permute-done | bytes 393248 | tf_op jit(solution)/shard_map/ppermute | solution.py:285
  37.9 1.3 collective-permute-start.16
  39.2 1.1 broadcast_select_fusion.1.refs_0_
  40.3 5.2 %collective-permute-done.refs_1_ = bf16[144,2048]{1,0:T(8,128)(2,1)S(1)} collective-permute-done((bf16[144,2048]{1,0:T(8,128)(2,1)}, bf16[144,2048]{1,0:T(8,128)(2,1)S(1)}, u32[]{:S(2)}, u32[]{:S(2)}) %collective-permute-start) | collective-permute-done | bytes 589856 | tf_op jit(solution)/shard_map/ppermute | solution.py:291
  46.2 0.8 collective-permute-done.7
  46.9 1.3 collective-permute-start.38
  48.2 1.1 broadcast_select_fusion.6.refs_8_
  49.3 2.8 %collective-permute-start.2 = (bf16[144,2048]{1,0:T(8,128)(2,1)S(1)}, bf16[144,2048]{1,0:T(8,128)(2,1)S(1)}, u32[]{:S(2)}, u32[]{:S(2)}) collective-permute-start(bf16[144,2048]{1,0:T(8,128)(2,1)S(1)} %copy-done.3), channel_id=1, source_target_pairs={{0,3},{1,2},{2,1},{3,0},{4,7},{5,6},{6,5},{7,4},{8,11},{9,10},{10,... | collective-permute-start | bytes 1769480 | tf_op jit(solution)/shard_map/ppermute | solution.py:291
  52.8 2.5 %collective-permute-done.16 = bf16[256,768]{1,0:T(8,128)(2,1)S(1)} collective-permute-done((bf16[256,768]{1,0:T(8,128)(2,1)}, bf16[256,768]{1,0:T(8,128)(2,1)S(1)}, u32[]{:S(2)}, u32[]{:S(2)}) %collective-permute-start.16) | collective-permute-done | bytes 393248 | tf_op jit(solution)/shard_map/ppermute | solution.py:285
  55.3 1.3 collective-permute-start.19
  56.7 7.0 %collective-permute-done.38 = bf16[256,768]{1,0:T(8,128)(2,1)S(1)} collective-permute-done((bf16[256,768]{1,0:T(8,128)(2,1)}, bf16[256,768]{1,0:T(8,128)(2,1)S(1)}, u32[]{:S(2)}, u32[]{:S(2)}) %collective-permute-start.38) | collective-permute-done | bytes 393248 | tf_op jit(solution)/shard_map/ppermute | solution.py:285
  63.7 1.3 collective-permute-start.11
  65.2 6.9 %collective-permute-done.19 = bf16[256,768]{1,0:T(8,128)(2,1)S(1)} collective-permute-done((bf16[256,768]{1,0:T(8,128)(2,1)S(1)}, bf16[256,768]{1,0:T(8,128)(2,1)S(1)}, u32[]{:S(2)}, u32[]{:S(2)}) %collective-permute-start.19) | collective-permute-done | bytes 393248 | tf_op jit(solution)/shard_map/ppermute | solution.py:285
  72.1 1.5 %collective-permute-start.23 = (bf16[256,768]{1,0:T(8,128)(2,1)S(1)}, bf16[256,768]{1,0:T(8,128)(2,1)S(1)}, u32[]{:S(2)}, u32[]{:S(2)}) collective-permute-start(bf16[256,768]{1,0:T(8,128)(2,1)S(1)} %collective-permute-done.22), channel_id=1, source_target_pairs={{8,0},{12,4},{16,24},{20,28},{9,1},{13,5},{17,25},{21,29},{10,2},{... | collective-permute-start | bytes 1179656 | tf_op jit(solution)/shard_map/ppermute | solution.py:285
  74.2 6.3 %collective-permute-done.11 = bf16[256,768]{1,0:T(8,128)(2,1)S(1)} collective-permute-done((bf16[256,768]{1,0:T(8,128)(2,1)S(1)}, bf16[256,768]{1,0:T(8,128)(2,1)S(1)}, u32[]{:S(2)}, u32[]{:S(2)}) %collective-permute-start.11) | collective-permute-done | bytes 393248 | tf_op jit(solution)/shard_map/ppermute | solution.py:285
  81.2 6.6 %collective-permute-done.23 = bf16[256,768]{1,0:T(8,128)(2,1)S(1)} collective-permute-done((bf16[256,768]{1,0:T(8,128)(2,1)S(1)}, bf16[256,768]{1,0:T(8,128)(2,1)S(1)}, u32[]{:S(2)}, u32[]{:S(2)}) %collective-permute-start.23) | collective-permute-done | bytes 393248 | tf_op jit(solution)/shard_map/ppermute | solution.py:285
  89.0 4.1 %shard_map.74 = (f32[576,768]{1,0:T(8,128)S(1)}, bf16[576,2048]{1,0:T(8,128)(2,1)S(1)}) custom-call(bf16[144,2048]{1,0:T(8,128)(2,1)S(1)} %copy-done.10, bf16[144,2048]{1,0:T(8,128)(2,1)S(1)} %collective-permute-done.refs_1_, bf16[144,2048]{1,0:T(8,128)(2,1)} %collective-permute-done.1.refs_2_, bf16[144,2048]{1,0:T(8,128)(2,1)S(1)} %collective-permute-done.2.refs_3_, ...), custom_call_target="tpu_custom_call" | custom-call | flops 1358954496 | bytes 6488064 | tf_op jit(solution)/shard_map/pallas_call | solution.py:83
  93.1 1.5 %shard_map.75.acc = f32[576,768]{1,0:T(8,128)S(1)} custom-call(bf16[576,2048]{1,0:T(8,128)(2,1)S(1)} %get-tuple-element.39.rows, bf16[256,768]{1,0:T(8,128)(2,1)S(1)} %bitcast.9, bf16[256,768]{1,0:T(8,128)(2,1)S(1)} %collective-permute-done.13.refs_1_, bf16[256,768]{1,0:T(8,128)(2,1)S(1)} %collective-permute-done.9.refs_2_, ...), custom_call_target="tpu_custom_call" | custom-call | flops 1358954496 | bytes 6488064 | tf_op jit(solution)/shard_map/pallas_call | solution.py:83
  95.0 0.8 shard_map.77.act
  96.7 1.6 %collective-permute-start.43 = (bf16[144,256]{1,0:T(8,128)(2,1)S(1)}, bf16[144,256]{1,0:T(8,128)(2,1)S(1)}, u32[]{:S(2)}, u32[]{:S(2)}) collective-permute-start(bf16[144,256]{1,0:T(8,128)(2,1)S(1)} %get-tuple-element.58), channel_id=1, source_target_pairs={{0,1},{1,0},{2,3},{3,2},{4,5},{5,4},{6,7},{7,6},{8,9},{9,8},{10,11... | collective-permute-start | bytes 221192 | tf_op jit(solution)/shard_map/ppermute | solution.py:291
  99.5 1.5 %collective-permute-start.44 = (bf16[144,256]{1,0:T(8,128)(2,1)S(1)}, bf16[144,256]{1,0:T(8,128)(2,1)S(1)}, u32[]{:S(2)}, u32[]{:S(2)}) collective-permute-start(bf16[144,256]{1,0:T(8,128)(2,1)S(1)} %get-tuple-element.59), channel_id=1, source_target_pairs={{0,2},{1,3},{2,0},{3,1},{4,6},{5,7},{6,4},{7,5},{8,10},{9,11},{10,... | collective-permute-start | bytes 221192 | tf_op jit(solution)/shard_map/ppermute | solution.py:291
  102.3 2.5 %collective-permute-start.42 = (bf16[144,512]{1,0:T(8,128)(2,1)S(1)}, bf16[144,512]{1,0:T(8,128)(2,1)S(1)}, u32[]{:S(2)}, u32[]{:S(2)}) collective-permute-start(bf16[144,512]{1,0:T(8,128)(2,1)S(1)} %get-tuple-element.56), channel_id=1, source_target_pairs={{0,3},{1,2},{2,1},{3,0},{4,7},{5,6},{6,5},{7,4},{8,11},{9,10},{10,... | collective-permute-start | bytes 442376 | tf_op jit(solution)/shard_map/ppermute | solution.py:291
  105.3 1.8 %collective-permute-start.45 = (bf16[144,256]{1,0:T(8,128)(2,1)S(1)}, bf16[144,256]{1,0:T(8,128)(2,1)S(1)}, u32[]{:S(2)}, u32[]{:S(2)}) collective-permute-start(bf16[144,256]{1,0:T(8,128)(2,1)S(1)} %get-tuple-element.60), channel_id=1, source_target_pairs={{0,3},{1,2},{2,1},{3,0},{4,7},{5,6},{6,5},{7,4},{8,11},{9,10},{10,... | collective-permute-start | bytes 221192 | tf_op jit(solution)/shard_map/ppermute | solution.py:291
  107.8 5.7 %collective-permute-done.45.refs_15_ = bf16[144,256]{1,0:T(8,128)(2,1)S(1)} collective-permute-done((bf16[144,256]{1,0:T(8,128)(2,1)S(1)}, bf16[144,256]{1,0:T(8,128)(2,1)S(1)}, u32[]{:S(2)}, u32[]{:S(2)}) %collective-permute-start.45) | collective-permute-done | bytes 73760 | tf_op jit(solution)/shard_map/ppermute | solution.py:291
  114.2 1.9 %collective-permute-start.36 = (bf16[144,512]{1,0:T(8,128)(2,1)S(1)}, bf16[144,512]{1,0:T(8,128)(2,1)S(1)}, u32[]{:S(2)}, u32[]{:S(2)}) collective-permute-start(bf16[144,512]{1,0:T(8,128)(2,1)S(1)} %get-tuple-element.52), channel_id=1, source_target_pairs={{0,3},{1,2},{2,1},{3,0},{4,7},{5,6},{6,5},{7,4},{8,11},{9,10},{10,... | collective-permute-start | bytes 442376 | tf_op jit(solution)/shard_map/ppermute | solution.py:291
  116.2 0.8 collective-permute-start.29
  117.7 1.9 %collective-permute-start.31 = (bf16[144,512]{1,0:T(8,128)(2,1)S(1)}, bf16[144,512]{1,0:T(8,128)(2,1)S(1)}, u32[]{:S(2)}, u32[]{:S(2)}) collective-permute-start(bf16[144,512]{1,0:T(8,128)(2,1)S(1)} %get-tuple-element.48), channel_id=1, source_target_pairs={{0,3},{1,2},{2,1},{3,0},{4,7},{5,6},{6,5},{7,4},{8,11},{9,10},{10,... | collective-permute-start | bytes 442376 | tf_op jit(solution)/shard_map/ppermute | solution.py:291
  120.1 3.4 %collective-permute-done.35.refs_6_ = bf16[144,512]{1,0:T(8,128)(2,1)S(1)} collective-permute-done((bf16[144,512]{1,0:T(8,128)(2,1)S(1)}, bf16[144,512]{1,0:T(8,128)(2,1)S(1)}, u32[]{:S(2)}, u32[]{:S(2)}) %collective-permute-start.35) | collective-permute-done | bytes 147488 | tf_op jit(solution)/shard_map/ppermute | solution.py:291
  123.5 1.5 %collective-permute-start.25 = (bf16[144,256]{1,0:T(8,128)(2,1)S(1)}, bf16[144,256]{1,0:T(8,128)(2,1)S(1)}, u32[]{:S(2)}, u32[]{:S(2)}) collective-permute-start(bf16[144,256]{1,0:T(8,128)(2,1)S(1)} %get-tuple-element.42), channel_id=1, source_target_pairs={{0,1},{1,0},{2,3},{3,2},{4,5},{5,4},{6,7},{7,6},{8,9},{9,8},{10,11... | collective-permute-start | bytes 221192 | tf_op jit(solution)/shard_map/ppermute | solution.py:291
  125.0 1.2 collective-permute-start.26
  126.2 0.8 collective-permute-start.27
  127.0 1.8 %collective-permute-done.30.refs_2_ = bf16[144,512]{1,0:T(8,128)(2,1)S(1)} collective-permute-done((bf16[144,512]{1,0:T(8,128)(2,1)S(1)}, bf16[144,512]{1,0:T(8,128)(2,1)S(1)}, u32[]{:S(2)}, u32[]{:S(2)}) %collective-permute-start.30) | collective-permute-done | bytes 147488 | tf_op jit(solution)/shard_map/ppermute | solution.py:291
  128.8 1.3 shard_map.84
  130.2 1.3 collective-permute-done.27.refs_3_
  131.5 1.7 %shard_map.85 = f32[192,2048]{1,0:T(8,128)} custom-call(bf16[144,256]{1,0:T(8,128)(2,1)S(1)} %get-tuple-element.41.refs_0_, bf16[144,256]{1,0:T(8,128)(2,1)S(1)} %collective-permute-done.25.refs_1_, bf16[144,256]{1,0:T(8,128)(2,1)S(1)} %collective-permute-done.26.refs_2_, bf16[144,256]{1,0:T(8,128)(2,1)S(1)} %collective-permute-done.27.refs_3_, ...), custom_call_target="tpu_custom_call" | custom-call | flops 113246208 | bytes 3145728 | tf_op jit(solution)/shard_map/pallas_call | solution.py:83
  (90 shorter events, 12.4 us)
Async XLA Ops:
  0.0 9.6 %collective-permute-start.6 = (bf16[256,768]{1,0:T(8,128)(2,1)}, bf16[256,768]{1,0:T(8,128)(2,1)}, u32[]{:S(2)}, u32[]{:S(2)}) collective-permute-start(bf16[256,768]{1,0:T(8,128)(2,1)} %bitcast.11), channel_id=1, source_target_pairs={{8,16},{12,20},{16,8},{20,12},{9,17},{13,21},{17,9},{21,13},{10,18... | collective-permute-start | bytes 1179656 | tf_op jit(solution)/shard_map/ppermute | solution.py:285
  1.4 15.4 %collective-permute-start.4 = (bf16[256,768]{1,0:T(8,128)(2,1)}, bf16[256,768]{1,0:T(8,128)(2,1)S(1)}, u32[]{:S(2)}, u32[]{:S(2)}) collective-permute-start(bf16[256,768]{1,0:T(8,128)(2,1)} %bitcast.12), channel_id=1, source_target_pairs={{0,8},{4,12},{8,0},{12,4},{16,24},{20,28},{24,16},{28,20},{1,9},{5... | collective-permute-start | bytes 1179656 | tf_op jit(solution)/shard_map/ppermute | solution.py:285
  6.6 11.6 %collective-permute-start.3 = (bf16[256,768]{1,0:T(8,128)(2,1)}, bf16[256,768]{1,0:T(8,128)(2,1)S(1)}, u32[]{:S(2)}, u32[]{:S(2)}) collective-permute-start(bf16[256,768]{1,0:T(8,128)(2,1)} %bitcast.13), channel_id=1, source_target_pairs={{0,4},{4,0},{8,12},{12,8},{16,20},{20,16},{24,28},{28,24},{1,5},{5... | collective-permute-start | bytes 1179656 | tf_op jit(solution)/shard_map/ppermute | solution.py:288
  6.6 18.0 %collective-permute-start.15 = (bf16[256,768]{1,0:T(8,128)(2,1)}, bf16[256,768]{1,0:T(8,128)(2,1)S(1)}, u32[]{:S(2)}, u32[]{:S(2)}) collective-permute-start(bf16[256,768]{1,0:T(8,128)(2,1)} %bitcast.6), channel_id=1, source_target_pairs={{8,16},{12,20},{16,8},{20,12},{9,17},{13,21},{17,9},{21,13},{10,18... | collective-permute-start | bytes 1179656 | tf_op jit(solution)/shard_map/ppermute | solution.py:285
  7.3 23.2 %collective-permute-start.9 = (bf16[256,768]{1,0:T(8,128)(2,1)}, bf16[256,768]{1,0:T(8,128)(2,1)S(1)}, u32[]{:S(2)}, u32[]{:S(2)}) collective-permute-start(bf16[256,768]{1,0:T(8,128)(2,1)} %bitcast.7), channel_id=1, source_target_pairs={{0,8},{4,12},{8,0},{12,4},{16,24},{20,28},{24,16},{28,20},{1,9},{5... | collective-permute-start | bytes 1179656 | tf_op jit(solution)/shard_map/ppermute | solution.py:285
  9.6 22.4 %collective-permute-start.13 = (bf16[256,768]{1,0:T(8,128)(2,1)}, bf16[256,768]{1,0:T(8,128)(2,1)S(1)}, u32[]{:S(2)}, u32[]{:S(2)}) collective-permute-start(bf16[256,768]{1,0:T(8,128)(2,1)} %bitcast.8), channel_id=1, source_target_pairs={{0,4},{4,0},{8,12},{12,8},{16,20},{20,16},{24,28},{28,24},{1,5},{5... | collective-permute-start | bytes 1179656 | tf_op jit(solution)/shard_map/ppermute | solution.py:288
  16.8 16.5 %collective-permute-start.37 = (bf16[256,768]{1,0:T(8,128)(2,1)}, bf16[256,768]{1,0:T(8,128)(2,1)}, u32[]{:S(2)}, u32[]{:S(2)}) collective-permute-start(bf16[256,768]{1,0:T(8,128)(2,1)} %bitcast.15), channel_id=1, source_target_pairs={{8,16},{12,20},{16,8},{20,12},{9,17},{13,21},{17,9},{21,13},{10,18... | collective-permute-start | bytes 1179656 | tf_op jit(solution)/shard_map/ppermute | solution.py:285
  19.0 15.9 %collective-permute-start.21 = (bf16[256,768]{1,0:T(8,128)(2,1)}, bf16[256,768]{1,0:T(8,128)(2,1)}, u32[]{:S(2)}, u32[]{:S(2)}) collective-permute-start(bf16[256,768]{1,0:T(8,128)(2,1)} %bitcast.16), channel_id=1, source_target_pairs={{0,8},{4,12},{24,16},{28,20},{1,9},{5,13},{25,17},{29,21},{2,10},{... | collective-permute-start | bytes 1179656 | tf_op jit(solution)/shard_map/ppermute | solution.py:285
  24.6 13.3 %collective-permute-start.32 = (bf16[256,768]{1,0:T(8,128)(2,1)}, bf16[256,768]{1,0:T(8,128)(2,1)}, u32[]{:S(2)}, u32[]{:S(2)}) collective-permute-start(bf16[256,768]{1,0:T(8,128)(2,1)} %bitcast.17), channel_id=1, source_target_pairs={{8,0},{12,4},{16,24},{20,28},{9,1},{13,5},{17,25},{21,29},{10,2},{... | collective-permute-start | bytes 1179656 | tf_op jit(solution)/shard_map/ppermute | solution.py:285
  30.5 15.0 %collective-permute-start = (bf16[144,2048]{1,0:T(8,128)(2,1)}, bf16[144,2048]{1,0:T(8,128)(2,1)S(1)}, u32[]{:S(2)}, u32[]{:S(2)}) collective-permute-start(bf16[144,2048]{1,0:T(8,128)(2,1)} %get-tuple-element.36), channel_id=1, source_target_pairs={{0,1},{1,0},{2,3},{3,2},{4,5},{5,4},{6,7},{7,6},{8,9},{9,8},{10,11... | collective-permute-start | bytes 1769480 | tf_op jit(solution)/shard_map/ppermute | solution.py:291
  32.0 14.9 %collective-permute-start.7 = (bf16[256,768]{1,0:T(8,128)(2,1)}, bf16[256,768]{1,0:T(8,128)(2,1)}, u32[]{:S(2)}, u32[]{:S(2)}) collective-permute-start(bf16[256,768]{1,0:T(8,128)(2,1)} %collective-permute-done.6), channel_id=1, source_target_pairs={{8,0},{12,4},{16,24},{20,28},{9,1},{13,5},{17,25},{21,29},{10,2},{... | collective-permute-start | bytes 1179656 | tf_op jit(solution)/shard_map/ppermute | solution.py:285
  33.3 16.0 %collective-permute-start.1 = (bf16[144,2048]{1,0:T(8,128)(2,1)}, bf16[144,2048]{1,0:T(8,128)(2,1)}, u32[]{:S(2)}, u32[]{:S(2)}) collective-permute-start(bf16[144,2048]{1,0:T(8,128)(2,1)} %get-tuple-element.37), channel_id=1, source_target_pairs={{0,2},{1,3},{2,0},{3,1},{4,6},{5,7},{6,4},{7,5},{8,10},{9,11},{10,... | collective-permute-start | bytes 1769480 | tf_op jit(solution)/shard_map/ppermute | solution.py:291
  34.9 17.2 %collective-permute-start.18 = (bf16[256,768]{1,0:T(8,128)(2,1)}, bf16[256,768]{1,0:T(8,128)(2,1)S(1)}, u32[]{:S(2)}, u32[]{:S(2)}) collective-permute-start(bf16[256,768]{1,0:T(8,128)(2,1)} %copy-done.6), channel_id=1, source_target_pairs={{8,16},{12,20},{16,8},{20,12},{9,17},{13,21},{17,9},{21,13},{10,18... | collective-permute-start | bytes 1179656 | tf_op jit(solution)/shard_map/ppermute | solution.py:285
  37.9 17.3 %collective-permute-start.16 = (bf16[256,768]{1,0:T(8,128)(2,1)}, bf16[256,768]{1,0:T(8,128)(2,1)S(1)}, u32[]{:S(2)}, u32[]{:S(2)}) collective-permute-start(bf16[256,768]{1,0:T(8,128)(2,1)} %copy-done.11), channel_id=1, source_target_pairs={{8,0},{12,4},{16,24},{20,28},{9,1},{13,5},{17,25},{21,29},{10,2},{... | collective-permute-start | bytes 1179656 | tf_op jit(solution)/shard_map/ppermute | solution.py:285
  45.5 11.1 %collective-permute-start.10 = (bf16[256,768]{1,0:T(8,128)(2,1)S(1)}, bf16[256,768]{1,0:T(8,128)(2,1)S(1)}, u32[]{:S(2)}, u32[]{:S(2)}) collective-permute-start(bf16[256,768]{1,0:T(8,128)(2,1)S(1)} %collective-permute-done.9.refs_2_), channel_id=1, source_target_pairs={{8,16},{12,20},{16,8},{20,12},{9,17},{13,21},{17,9},{21,13},{10,18... | collective-permute-start | bytes 1179656 | tf_op jit(solution)/shard_map/ppermute | solution.py:285
  46.9 16.7 %collective-permute-start.38 = (bf16[256,768]{1,0:T(8,128)(2,1)}, bf16[256,768]{1,0:T(8,128)(2,1)S(1)}, u32[]{:S(2)}, u32[]{:S(2)}) collective-permute-start(bf16[256,768]{1,0:T(8,128)(2,1)} %collective-permute-done.37), channel_id=1, source_target_pairs={{8,0},{12,4},{16,24},{20,28},{9,1},{13,5},{17,25},{21,29},{10,2},{... | collective-permute-start | bytes 1179656 | tf_op jit(solution)/shard_map/ppermute | solution.py:285
  49.3 24.3 %collective-permute-start.2 = (bf16[144,2048]{1,0:T(8,128)(2,1)S(1)}, bf16[144,2048]{1,0:T(8,128)(2,1)S(1)}, u32[]{:S(2)}, u32[]{:S(2)}) collective-permute-start(bf16[144,2048]{1,0:T(8,128)(2,1)S(1)} %copy-done.3), channel_id=1, source_target_pairs={{0,3},{1,2},{2,1},{3,0},{4,7},{5,6},{6,5},{7,4},{8,11},{9,10},{10,... | collective-permute-start | bytes 1769480 | tf_op jit(solution)/shard_map/ppermute | solution.py:291
  52.1 13.0 %collective-permute-start.22 = (bf16[256,768]{1,0:T(8,128)(2,1)}, bf16[256,768]{1,0:T(8,128)(2,1)S(1)}, u32[]{:S(2)}, u32[]{:S(2)}) collective-permute-start(bf16[256,768]{1,0:T(8,128)(2,1)} %collective-permute-done.21), channel_id=1, source_target_pairs={{8,16},{12,20},{16,8},{20,12},{9,17},{13,21},{17,9},{21,13},{10,18... | collective-permute-start | bytes 1179656 | tf_op jit(solution)/shard_map/ppermute | solution.py:285
  55.3 16.9 %collective-permute-start.19 = (bf16[256,768]{1,0:T(8,128)(2,1)S(1)}, bf16[256,768]{1,0:T(8,128)(2,1)S(1)}, u32[]{:S(2)}, u32[]{:S(2)}) collective-permute-start(bf16[256,768]{1,0:T(8,128)(2,1)S(1)} %collective-permute-done.18), channel_id=1, source_target_pairs={{8,0},{12,4},{16,24},{20,28},{9,1},{13,5},{17,25},{21,29},{10,2},{... | collective-permute-start | bytes 1179656 | tf_op jit(solution)/shard_map/ppermute | solution.py:285
  56.6 17.1 %collective-permute-start.5 = (bf16[256,768]{1,0:T(8,128)(2,1)S(1)}, bf16[256,768]{1,0:T(8,128)(2,1)S(1)}, u32[]{:S(2)}, u32[]{:S(2)}) collective-permute-start(bf16[256,768]{1,0:T(8,128)(2,1)S(1)} %copy-done.7), channel_id=1, source_target_pairs={{0,4},{4,0},{8,12},{12,8},{16,20},{20,16},{24,28},{28,24},{1,5},{5... | collective-permute-start | bytes 1179656 | tf_op jit(solution)/shard_map/ppermute | solution.py:288
  63.7 16.9 %collective-permute-start.11 = (bf16[256,768]{1,0:T(8,128)(2,1)S(1)}, bf16[256,768]{1,0:T(8,128)(2,1)S(1)}, u32[]{:S(2)}, u32[]{:S(2)}) collective-permute-start(bf16[256,768]{1,0:T(8,128)(2,1)S(1)} %collective-permute-done.10), channel_id=1, source_target_pairs={{8,0},{12,4},{16,24},{20,28},{9,1},{13,5},{17,25},{21,29},{10,2},{... | collective-permute-start | bytes 1179656 | tf_op jit(solution)/shard_map/ppermute | solution.py:285
  65.0 23.9 %copy-start.4 = (bf16[1,256,768]{2,1,0:T(8,128)(2,1)S(1)}, bf16[1,256,768]{2,1,0:T(8,128)(2,1)}, u32[]{:S(2)}) copy-start(bf16[1,256,768]{2,1,0:T(8,128)(2,1)} %param.10) | copy-start | bytes 1179652
  65.1 23.9 %copy-start.9 = (bf16[256,768]{1,0:T(8,128)(2,1)S(1)}, bf16[256,768]{1,0:T(8,128)(2,1)}, u32[]{:S(2)}) copy-start(bf16[256,768]{1,0:T(8,128)(2,1)} %copy-done.8) | copy-start | bytes 1179652
  65.1 15.5 %collective-permute-start.14 = (bf16[256,768]{1,0:T(8,128)(2,1)S(1)}, bf16[256,768]{1,0:T(8,128)(2,1)S(1)}, u32[]{:S(2)}, u32[]{:S(2)}) collective-permute-start(bf16[256,768]{1,0:T(8,128)(2,1)S(1)} %collective-permute-done.9.refs_2_), channel_id=1, source_target_pairs={{0,4},{4,0},{8,12},{12,8},{16,20},{20,16},{24,28},{28,24},{1,5},{5... | collective-permute-start | bytes 1179656 | tf_op jit(solution)/shard_map/ppermute | solution.py:288
  72.1 15.7 %collective-permute-start.23 = (bf16[256,768]{1,0:T(8,128)(2,1)S(1)}, bf16[256,768]{1,0:T(8,128)(2,1)S(1)}, u32[]{:S(2)}, u32[]{:S(2)}) collective-permute-start(bf16[256,768]{1,0:T(8,128)(2,1)S(1)} %collective-permute-done.22), channel_id=1, source_target_pairs={{8,0},{12,4},{16,24},{20,28},{9,1},{13,5},{17,25},{21,29},{10,2},{... | collective-permute-start | bytes 1179656 | tf_op jit(solution)/shard_map/ppermute | solution.py:285
  73.6 14.2 %collective-permute-start.8 = (bf16[256,768]{1,0:T(8,128)(2,1)S(1)}, bf16[256,768]{1,0:T(8,128)(2,1)S(1)}, u32[]{:S(2)}, u32[]{:S(2)}) collective-permute-start(bf16[256,768]{1,0:T(8,128)(2,1)S(1)} %broadcast_select_fusion.6.refs_8_), channel_id=1, source_target_pairs={{0,4},{4,0},{8,12},{12,8},{16,20},{20,16},{24,28},{28,24},{1,5},{5... | collective-permute-start | bytes 1179656 | tf_op jit(solution)/shard_map/ppermute | solution.py:288
  73.7 14.7 %collective-permute-start.17 = (bf16[256,768]{1,0:T(8,128)(2,1)S(1)}, bf16[256,768]{1,0:T(8,128)(2,1)S(1)}, u32[]{:S(2)}, u32[]{:S(2)}) collective-permute-start(bf16[256,768]{1,0:T(8,128)(2,1)S(1)} %broadcast_select_fusion.4.refs_4_), channel_id=1, source_target_pairs={{0,4},{4,0},{8,12},{12,8},{16,20},{20,16},{24,28},{28,24},{1,5},{5... | collective-permute-start | bytes 1179656 | tf_op jit(solution)/shard_map/ppermute | solution.py:288
  80.5 8.0 %collective-permute-start.20 = (bf16[256,768]{1,0:T(8,128)(2,1)S(1)}, bf16[256,768]{1,0:T(8,128)(2,1)S(1)}, u32[]{:S(2)}, u32[]{:S(2)}) collective-permute-start(bf16[256,768]{1,0:T(8,128)(2,1)S(1)} %broadcast_select_fusion.3.own), channel_id=1, source_target_pairs={{0,4},{4,0},{8,12},{12,8},{16,20},{20,16},{24,28},{28,24},{1,5},{5... | collective-permute-start | bytes 1179656 | tf_op jit(solution)/shard_map/ppermute | solution.py:288
  80.6 17.7 %collective-permute-start.39 = (bf16[256,768]{1,0:T(8,128)(2,1)S(1)}, bf16[256,768]{1,0:T(8,128)(2,1)S(1)}, u32[]{:S(2)}, u32[]{:S(2)}) collective-permute-start(bf16[256,768]{1,0:T(8,128)(2,1)S(1)} %broadcast_select_fusion.refs_0_), channel_id=1, source_target_pairs={{0,4},{4,0},{8,12},{12,8},{16,20},{20,16},{24,28},{28,24},{1,5},{5... | collective-permute-start | bytes 1179656 | tf_op jit(solution)/shard_map/ppermute | solution.py:288
  87.8 8.0 %collective-permute-start.12 = (bf16[256,768]{1,0:T(8,128)(2,1)S(1)}, bf16[256,768]{1,0:T(8,128)(2,1)S(1)}, u32[]{:S(2)}, u32[]{:S(2)}) collective-permute-start(bf16[256,768]{1,0:T(8,128)(2,1)S(1)} %broadcast_select_fusion.5.own), channel_id=1, source_target_pairs={{0,4},{4,0},{8,12},{12,8},{16,20},{20,16},{24,28},{28,24},{1,5},{5... | collective-permute-start | bytes 1179656 | tf_op jit(solution)/shard_map/ppermute | solution.py:288
  87.9 13.8 %collective-permute-start.28 = (bf16[256,768]{1,0:T(8,128)(2,1)S(1)}, bf16[256,768]{1,0:T(8,128)(2,1)S(1)}, u32[]{:S(2)}, u32[]{:S(2)}) collective-permute-start(bf16[256,768]{1,0:T(8,128)(2,1)S(1)} %bitcast.18), channel_id=1, source_target_pairs={{0,4},{4,0},{8,12},{12,8},{16,20},{20,16},{24,28},{28,24},{1,5},{5... | collective-permute-start | bytes 1179656 | tf_op jit(solution)/shard_map/ppermute | solution.py:288
  88.4 11.1 %collective-permute-start.33 = (bf16[256,768]{1,0:T(8,128)(2,1)S(1)}, bf16[256,768]{1,0:T(8,128)(2,1)S(1)}, u32[]{:S(2)}, u32[]{:S(2)}) collective-permute-start(bf16[256,768]{1,0:T(8,128)(2,1)S(1)} %broadcast_select_fusion.1.refs_0_), channel_id=1, source_target_pairs={{0,4},{4,0},{8,12},{12,8},{16,20},{20,16},{24,28},{28,24},{1,5},{5... | collective-permute-start | bytes 1179656 | tf_op jit(solution)/shard_map/ppermute | solution.py:288
  88.5 13.8 %collective-permute-start.24 = (bf16[256,768]{1,0:T(8,128)(2,1)S(1)}, bf16[256,768]{1,0:T(8,128)(2,1)S(1)}, u32[]{:S(2)}, u32[]{:S(2)}) collective-permute-start(bf16[256,768]{1,0:T(8,128)(2,1)S(1)} %broadcast_select_fusion.2.refs_0_), channel_id=1, source_target_pairs={{0,4},{4,0},{8,12},{12,8},{16,20},{20,16},{24,28},{28,24},{1,5},{5... | collective-permute-start | bytes 1179656 | tf_op jit(solution)/shard_map/ppermute | solution.py:288
  96.7 8.0 %collective-permute-start.43 = (bf16[144,256]{1,0:T(8,128)(2,1)S(1)}, bf16[144,256]{1,0:T(8,128)(2,1)S(1)}, u32[]{:S(2)}, u32[]{:S(2)}) collective-permute-start(bf16[144,256]{1,0:T(8,128)(2,1)S(1)} %get-tuple-element.58), channel_id=1, source_target_pairs={{0,1},{1,0},{2,3},{3,2},{4,5},{5,4},{6,7},{7,6},{8,9},{9,8},{10,11... | collective-permute-start | bytes 221192 | tf_op jit(solution)/shard_map/ppermute | solution.py:291
  98.9 15.3 %collective-permute-start.40 = (bf16[144,512]{1,0:T(8,128)(2,1)S(1)}, bf16[144,512]{1,0:T(8,128)(2,1)S(1)}, u32[]{:S(2)}, u32[]{:S(2)}) collective-permute-start(bf16[144,512]{1,0:T(8,128)(2,1)S(1)} %get-tuple-element.54), channel_id=1, source_target_pairs={{0,1},{1,0},{2,3},{3,2},{4,5},{5,4},{6,7},{7,6},{8,9},{9,8},{10,11... | collective-permute-start | bytes 442376 | tf_op jit(solution)/shard_map/ppermute | solution.py:291
  99.5 5.8 %collective-permute-start.44 = (bf16[144,256]{1,0:T(8,128)(2,1)S(1)}, bf16[144,256]{1,0:T(8,128)(2,1)S(1)}, u32[]{:S(2)}, u32[]{:S(2)}) collective-permute-start(bf16[144,256]{1,0:T(8,128)(2,1)S(1)} %get-tuple-element.59), channel_id=1, source_target_pairs={{0,2},{1,3},{2,0},{3,1},{4,6},{5,7},{6,4},{7,5},{8,10},{9,11},{10,... | collective-permute-start | bytes 221192 | tf_op jit(solution)/shard_map/ppermute | solution.py:291
  101.7 14.4 %collective-permute-start.41 = (bf16[144,512]{1,0:T(8,128)(2,1)S(1)}, bf16[144,512]{1,0:T(8,128)(2,1)S(1)}, u32[]{:S(2)}, u32[]{:S(2)}) collective-permute-start(bf16[144,512]{1,0:T(8,128)(2,1)S(1)} %get-tuple-element.55), channel_id=1, source_target_pairs={{0,2},{1,3},{2,0},{3,1},{4,6},{5,7},{6,4},{7,5},{8,10},{9,11},{10,... | collective-permute-start | bytes 442376 | tf_op jit(solution)/shard_map/ppermute | solution.py:291
  102.3 14.7 %collective-permute-start.42 = (bf16[144,512]{1,0:T(8,128)(2,1)S(1)}, bf16[144,512]{1,0:T(8,128)(2,1)S(1)}, u32[]{:S(2)}, u32[]{:S(2)}) collective-permute-start(bf16[144,512]{1,0:T(8,128)(2,1)S(1)} %get-tuple-element.56), channel_id=1, source_target_pairs={{0,3},{1,2},{2,1},{3,0},{4,7},{5,6},{6,5},{7,4},{8,11},{9,10},{10,... | collective-permute-start | bytes 442376 | tf_op jit(solution)/shard_map/ppermute | solution.py:291
  104.8 13.0 %collective-permute-start.34 = (bf16[144,512]{1,0:T(8,128)(2,1)S(1)}, bf16[144,512]{1,0:T(8,128)(2,1)S(1)}, u32[]{:S(2)}, u32[]{:S(2)}) collective-permute-start(bf16[144,512]{1,0:T(8,128)(2,1)S(1)} %get-tuple-element.50), channel_id=1, source_target_pairs={{0,1},{1,0},{2,3},{3,2},{4,5},{5,4},{6,7},{7,6},{8,9},{9,8},{10,11... | collective-permute-start | bytes 442376 | tf_op jit(solution)/shard_map/ppermute | solution.py:291
  105.3 8.2 %collective-permute-start.45 = (bf16[144,256]{1,0:T(8,128)(2,1)S(1)}, bf16[144,256]{1,0:T(8,128)(2,1)S(1)}, u32[]{:S(2)}, u32[]{:S(2)}) collective-permute-start(bf16[144,256]{1,0:T(8,128)(2,1)S(1)} %get-tuple-element.60), channel_id=1, source_target_pairs={{0,3},{1,2},{2,1},{3,0},{4,7},{5,6},{6,5},{7,4},{8,11},{9,10},{10,... | collective-permute-start | bytes 221192 | tf_op jit(solution)/shard_map/ppermute | solution.py:291
  113.5 10.1 %collective-permute-start.35 = (bf16[144,512]{1,0:T(8,128)(2,1)S(1)}, bf16[144,512]{1,0:T(8,128)(2,1)S(1)}, u32[]{:S(2)}, u32[]{:S(2)}) collective-permute-start(bf16[144,512]{1,0:T(8,128)(2,1)S(1)} %get-tuple-element.51), channel_id=1, source_target_pairs={{0,2},{1,3},{2,0},{3,1},{4,6},{5,7},{6,4},{7,5},{8,10},{9,11},{10,... | collective-permute-start | bytes 442376 | tf_op jit(solution)/shard_map/ppermute | solution.py:291
  114.2 10.8 %collective-permute-start.36 = (bf16[144,512]{1,0:T(8,128)(2,1)S(1)}, bf16[144,512]{1,0:T(8,128)(2,1)S(1)}, u32[]{:S(2)}, u32[]{:S(2)}) collective-permute-start(bf16[144,512]{1,0:T(8,128)(2,1)S(1)} %get-tuple-element.52), channel_id=1, source_target_pairs={{0,3},{1,2},{2,1},{3,0},{4,7},{5,6},{6,5},{7,4},{8,11},{9,10},{10,... | collective-permute-start | bytes 442376 | tf_op jit(solution)/shard_map/ppermute | solution.py:291
  116.2 10.1 %collective-permute-start.29 = (bf16[144,512]{1,0:T(8,128)(2,1)S(1)}, bf16[144,512]{1,0:T(8,128)(2,1)S(1)}, u32[]{:S(2)}, u32[]{:S(2)}) collective-permute-start(bf16[144,512]{1,0:T(8,128)(2,1)S(1)} %get-tuple-element.46), channel_id=1, source_target_pairs={{0,1},{1,0},{2,3},{3,2},{4,5},{5,4},{6,7},{7,6},{8,9},{9,8},{10,11... | collective-permute-start | bytes 442376 | tf_op jit(solution)/shard_map/ppermute | solution.py:291
  117.0 11.9 %collective-permute-start.30 = (bf16[144,512]{1,0:T(8,128)(2,1)S(1)}, bf16[144,512]{1,0:T(8,128)(2,1)S(1)}, u32[]{:S(2)}, u32[]{:S(2)}) collective-permute-start(bf16[144,512]{1,0:T(8,128)(2,1)S(1)} %get-tuple-element.47), channel_id=1, source_target_pairs={{0,2},{1,3},{2,0},{3,1},{4,6},{5,7},{6,4},{7,5},{8,10},{9,11},{10,... | collective-permute-start | bytes 442376 | tf_op jit(solution)/shard_map/ppermute | solution.py:291
  117.7 11.1 %collective-permute-start.31 = (bf16[144,512]{1,0:T(8,128)(2,1)S(1)}, bf16[144,512]{1,0:T(8,128)(2,1)S(1)}, u32[]{:S(2)}, u32[]{:S(2)}) collective-permute-start(bf16[144,512]{1,0:T(8,128)(2,1)S(1)} %get-tuple-element.48), channel_id=1, source_target_pairs={{0,3},{1,2},{2,1},{3,0},{4,7},{5,6},{6,5},{7,4},{8,11},{9,10},{10,... | collective-permute-start | bytes 442376 | tf_op jit(solution)/shard_map/ppermute | solution.py:291
  123.5 6.6 %collective-permute-start.25 = (bf16[144,256]{1,0:T(8,128)(2,1)S(1)}, bf16[144,256]{1,0:T(8,128)(2,1)S(1)}, u32[]{:S(2)}, u32[]{:S(2)}) collective-permute-start(bf16[144,256]{1,0:T(8,128)(2,1)S(1)} %get-tuple-element.42), channel_id=1, source_target_pairs={{0,1},{1,0},{2,3},{3,2},{4,5},{5,4},{6,7},{7,6},{8,9},{9,8},{10,11... | collective-permute-start | bytes 221192 | tf_op jit(solution)/shard_map/ppermute | solution.py:291
  125.0 5.2 %collective-permute-start.26 = (bf16[144,256]{1,0:T(8,128)(2,1)S(1)}, bf16[144,256]{1,0:T(8,128)(2,1)S(1)}, u32[]{:S(2)}, u32[]{:S(2)}) collective-permute-start(bf16[144,256]{1,0:T(8,128)(2,1)S(1)} %get-tuple-element.43), channel_id=1, source_target_pairs={{0,2},{1,3},{2,0},{3,1},{4,6},{5,7},{6,4},{7,5},{8,10},{9,11},{10,... | collective-permute-start | bytes 221192 | tf_op jit(solution)/shard_map/ppermute | solution.py:291
  126.2 5.3 %collective-permute-start.27 = (bf16[144,256]{1,0:T(8,128)(2,1)S(1)}, bf16[144,256]{1,0:T(8,128)(2,1)S(1)}, u32[]{:S(2)}, u32[]{:S(2)}) collective-permute-start(bf16[144,256]{1,0:T(8,128)(2,1)S(1)} %get-tuple-element.44), channel_id=1, source_target_pairs={{0,3},{1,2},{2,1},{3,0},{4,7},{5,6},{6,5},{7,4},{8,11},{9,10},{10,... | collective-permute-start | bytes 221192 | tf_op jit(solution)/shard_map/ppermute | solution.py:291
  (11 other events, 123.2 us)

commit v5 on v4

--- a/solution.py
+++ b/solution.py
@@ -139,16 +139,16 @@
         value = tok_ref[:, pl.ds(pl.multiple_of(s * part, part), part)]
         tokf[:, place * part : (place + 1) * part] = value
         tokp[:, place * part : (place + 1) * part] = value.astype(BF16)
+    started = []
     for m in range(experts):
         select = jnp.where(slot == rank[m : m + 1, :], 1.0, 0.0).astype(BF16)
         block = jnp.dot(select, tokp[...], preferred_element_type=F32).astype(BF16)
-        if m == 0:
-            local[...] = block
-            local_copy = pltpu.make_async_copy(local, outs[0], sems.at[3])
-            local_copy.start()
-        else:
-            outs[m][...] = block
-    local_copy.wait()
+        local[m] = block
+        copy = pltpu.make_async_copy(local.at[m], outs[m], sems.at[3 + m])
+        copy.start()
+        started.append(copy)
+    for copy in started:
+        copy.wait()
 
 
 def copies(pairs, sems):
@@ -239,18 +239,21 @@
     part = width // (2 * CHAIN)
     total = total + square[:, 0:1]
     scale = lax.rsqrt(total * (1.0 / width) + 1e-06)
+    count = out.shape[0]
+    rows = count // ROW_BLOCKS
     started = []
-    for place, s in enumerate(slice_order()):
-        lo = place * part
-        if place < places[0]:
-            value = mixed[:, lo : lo + part]
-        else:
-            value = late[:, lo - places[0] * part :][:, :part]
-        at = pl.ds(pl.multiple_of(s * part, part), part)
-        out[:, lo : lo + part] = value * scale * gain[:, at]
-        copy = pltpu.make_async_copy(
-            out.at[:, pl.ds(lo, part)], out_hbm.at[:, at], sems.at[place]
-        )
+    for i in range(ROW_BLOCKS):
+        here = slice(i * rows, (i + 1) * rows)
+        for place, s in enumerate(slice_order()):
+            lo = place * part
+            if place < places[0]:
+                value = mixed[here, lo : lo + part]
+            else:
+                value = late[here, lo - places[0] * part :][:, :part]
+            at = pl.ds(pl.multiple_of(s * part, part), part)
+            out[here, at] = value * scale[here] * gain[:, at]
+        block = pl.ds(i * rows, rows)
+        copy = pltpu.make_async_copy(out.at[block, :], out_hbm.at[block, :], sems.at[i])
         copy.start()
         started.append(copy)
     for copy in started:
@@ -268,6 +271,7 @@
 INWARD = [(0, 1), (3, 2)]
 OUTWARD = [(1, 0), (2, 3)]
 CHUNKS = [(2 * s, 2 * s + 1) for s in range(CHAIN - 1)] + [(2 * CHAIN - 2,), (2 * CHAIN - 1,)]
+ROW_BLOCKS = 8
 LATE = 1
 
 
@@ -308,8 +312,7 @@
 
     *placed, mix, sorted_tokens = call(
         functools.partial(place_kernel, experts, capacity),
-        [pltpu.HBM((capacity, width), BF16)]
-        + [jax.ShapeDtypeStruct((capacity, width), BF16)] * (experts - 1)
+        [pltpu.HBM((capacity, width), BF16)] * experts
         + [jax.ShapeDtypeStruct((2 * count, slots), BF16)]
         + [jax.ShapeDtypeStruct((count, width), F32)],
         tuple(stay(x) for x in (expert_ids.T, combine_weights.T, tokens)),
@@ -319,12 +322,12 @@
             pltpu.VMEM((2, count), jnp.int32),
             pltpu.VMEM((2, count), F32),
             pltpu.VMEM((count, width), F32),
-            pltpu.VMEM((capacity, width), BF16),
-            pltpu.SemaphoreType.DMA((4,)),
+            pltpu.VMEM((experts, capacity, width), BF16),
+            pltpu.SemaphoreType.DMA((3 + experts,)),
         ],
         flops=2 * slots * count * width,
         moved=count * width * 4 + slots * width * 2,
-        outs=[HBM] + [VMEM] * (experts + 1),
+        outs=[HBM] * experts + [VMEM] * 2,
         grant=10,
     )
     rows = [placed[0]] + [across(placed[m], m) for m in range(1, experts)]

time: 134 us -> 134 us (level)
  waiting for transfers between devices: 57 us -> 58.5 us
    ppermute x16, waiting for transfers between devices: 39.5 us -> 43 us  [along(): return lax.ppermute(x, 'replica', devices)]
    ppermute x18, waiting for transfers between devices: 17.5 us -> 15.4 us  [across(): return lax.ppermute(x, 'expert', [(e, e ^ m) for e in range(experts)])]
where the time goes in v5:
time: 134 us; the launch traced here: 133 us
  waiting for transfers between devices  58.5 us (44%)
  starting transfers between devices  54.7 us (41%)
  Pallas kernels  16.4 us (12%)
  other arithmetic  2.33 us (2%)
    ppermute x16, waiting for transfers between devices, along(): return lax.ppermute(x, 'replica', devices)  43 us
    ppermute x16, starting transfers between devices, along(): return lax.ppermute(x, 'replica', devices)  27.9 us
    ppermute x18, starting transfers between devices, across(): return lax.ppermute(x, 'expert', [(e, e ^ m) for e in range(experts)])  24.4 us
    pallas_call x13, Pallas kernels, call(): pl.pallas_call(kernel, out_shape=out_shape, in_specs=list(specs), out_spe...  16.4 us
    ppermute x18, waiting for transfers between devices, across(): return lax.ppermute(x, 'expert', [(e, e ^ m) for e in range(experts)])  15.4 us
  transfers between devices with their start and end apart: 46, of which 13 were waited for; matrix products, arithmetic and copies ran while one was open for 2% of the time, Pallas kernels for 11%

profile of v5, /device:TPU:0, one launch (start us, length us, event | category | flops | bytes accessed | tf_op | source)
XLA Modules:
  0.0 133.3 jit_solution(9144349299068797317)
XLA Ops:
  0.0 1.4 %collective-permute-start.6 = (bf16[256,768]{1,0:T(8,128)(2,1)}, bf16[256,768]{1,0:T(8,128)(2,1)}, u32[]{:S(2)}, u32[]{:S(2)}) collective-permute-start(bf16[256,768]{1,0:T(8,128)(2,1)} %bitcast.11), channel_id=1, source_target_pairs={{8,16},{12,20},{16,8},{20,12},{9,17},{13,21},{17,9},{21,13},{10,18... | collective-permute-start | bytes 1179656 | tf_op jit(solution)/shard_map/ppermute | solution.py:289
  1.4 5.2 %collective-permute-start.4 = (bf16[256,768]{1,0:T(8,128)(2,1)}, bf16[256,768]{1,0:T(8,128)(2,1)S(1)}, u32[]{:S(2)}, u32[]{:S(2)}) collective-permute-start(bf16[256,768]{1,0:T(8,128)(2,1)} %bitcast.12), channel_id=1, source_target_pairs={{0,8},{4,12},{8,0},{12,4},{16,24},{20,28},{24,16},{28,20},{1,9},{5... | collective-permute-start | bytes 1179656 | tf_op jit(solution)/shard_map/ppermute | solution.py:289
  7.3 2.3 %collective-permute-start.9 = (bf16[256,768]{1,0:T(8,128)(2,1)}, bf16[256,768]{1,0:T(8,128)(2,1)S(1)}, u32[]{:S(2)}, u32[]{:S(2)}) collective-permute-start(bf16[256,768]{1,0:T(8,128)(2,1)} %bitcast.7), channel_id=1, source_target_pairs={{0,8},{4,12},{8,0},{12,4},{16,24},{20,28},{24,16},{28,20},{1,9},{5... | collective-permute-start | bytes 1179656 | tf_op jit(solution)/shard_map/ppermute | solution.py:289
  9.6 7.2 %collective-permute-done.4.refs_6_ = bf16[256,768]{1,0:T(8,128)(2,1)S(1)} collective-permute-done((bf16[256,768]{1,0:T(8,128)(2,1)}, bf16[256,768]{1,0:T(8,128)(2,1)S(1)}, u32[]{:S(2)}, u32[]{:S(2)}) %collective-permute-start.4) | collective-permute-done | bytes 393248 | tf_op jit(solution)/shard_map/ppermute | solution.py:289
  16.8 1.4 %collective-permute-start.37 = (bf16[256,768]{1,0:T(8,128)(2,1)}, bf16[256,768]{1,0:T(8,128)(2,1)}, u32[]{:S(2)}, u32[]{:S(2)}) collective-permute-start(bf16[256,768]{1,0:T(8,128)(2,1)} %bitcast.15), channel_id=1, source_target_pairs={{8,16},{12,20},{16,8},{20,12},{9,17},{13,21},{17,9},{21,13},{10,18... | collective-permute-start | bytes 1179656 | tf_op jit(solution)/shard_map/ppermute | solution.py:289
  18.9 5.6 %collective-permute-start.21 = (bf16[256,768]{1,0:T(8,128)(2,1)}, bf16[256,768]{1,0:T(8,128)(2,1)}, u32[]{:S(2)}, u32[]{:S(2)}) collective-permute-start(bf16[256,768]{1,0:T(8,128)(2,1)} %bitcast.16), channel_id=1, source_target_pairs={{0,8},{4,12},{24,16},{28,20},{1,9},{5,13},{25,17},{29,21},{2,10},{... | collective-permute-start | bytes 1179656 | tf_op jit(solution)/shard_map/ppermute | solution.py:289
  24.6 1.3 collective-permute-start.32
  25.9 3.3 %shard_map.73 = (bf16[144,2048]{1,0:T(8,128)(2,1)}, bf16[144,2048]{1,0:T(8,128)(2,1)}, bf16[144,2048]{1,0:T(8,128)(2,1)}, bf16[144,2048]{1,0:T(8,128)(2,1)}, bf1...) custom-call(s32[2,192]{1,0:T(2,128)} %bitcast.20, f32[2,192]{1,0:T(2,128)} %bitcast.21, f32[192,2048]{1,0:T(8,128)} %tok_hbm.1), custom_call_target="tpu_custom_call" | custom-call | flops 452984832 | bytes 3932160 | tf_op jit(solution)/shard_map/pallas_call | solution.py:83
  29.2 1.6 %collective-permute-start = (bf16[144,2048]{1,0:T(8,128)(2,1)}, bf16[144,2048]{1,0:T(8,128)(2,1)S(1)}, u32[]{:S(2)}, u32[]{:S(2)}) collective-permute-start(bf16[144,2048]{1,0:T(8,128)(2,1)} %get-tuple-element.36), channel_id=1, source_target_pairs={{0,1},{1,0},{2,3},{3,2},{4,5},{5,4},{6,7},{7,6},{8,9},{9,8},{10,11... | collective-permute-start | bytes 1769480 | tf_op jit(solution)/shard_map/ppermute | solution.py:295
  30.8 1.3 collective-permute-start.7
  32.1 1.6 %collective-permute-start.1 = (bf16[144,2048]{1,0:T(8,128)(2,1)}, bf16[144,2048]{1,0:T(8,128)(2,1)}, u32[]{:S(2)}, u32[]{:S(2)}) collective-permute-start(bf16[144,2048]{1,0:T(8,128)(2,1)} %get-tuple-element.37), channel_id=1, source_target_pairs={{0,2},{1,3},{2,0},{3,1},{4,6},{5,7},{6,4},{7,5},{8,10},{9,11},{10,... | collective-permute-start | bytes 1769480 | tf_op jit(solution)/shard_map/ppermute | solution.py:295
  33.7 0.8 collective-permute-start.18
  34.5 4.2 %collective-permute-done.32 = bf16[256,768]{1,0:T(8,128)(2,1)} collective-permute-done((bf16[256,768]{1,0:T(8,128)(2,1)}, bf16[256,768]{1,0:T(8,128)(2,1)}, u32[]{:S(2)}, u32[]{:S(2)}) %collective-permute-start.32) | collective-permute-done | bytes 393248 | tf_op jit(solution)/shard_map/ppermute | solution.py:289
  38.8 1.3 collective-permute-start.16
  40.1 1.1 broadcast_select_fusion.1.refs_0_
  41.1 3.2 %collective-permute-done.refs_1_ = bf16[144,2048]{1,0:T(8,128)(2,1)S(1)} collective-permute-done((bf16[144,2048]{1,0:T(8,128)(2,1)}, bf16[144,2048]{1,0:T(8,128)(2,1)S(1)}, u32[]{:S(2)}, u32[]{:S(2)}) %collective-permute-start) | collective-permute-done | bytes 589856 | tf_op jit(solution)/shard_map/ppermute | solution.py:295
  45.0 2.2 %collective-permute-done.7 = bf16[256,768]{1,0:T(8,128)(2,1)} collective-permute-done((bf16[256,768]{1,0:T(8,128)(2,1)}, bf16[256,768]{1,0:T(8,128)(2,1)}, u32[]{:S(2)}, u32[]{:S(2)}) %collective-permute-start.7) | collective-permute-done | bytes 393248 | tf_op jit(solution)/shard_map/ppermute | solution.py:289
  47.2 1.3 collective-permute-start.38
  48.5 1.1 broadcast_select_fusion.6.refs_8_
  49.6 2.5 %collective-permute-start.2 = (bf16[144,2048]{1,0:T(8,128)(2,1)S(1)}, bf16[144,2048]{1,0:T(8,128)(2,1)S(1)}, u32[]{:S(2)}, u32[]{:S(2)}) collective-permute-start(bf16[144,2048]{1,0:T(8,128)(2,1)S(1)} %copy-done.11), channel_id=1, source_target_pairs={{0,3},{1,2},{2,1},{3,0},{4,7},{5,6},{6,5},{7,4},{8,11},{9,10},{10,... | collective-permute-start | bytes 1769480 | tf_op jit(solution)/shard_map/ppermute | solution.py:295
  52.8 2.8 %collective-permute-done.16 = bf16[256,768]{1,0:T(8,128)(2,1)S(1)} collective-permute-done((bf16[256,768]{1,0:T(8,128)(2,1)}, bf16[256,768]{1,0:T(8,128)(2,1)S(1)}, u32[]{:S(2)}, u32[]{:S(2)}) %collective-permute-start.16) | collective-permute-done | bytes 393248 | tf_op jit(solution)/shard_map/ppermute | solution.py:289
  55.5 1.3 collective-permute-start.19
  57.0 7.0 %collective-permute-done.38 = bf16[256,768]{1,0:T(8,128)(2,1)S(1)} collective-permute-done((bf16[256,768]{1,0:T(8,128)(2,1)}, bf16[256,768]{1,0:T(8,128)(2,1)S(1)}, u32[]{:S(2)}, u32[]{:S(2)}) %collective-permute-start.38) | collective-permute-done | bytes 393248 | tf_op jit(solution)/shard_map/ppermute | solution.py:289
  63.9 1.3 collective-permute-start.11
  65.4 6.9 %collective-permute-done.19 = bf16[256,768]{1,0:T(8,128)(2,1)S(1)} collective-permute-done((bf16[256,768]{1,0:T(8,128)(2,1)S(1)}, bf16[256,768]{1,0:T(8,128)(2,1)S(1)}, u32[]{:S(2)}, u32[]{:S(2)}) %collective-permute-start.19) | collective-permute-done | bytes 393248 | tf_op jit(solution)/shard_map/ppermute | solution.py:289
  72.4 1.5 %collective-permute-start.23 = (bf16[256,768]{1,0:T(8,128)(2,1)S(1)}, bf16[256,768]{1,0:T(8,128)(2,1)S(1)}, u32[]{:S(2)}, u32[]{:S(2)}) collective-permute-start(bf16[256,768]{1,0:T(8,128)(2,1)S(1)} %collective-permute-done.22), channel_id=1, source_target_pairs={{8,0},{12,4},{16,24},{20,28},{9,1},{13,5},{17,25},{21,29},{10,2},{... | collective-permute-start | bytes 1179656 | tf_op jit(solution)/shard_map/ppermute | solution.py:289
  74.5 6.3 %collective-permute-done.11 = bf16[256,768]{1,0:T(8,128)(2,1)S(1)} collective-permute-done((bf16[256,768]{1,0:T(8,128)(2,1)S(1)}, bf16[256,768]{1,0:T(8,128)(2,1)S(1)}, u32[]{:S(2)}, u32[]{:S(2)}) %collective-permute-start.11) | collective-permute-done | bytes 393248 | tf_op jit(solution)/shard_map/ppermute | solution.py:289
  81.4 6.4 %collective-permute-done.23 = bf16[256,768]{1,0:T(8,128)(2,1)S(1)} collective-permute-done((bf16[256,768]{1,0:T(8,128)(2,1)S(1)}, bf16[256,768]{1,0:T(8,128)(2,1)S(1)}, u32[]{:S(2)}, u32[]{:S(2)}) %collective-permute-start.23) | collective-permute-done | bytes 393248 | tf_op jit(solution)/shard_map/ppermute | solution.py:289
  89.0 4.1 %shard_map.74 = (f32[576,768]{1,0:T(8,128)S(1)}, bf16[576,2048]{1,0:T(8,128)(2,1)S(1)}) custom-call(bf16[144,2048]{1,0:T(8,128)(2,1)S(1)} %copy-done.8, bf16[144,2048]{1,0:T(8,128)(2,1)S(1)} %collective-permute-done.refs_1_, bf16[144,2048]{1,0:T(8,128)(2,1)} %collective-permute-done.1.refs_2_, bf16[144,2048]{1,0:T(8,128)(2,1)S(1)} %collective-permute-done.2.refs_3_, ...), custom_call_target="tpu_custom_call" | custom-call | flops 1358954496 | bytes 6488064 | tf_op jit(solution)/shard_map/pallas_call | solution.py:83
  93.0 1.5 %shard_map.75.acc = f32[576,768]{1,0:T(8,128)S(1)} custom-call(bf16[576,2048]{1,0:T(8,128)(2,1)S(1)} %get-tuple-element.39.rows, bf16[256,768]{1,0:T(8,128)(2,1)S(1)} %bitcast.9, bf16[256,768]{1,0:T(8,128)(2,1)S(1)} %collective-permute-done.13.refs_1_, bf16[256,768]{1,0:T(8,128)(2,1)S(1)} %collective-permute-done.9.refs_2_, ...), custom_call_target="tpu_custom_call" | custom-call | flops 1358954496 | bytes 6488064 | tf_op jit(solution)/shard_map/pallas_call | solution.py:83
  95.0 0.8 shard_map.77.act
  96.7 1.6 %collective-permute-start.43 = (bf16[144,256]{1,0:T(8,128)(2,1)S(1)}, bf16[144,256]{1,0:T(8,128)(2,1)S(1)}, u32[]{:S(2)}, u32[]{:S(2)}) collective-permute-start(bf16[144,256]{1,0:T(8,128)(2,1)S(1)} %get-tuple-element.58), channel_id=1, source_target_pairs={{0,1},{1,0},{2,3},{3,2},{4,5},{5,4},{6,7},{7,6},{8,9},{9,8},{10,11... | collective-permute-start | bytes 221192 | tf_op jit(solution)/shard_map/ppermute | solution.py:295
  99.5 1.5 %collective-permute-start.44 = (bf16[144,256]{1,0:T(8,128)(2,1)S(1)}, bf16[144,256]{1,0:T(8,128)(2,1)S(1)}, u32[]{:S(2)}, u32[]{:S(2)}) collective-permute-start(bf16[144,256]{1,0:T(8,128)(2,1)S(1)} %get-tuple-element.59), channel_id=1, source_target_pairs={{0,2},{1,3},{2,0},{3,1},{4,6},{5,7},{6,4},{7,5},{8,10},{9,11},{10,... | collective-permute-start | bytes 221192 | tf_op jit(solution)/shard_map/ppermute | solution.py:295
  102.3 2.4 %collective-permute-start.42 = (bf16[144,512]{1,0:T(8,128)(2,1)S(1)}, bf16[144,512]{1,0:T(8,128)(2,1)S(1)}, u32[]{:S(2)}, u32[]{:S(2)}) collective-permute-start(bf16[144,512]{1,0:T(8,128)(2,1)S(1)} %get-tuple-element.56), channel_id=1, source_target_pairs={{0,3},{1,2},{2,1},{3,0},{4,7},{5,6},{6,5},{7,4},{8,11},{9,10},{10,... | collective-permute-start | bytes 442376 | tf_op jit(solution)/shard_map/ppermute | solution.py:295
  105.3 1.8 %collective-permute-start.45 = (bf16[144,256]{1,0:T(8,128)(2,1)S(1)}, bf16[144,256]{1,0:T(8,128)(2,1)S(1)}, u32[]{:S(2)}, u32[]{:S(2)}) collective-permute-start(bf16[144,256]{1,0:T(8,128)(2,1)S(1)} %get-tuple-element.60), channel_id=1, source_target_pairs={{0,3},{1,2},{2,1},{3,0},{4,7},{5,6},{6,5},{7,4},{8,11},{9,10},{10,... | collective-permute-start | bytes 221192 | tf_op jit(solution)/shard_map/ppermute | solution.py:295
  107.8 5.7 %collective-permute-done.45.refs_15_ = bf16[144,256]{1,0:T(8,128)(2,1)S(1)} collective-permute-done((bf16[144,256]{1,0:T(8,128)(2,1)S(1)}, bf16[144,256]{1,0:T(8,128)(2,1)S(1)}, u32[]{:S(2)}, u32[]{:S(2)}) %collective-permute-start.45) | collective-permute-done | bytes 73760 | tf_op jit(solution)/shard_map/ppermute | solution.py:295
  114.2 1.9 %collective-permute-start.36 = (bf16[144,512]{1,0:T(8,128)(2,1)S(1)}, bf16[144,512]{1,0:T(8,128)(2,1)S(1)}, u32[]{:S(2)}, u32[]{:S(2)}) collective-permute-start(bf16[144,512]{1,0:T(8,128)(2,1)S(1)} %get-tuple-element.52), channel_id=1, source_target_pairs={{0,3},{1,2},{2,1},{3,0},{4,7},{5,6},{6,5},{7,4},{8,11},{9,10},{10,... | collective-permute-start | bytes 442376 | tf_op jit(solution)/shard_map/ppermute | solution.py:295
  116.1 0.8 collective-permute-start.29
  116.9 0.8 collective-permute-start.30
  117.7 1.9 %collective-permute-start.31 = (bf16[144,512]{1,0:T(8,128)(2,1)S(1)}, bf16[144,512]{1,0:T(8,128)(2,1)S(1)}, u32[]{:S(2)}, u32[]{:S(2)}) collective-permute-start(bf16[144,512]{1,0:T(8,128)(2,1)S(1)} %get-tuple-element.48), channel_id=1, source_target_pairs={{0,3},{1,2},{2,1},{3,0},{4,7},{5,6},{6,5},{7,4},{8,11},{9,10},{10,... | collective-permute-start | bytes 442376 | tf_op jit(solution)/shard_map/ppermute | solution.py:295
  120.1 3.4 %collective-permute-done.35.refs_6_ = bf16[144,512]{1,0:T(8,128)(2,1)S(1)} collective-permute-done((bf16[144,512]{1,0:T(8,128)(2,1)S(1)}, bf16[144,512]{1,0:T(8,128)(2,1)S(1)}, u32[]{:S(2)}, u32[]{:S(2)}) %collective-permute-start.35) | collective-permute-done | bytes 147488 | tf_op jit(solution)/shard_map/ppermute | solution.py:295
  123.5 1.5 %collective-permute-start.25 = (bf16[144,256]{1,0:T(8,128)(2,1)S(1)}, bf16[144,256]{1,0:T(8,128)(2,1)S(1)}, u32[]{:S(2)}, u32[]{:S(2)}) collective-permute-start(bf16[144,256]{1,0:T(8,128)(2,1)S(1)} %get-tuple-element.42), channel_id=1, source_target_pairs={{0,1},{1,0},{2,3},{3,2},{4,5},{5,4},{6,7},{7,6},{8,9},{9,8},{10,11... | collective-permute-start | bytes 221192 | tf_op jit(solution)/shard_map/ppermute | solution.py:295
  125.0 1.2 collective-permute-start.26
  126.2 0.8 collective-permute-start.27
  127.0 1.8 %collective-permute-done.30.refs_2_ = bf16[144,512]{1,0:T(8,128)(2,1)S(1)} collective-permute-done((bf16[144,512]{1,0:T(8,128)(2,1)S(1)}, bf16[144,512]{1,0:T(8,128)(2,1)S(1)}, u32[]{:S(2)}, u32[]{:S(2)}) %collective-permute-start.30) | collective-permute-done | bytes 147488 | tf_op jit(solution)/shard_map/ppermute | solution.py:295
  128.8 1.3 shard_map.84
  130.2 1.3 collective-permute-done.27.refs_3_
  131.5 1.7 %shard_map.85 = f32[192,2048]{1,0:T(8,128)} custom-call(bf16[144,256]{1,0:T(8,128)(2,1)S(1)} %get-tuple-element.41.refs_0_, bf16[144,256]{1,0:T(8,128)(2,1)S(1)} %collective-permute-done.25.refs_1_, bf16[144,256]{1,0:T(8,128)(2,1)S(1)} %collective-permute-done.26.refs_2_, bf16[144,256]{1,0:T(8,128)(2,1)S(1)} %collective-permute-done.27.refs_3_, ...), custom_call_target="tpu_custom_call" | custom-call | flops 113246208 | bytes 3145728 | tf_op jit(solution)/shard_map/pallas_call | solution.py:83
  (88 shorter events, 11.6 us)
Async XLA Ops:
  0.0 9.6 %collective-permute-start.6 = (bf16[256,768]{1,0:T(8,128)(2,1)}, bf16[256,768]{1,0:T(8,128)(2,1)}, u32[]{:S(2)}, u32[]{:S(2)}) collective-permute-start(bf16[256,768]{1,0:T(8,128)(2,1)} %bitcast.11), channel_id=1, source_target_pairs={{8,16},{12,20},{16,8},{20,12},{9,17},{13,21},{17,9},{21,13},{10,18... | collective-permute-start | bytes 1179656 | tf_op jit(solution)/shard_map/ppermute | solution.py:289
  1.4 15.4 %collective-permute-start.4 = (bf16[256,768]{1,0:T(8,128)(2,1)}, bf16[256,768]{1,0:T(8,128)(2,1)S(1)}, u32[]{:S(2)}, u32[]{:S(2)}) collective-permute-start(bf16[256,768]{1,0:T(8,128)(2,1)} %bitcast.12), channel_id=1, source_target_pairs={{0,8},{4,12},{8,0},{12,4},{16,24},{20,28},{24,16},{28,20},{1,9},{5... | collective-permute-start | bytes 1179656 | tf_op jit(solution)/shard_map/ppermute | solution.py:289
  6.6 11.6 %collective-permute-start.3 = (bf16[256,768]{1,0:T(8,128)(2,1)}, bf16[256,768]{1,0:T(8,128)(2,1)S(1)}, u32[]{:S(2)}, u32[]{:S(2)}) collective-permute-start(bf16[256,768]{1,0:T(8,128)(2,1)} %bitcast.13), channel_id=1, source_target_pairs={{0,4},{4,0},{8,12},{12,8},{16,20},{20,16},{24,28},{28,24},{1,5},{5... | collective-permute-start | bytes 1179656 | tf_op jit(solution)/shard_map/ppermute | solution.py:292
  6.6 18.0 %collective-permute-start.15 = (bf16[256,768]{1,0:T(8,128)(2,1)}, bf16[256,768]{1,0:T(8,128)(2,1)S(1)}, u32[]{:S(2)}, u32[]{:S(2)}) collective-permute-start(bf16[256,768]{1,0:T(8,128)(2,1)} %bitcast.6), channel_id=1, source_target_pairs={{8,16},{12,20},{16,8},{20,12},{9,17},{13,21},{17,9},{21,13},{10,18... | collective-permute-start | bytes 1179656 | tf_op jit(solution)/shard_map/ppermute | solution.py:289
  7.3 21.9 %collective-permute-start.9 = (bf16[256,768]{1,0:T(8,128)(2,1)}, bf16[256,768]{1,0:T(8,128)(2,1)S(1)}, u32[]{:S(2)}, u32[]{:S(2)}) collective-permute-start(bf16[256,768]{1,0:T(8,128)(2,1)} %bitcast.7), channel_id=1, source_target_pairs={{0,8},{4,12},{8,0},{12,4},{16,24},{20,28},{24,16},{28,20},{1,9},{5... | collective-permute-start | bytes 1179656 | tf_op jit(solution)/shard_map/ppermute | solution.py:289
  9.6 21.2 %collective-permute-start.13 = (bf16[256,768]{1,0:T(8,128)(2,1)}, bf16[256,768]{1,0:T(8,128)(2,1)S(1)}, u32[]{:S(2)}, u32[]{:S(2)}) collective-permute-start(bf16[256,768]{1,0:T(8,128)(2,1)} %bitcast.8), channel_id=1, source_target_pairs={{0,4},{4,0},{8,12},{12,8},{16,20},{20,16},{24,28},{28,24},{1,5},{5... | collective-permute-start | bytes 1179656 | tf_op jit(solution)/shard_map/ppermute | solution.py:292
  16.8 15.3 %collective-permute-start.37 = (bf16[256,768]{1,0:T(8,128)(2,1)}, bf16[256,768]{1,0:T(8,128)(2,1)}, u32[]{:S(2)}, u32[]{:S(2)}) collective-permute-start(bf16[256,768]{1,0:T(8,128)(2,1)} %bitcast.15), channel_id=1, source_target_pairs={{8,16},{12,20},{16,8},{20,12},{9,17},{13,21},{17,9},{21,13},{10,18... | collective-permute-start | bytes 1179656 | tf_op jit(solution)/shard_map/ppermute | solution.py:289
  18.9 14.8 %collective-permute-start.21 = (bf16[256,768]{1,0:T(8,128)(2,1)}, bf16[256,768]{1,0:T(8,128)(2,1)}, u32[]{:S(2)}, u32[]{:S(2)}) collective-permute-start(bf16[256,768]{1,0:T(8,128)(2,1)} %bitcast.16), channel_id=1, source_target_pairs={{0,8},{4,12},{24,16},{28,20},{1,9},{5,13},{25,17},{29,21},{2,10},{... | collective-permute-start | bytes 1179656 | tf_op jit(solution)/shard_map/ppermute | solution.py:289
  24.6 14.2 %collective-permute-start.32 = (bf16[256,768]{1,0:T(8,128)(2,1)}, bf16[256,768]{1,0:T(8,128)(2,1)}, u32[]{:S(2)}, u32[]{:S(2)}) collective-permute-start(bf16[256,768]{1,0:T(8,128)(2,1)} %bitcast.17), channel_id=1, source_target_pairs={{8,0},{12,4},{16,24},{20,28},{9,1},{13,5},{17,25},{21,29},{10,2},{... | collective-permute-start | bytes 1179656 | tf_op jit(solution)/shard_map/ppermute | solution.py:289
  29.2 15.0 %collective-permute-start = (bf16[144,2048]{1,0:T(8,128)(2,1)}, bf16[144,2048]{1,0:T(8,128)(2,1)S(1)}, u32[]{:S(2)}, u32[]{:S(2)}) collective-permute-start(bf16[144,2048]{1,0:T(8,128)(2,1)} %get-tuple-element.36), channel_id=1, source_target_pairs={{0,1},{1,0},{2,3},{3,2},{4,5},{5,4},{6,7},{7,6},{8,9},{9,8},{10,11... | collective-permute-start | bytes 1769480 | tf_op jit(solution)/shard_map/ppermute | solution.py:295
  30.8 16.4 %collective-permute-start.7 = (bf16[256,768]{1,0:T(8,128)(2,1)}, bf16[256,768]{1,0:T(8,128)(2,1)}, u32[]{:S(2)}, u32[]{:S(2)}) collective-permute-start(bf16[256,768]{1,0:T(8,128)(2,1)} %collective-permute-done.6), channel_id=1, source_target_pairs={{8,0},{12,4},{16,24},{20,28},{9,1},{13,5},{17,25},{21,29},{10,2},{... | collective-permute-start | bytes 1179656 | tf_op jit(solution)/shard_map/ppermute | solution.py:289
  32.1 17.4 %collective-permute-start.1 = (bf16[144,2048]{1,0:T(8,128)(2,1)}, bf16[144,2048]{1,0:T(8,128)(2,1)}, u32[]{:S(2)}, u32[]{:S(2)}) collective-permute-start(bf16[144,2048]{1,0:T(8,128)(2,1)} %get-tuple-element.37), channel_id=1, source_target_pairs={{0,2},{1,3},{2,0},{3,1},{4,6},{5,7},{6,4},{7,5},{8,10},{9,11},{10,... | collective-permute-start | bytes 1769480 | tf_op jit(solution)/shard_map/ppermute | solution.py:295
  33.7 18.4 %collective-permute-start.18 = (bf16[256,768]{1,0:T(8,128)(2,1)}, bf16[256,768]{1,0:T(8,128)(2,1)S(1)}, u32[]{:S(2)}, u32[]{:S(2)}) collective-permute-start(bf16[256,768]{1,0:T(8,128)(2,1)} %copy-done.4), channel_id=1, source_target_pairs={{8,16},{12,20},{16,8},{20,12},{9,17},{13,21},{17,9},{21,13},{10,18... | collective-permute-start | bytes 1179656 | tf_op jit(solution)/shard_map/ppermute | solution.py:289
  38.8 16.7 %collective-permute-start.16 = (bf16[256,768]{1,0:T(8,128)(2,1)}, bf16[256,768]{1,0:T(8,128)(2,1)S(1)}, u32[]{:S(2)}, u32[]{:S(2)}) collective-permute-start(bf16[256,768]{1,0:T(8,128)(2,1)} %copy-done.9), channel_id=1, source_target_pairs={{8,0},{12,4},{16,24},{20,28},{9,1},{13,5},{17,25},{21,29},{10,2},{... | collective-permute-start | bytes 1179656 | tf_op jit(solution)/shard_map/ppermute | solution.py:289
  44.3 12.6 %collective-permute-start.10 = (bf16[256,768]{1,0:T(8,128)(2,1)S(1)}, bf16[256,768]{1,0:T(8,128)(2,1)S(1)}, u32[]{:S(2)}, u32[]{:S(2)}) collective-permute-start(bf16[256,768]{1,0:T(8,128)(2,1)S(1)} %collective-permute-done.9.refs_2_), channel_id=1, source_target_pairs={{8,16},{12,20},{16,8},{20,12},{9,17},{13,21},{17,9},{21,13},{10,18... | collective-permute-start | bytes 1179656 | tf_op jit(solution)/shard_map/ppermute | solution.py:289
  47.2 16.7 %collective-permute-start.38 = (bf16[256,768]{1,0:T(8,128)(2,1)}, bf16[256,768]{1,0:T(8,128)(2,1)S(1)}, u32[]{:S(2)}, u32[]{:S(2)}) collective-permute-start(bf16[256,768]{1,0:T(8,128)(2,1)} %collective-permute-done.37), channel_id=1, source_target_pairs={{8,0},{12,4},{16,24},{20,28},{9,1},{13,5},{17,25},{21,29},{10,2},{... | collective-permute-start | bytes 1179656 | tf_op jit(solution)/shard_map/ppermute | solution.py:289
  49.6 24.3 %collective-permute-start.2 = (bf16[144,2048]{1,0:T(8,128)(2,1)S(1)}, bf16[144,2048]{1,0:T(8,128)(2,1)S(1)}, u32[]{:S(2)}, u32[]{:S(2)}) collective-permute-start(bf16[144,2048]{1,0:T(8,128)(2,1)S(1)} %copy-done.11), channel_id=1, source_target_pairs={{0,3},{1,2},{2,1},{3,0},{4,7},{5,6},{6,5},{7,4},{8,11},{9,10},{10,... | collective-permute-start | bytes 1769480 | tf_op jit(solution)/shard_map/ppermute | solution.py:295
  52.1 13.3 %collective-permute-start.22 = (bf16[256,768]{1,0:T(8,128)(2,1)}, bf16[256,768]{1,0:T(8,128)(2,1)S(1)}, u32[]{:S(2)}, u32[]{:S(2)}) collective-permute-start(bf16[256,768]{1,0:T(8,128)(2,1)} %collective-permute-done.21), channel_id=1, source_target_pairs={{8,16},{12,20},{16,8},{20,12},{9,17},{13,21},{17,9},{21,13},{10,18... | collective-permute-start | bytes 1179656 | tf_op jit(solution)/shard_map/ppermute | solution.py:289
  55.5 16.9 %collective-permute-start.19 = (bf16[256,768]{1,0:T(8,128)(2,1)S(1)}, bf16[256,768]{1,0:T(8,128)(2,1)S(1)}, u32[]{:S(2)}, u32[]{:S(2)}) collective-permute-start(bf16[256,768]{1,0:T(8,128)(2,1)S(1)} %collective-permute-done.18), channel_id=1, source_target_pairs={{8,0},{12,4},{16,24},{20,28},{9,1},{13,5},{17,25},{21,29},{10,2},{... | collective-permute-start | bytes 1179656 | tf_op jit(solution)/shard_map/ppermute | solution.py:289
  56.9 17.1 %collective-permute-start.5 = (bf16[256,768]{1,0:T(8,128)(2,1)S(1)}, bf16[256,768]{1,0:T(8,128)(2,1)S(1)}, u32[]{:S(2)}, u32[]{:S(2)}) collective-permute-start(bf16[256,768]{1,0:T(8,128)(2,1)S(1)} %copy-done.5), channel_id=1, source_target_pairs={{0,4},{4,0},{8,12},{12,8},{16,20},{20,16},{24,28},{28,24},{1,5},{5... | collective-permute-start | bytes 1179656 | tf_op jit(solution)/shard_map/ppermute | solution.py:292
  63.9 16.9 %collective-permute-start.11 = (bf16[256,768]{1,0:T(8,128)(2,1)S(1)}, bf16[256,768]{1,0:T(8,128)(2,1)S(1)}, u32[]{:S(2)}, u32[]{:S(2)}) collective-permute-start(bf16[256,768]{1,0:T(8,128)(2,1)S(1)} %collective-permute-done.10), channel_id=1, source_target_pairs={{8,0},{12,4},{16,24},{20,28},{9,1},{13,5},{17,25},{21,29},{10,2},{... | collective-permute-start | bytes 1179656 | tf_op jit(solution)/shard_map/ppermute | solution.py:289
  65.3 23.6 %copy-start.2 = (bf16[1,256,768]{2,1,0:T(8,128)(2,1)S(1)}, bf16[1,256,768]{2,1,0:T(8,128)(2,1)}, u32[]{:S(2)}) copy-start(bf16[1,256,768]{2,1,0:T(8,128)(2,1)} %param.10) | copy-start | bytes 1179652
  65.3 23.6 %copy-start.7 = (bf16[256,768]{1,0:T(8,128)(2,1)S(1)}, bf16[256,768]{1,0:T(8,128)(2,1)}, u32[]{:S(2)}) copy-start(bf16[256,768]{1,0:T(8,128)(2,1)} %copy-done.6) | copy-start | bytes 1179652
  65.4 15.5 %collective-permute-start.14 = (bf16[256,768]{1,0:T(8,128)(2,1)S(1)}, bf16[256,768]{1,0:T(8,128)(2,1)S(1)}, u32[]{:S(2)}, u32[]{:S(2)}) collective-permute-start(bf16[256,768]{1,0:T(8,128)(2,1)S(1)} %collective-permute-done.9.refs_2_), channel_id=1, source_target_pairs={{0,4},{4,0},{8,12},{12,8},{16,20},{20,16},{24,28},{28,24},{1,5},{5... | collective-permute-start | bytes 1179656 | tf_op jit(solution)/shard_map/ppermute | solution.py:292
  72.4 15.4 %collective-permute-start.23 = (bf16[256,768]{1,0:T(8,128)(2,1)S(1)}, bf16[256,768]{1,0:T(8,128)(2,1)S(1)}, u32[]{:S(2)}, u32[]{:S(2)}) collective-permute-start(bf16[256,768]{1,0:T(8,128)(2,1)S(1)} %collective-permute-done.22), channel_id=1, source_target_pairs={{8,0},{12,4},{16,24},{20,28},{9,1},{13,5},{17,25},{21,29},{10,2},{... | collective-permute-start | bytes 1179656 | tf_op jit(solution)/shard_map/ppermute | solution.py:289
  73.9 13.9 %collective-permute-start.8 = (bf16[256,768]{1,0:T(8,128)(2,1)S(1)}, bf16[256,768]{1,0:T(8,128)(2,1)S(1)}, u32[]{:S(2)}, u32[]{:S(2)}) collective-permute-start(bf16[256,768]{1,0:T(8,128)(2,1)S(1)} %broadcast_select_fusion.6.refs_8_), channel_id=1, source_target_pairs={{0,4},{4,0},{8,12},{12,8},{16,20},{20,16},{24,28},{28,24},{1,5},{5... | collective-permute-start | bytes 1179656 | tf_op jit(solution)/shard_map/ppermute | solution.py:292
  74.0 14.4 %collective-permute-start.17 = (bf16[256,768]{1,0:T(8,128)(2,1)S(1)}, bf16[256,768]{1,0:T(8,128)(2,1)S(1)}, u32[]{:S(2)}, u32[]{:S(2)}) collective-permute-start(bf16[256,768]{1,0:T(8,128)(2,1)S(1)} %broadcast_select_fusion.4.refs_4_), channel_id=1, source_target_pairs={{0,4},{4,0},{8,12},{12,8},{16,20},{20,16},{24,28},{28,24},{1,5},{5... | collective-permute-start | bytes 1179656 | tf_op jit(solution)/shard_map/ppermute | solution.py:292
  80.8 7.7 %collective-permute-start.20 = (bf16[256,768]{1,0:T(8,128)(2,1)S(1)}, bf16[256,768]{1,0:T(8,128)(2,1)S(1)}, u32[]{:S(2)}, u32[]{:S(2)}) collective-permute-start(bf16[256,768]{1,0:T(8,128)(2,1)S(1)} %broadcast_select_fusion.3.own), channel_id=1, source_target_pairs={{0,4},{4,0},{8,12},{12,8},{16,20},{20,16},{24,28},{28,24},{1,5},{5... | collective-permute-start | bytes 1179656 | tf_op jit(solution)/shard_map/ppermute | solution.py:292
  80.9 17.4 %collective-permute-start.39 = (bf16[256,768]{1,0:T(8,128)(2,1)S(1)}, bf16[256,768]{1,0:T(8,128)(2,1)S(1)}, u32[]{:S(2)}, u32[]{:S(2)}) collective-permute-start(bf16[256,768]{1,0:T(8,128)(2,1)S(1)} %broadcast_select_fusion.refs_0_), channel_id=1, source_target_pairs={{0,4},{4,0},{8,12},{12,8},{16,20},{20,16},{24,28},{28,24},{1,5},{5... | collective-permute-start | bytes 1179656 | tf_op jit(solution)/shard_map/ppermute | solution.py:292
  87.8 8.0 %collective-permute-start.12 = (bf16[256,768]{1,0:T(8,128)(2,1)S(1)}, bf16[256,768]{1,0:T(8,128)(2,1)S(1)}, u32[]{:S(2)}, u32[]{:S(2)}) collective-permute-start(bf16[256,768]{1,0:T(8,128)(2,1)S(1)} %broadcast_select_fusion.5.own), channel_id=1, source_target_pairs={{0,4},{4,0},{8,12},{12,8},{16,20},{20,16},{24,28},{28,24},{1,5},{5... | collective-permute-start | bytes 1179656 | tf_op jit(solution)/shard_map/ppermute | solution.py:292
  87.8 13.8 %collective-permute-start.28 = (bf16[256,768]{1,0:T(8,128)(2,1)S(1)}, bf16[256,768]{1,0:T(8,128)(2,1)S(1)}, u32[]{:S(2)}, u32[]{:S(2)}) collective-permute-start(bf16[256,768]{1,0:T(8,128)(2,1)S(1)} %bitcast.18), channel_id=1, source_target_pairs={{0,4},{4,0},{8,12},{12,8},{16,20},{20,16},{24,28},{28,24},{1,5},{5... | collective-permute-start | bytes 1179656 | tf_op jit(solution)/shard_map/ppermute | solution.py:292
  88.4 11.1 %collective-permute-start.33 = (bf16[256,768]{1,0:T(8,128)(2,1)S(1)}, bf16[256,768]{1,0:T(8,128)(2,1)S(1)}, u32[]{:S(2)}, u32[]{:S(2)}) collective-permute-start(bf16[256,768]{1,0:T(8,128)(2,1)S(1)} %broadcast_select_fusion.1.refs_0_), channel_id=1, source_target_pairs={{0,4},{4,0},{8,12},{12,8},{16,20},{20,16},{24,28},{28,24},{1,5},{5... | collective-permute-start | bytes 1179656 | tf_op jit(solution)/shard_map/ppermute | solution.py:292
  88.5 13.8 %collective-permute-start.24 = (bf16[256,768]{1,0:T(8,128)(2,1)S(1)}, bf16[256,768]{1,0:T(8,128)(2,1)S(1)}, u32[]{:S(2)}, u32[]{:S(2)}) collective-permute-start(bf16[256,768]{1,0:T(8,128)(2,1)S(1)} %broadcast_select_fusion.2.refs_0_), channel_id=1, source_target_pairs={{0,4},{4,0},{8,12},{12,8},{16,20},{20,16},{24,28},{28,24},{1,5},{5... | collective-permute-start | bytes 1179656 | tf_op jit(solution)/shard_map/ppermute | solution.py:292
  96.7 8.0 %collective-permute-start.43 = (bf16[144,256]{1,0:T(8,128)(2,1)S(1)}, bf16[144,256]{1,0:T(8,128)(2,1)S(1)}, u32[]{:S(2)}, u32[]{:S(2)}) collective-permute-start(bf16[144,256]{1,0:T(8,128)(2,1)S(1)} %get-tuple-element.58), channel_id=1, source_target_pairs={{0,1},{1,0},{2,3},{3,2},{4,5},{5,4},{6,7},{7,6},{8,9},{9,8},{10,11... | collective-permute-start | bytes 221192 | tf_op jit(solution)/shard_map/ppermute | solution.py:295
  98.9 15.3 %collective-permute-start.40 = (bf16[144,512]{1,0:T(8,128)(2,1)S(1)}, bf16[144,512]{1,0:T(8,128)(2,1)S(1)}, u32[]{:S(2)}, u32[]{:S(2)}) collective-permute-start(bf16[144,512]{1,0:T(8,128)(2,1)S(1)} %get-tuple-element.54), channel_id=1, source_target_pairs={{0,1},{1,0},{2,3},{3,2},{4,5},{5,4},{6,7},{7,6},{8,9},{9,8},{10,11... | collective-permute-start | bytes 442376 | tf_op jit(solution)/shard_map/ppermute | solution.py:295
  99.5 5.7 %collective-permute-start.44 = (bf16[144,256]{1,0:T(8,128)(2,1)S(1)}, bf16[144,256]{1,0:T(8,128)(2,1)S(1)}, u32[]{:S(2)}, u32[]{:S(2)}) collective-permute-start(bf16[144,256]{1,0:T(8,128)(2,1)S(1)} %get-tuple-element.59), channel_id=1, source_target_pairs={{0,2},{1,3},{2,0},{3,1},{4,6},{5,7},{6,4},{7,5},{8,10},{9,11},{10,... | collective-permute-start | bytes 221192 | tf_op jit(solution)/shard_map/ppermute | solution.py:295
  101.7 14.4 %collective-permute-start.41 = (bf16[144,512]{1,0:T(8,128)(2,1)S(1)}, bf16[144,512]{1,0:T(8,128)(2,1)S(1)}, u32[]{:S(2)}, u32[]{:S(2)}) collective-permute-start(bf16[144,512]{1,0:T(8,128)(2,1)S(1)} %get-tuple-element.55), channel_id=1, source_target_pairs={{0,2},{1,3},{2,0},{3,1},{4,6},{5,7},{6,4},{7,5},{8,10},{9,11},{10,... | collective-permute-start | bytes 442376 | tf_op jit(solution)/shard_map/ppermute | solution.py:295
  102.3 14.7 %collective-permute-start.42 = (bf16[144,512]{1,0:T(8,128)(2,1)S(1)}, bf16[144,512]{1,0:T(8,128)(2,1)S(1)}, u32[]{:S(2)}, u32[]{:S(2)}) collective-permute-start(bf16[144,512]{1,0:T(8,128)(2,1)S(1)} %get-tuple-element.56), channel_id=1, source_target_pairs={{0,3},{1,2},{2,1},{3,0},{4,7},{5,6},{6,5},{7,4},{8,11},{9,10},{10,... | collective-permute-start | bytes 442376 | tf_op jit(solution)/shard_map/ppermute | solution.py:295
  104.7 13.0 %collective-permute-start.34 = (bf16[144,512]{1,0:T(8,128)(2,1)S(1)}, bf16[144,512]{1,0:T(8,128)(2,1)S(1)}, u32[]{:S(2)}, u32[]{:S(2)}) collective-permute-start(bf16[144,512]{1,0:T(8,128)(2,1)S(1)} %get-tuple-element.50), channel_id=1, source_target_pairs={{0,1},{1,0},{2,3},{3,2},{4,5},{5,4},{6,7},{7,6},{8,9},{9,8},{10,11... | collective-permute-start | bytes 442376 | tf_op jit(solution)/shard_map/ppermute | solution.py:295
  105.3 8.2 %collective-permute-start.45 = (bf16[144,256]{1,0:T(8,128)(2,1)S(1)}, bf16[144,256]{1,0:T(8,128)(2,1)S(1)}, u32[]{:S(2)}, u32[]{:S(2)}) collective-permute-start(bf16[144,256]{1,0:T(8,128)(2,1)S(1)} %get-tuple-element.60), channel_id=1, source_target_pairs={{0,3},{1,2},{2,1},{3,0},{4,7},{5,6},{6,5},{7,4},{8,11},{9,10},{10,... | collective-permute-start | bytes 221192 | tf_op jit(solution)/shard_map/ppermute | solution.py:295
  113.4 10.1 %collective-permute-start.35 = (bf16[144,512]{1,0:T(8,128)(2,1)S(1)}, bf16[144,512]{1,0:T(8,128)(2,1)S(1)}, u32[]{:S(2)}, u32[]{:S(2)}) collective-permute-start(bf16[144,512]{1,0:T(8,128)(2,1)S(1)} %get-tuple-element.51), channel_id=1, source_target_pairs={{0,2},{1,3},{2,0},{3,1},{4,6},{5,7},{6,4},{7,5},{8,10},{9,11},{10,... | collective-permute-start | bytes 442376 | tf_op jit(solution)/shard_map/ppermute | solution.py:295
  114.2 10.7 %collective-permute-start.36 = (bf16[144,512]{1,0:T(8,128)(2,1)S(1)}, bf16[144,512]{1,0:T(8,128)(2,1)S(1)}, u32[]{:S(2)}, u32[]{:S(2)}) collective-permute-start(bf16[144,512]{1,0:T(8,128)(2,1)S(1)} %get-tuple-element.52), channel_id=1, source_target_pairs={{0,3},{1,2},{2,1},{3,0},{4,7},{5,6},{6,5},{7,4},{8,11},{9,10},{10,... | collective-permute-start | bytes 442376 | tf_op jit(solution)/shard_map/ppermute | solution.py:295
  116.1 10.1 %collective-permute-start.29 = (bf16[144,512]{1,0:T(8,128)(2,1)S(1)}, bf16[144,512]{1,0:T(8,128)(2,1)S(1)}, u32[]{:S(2)}, u32[]{:S(2)}) collective-permute-start(bf16[144,512]{1,0:T(8,128)(2,1)S(1)} %get-tuple-element.46), channel_id=1, source_target_pairs={{0,1},{1,0},{2,3},{3,2},{4,5},{5,4},{6,7},{7,6},{8,9},{9,8},{10,11... | collective-permute-start | bytes 442376 | tf_op jit(solution)/shard_map/ppermute | solution.py:295
  116.9 11.9 %collective-permute-start.30 = (bf16[144,512]{1,0:T(8,128)(2,1)S(1)}, bf16[144,512]{1,0:T(8,128)(2,1)S(1)}, u32[]{:S(2)}, u32[]{:S(2)}) collective-permute-start(bf16[144,512]{1,0:T(8,128)(2,1)S(1)} %get-tuple-element.47), channel_id=1, source_target_pairs={{0,2},{1,3},{2,0},{3,1},{4,6},{5,7},{6,4},{7,5},{8,10},{9,11},{10,... | collective-permute-start | bytes 442376 | tf_op jit(solution)/shard_map/ppermute | solution.py:295
  117.7 11.1 %collective-permute-start.31 = (bf16[144,512]{1,0:T(8,128)(2,1)S(1)}, bf16[144,512]{1,0:T(8,128)(2,1)S(1)}, u32[]{:S(2)}, u32[]{:S(2)}) collective-permute-start(bf16[144,512]{1,0:T(8,128)(2,1)S(1)} %get-tuple-element.48), channel_id=1, source_target_pairs={{0,3},{1,2},{2,1},{3,0},{4,7},{5,6},{6,5},{7,4},{8,11},{9,10},{10,... | collective-permute-start | bytes 442376 | tf_op jit(solution)/shard_map/ppermute | solution.py:295
  123.5 6.6 %collective-permute-start.25 = (bf16[144,256]{1,0:T(8,128)(2,1)S(1)}, bf16[144,256]{1,0:T(8,128)(2,1)S(1)}, u32[]{:S(2)}, u32[]{:S(2)}) collective-permute-start(bf16[144,256]{1,0:T(8,128)(2,1)S(1)} %get-tuple-element.42), channel_id=1, source_target_pairs={{0,1},{1,0},{2,3},{3,2},{4,5},{5,4},{6,7},{7,6},{8,9},{9,8},{10,11... | collective-permute-start | bytes 221192 | tf_op jit(solution)/shard_map/ppermute | solution.py:295
  125.0 5.2 %collective-permute-start.26 = (bf16[144,256]{1,0:T(8,128)(2,1)S(1)}, bf16[144,256]{1,0:T(8,128)(2,1)S(1)}, u32[]{:S(2)}, u32[]{:S(2)}) collective-permute-start(bf16[144,256]{1,0:T(8,128)(2,1)S(1)} %get-tuple-element.43), channel_id=1, source_target_pairs={{0,2},{1,3},{2,0},{3,1},{4,6},{5,7},{6,4},{7,5},{8,10},{9,11},{10,... | collective-permute-start | bytes 221192 | tf_op jit(solution)/shard_map/ppermute | solution.py:295
  126.2 5.3 %collective-permute-start.27 = (bf16[144,256]{1,0:T(8,128)(2,1)S(1)}, bf16[144,256]{1,0:T(8,128)(2,1)S(1)}, u32[]{:S(2)}, u32[]{:S(2)}) collective-permute-start(bf16[144,256]{1,0:T(8,128)(2,1)S(1)} %get-tuple-element.44), channel_id=1, source_target_pairs={{0,3},{1,2},{2,1},{3,0},{4,7},{5,6},{6,5},{7,4},{8,11},{9,10},{10,... | collective-permute-start | bytes 221192 | tf_op jit(solution)/shard_map/ppermute | solution.py:295
  (10 other events, 126.2 us)

commit v6 on v5

--- a/solution.py
+++ b/solution.py
@@ -211,6 +211,23 @@
         outs[m][...] = result[m * capacity : (m + 1) * capacity]
 
 
+def half_kernel(hidden, weight, out):
+    out[...] = lax.dot_general(
+        hidden[...], weight[...], (((1,), (1,)), ((), ())), preferred_element_type=F32
+    ).astype(BF16)
+
+
+def join_kernel(experts, capacity, hidden, weight, first, *outs):
+    result = lax.dot_general(
+        hidden[...], weight[...], (((1,), (1,)), ((), ())), preferred_element_type=F32
+    ).astype(BF16)
+    part = first.shape[1]
+    for m in range(experts):
+        rows = slice(m * capacity, (m + 1) * capacity)
+        outs[m][:, :part] = first[rows, :]
+        outs[m][:, part:] = result[rows]
+
+
 def mixed_columns(experts, places, blocks, tokens, c_ref, back):
     capacity = blocks[0].shape[0]
     count = tokens.shape[0]
@@ -272,6 +289,7 @@
 OUTWARD = [(1, 0), (2, 3)]
 CHUNKS = [(2 * s, 2 * s + 1) for s in range(CHAIN - 1)] + [(2 * CHAIN - 2,), (2 * CHAIN - 1,)]
 ROW_BLOCKS = 8
+EARLY = (2,)
 LATE = 1
 
 
@@ -377,14 +395,27 @@
     )
 
     backs = []
-    for chunk in CHUNKS:
+    for i, chunk in enumerate(CHUNKS):
         weights = [d_all[p] for p in chunk]
         wide = sum(w.shape[0] for w in weights)
+        kernel, args = functools.partial(down_kernel, experts, capacity), (hidden, *weights)
+        if i in EARLY:
+            own, other = weights
+            half = call(
+                half_kernel,
+                jax.ShapeDtypeStruct((slots, part), BF16),
+                (hidden, own),
+                [VMEM] * 2,
+                flops=2 * slots * ff * part,
+                moved=slots * ff * 2 + 2 * part * ff + slots * part * 2,
+            )
+            kernel = functools.partial(join_kernel, experts, capacity)
+            args = (hidden, other, half)
         outs = call(
-            functools.partial(down_kernel, experts, capacity),
+            kernel,
             [jax.ShapeDtypeStruct((capacity, wide), BF16)] * experts,
-            (hidden, *weights),
-            [VMEM] * (1 + len(weights)),
+            args,
+            [VMEM] * len(args),
             flops=2 * slots * ff * wide,
             moved=slots * ff * 2 + 2 * wide * ff + slots * wide * 2,
         )

time: 134 us -> 134 us (level)
    pallas_call x13 -> x14, Pallas kernels: 16.4 us -> 16.6 us  [call(): pl.pallas_call(kernel, out_shape=out_shape, in_specs=list(specs), out_spe...]
where the time goes in v6:
time: 134 us; the launch traced here: 133 us
  waiting for transfers between devices  58.3 us (44%)
  starting transfers between devices  54.4 us (41%)
  Pallas kernels  16.6 us (12%)
  other arithmetic  2.33 us (2%)
    ppermute x16, waiting for transfers between devices, along(): return lax.ppermute(x, 'replica', devices)  43 us
    ppermute x16, starting transfers between devices, along(): return lax.ppermute(x, 'replica', devices)  27.9 us
    ppermute x18, starting transfers between devices, across(): return lax.ppermute(x, 'expert', [(e, e ^ m) for e in range(experts)])  24.2 us
    pallas_call x14, Pallas kernels, call(): pl.pallas_call(kernel, out_shape=out_shape, in_specs=list(specs), out_spe...  16.6 us
    ppermute x18, waiting for transfers between devices, across(): return lax.ppermute(x, 'expert', [(e, e ^ m) for e in range(experts)])  15.2 us
  transfers between devices with their start and end apart: 46, of which 13 were waited for; matrix products, arithmetic and copies ran while one was open for 2% of the time, Pallas kernels for 11%

profile of v6, /device:TPU:0, one launch (start us, length us, event | category | flops | bytes accessed | tf_op | source)
XLA Modules:
  0.0 133.1 jit_solution(13236581414619250970)
XLA Ops:
  0.0 1.4 %collective-permute-start.6 = (bf16[256,768]{1,0:T(8,128)(2,1)}, bf16[256,768]{1,0:T(8,128)(2,1)}, u32[]{:S(2)}, u32[]{:S(2)}) collective-permute-start(bf16[256,768]{1,0:T(8,128)(2,1)} %bitcast.11), channel_id=1, source_target_pairs={{8,16},{12,20},{16,8},{20,12},{9,17},{13,21},{17,9},{21,13},{10,18... | collective-permute-start | bytes 1179656 | tf_op jit(solution)/shard_map/ppermute | solution.py:307
  1.4 5.2 %collective-permute-start.4 = (bf16[256,768]{1,0:T(8,128)(2,1)}, bf16[256,768]{1,0:T(8,128)(2,1)S(1)}, u32[]{:S(2)}, u32[]{:S(2)}) collective-permute-start(bf16[256,768]{1,0:T(8,128)(2,1)} %bitcast.12), channel_id=1, source_target_pairs={{0,8},{4,12},{8,0},{12,4},{16,24},{20,28},{24,16},{28,20},{1,9},{5... | collective-permute-start | bytes 1179656 | tf_op jit(solution)/shard_map/ppermute | solution.py:307
  7.3 2.3 %collective-permute-start.9 = (bf16[256,768]{1,0:T(8,128)(2,1)}, bf16[256,768]{1,0:T(8,128)(2,1)S(1)}, u32[]{:S(2)}, u32[]{:S(2)}) collective-permute-start(bf16[256,768]{1,0:T(8,128)(2,1)} %bitcast.7), channel_id=1, source_target_pairs={{0,8},{4,12},{8,0},{12,4},{16,24},{20,28},{24,16},{28,20},{1,9},{5... | collective-permute-start | bytes 1179656 | tf_op jit(solution)/shard_map/ppermute | solution.py:307
  9.6 7.2 %collective-permute-done.4.refs_6_ = bf16[256,768]{1,0:T(8,128)(2,1)S(1)} collective-permute-done((bf16[256,768]{1,0:T(8,128)(2,1)}, bf16[256,768]{1,0:T(8,128)(2,1)S(1)}, u32[]{:S(2)}, u32[]{:S(2)}) %collective-permute-start.4) | collective-permute-done | bytes 393248 | tf_op jit(solution)/shard_map/ppermute | solution.py:307
  16.8 1.4 %collective-permute-start.37 = (bf16[256,768]{1,0:T(8,128)(2,1)}, bf16[256,768]{1,0:T(8,128)(2,1)}, u32[]{:S(2)}, u32[]{:S(2)}) collective-permute-start(bf16[256,768]{1,0:T(8,128)(2,1)} %bitcast.15), channel_id=1, source_target_pairs={{8,16},{12,20},{16,8},{20,12},{9,17},{13,21},{17,9},{21,13},{10,18... | collective-permute-start | bytes 1179656 | tf_op jit(solution)/shard_map/ppermute | solution.py:307
  18.9 5.6 %collective-permute-start.21 = (bf16[256,768]{1,0:T(8,128)(2,1)}, bf16[256,768]{1,0:T(8,128)(2,1)}, u32[]{:S(2)}, u32[]{:S(2)}) collective-permute-start(bf16[256,768]{1,0:T(8,128)(2,1)} %bitcast.16), channel_id=1, source_target_pairs={{0,8},{4,12},{24,16},{28,20},{1,9},{5,13},{25,17},{29,21},{2,10},{... | collective-permute-start | bytes 1179656 | tf_op jit(solution)/shard_map/ppermute | solution.py:307
  24.6 1.3 collective-permute-start.32
  25.9 3.3 %shard_map.73 = (bf16[144,2048]{1,0:T(8,128)(2,1)}, bf16[144,2048]{1,0:T(8,128)(2,1)}, bf16[144,2048]{1,0:T(8,128)(2,1)}, bf16[144,2048]{1,0:T(8,128)(2,1)}, bf1...) custom-call(s32[2,192]{1,0:T(2,128)} %bitcast.20, f32[2,192]{1,0:T(2,128)} %bitcast.21, f32[192,2048]{1,0:T(8,128)} %tok_hbm.1), custom_call_target="tpu_custom_call" | custom-call | flops 452984832 | bytes 3932160 | tf_op jit(solution)/shard_map/pallas_call | solution.py:83
  29.2 1.6 %collective-permute-start = (bf16[144,2048]{1,0:T(8,128)(2,1)}, bf16[144,2048]{1,0:T(8,128)(2,1)S(1)}, u32[]{:S(2)}, u32[]{:S(2)}) collective-permute-start(bf16[144,2048]{1,0:T(8,128)(2,1)} %get-tuple-element.36), channel_id=1, source_target_pairs={{0,1},{1,0},{2,3},{3,2},{4,5},{5,4},{6,7},{7,6},{8,9},{9,8},{10,11... | collective-permute-start | bytes 1769480 | tf_op jit(solution)/shard_map/ppermute | solution.py:313
  30.8 1.3 collective-permute-start.7
  32.1 1.6 %collective-permute-start.1 = (bf16[144,2048]{1,0:T(8,128)(2,1)}, bf16[144,2048]{1,0:T(8,128)(2,1)}, u32[]{:S(2)}, u32[]{:S(2)}) collective-permute-start(bf16[144,2048]{1,0:T(8,128)(2,1)} %get-tuple-element.37), channel_id=1, source_target_pairs={{0,2},{1,3},{2,0},{3,1},{4,6},{5,7},{6,4},{7,5},{8,10},{9,11},{10,... | collective-permute-start | bytes 1769480 | tf_op jit(solution)/shard_map/ppermute | solution.py:313
  33.7 0.8 collective-permute-start.18
  34.5 4.2 %collective-permute-done.32 = bf16[256,768]{1,0:T(8,128)(2,1)} collective-permute-done((bf16[256,768]{1,0:T(8,128)(2,1)}, bf16[256,768]{1,0:T(8,128)(2,1)}, u32[]{:S(2)}, u32[]{:S(2)}) %collective-permute-start.32) | collective-permute-done | bytes 393248 | tf_op jit(solution)/shard_map/ppermute | solution.py:307
  38.8 1.3 collective-permute-start.16
  40.1 1.1 broadcast_select_fusion.1.refs_0_
  41.1 3.2 %collective-permute-done.refs_1_ = bf16[144,2048]{1,0:T(8,128)(2,1)S(1)} collective-permute-done((bf16[144,2048]{1,0:T(8,128)(2,1)}, bf16[144,2048]{1,0:T(8,128)(2,1)S(1)}, u32[]{:S(2)}, u32[]{:S(2)}) %collective-permute-start) | collective-permute-done | bytes 589856 | tf_op jit(solution)/shard_map/ppermute | solution.py:313
  45.0 2.2 %collective-permute-done.7 = bf16[256,768]{1,0:T(8,128)(2,1)} collective-permute-done((bf16[256,768]{1,0:T(8,128)(2,1)}, bf16[256,768]{1,0:T(8,128)(2,1)}, u32[]{:S(2)}, u32[]{:S(2)}) %collective-permute-start.7) | collective-permute-done | bytes 393248 | tf_op jit(solution)/shard_map/ppermute | solution.py:307
  47.2 1.3 collective-permute-start.38
  48.5 1.1 broadcast_select_fusion.6.refs_8_
  49.6 2.5 %collective-permute-start.2 = (bf16[144,2048]{1,0:T(8,128)(2,1)S(1)}, bf16[144,2048]{1,0:T(8,128)(2,1)S(1)}, u32[]{:S(2)}, u32[]{:S(2)}) collective-permute-start(bf16[144,2048]{1,0:T(8,128)(2,1)S(1)} %copy-done.11), channel_id=1, source_target_pairs={{0,3},{1,2},{2,1},{3,0},{4,7},{5,6},{6,5},{7,4},{8,11},{9,10},{10,... | collective-permute-start | bytes 1769480 | tf_op jit(solution)/shard_map/ppermute | solution.py:313
  52.8 2.8 %collective-permute-done.16 = bf16[256,768]{1,0:T(8,128)(2,1)S(1)} collective-permute-done((bf16[256,768]{1,0:T(8,128)(2,1)}, bf16[256,768]{1,0:T(8,128)(2,1)S(1)}, u32[]{:S(2)}, u32[]{:S(2)}) %collective-permute-start.16) | collective-permute-done | bytes 393248 | tf_op jit(solution)/shard_map/ppermute | solution.py:307
  55.5 1.3 collective-permute-start.19
  57.0 7.0 %collective-permute-done.38 = bf16[256,768]{1,0:T(8,128)(2,1)S(1)} collective-permute-done((bf16[256,768]{1,0:T(8,128)(2,1)}, bf16[256,768]{1,0:T(8,128)(2,1)S(1)}, u32[]{:S(2)}, u32[]{:S(2)}) %collective-permute-start.38) | collective-permute-done | bytes 393248 | tf_op jit(solution)/shard_map/ppermute | solution.py:307
  63.9 1.3 collective-permute-start.11
  65.4 6.9 %collective-permute-done.19 = bf16[256,768]{1,0:T(8,128)(2,1)S(1)} collective-permute-done((bf16[256,768]{1,0:T(8,128)(2,1)S(1)}, bf16[256,768]{1,0:T(8,128)(2,1)S(1)}, u32[]{:S(2)}, u32[]{:S(2)}) %collective-permute-start.19) | collective-permute-done | bytes 393248 | tf_op jit(solution)/shard_map/ppermute | solution.py:307
  72.4 1.5 %collective-permute-start.23 = (bf16[256,768]{1,0:T(8,128)(2,1)S(1)}, bf16[256,768]{1,0:T(8,128)(2,1)S(1)}, u32[]{:S(2)}, u32[]{:S(2)}) collective-permute-start(bf16[256,768]{1,0:T(8,128)(2,1)S(1)} %collective-permute-done.22), channel_id=1, source_target_pairs={{8,0},{12,4},{16,24},{20,28},{9,1},{13,5},{17,25},{21,29},{10,2},{... | collective-permute-start | bytes 1179656 | tf_op jit(solution)/shard_map/ppermute | solution.py:307
  74.5 6.3 %collective-permute-done.11 = bf16[256,768]{1,0:T(8,128)(2,1)S(1)} collective-permute-done((bf16[256,768]{1,0:T(8,128)(2,1)S(1)}, bf16[256,768]{1,0:T(8,128)(2,1)S(1)}, u32[]{:S(2)}, u32[]{:S(2)}) %collective-permute-start.11) | collective-permute-done | bytes 393248 | tf_op jit(solution)/shard_map/ppermute | solution.py:307
  81.4 6.4 %collective-permute-done.23 = bf16[256,768]{1,0:T(8,128)(2,1)S(1)} collective-permute-done((bf16[256,768]{1,0:T(8,128)(2,1)S(1)}, bf16[256,768]{1,0:T(8,128)(2,1)S(1)}, u32[]{:S(2)}, u32[]{:S(2)}) %collective-permute-start.23) | collective-permute-done | bytes 393248 | tf_op jit(solution)/shard_map/ppermute | solution.py:307
  89.0 4.1 %shard_map.74 = (f32[576,768]{1,0:T(8,128)S(1)}, bf16[576,2048]{1,0:T(8,128)(2,1)S(1)}) custom-call(bf16[144,2048]{1,0:T(8,128)(2,1)S(1)} %copy-done.8, bf16[144,2048]{1,0:T(8,128)(2,1)S(1)} %collective-permute-done.refs_1_, bf16[144,2048]{1,0:T(8,128)(2,1)} %collective-permute-done.1.refs_2_, bf16[144,2048]{1,0:T(8,128)(2,1)S(1)} %collective-permute-done.2.refs_3_, ...), custom_call_target="tpu_custom_call" | custom-call | flops 1358954496 | bytes 6488064 | tf_op jit(solution)/shard_map/pallas_call | solution.py:83
  93.0 1.5 %shard_map.75.acc = f32[576,768]{1,0:T(8,128)S(1)} custom-call(bf16[576,2048]{1,0:T(8,128)(2,1)S(1)} %get-tuple-element.39.rows, bf16[256,768]{1,0:T(8,128)(2,1)S(1)} %bitcast.9, bf16[256,768]{1,0:T(8,128)(2,1)S(1)} %collective-permute-done.13.refs_1_, bf16[256,768]{1,0:T(8,128)(2,1)S(1)} %collective-permute-done.9.refs_2_, ...), custom_call_target="tpu_custom_call" | custom-call | flops 1358954496 | bytes 6488064 | tf_op jit(solution)/shard_map/pallas_call | solution.py:83
  95.0 0.8 shard_map.77.act
  96.7 1.6 %collective-permute-start.43 = (bf16[144,256]{1,0:T(8,128)(2,1)S(1)}, bf16[144,256]{1,0:T(8,128)(2,1)S(1)}, u32[]{:S(2)}, u32[]{:S(2)}) collective-permute-start(bf16[144,256]{1,0:T(8,128)(2,1)S(1)} %get-tuple-element.58), channel_id=1, source_target_pairs={{0,1},{1,0},{2,3},{3,2},{4,5},{5,4},{6,7},{7,6},{8,9},{9,8},{10,11... | collective-permute-start | bytes 221192 | tf_op jit(solution)/shard_map/ppermute | solution.py:313
  99.7 1.5 %collective-permute-start.44 = (bf16[144,256]{1,0:T(8,128)(2,1)S(1)}, bf16[144,256]{1,0:T(8,128)(2,1)S(1)}, u32[]{:S(2)}, u32[]{:S(2)}) collective-permute-start(bf16[144,256]{1,0:T(8,128)(2,1)S(1)} %get-tuple-element.59), channel_id=1, source_target_pairs={{0,2},{1,3},{2,0},{3,1},{4,6},{5,7},{6,4},{7,5},{8,10},{9,11},{10,... | collective-permute-start | bytes 221192 | tf_op jit(solution)/shard_map/ppermute | solution.py:313
  102.5 2.4 %collective-permute-start.42 = (bf16[144,512]{1,0:T(8,128)(2,1)S(1)}, bf16[144,512]{1,0:T(8,128)(2,1)S(1)}, u32[]{:S(2)}, u32[]{:S(2)}) collective-permute-start(bf16[144,512]{1,0:T(8,128)(2,1)S(1)} %get-tuple-element.56), channel_id=1, source_target_pairs={{0,3},{1,2},{2,1},{3,0},{4,7},{5,6},{6,5},{7,4},{8,11},{9,10},{10,... | collective-permute-start | bytes 442376 | tf_op jit(solution)/shard_map/ppermute | solution.py:313
  105.5 1.8 %collective-permute-start.45 = (bf16[144,256]{1,0:T(8,128)(2,1)S(1)}, bf16[144,256]{1,0:T(8,128)(2,1)S(1)}, u32[]{:S(2)}, u32[]{:S(2)}) collective-permute-start(bf16[144,256]{1,0:T(8,128)(2,1)S(1)} %get-tuple-element.60), channel_id=1, source_target_pairs={{0,3},{1,2},{2,1},{3,0},{4,7},{5,6},{6,5},{7,4},{8,11},{9,10},{10,... | collective-permute-start | bytes 221192 | tf_op jit(solution)/shard_map/ppermute | solution.py:313
  108.0 5.7 %collective-permute-done.45.refs_15_ = bf16[144,256]{1,0:T(8,128)(2,1)S(1)} collective-permute-done((bf16[144,256]{1,0:T(8,128)(2,1)S(1)}, bf16[144,256]{1,0:T(8,128)(2,1)S(1)}, u32[]{:S(2)}, u32[]{:S(2)}) %collective-permute-start.45) | collective-permute-done | bytes 73760 | tf_op jit(solution)/shard_map/ppermute | solution.py:313
  114.4 1.7 %collective-permute-start.36 = (bf16[144,512]{1,0:T(8,128)(2,1)S(1)}, bf16[144,512]{1,0:T(8,128)(2,1)S(1)}, u32[]{:S(2)}, u32[]{:S(2)}) collective-permute-start(bf16[144,512]{1,0:T(8,128)(2,1)S(1)} %get-tuple-element.52), channel_id=1, source_target_pairs={{0,3},{1,2},{2,1},{3,0},{4,7},{5,6},{6,5},{7,4},{8,11},{9,10},{10,... | collective-permute-start | bytes 442376 | tf_op jit(solution)/shard_map/ppermute | solution.py:313
  116.1 1.0 collective-permute-start.29
  117.1 0.8 collective-permute-start.30
  117.9 1.7 %collective-permute-start.31 = (bf16[144,512]{1,0:T(8,128)(2,1)S(1)}, bf16[144,512]{1,0:T(8,128)(2,1)S(1)}, u32[]{:S(2)}, u32[]{:S(2)}) collective-permute-start(bf16[144,512]{1,0:T(8,128)(2,1)S(1)} %get-tuple-element.48), channel_id=1, source_target_pairs={{0,3},{1,2},{2,1},{3,0},{4,7},{5,6},{6,5},{7,4},{8,11},{9,10},{10,... | collective-permute-start | bytes 442376 | tf_op jit(solution)/shard_map/ppermute | solution.py:313
  120.1 3.7 %collective-permute-done.35.refs_6_ = bf16[144,512]{1,0:T(8,128)(2,1)S(1)} collective-permute-done((bf16[144,512]{1,0:T(8,128)(2,1)S(1)}, bf16[144,512]{1,0:T(8,128)(2,1)S(1)}, u32[]{:S(2)}, u32[]{:S(2)}) %collective-permute-start.35) | collective-permute-done | bytes 147488 | tf_op jit(solution)/shard_map/ppermute | solution.py:313
  123.7 1.4 %collective-permute-start.25 = (bf16[144,256]{1,0:T(8,128)(2,1)S(1)}, bf16[144,256]{1,0:T(8,128)(2,1)S(1)}, u32[]{:S(2)}, u32[]{:S(2)}) collective-permute-start(bf16[144,256]{1,0:T(8,128)(2,1)S(1)} %get-tuple-element.42), channel_id=1, source_target_pairs={{0,1},{1,0},{2,3},{3,2},{4,5},{5,4},{6,7},{7,6},{8,9},{9,8},{10,11... | collective-permute-start | bytes 221192 | tf_op jit(solution)/shard_map/ppermute | solution.py:313
  125.1 0.9 collective-permute-start.26
  126.0 1.2 collective-permute-start.27
  127.2 1.8 %collective-permute-done.30.refs_2_ = bf16[144,512]{1,0:T(8,128)(2,1)S(1)} collective-permute-done((bf16[144,512]{1,0:T(8,128)(2,1)S(1)}, bf16[144,512]{1,0:T(8,128)(2,1)S(1)}, u32[]{:S(2)}, u32[]{:S(2)}) %collective-permute-start.30) | collective-permute-done | bytes 147488 | tf_op jit(solution)/shard_map/ppermute | solution.py:313
  129.0 1.3 %shard_map.85 = (f32[192,1792]{1,0:T(8,128)S(1)}, f32[192,128]{1,0:T(8,128)S(1)}) custom-call(bf16[144,512]{1,0:T(8,128)(2,1)S(1)} %get-tuple-element.45.refs_0_, bf16[144,512]{1,0:T(8,128)(2,1)S(1)} %collective-permute-done.29.refs_1_, bf16[144,512]{1,0:T(8,128)(2,1)S(1)} %collective-permute-done.30.refs_2_, ...), custom_call_target="tpu_custom_call" | custom-call | flops 792723456 | bytes 4816896 | tf_op jit(solution)/shard_map/pallas_call | solution.py:83
  130.4 0.8 collective-permute-done.27.refs_3_
  131.2 1.7 %shard_map.86 = f32[192,2048]{1,0:T(8,128)} custom-call(bf16[144,256]{1,0:T(8,128)(2,1)S(1)} %get-tuple-element.41.refs_0_, bf16[144,256]{1,0:T(8,128)(2,1)S(1)} %collective-permute-done.25.refs_1_, bf16[144,256]{1,0:T(8,128)(2,1)S(1)} %collective-permute-done.26.refs_2_, bf16[144,256]{1,0:T(8,128)(2,1)S(1)} %collective-permute-done.27.refs_3_, ...), custom_call_target="tpu_custom_call" | custom-call | flops 113246208 | bytes 3145728 | tf_op jit(solution)/shard_map/pallas_call | solution.py:83
  (89 shorter events, 11.8 us)
Async XLA Ops:
  0.0 9.6 %collective-permute-start.6 = (bf16[256,768]{1,0:T(8,128)(2,1)}, bf16[256,768]{1,0:T(8,128)(2,1)}, u32[]{:S(2)}, u32[]{:S(2)}) collective-permute-start(bf16[256,768]{1,0:T(8,128)(2,1)} %bitcast.11), channel_id=1, source_target_pairs={{8,16},{12,20},{16,8},{20,12},{9,17},{13,21},{17,9},{21,13},{10,18... | collective-permute-start | bytes 1179656 | tf_op jit(solution)/shard_map/ppermute | solution.py:307
  1.4 15.4 %collective-permute-start.4 = (bf16[256,768]{1,0:T(8,128)(2,1)}, bf16[256,768]{1,0:T(8,128)(2,1)S(1)}, u32[]{:S(2)}, u32[]{:S(2)}) collective-permute-start(bf16[256,768]{1,0:T(8,128)(2,1)} %bitcast.12), channel_id=1, source_target_pairs={{0,8},{4,12},{8,0},{12,4},{16,24},{20,28},{24,16},{28,20},{1,9},{5... | collective-permute-start | bytes 1179656 | tf_op jit(solution)/shard_map/ppermute | solution.py:307
  6.6 11.6 %collective-permute-start.3 = (bf16[256,768]{1,0:T(8,128)(2,1)}, bf16[256,768]{1,0:T(8,128)(2,1)S(1)}, u32[]{:S(2)}, u32[]{:S(2)}) collective-permute-start(bf16[256,768]{1,0:T(8,128)(2,1)} %bitcast.13), channel_id=1, source_target_pairs={{0,4},{4,0},{8,12},{12,8},{16,20},{20,16},{24,28},{28,24},{1,5},{5... | collective-permute-start | bytes 1179656 | tf_op jit(solution)/shard_map/ppermute | solution.py:310
  6.6 18.0 %collective-permute-start.15 = (bf16[256,768]{1,0:T(8,128)(2,1)}, bf16[256,768]{1,0:T(8,128)(2,1)S(1)}, u32[]{:S(2)}, u32[]{:S(2)}) collective-permute-start(bf16[256,768]{1,0:T(8,128)(2,1)} %bitcast.6), channel_id=1, source_target_pairs={{8,16},{12,20},{16,8},{20,12},{9,17},{13,21},{17,9},{21,13},{10,18... | collective-permute-start | bytes 1179656 | tf_op jit(solution)/shard_map/ppermute | solution.py:307
  7.3 21.9 %collective-permute-start.9 = (bf16[256,768]{1,0:T(8,128)(2,1)}, bf16[256,768]{1,0:T(8,128)(2,1)S(1)}, u32[]{:S(2)}, u32[]{:S(2)}) collective-permute-start(bf16[256,768]{1,0:T(8,128)(2,1)} %bitcast.7), channel_id=1, source_target_pairs={{0,8},{4,12},{8,0},{12,4},{16,24},{20,28},{24,16},{28,20},{1,9},{5... | collective-permute-start | bytes 1179656 | tf_op jit(solution)/shard_map/ppermute | solution.py:307
  9.6 21.2 %collective-permute-start.13 = (bf16[256,768]{1,0:T(8,128)(2,1)}, bf16[256,768]{1,0:T(8,128)(2,1)S(1)}, u32[]{:S(2)}, u32[]{:S(2)}) collective-permute-start(bf16[256,768]{1,0:T(8,128)(2,1)} %bitcast.8), channel_id=1, source_target_pairs={{0,4},{4,0},{8,12},{12,8},{16,20},{20,16},{24,28},{28,24},{1,5},{5... | collective-permute-start | bytes 1179656 | tf_op jit(solution)/shard_map/ppermute | solution.py:310
  16.8 15.3 %collective-permute-start.37 = (bf16[256,768]{1,0:T(8,128)(2,1)}, bf16[256,768]{1,0:T(8,128)(2,1)}, u32[]{:S(2)}, u32[]{:S(2)}) collective-permute-start(bf16[256,768]{1,0:T(8,128)(2,1)} %bitcast.15), channel_id=1, source_target_pairs={{8,16},{12,20},{16,8},{20,12},{9,17},{13,21},{17,9},{21,13},{10,18... | collective-permute-start | bytes 1179656 | tf_op jit(solution)/shard_map/ppermute | solution.py:307
  18.9 14.8 %collective-permute-start.21 = (bf16[256,768]{1,0:T(8,128)(2,1)}, bf16[256,768]{1,0:T(8,128)(2,1)}, u32[]{:S(2)}, u32[]{:S(2)}) collective-permute-start(bf16[256,768]{1,0:T(8,128)(2,1)} %bitcast.16), channel_id=1, source_target_pairs={{0,8},{4,12},{24,16},{28,20},{1,9},{5,13},{25,17},{29,21},{2,10},{... | collective-permute-start | bytes 1179656 | tf_op jit(solution)/shard_map/ppermute | solution.py:307
  24.6 14.2 %collective-permute-start.32 = (bf16[256,768]{1,0:T(8,128)(2,1)}, bf16[256,768]{1,0:T(8,128)(2,1)}, u32[]{:S(2)}, u32[]{:S(2)}) collective-permute-start(bf16[256,768]{1,0:T(8,128)(2,1)} %bitcast.17), channel_id=1, source_target_pairs={{8,0},{12,4},{16,24},{20,28},{9,1},{13,5},{17,25},{21,29},{10,2},{... | collective-permute-start | bytes 1179656 | tf_op jit(solution)/shard_map/ppermute | solution.py:307
  29.2 15.0 %collective-permute-start = (bf16[144,2048]{1,0:T(8,128)(2,1)}, bf16[144,2048]{1,0:T(8,128)(2,1)S(1)}, u32[]{:S(2)}, u32[]{:S(2)}) collective-permute-start(bf16[144,2048]{1,0:T(8,128)(2,1)} %get-tuple-element.36), channel_id=1, source_target_pairs={{0,1},{1,0},{2,3},{3,2},{4,5},{5,4},{6,7},{7,6},{8,9},{9,8},{10,11... | collective-permute-start | bytes 1769480 | tf_op jit(solution)/shard_map/ppermute | solution.py:313
  30.8 16.4 %collective-permute-start.7 = (bf16[256,768]{1,0:T(8,128)(2,1)}, bf16[256,768]{1,0:T(8,128)(2,1)}, u32[]{:S(2)}, u32[]{:S(2)}) collective-permute-start(bf16[256,768]{1,0:T(8,128)(2,1)} %collective-permute-done.6), channel_id=1, source_target_pairs={{8,0},{12,4},{16,24},{20,28},{9,1},{13,5},{17,25},{21,29},{10,2},{... | collective-permute-start | bytes 1179656 | tf_op jit(solution)/shard_map/ppermute | solution.py:307
  32.1 17.4 %collective-permute-start.1 = (bf16[144,2048]{1,0:T(8,128)(2,1)}, bf16[144,2048]{1,0:T(8,128)(2,1)}, u32[]{:S(2)}, u32[]{:S(2)}) collective-permute-start(bf16[144,2048]{1,0:T(8,128)(2,1)} %get-tuple-element.37), channel_id=1, source_target_pairs={{0,2},{1,3},{2,0},{3,1},{4,6},{5,7},{6,4},{7,5},{8,10},{9,11},{10,... | collective-permute-start | bytes 1769480 | tf_op jit(solution)/shard_map/ppermute | solution.py:313
  33.7 18.4 %collective-permute-start.18 = (bf16[256,768]{1,0:T(8,128)(2,1)}, bf16[256,768]{1,0:T(8,128)(2,1)S(1)}, u32[]{:S(2)}, u32[]{:S(2)}) collective-permute-start(bf16[256,768]{1,0:T(8,128)(2,1)} %copy-done.4), channel_id=1, source_target_pairs={{8,16},{12,20},{16,8},{20,12},{9,17},{13,21},{17,9},{21,13},{10,18... | collective-permute-start | bytes 1179656 | tf_op jit(solution)/shard_map/ppermute | solution.py:307
  38.8 16.7 %collective-permute-start.16 = (bf16[256,768]{1,0:T(8,128)(2,1)}, bf16[256,768]{1,0:T(8,128)(2,1)S(1)}, u32[]{:S(2)}, u32[]{:S(2)}) collective-permute-start(bf16[256,768]{1,0:T(8,128)(2,1)} %copy-done.9), channel_id=1, source_target_pairs={{8,0},{12,4},{16,24},{20,28},{9,1},{13,5},{17,25},{21,29},{10,2},{... | collective-permute-start | bytes 1179656 | tf_op jit(solution)/shard_map/ppermute | solution.py:307
  44.3 12.6 %collective-permute-start.10 = (bf16[256,768]{1,0:T(8,128)(2,1)S(1)}, bf16[256,768]{1,0:T(8,128)(2,1)S(1)}, u32[]{:S(2)}, u32[]{:S(2)}) collective-permute-start(bf16[256,768]{1,0:T(8,128)(2,1)S(1)} %collective-permute-done.9.refs_2_), channel_id=1, source_target_pairs={{8,16},{12,20},{16,8},{20,12},{9,17},{13,21},{17,9},{21,13},{10,18... | collective-permute-start | bytes 1179656 | tf_op jit(solution)/shard_map/ppermute | solution.py:307
  47.2 16.7 %collective-permute-start.38 = (bf16[256,768]{1,0:T(8,128)(2,1)}, bf16[256,768]{1,0:T(8,128)(2,1)S(1)}, u32[]{:S(2)}, u32[]{:S(2)}) collective-permute-start(bf16[256,768]{1,0:T(8,128)(2,1)} %collective-permute-done.37), channel_id=1, source_target_pairs={{8,0},{12,4},{16,24},{20,28},{9,1},{13,5},{17,25},{21,29},{10,2},{... | collective-permute-start | bytes 1179656 | tf_op jit(solution)/shard_map/ppermute | solution.py:307
  49.6 24.3 %collective-permute-start.2 = (bf16[144,2048]{1,0:T(8,128)(2,1)S(1)}, bf16[144,2048]{1,0:T(8,128)(2,1)S(1)}, u32[]{:S(2)}, u32[]{:S(2)}) collective-permute-start(bf16[144,2048]{1,0:T(8,128)(2,1)S(1)} %copy-done.11), channel_id=1, source_target_pairs={{0,3},{1,2},{2,1},{3,0},{4,7},{5,6},{6,5},{7,4},{8,11},{9,10},{10,... | collective-permute-start | bytes 1769480 | tf_op jit(solution)/shard_map/ppermute | solution.py:313
  52.1 13.3 %collective-permute-start.22 = (bf16[256,768]{1,0:T(8,128)(2,1)}, bf16[256,768]{1,0:T(8,128)(2,1)S(1)}, u32[]{:S(2)}, u32[]{:S(2)}) collective-permute-start(bf16[256,768]{1,0:T(8,128)(2,1)} %collective-permute-done.21), channel_id=1, source_target_pairs={{8,16},{12,20},{16,8},{20,12},{9,17},{13,21},{17,9},{21,13},{10,18... | collective-permute-start | bytes 1179656 | tf_op jit(solution)/shard_map/ppermute | solution.py:307
  55.5 16.9 %collective-permute-start.19 = (bf16[256,768]{1,0:T(8,128)(2,1)S(1)}, bf16[256,768]{1,0:T(8,128)(2,1)S(1)}, u32[]{:S(2)}, u32[]{:S(2)}) collective-permute-start(bf16[256,768]{1,0:T(8,128)(2,1)S(1)} %collective-permute-done.18), channel_id=1, source_target_pairs={{8,0},{12,4},{16,24},{20,28},{9,1},{13,5},{17,25},{21,29},{10,2},{... | collective-permute-start | bytes 1179656 | tf_op jit(solution)/shard_map/ppermute | solution.py:307
  56.9 17.1 %collective-permute-start.5 = (bf16[256,768]{1,0:T(8,128)(2,1)S(1)}, bf16[256,768]{1,0:T(8,128)(2,1)S(1)}, u32[]{:S(2)}, u32[]{:S(2)}) collective-permute-start(bf16[256,768]{1,0:T(8,128)(2,1)S(1)} %copy-done.5), channel_id=1, source_target_pairs={{0,4},{4,0},{8,12},{12,8},{16,20},{20,16},{24,28},{28,24},{1,5},{5... | collective-permute-start | bytes 1179656 | tf_op jit(solution)/shard_map/ppermute | solution.py:310
  63.9 16.9 %collective-permute-start.11 = (bf16[256,768]{1,0:T(8,128)(2,1)S(1)}, bf16[256,768]{1,0:T(8,128)(2,1)S(1)}, u32[]{:S(2)}, u32[]{:S(2)}) collective-permute-start(bf16[256,768]{1,0:T(8,128)(2,1)S(1)} %collective-permute-done.10), channel_id=1, source_target_pairs={{8,0},{12,4},{16,24},{20,28},{9,1},{13,5},{17,25},{21,29},{10,2},{... | collective-permute-start | bytes 1179656 | tf_op jit(solution)/shard_map/ppermute | solution.py:307
  65.3 23.6 %copy-start.2 = (bf16[1,256,768]{2,1,0:T(8,128)(2,1)S(1)}, bf16[1,256,768]{2,1,0:T(8,128)(2,1)}, u32[]{:S(2)}) copy-start(bf16[1,256,768]{2,1,0:T(8,128)(2,1)} %param.10) | copy-start | bytes 1179652
  65.3 23.6 %copy-start.7 = (bf16[256,768]{1,0:T(8,128)(2,1)S(1)}, bf16[256,768]{1,0:T(8,128)(2,1)}, u32[]{:S(2)}) copy-start(bf16[256,768]{1,0:T(8,128)(2,1)} %copy-done.6) | copy-start | bytes 1179652
  65.4 15.5 %collective-permute-start.14 = (bf16[256,768]{1,0:T(8,128)(2,1)S(1)}, bf16[256,768]{1,0:T(8,128)(2,1)S(1)}, u32[]{:S(2)}, u32[]{:S(2)}) collective-permute-start(bf16[256,768]{1,0:T(8,128)(2,1)S(1)} %collective-permute-done.9.refs_2_), channel_id=1, source_target_pairs={{0,4},{4,0},{8,12},{12,8},{16,20},{20,16},{24,28},{28,24},{1,5},{5... | collective-permute-start | bytes 1179656 | tf_op jit(solution)/shard_map/ppermute | solution.py:310
  72.4 15.4 %collective-permute-start.23 = (bf16[256,768]{1,0:T(8,128)(2,1)S(1)}, bf16[256,768]{1,0:T(8,128)(2,1)S(1)}, u32[]{:S(2)}, u32[]{:S(2)}) collective-permute-start(bf16[256,768]{1,0:T(8,128)(2,1)S(1)} %collective-permute-done.22), channel_id=1, source_target_pairs={{8,0},{12,4},{16,24},{20,28},{9,1},{13,5},{17,25},{21,29},{10,2},{... | collective-permute-start | bytes 1179656 | tf_op jit(solution)/shard_map/ppermute | solution.py:307
  73.9 13.9 %collective-permute-start.8 = (bf16[256,768]{1,0:T(8,128)(2,1)S(1)}, bf16[256,768]{1,0:T(8,128)(2,1)S(1)}, u32[]{:S(2)}, u32[]{:S(2)}) collective-permute-start(bf16[256,768]{1,0:T(8,128)(2,1)S(1)} %broadcast_select_fusion.6.refs_8_), channel_id=1, source_target_pairs={{0,4},{4,0},{8,12},{12,8},{16,20},{20,16},{24,28},{28,24},{1,5},{5... | collective-permute-start | bytes 1179656 | tf_op jit(solution)/shard_map/ppermute | solution.py:310
  74.0 14.4 %collective-permute-start.17 = (bf16[256,768]{1,0:T(8,128)(2,1)S(1)}, bf16[256,768]{1,0:T(8,128)(2,1)S(1)}, u32[]{:S(2)}, u32[]{:S(2)}) collective-permute-start(bf16[256,768]{1,0:T(8,128)(2,1)S(1)} %broadcast_select_fusion.4.refs_4_), channel_id=1, source_target_pairs={{0,4},{4,0},{8,12},{12,8},{16,20},{20,16},{24,28},{28,24},{1,5},{5... | collective-permute-start | bytes 1179656 | tf_op jit(solution)/shard_map/ppermute | solution.py:310
  80.8 7.7 %collective-permute-start.20 = (bf16[256,768]{1,0:T(8,128)(2,1)S(1)}, bf16[256,768]{1,0:T(8,128)(2,1)S(1)}, u32[]{:S(2)}, u32[]{:S(2)}) collective-permute-start(bf16[256,768]{1,0:T(8,128)(2,1)S(1)} %broadcast_select_fusion.3.own), channel_id=1, source_target_pairs={{0,4},{4,0},{8,12},{12,8},{16,20},{20,16},{24,28},{28,24},{1,5},{5... | collective-permute-start | bytes 1179656 | tf_op jit(solution)/shard_map/ppermute | solution.py:310
  80.9 17.8 %collective-permute-start.39 = (bf16[256,768]{1,0:T(8,128)(2,1)S(1)}, bf16[256,768]{1,0:T(8,128)(2,1)S(1)}, u32[]{:S(2)}, u32[]{:S(2)}) collective-permute-start(bf16[256,768]{1,0:T(8,128)(2,1)S(1)} %broadcast_select_fusion.weight), channel_id=1, source_target_pairs={{0,4},{4,0},{8,12},{12,8},{16,20},{20,16},{24,28},{28,24},{1,5},{5... | collective-permute-start | bytes 1179656 | tf_op jit(solution)/shard_map/ppermute | solution.py:310
  87.8 8.0 %collective-permute-start.12 = (bf16[256,768]{1,0:T(8,128)(2,1)S(1)}, bf16[256,768]{1,0:T(8,128)(2,1)S(1)}, u32[]{:S(2)}, u32[]{:S(2)}) collective-permute-start(bf16[256,768]{1,0:T(8,128)(2,1)S(1)} %broadcast_select_fusion.5.own), channel_id=1, source_target_pairs={{0,4},{4,0},{8,12},{12,8},{16,20},{20,16},{24,28},{28,24},{1,5},{5... | collective-permute-start | bytes 1179656 | tf_op jit(solution)/shard_map/ppermute | solution.py:310
  87.8 14.1 %collective-permute-start.28 = (bf16[256,768]{1,0:T(8,128)(2,1)S(1)}, bf16[256,768]{1,0:T(8,128)(2,1)S(1)}, u32[]{:S(2)}, u32[]{:S(2)}) collective-permute-start(bf16[256,768]{1,0:T(8,128)(2,1)S(1)} %bitcast.18), channel_id=1, source_target_pairs={{0,4},{4,0},{8,12},{12,8},{16,20},{20,16},{24,28},{28,24},{1,5},{5... | collective-permute-start | bytes 1179656 | tf_op jit(solution)/shard_map/ppermute | solution.py:310
  88.4 11.3 %collective-permute-start.33 = (bf16[256,768]{1,0:T(8,128)(2,1)S(1)}, bf16[256,768]{1,0:T(8,128)(2,1)S(1)}, u32[]{:S(2)}, u32[]{:S(2)}) collective-permute-start(bf16[256,768]{1,0:T(8,128)(2,1)S(1)} %broadcast_select_fusion.1.refs_0_), channel_id=1, source_target_pairs={{0,4},{4,0},{8,12},{12,8},{16,20},{20,16},{24,28},{28,24},{1,5},{5... | collective-permute-start | bytes 1179656 | tf_op jit(solution)/shard_map/ppermute | solution.py:310
  88.5 14.0 %collective-permute-start.24 = (bf16[256,768]{1,0:T(8,128)(2,1)S(1)}, bf16[256,768]{1,0:T(8,128)(2,1)S(1)}, u32[]{:S(2)}, u32[]{:S(2)}) collective-permute-start(bf16[256,768]{1,0:T(8,128)(2,1)S(1)} %broadcast_select_fusion.2.refs_0_), channel_id=1, source_target_pairs={{0,4},{4,0},{8,12},{12,8},{16,20},{20,16},{24,28},{28,24},{1,5},{5... | collective-permute-start | bytes 1179656 | tf_op jit(solution)/shard_map/ppermute | solution.py:310
  96.7 8.2 %collective-permute-start.43 = (bf16[144,256]{1,0:T(8,128)(2,1)S(1)}, bf16[144,256]{1,0:T(8,128)(2,1)S(1)}, u32[]{:S(2)}, u32[]{:S(2)}) collective-permute-start(bf16[144,256]{1,0:T(8,128)(2,1)S(1)} %get-tuple-element.58), channel_id=1, source_target_pairs={{0,1},{1,0},{2,3},{3,2},{4,5},{5,4},{6,7},{7,6},{8,9},{9,8},{10,11... | collective-permute-start | bytes 221192 | tf_op jit(solution)/shard_map/ppermute | solution.py:313
  99.1 15.3 %collective-permute-start.40 = (bf16[144,512]{1,0:T(8,128)(2,1)S(1)}, bf16[144,512]{1,0:T(8,128)(2,1)S(1)}, u32[]{:S(2)}, u32[]{:S(2)}) collective-permute-start(bf16[144,512]{1,0:T(8,128)(2,1)S(1)} %get-tuple-element.54), channel_id=1, source_target_pairs={{0,1},{1,0},{2,3},{3,2},{4,5},{5,4},{6,7},{7,6},{8,9},{9,8},{10,11... | collective-permute-start | bytes 442376 | tf_op jit(solution)/shard_map/ppermute | solution.py:313
  99.7 5.7 %collective-permute-start.44 = (bf16[144,256]{1,0:T(8,128)(2,1)S(1)}, bf16[144,256]{1,0:T(8,128)(2,1)S(1)}, u32[]{:S(2)}, u32[]{:S(2)}) collective-permute-start(bf16[144,256]{1,0:T(8,128)(2,1)S(1)} %get-tuple-element.59), channel_id=1, source_target_pairs={{0,2},{1,3},{2,0},{3,1},{4,6},{5,7},{6,4},{7,5},{8,10},{9,11},{10,... | collective-permute-start | bytes 221192 | tf_op jit(solution)/shard_map/ppermute | solution.py:313
  101.9 14.2 %collective-permute-start.41 = (bf16[144,512]{1,0:T(8,128)(2,1)S(1)}, bf16[144,512]{1,0:T(8,128)(2,1)S(1)}, u32[]{:S(2)}, u32[]{:S(2)}) collective-permute-start(bf16[144,512]{1,0:T(8,128)(2,1)S(1)} %get-tuple-element.55), channel_id=1, source_target_pairs={{0,2},{1,3},{2,0},{3,1},{4,6},{5,7},{6,4},{7,5},{8,10},{9,11},{10,... | collective-permute-start | bytes 442376 | tf_op jit(solution)/shard_map/ppermute | solution.py:313
  102.5 14.7 %collective-permute-start.42 = (bf16[144,512]{1,0:T(8,128)(2,1)S(1)}, bf16[144,512]{1,0:T(8,128)(2,1)S(1)}, u32[]{:S(2)}, u32[]{:S(2)}) collective-permute-start(bf16[144,512]{1,0:T(8,128)(2,1)S(1)} %get-tuple-element.56), channel_id=1, source_target_pairs={{0,3},{1,2},{2,1},{3,0},{4,7},{5,6},{6,5},{7,4},{8,11},{9,10},{10,... | collective-permute-start | bytes 442376 | tf_op jit(solution)/shard_map/ppermute | solution.py:313
  104.9 13.0 %collective-permute-start.34 = (bf16[144,512]{1,0:T(8,128)(2,1)S(1)}, bf16[144,512]{1,0:T(8,128)(2,1)S(1)}, u32[]{:S(2)}, u32[]{:S(2)}) collective-permute-start(bf16[144,512]{1,0:T(8,128)(2,1)S(1)} %get-tuple-element.50), channel_id=1, source_target_pairs={{0,1},{1,0},{2,3},{3,2},{4,5},{5,4},{6,7},{7,6},{8,9},{9,8},{10,11... | collective-permute-start | bytes 442376 | tf_op jit(solution)/shard_map/ppermute | solution.py:313
  105.5 8.2 %collective-permute-start.45 = (bf16[144,256]{1,0:T(8,128)(2,1)S(1)}, bf16[144,256]{1,0:T(8,128)(2,1)S(1)}, u32[]{:S(2)}, u32[]{:S(2)}) collective-permute-start(bf16[144,256]{1,0:T(8,128)(2,1)S(1)} %get-tuple-element.60), channel_id=1, source_target_pairs={{0,3},{1,2},{2,1},{3,0},{4,7},{5,6},{6,5},{7,4},{8,11},{9,10},{10,... | collective-permute-start | bytes 221192 | tf_op jit(solution)/shard_map/ppermute | solution.py:313
  113.6 10.1 %collective-permute-start.35 = (bf16[144,512]{1,0:T(8,128)(2,1)S(1)}, bf16[144,512]{1,0:T(8,128)(2,1)S(1)}, u32[]{:S(2)}, u32[]{:S(2)}) collective-permute-start(bf16[144,512]{1,0:T(8,128)(2,1)S(1)} %get-tuple-element.51), channel_id=1, source_target_pairs={{0,2},{1,3},{2,0},{3,1},{4,6},{5,7},{6,4},{7,5},{8,10},{9,11},{10,... | collective-permute-start | bytes 442376 | tf_op jit(solution)/shard_map/ppermute | solution.py:313
  114.4 10.7 %collective-permute-start.36 = (bf16[144,512]{1,0:T(8,128)(2,1)S(1)}, bf16[144,512]{1,0:T(8,128)(2,1)S(1)}, u32[]{:S(2)}, u32[]{:S(2)}) collective-permute-start(bf16[144,512]{1,0:T(8,128)(2,1)S(1)} %get-tuple-element.52), channel_id=1, source_target_pairs={{0,3},{1,2},{2,1},{3,0},{4,7},{5,6},{6,5},{7,4},{8,11},{9,10},{10,... | collective-permute-start | bytes 442376 | tf_op jit(solution)/shard_map/ppermute | solution.py:313
  116.1 9.8 %collective-permute-start.29 = (bf16[144,512]{1,0:T(8,128)(2,1)S(1)}, bf16[144,512]{1,0:T(8,128)(2,1)S(1)}, u32[]{:S(2)}, u32[]{:S(2)}) collective-permute-start(bf16[144,512]{1,0:T(8,128)(2,1)S(1)} %get-tuple-element.46), channel_id=1, source_target_pairs={{0,1},{1,0},{2,3},{3,2},{4,5},{5,4},{6,7},{7,6},{8,9},{9,8},{10,11... | collective-permute-start | bytes 442376 | tf_op jit(solution)/shard_map/ppermute | solution.py:313
  117.1 11.9 %collective-permute-start.30 = (bf16[144,512]{1,0:T(8,128)(2,1)S(1)}, bf16[144,512]{1,0:T(8,128)(2,1)S(1)}, u32[]{:S(2)}, u32[]{:S(2)}) collective-permute-start(bf16[144,512]{1,0:T(8,128)(2,1)S(1)} %get-tuple-element.47), channel_id=1, source_target_pairs={{0,2},{1,3},{2,0},{3,1},{4,6},{5,7},{6,4},{7,5},{8,10},{9,11},{10,... | collective-permute-start | bytes 442376 | tf_op jit(solution)/shard_map/ppermute | solution.py:313
  117.9 11.1 %collective-permute-start.31 = (bf16[144,512]{1,0:T(8,128)(2,1)S(1)}, bf16[144,512]{1,0:T(8,128)(2,1)S(1)}, u32[]{:S(2)}, u32[]{:S(2)}) collective-permute-start(bf16[144,512]{1,0:T(8,128)(2,1)S(1)} %get-tuple-element.48), channel_id=1, source_target_pairs={{0,3},{1,2},{2,1},{3,0},{4,7},{5,6},{6,5},{7,4},{8,11},{9,10},{10,... | collective-permute-start | bytes 442376 | tf_op jit(solution)/shard_map/ppermute | solution.py:313
  123.7 6.7 %collective-permute-start.25 = (bf16[144,256]{1,0:T(8,128)(2,1)S(1)}, bf16[144,256]{1,0:T(8,128)(2,1)S(1)}, u32[]{:S(2)}, u32[]{:S(2)}) collective-permute-start(bf16[144,256]{1,0:T(8,128)(2,1)S(1)} %get-tuple-element.42), channel_id=1, source_target_pairs={{0,1},{1,0},{2,3},{3,2},{4,5},{5,4},{6,7},{7,6},{8,9},{9,8},{10,11... | collective-permute-start | bytes 221192 | tf_op jit(solution)/shard_map/ppermute | solution.py:313
  125.1 5.3 %collective-permute-start.26 = (bf16[144,256]{1,0:T(8,128)(2,1)S(1)}, bf16[144,256]{1,0:T(8,128)(2,1)S(1)}, u32[]{:S(2)}, u32[]{:S(2)}) collective-permute-start(bf16[144,256]{1,0:T(8,128)(2,1)S(1)} %get-tuple-element.43), channel_id=1, source_target_pairs={{0,2},{1,3},{2,0},{3,1},{4,6},{5,7},{6,4},{7,5},{8,10},{9,11},{10,... | collective-permute-start | bytes 221192 | tf_op jit(solution)/shard_map/ppermute | solution.py:313
  126.0 5.3 %collective-permute-start.27 = (bf16[144,256]{1,0:T(8,128)(2,1)S(1)}, bf16[144,256]{1,0:T(8,128)(2,1)S(1)}, u32[]{:S(2)}, u32[]{:S(2)}) collective-permute-start(bf16[144,256]{1,0:T(8,128)(2,1)S(1)} %get-tuple-element.44), channel_id=1, source_target_pairs={{0,3},{1,2},{2,1},{3,0},{4,7},{5,6},{6,5},{7,4},{8,11},{9,10},{10,... | collective-permute-start | bytes 221192 | tf_op jit(solution)/shard_map/ppermute | solution.py:313
  (10 other events, 125.8 us)
